TPU v7x, 32 devices: a whole 2x2x4 slice. The times are simulated.
32 devices in a mesh: leaf: 8 (over z, y), front: 4 (over x, core).
Axes of the slice: x: 2, y: 2, z: 4, core: 2. Of those that a mesh axis runs over, the one named last changes fastest.
Arguments:
- rhs_local: float32 [256, 256, 256], P(('leaf', 'front')), may hold values from -6 to 6
- dinv_local: float32 [256, 256, 256], P(('leaf', 'front')), may hold values from -1 to 2
- update_local: float32 [256, 256, 256], P(('leaf', 'front')), may hold values from -0.25 to 0.25
- parent: int32 [256], P(('leaf', 'front')), may hold values from 1 to 8, as said below
- row_blocks: int32 [256, 256], P(('leaf', 'front')), may hold values from 0 to 255, each once within a row
- sep_rhs: float32 [2048, 256], P(('leaf', 'front')), may hold values from -6 to 6
- sep_dinv: float32 [2048, 256], P(('leaf', 'front')), may hold values from -1 to 2
- sep_coupling: float32 [2048, 256], P(('leaf', 'front')), may hold values from -2 to 1
Outputs:
- sol_local: float32 [256, 256, 256], P(('leaf', 'front'))
- sep_solution: float32 [2048, 256], P(('leaf', 'front'))
Inputs may be any that keep to these rules, and one draw needn't show every extreme that they name: parent_k is the position of supernode k's parent within the same block of 8, always greater than k; the value 8 names the block's separator. `row_blocks`: each row is a permutation of 0 .. 255.
All inputs are finite; a program needn't handle non-finite values.
Results may differ from a plain program's by a relative error of at most 0.00024.
Values sent between devices are 32-bit elements; how exact they have to be, the bound alone decides.
No kernel may reach another device: no remote copies, remote signals or barrier semaphores. Data moves between devices by JAX's collectives and lax.ppermute only.
A program may use at most 128 MiB of HBM per device.

v0:
```python
import jax
import jax.numpy as jnp
from jax import lax
from jax.sharding import PartitionSpec as P


def entering(part, axis, combine, identity, reverse):
    count = lax.axis_size(axis)
    place = lax.axis_index(axis)
    ahead = count - 1 - place if reverse else place
    gathered = jax.tree.map(lambda a: lax.all_gather(a, axis), part)
    state = jax.tree.map(lambda a, e: jnp.zeros_like(a) + jnp.asarray(e, a.dtype), part, identity)

    def one(lap, state):
        source = count - 1 - lap if reverse else lap
        return combine(
            state, jax.tree.map(lambda a: lax.dynamic_index_in_dim(a, source, 0, False), gathered)
        )

    return lax.fori_loop(0, ahead, one, state)


def matmul(left, right):
    return jnp.dot(left, right, preferred_element_type=jnp.float32, precision=lax.Precision.HIGHEST)


def matmul_t(left, right):
    return lax.dot_general(
        left,
        right,
        (((0,), (0,)), ((), ())),
        precision=lax.Precision.HIGHEST,
        preferred_element_type=jnp.float32,
    )


def compose_ahead(earlier, latter):
    return (matmul(latter[0], earlier[0]), matmul(latter[0], earlier[1]) + latter[1])


def compose_back(earlier, latter):
    return (matmul(earlier[0], latter[0]), matmul_t(latter[0], earlier[1]) + latter[1])


def forward_block(rhs_block, inverse, update, parent_block, row_index):
    count_nodes = rhs_block.shape[0]
    pending = jnp.zeros((count_nodes + 1,) + rhs_block.shape[1:], jnp.float32)
    finished_solution = jnp.zeros(rhs_block.shape, jnp.float32)

    def advance(step_no, state_pair):
        pending_rows, finished_rows = state_pair
        solved_node = matmul(inverse[step_no], rhs_block[step_no] - pending_rows[step_no])
        update_rows = jnp.take(matmul(update[step_no], solved_node), row_index[step_no], axis=0)
        pending_rows = pending_rows.at[parent_block[step_no]].add(update_rows)
        return (pending_rows, finished_rows.at[step_no].set(solved_node))

    pending, finished_solution = lax.fori_loop(
        0, count_nodes, advance, (pending, finished_solution)
    )
    return (finished_solution, pending[count_nodes])


def backward_block(finished_solution, inverse, update, parent_block, row_index, top_value):
    count_nodes = finished_solution.shape[0]
    known_rows = jnp.concatenate(
        [jnp.zeros(finished_solution.shape, jnp.float32), top_value[None]], axis=0
    )

    def retreat(step_no, known_state):
        node_pos = count_nodes - 1 - step_no
        parent_value = known_state[parent_block[node_pos]]
        placed = (
            jnp.zeros(parent_value.shape, jnp.float32).at[row_index[node_pos]].set(parent_value)
        )
        result = matmul_t(
            inverse[node_pos], finished_solution[node_pos] - matmul_t(update[node_pos], placed)
        )
        return known_state.at[node_pos].set(result)

    known_rows = lax.fori_loop(0, count_nodes, retreat, known_rows)
    return known_rows[:count_nodes]


def local(rhs_local, dinv_local, update_local, parent, row_blocks, sep_rhs, sep_dinv, sep_coupling):
    finished_solution, top_term = forward_block(
        rhs_local, dinv_local, update_local, parent, row_blocks
    )
    front_pos = lax.axis_index("front")
    share_rows = sep_rhs.shape[0]
    block_order = sep_dinv.shape[1]
    drive_share = sep_rhs - lax.psum_scatter(top_term, "front", scatter_dimension=0, tiled=True)
    coupling, drive_full = (
        lax.all_gather(sep_coupling, "front", axis=0, tiled=True),
        lax.all_gather(drive_share, "front", axis=0, tiled=True),
    )
    chain_map, drive_term = (
        lax.all_gather(-matmul(sep_dinv, coupling), "front", axis=0, tiled=True),
        lax.all_gather(matmul(sep_dinv, drive_full), "front", axis=0, tiled=True),
    )
    unit_map = jnp.eye(block_order, dtype=jnp.float32)
    previous = entering(
        (chain_map, drive_term),
        "leaf",
        compose_ahead,
        (unit_map, jnp.zeros_like(drive_term)),
        False,
    )[1]
    forward_top = matmul(chain_map, previous) + drive_term
    back_drive = -matmul_t(chain_map, forward_top)
    following = entering(
        (chain_map, back_drive), "leaf", compose_back, (unit_map, jnp.zeros_like(back_drive)), True
    )[1]
    residue = forward_top - following
    own_residue = lax.dynamic_slice_in_dim(residue, front_pos * share_rows, share_rows, 0)
    top_value = lax.psum(matmul_t(sep_dinv, own_residue), "front")
    sep_solution = lax.dynamic_slice_in_dim(top_value, front_pos * share_rows, share_rows, 0)
    sol_local = backward_block(
        finished_solution, dinv_local, update_local, parent, row_blocks, top_value
    )
    return (sol_local, sep_solution)


def solution(mesh):
    placed = (
        P(("leaf", "front"), None, None),
        P(("leaf", "front"), None, None),
        P(("leaf", "front"), None, None),
        P(("leaf", "front")),
        P(("leaf", "front"), None),
        P(("leaf", "front"), None),
        P(("leaf", "front"), None),
        P(("leaf", "front"), None),
    )
    return jax.shard_map(
        local,
        mesh=mesh,
        in_specs=placed,
        out_specs=(P(("leaf", "front"), None, None), P(("leaf", "front"), None)),
        check_vma=False,
    )
```

profile of v0, /device:TPU:0, one launch (start us, length us, event | category | flops | bytes accessed | tf_op | source)
XLA Modules:
  0.0 391.7 jit_solution(16533572137065074752)
XLA Ops:
  9.8 79.2 %while.59 = (s32[]{:T(128)}, f32[9,256,256]{2,1,0:T(8,128)S(1)}, f32[8,256,256]{2,1,0:T(8,128)}, s32[8]{0:T(128)S(1)}, s32[8,256]{1,0:T(8,128)}, /*index=5*/f32[...) while((s32[]{:T(128)}, f32[9,256,256]{2,1,0:T(8,128)S(1)}, ...), condition=%wide.region_3.4_spmd, body=%wide.region_0.3_spmd.sunk | while | flops 402984224 | bytes 3683810 | solution.py:57
  13.1 2.8 fusion.67
  23.0 2.8 fusion.67
  32.9 2.8 fusion.67
  42.8 2.8 fusion.67
  52.7 2.8 fusion.67
  62.6 2.8 fusion.67
  72.5 2.8 fusion.67
  82.4 2.8 fusion.67
  89.9 7.2 %all_gather.32 = f32[256,256]{1,0:T(8,128)S(1)} all-gather(f32[64,256]{1,0:T(8,128)S(1)} %copy-done.3), channel_id=1, replica_groups=mesh['leaf'=8,'front'=4] {'front'}, dimensions={0}, use_global_device_ids=true | all-gather | bytes 327680 | tf_op jit(solution)/shard_map/all_gather | solution.py:93
  97.3 6.3 %all_gather.33 = f32[256,256]{1,0:T(8,128)} all-gather(f32[64,256]{1,0:T(8,128)S(1)} %convolution_negate_fusion.1), channel_id=1, replica_groups=mesh['leaf'=8,'front'=4] {'front'}, dimensions={0}, use_global_device_ids=true | all-gather | bytes 327680 | tf_op jit(solution)/shard_map/all_gather | solution.py:97
  103.7 9.0 %reduce-scatter.2.cloned.1.call-done = f32[64,256]{1,0:T(8,128)} async-done(((f32[256,256]{1,0:T(8,128)}), f32[64,256]{1,0:T(8,128)}) %reduce-scatter.2.cloned.1.call-update) | async-done | bytes 65552 | tf_op jit(solution)/shard_map/reduce_scatter | solution.py:91
  113.5 5.8 %all_gather.36 = f32[256,256]{1,0:T(8,128)S(1)} all-gather(f32[64,256]{1,0:T(8,128)S(1)} %sub.46), channel_id=1, replica_groups=mesh['leaf'=8,'front'=4] {'front'}, dimensions={0}, use_global_device_ids=true | all-gather | bytes 327680 | tf_op jit(solution)/shard_map/all_gather | solution.py:94
  119.6 6.3 %all_gather.37 = f32[256,256]{1,0:T(8,128)} all-gather(f32[64,256]{1,0:T(8,128)S(1)} %convolution_bitcast_fusion.2), channel_id=1, replica_groups=mesh['leaf'=8,'front'=4] {'front'}, dimensions={0}, use_global_device_ids=true | all-gather | bytes 327680 | tf_op jit(solution)/shard_map/all_gather | solution.py:98
  126.0 28.4 %all-gather.7.cloned.1.call-done = f32[2048,256]{1,0:T(8,128)} async-done(((f32[256,256]{1,0:T(8,128)}), f32[2048,256]{1,0:T(8,128)}) %all-gather.7.cloned.1.call-update) | async-done | bytes 2097168 | tf_op jit(solution)/shard_map/all_gather | solution.py:11
  154.4 49.9 %all-gather.9.cloned.1.call-done = f32[2048,256]{1,0:T(8,128)} async-done(((f32[256,256]{1,0:T(8,128)}), f32[2048,256]{1,0:T(8,128)}) %all-gather.9.cloned.1.call-update) | async-done | bytes 2097168 | tf_op jit(solution)/shard_map/all_gather | solution.py:11
  207.2 57.1 %all-gather.11.cloned.1.call-done = f32[2048,256]{1,0:T(8,128)} async-done(((f32[256,256]{1,0:T(8,128)}), f32[2048,256]{1,0:T(8,128)}) %all-gather.11.cloned.1.call-update) | async-done | bytes 2097168 | tf_op jit(solution)/shard_map/all_gather | solution.py:11
  264.3 11.9 %while.61 = (s32[]{:T(128)}, f32[256,256]{1,0:T(8,128)S(1)}, s32[]{:T(128)}, f32[8,256,256]{2,1,0:T(8,128)}, f32[8,256,256]{2,1,0:T(8,128)}, /*index=5*/s32[]{:T(128)}, s32[]{:T(128)}, s32[]{:T(128)}, s32[]{:T(128)}) while((s32[]{:T(128)}, f32[256,256]{1,0:T(8,128)S(1)}, s32[]{:T(128)}, f32[8,256,256]{2,1,0:T(8,128)}, ...), condition=%wide.region_8.9_spmd, body=%wide.region_7.8_spmd.sunk | while | flops 201392128 | bytes 1574027 | solution.py:20
  277.4 29.3 %all-reduce.3.cloned.1.call-done = f32[256,256]{0,1:T(8,128)} async-done(((f32[256,256]{0,1:T(8,128)}), f32[256,256]{0,1:T(8,128)}) %all-reduce.3.cloned.1.call-update) | async-done | bytes 262160 | tf_op jit(solution)/shard_map/psum | solution.py:115
  309.7 72.8 %while.62 = (s32[]{:T(128)}, f32[9,256,256]{2,1,0:T(8,128)S(1)}, f32[8,256,256]{2,1,0:T(8,128)}, f32[8,256,256]{2,1,0:T(8,128)}, f32[8,256,256]{2,1,0:T(8,128)},...) while((s32[]{:T(128)}, f32[9,256,256]{2,1,0:T(8,128)S(1)}, ...), condition=%wide.region_13.14_spmd, body=%wide.region_10.13_spmd.sunk | while | flops 402785056 | bytes 2625843 | solution.py:80
  316.6 2.2 fusion.80
  343.9 2.2 fusion.80
  362.1 2.2 fusion.80
  371.2 2.2 fusion.80
  (165 shorter events, 115.3 us)
Async XLA Ops:
  8.0 89.1 %copy-start = (f32[64,256]{1,0:T(8,128)S(1)}, f32[64,256]{1,0:T(8,128)}, u32[]{:S(2)}) copy-start(f32[64,256]{1,0:T(8,128)} %param.28) | copy-start | bytes 196612
  8.0 104.7 %reduce-scatter.2.cloned.1.call-start = ((), (), s32[]{:S(2)}) async-start(), calls=%async_computation.1 | async-start | bytes 327680 | tf_op jit(solution)/shard_map/reduce_scatter | solution.py:91
  8.1 1.7 copy-start.5
  8.1 1.7 copy-start.6
  8.1 1.7 copy-start.7
  9.8 80.1 %copy-start.3 = (f32[64,256]{1,0:T(8,128)S(1)}, f32[64,256]{1,0:T(8,128)}, u32[]{:S(2)}) copy-start(f32[64,256]{1,0:T(8,128)} %param.29) | copy-start | bytes 196612
  89.1 23.6 %copy-start.4 = (f32[64,256]{1,0:T(8,128)S(1)}, f32[64,256]{1,0:T(8,128)}, u32[]{:S(2)}) copy-start(f32[64,256]{1,0:T(8,128)} %param.27) | copy-start | bytes 196612
  89.8 64.6 %all-gather.7.cloned.1.call-start = ((), (), s32[]{:S(2)}) async-start(), calls=%async_computation.3 | async-start | bytes 2359296 | tf_op jit(solution)/shard_map/all_gather | solution.py:11
  103.7 100.7 %all-gather.9.cloned.1.call-start = ((), (), s32[]{:S(2)}) async-start(), calls=%async_computation.4 | async-start | bytes 2359296 | tf_op jit(solution)/shard_map/all_gather | solution.py:11
  125.9 138.4 %all-gather.11.cloned.1.call-start = ((), (), s32[]{:S(2)}) async-start(), calls=%async_computation.5 | async-start | bytes 2359296 | tf_op jit(solution)/shard_map/all_gather | solution.py:11
  204.4 1.0 copy-start.1
  204.4 1.0 copy-start.2
  207.1 99.6 %all-reduce.3.cloned.1.call-start = ((), (), s32[]{:S(2)}) async-start(), calls=%async_computation.2 | async-start | bytes 524288 | tf_op jit(solution)/shard_map/psum | solution.py:115
Sparse Core Ops, SparseCore 0:
  89.9 22.7 reduce-scatter.1
  277.5 29.1 all-reduce.2
Sparse Core Ops, SparseCore 1:
  103.7 50.6 all-gather.6
  156.6 47.7 all-gather.8
  207.2 57.1 all-gather.10
where the time goes:
time: 394 us; the launch traced here: 392 us
  waiting for transfers between devices  174 us (44%)
  matrix products  78.4 us (20%)
  local copies, waits for them, and re-layouts  37.6 us (10%)
  other arithmetic  30.3 us (8%)
  loops' own time  29.8 us (8%)
  blocking collectives  25.6 us (6%)
  between operations  15.8 us (4%)
    all_gather x3, waiting for transfers between devices, entering(): gathered = jax.tree.map(lambda a: lax.all_gather(a, axis), part)  136 us
    dot_general x25, matrix products, matmul_t(): lax.dot_general(left, right, (((0,), (0,)), ((), ())), precision=lax.Prec...  44.3 us
    dot_general x19, matrix products, matmul(): jnp.dot(left, right, preferred_element_type=jnp.float32, precision=lax.Pr...  34.1 us
    psum x1, waiting for transfers between devices, local(): top_value = lax.psum(matmul_t(sep_dinv, own_residue), 'front')  29.3 us
    another operation x1, loops' own time, forward_block(): lax.fori_loop(0, count_nodes, advance, (pending, finished_solution))  15.5 us
    another operation x1, loops' own time, backward_block(): known_rows = lax.fori_loop(0, count_nodes, retreat, known_rows)  14 us
    another operation x16, other arithmetic  12.1 us
    scatter x8, local copies, waits for them, and re-layouts, retreat(): jnp.zeros(parent_value.shape, jnp.float32).at[row_index[node_pos]]  12 us
  transfers between devices with their start and end apart: 5, of which 5 were waited for; matrix products, arithmetic and copies ran while one was open for 0% of the time, Pallas kernels for 0%

commit v1 on v0

v1 whole, which is shorter than its diff:
```python
import jax
import jax.numpy as jnp
from jax import lax
from jax.experimental import pallas as pl
from jax.experimental.pallas import tpu as pltpu
from jax.sharding import PartitionSpec as P

F32 = jnp.float32
BF16 = jnp.bfloat16
NN = (((1,), (0,)), ((), ()))
NT = (((1,), (1,)), ((), ()))
TN = (((0,), (0,)), ((), ()))
VMEM_BYTES = 48 << 20
HALVES = 2


def split(x):
    high = x.astype(BF16)
    return high, (x - high.astype(F32)).astype(BF16)


def dot1(a, b, dims):
    return lax.dot_general(a, b, dims, preferred_element_type=F32)


def dot3(a, b, dims):
    return dot1(a[0], b[0], dims) + (dot1(a[0], b[1], dims) + dot1(a[1], b[0], dims))


def keep_split(ref, value):
    ref[0], ref[1] = split(value)


def pair(ref):
    return ref[0], ref[1]


def bit_of(axis, bit):
    return (lax.axis_index(axis) // (1 << bit)) % 2


def call(kernel, name, ins, outs, scratch=()):
    specs = [pl.BlockSpec(memory_space=space) for space, _ in ins]
    return pl.pallas_call(
        kernel,
        name=name,
        in_specs=specs,
        out_specs=tuple(pl.BlockSpec(memory_space=pltpu.VMEM) for _ in outs),
        out_shape=tuple(jax.ShapeDtypeStruct(*o) for o in outs),
        scratch_shapes=list(scratch),
        compiler_params=pltpu.CompilerParams(vmem_limit_bytes=VMEM_BYTES),
    )(*[a for _, a in ins])


V = pltpu.VMEM


def exchange(x, axis, bit):
    n = lax.axis_size(axis)
    return lax.ppermute(x, axis, [(i, i ^ (1 << bit)) for i in range(n)])


def forward_kernel(nodes, fronts, *refs):
    (parent, rows, sep, rhs_h, dinv_h, upd_h), refs = refs[:6], refs[6:]
    (solved, inv_hi, inv_lo, upd_hi, upd_lo, send, keep), refs = refs[:7], refs[7:]
    (rhs_v, dinv_v, upd_v, square), refs = refs[:4], refs[4:]
    accs, sems = refs[:HALVES], refs[HALVES]
    size, cols = rhs_v.shape[1:]
    width = cols // HALVES
    copies = []
    for k in range(nodes):
        group = [
            pltpu.make_async_copy(dinv_h.at[k], dinv_v.at[k], sems.at[0, k]),
            pltpu.make_async_copy(rhs_h.at[k], rhs_v.at[k], sems.at[1, k]),
            pltpu.make_async_copy(upd_h.at[k], upd_v.at[k], sems.at[2, k]),
        ]
        for c in group:
            c.start()
        copies.append(group)
    front = lax.axis_index("front")
    share = sep.shape[0]
    square[...] = jnp.zeros_like(square)
    square[pl.ds(pl.multiple_of(front * share, 8), share), :] = sep[...]
    turned = square[...].T
    for h in range(HALVES):
        accs[h][nodes] = turned[h * width : (h + 1) * width]
    row_columns = rows[...].astype(F32).T
    lane = lax.broadcasted_iota(jnp.int32, (size, size), 1).astype(F32)
    for k in range(nodes):
        for c in copies[k]:
            c.wait()
        inv_hi[k], inv_lo[k] = split(dinv_v[k])
        high, low = split(upd_v[k])
        chosen = (lane == row_columns[:, k : k + 1]).astype(BF16)
        upd_hi[k] = dot1(chosen, high, NN).astype(BF16)
        upd_lo[k] = dot1(chosen, low, NN).astype(BF16)
        turned = rhs_v[k].T
        for h in range(HALVES):
            accs[h][k] = turned[h * width : (h + 1) * width]
    for k in range(nodes):
        inverse = (inv_hi[k], inv_lo[k])
        update = (upd_hi[k], upd_lo[k])
        above = parent[k]
        for h in range(HALVES):
            value = dot3(split(accs[h][k]), inverse, NT)
            solved[k, h * width : (h + 1) * width] = value
            accs[h][above] = accs[h][above] - dot3(split(value), update, NT)
    chunk = cols // fronts
    for h in range(HALVES):
        square[h * width : (h + 1) * width] = accs[h][nodes]
    low_bit = front % 2
    for i in range(fronts // 2):
        for ref, own in ((keep, low_bit), (send, 1 - low_bit)):
            start = pl.multiple_of((2 * i + own) * chunk, 8)
            ref[i * chunk : (i + 1) * chunk] = square[pl.ds(start, chunk), :]


def local_forward(rhs, dinv, update, parent, rows, sep, fronts):
    nodes, size, cols = rhs.shape
    big = pltpu.VMEM((nodes, size, size), F32)
    half = (nodes, size, size)
    part = (cols // 2, size)
    return call(
        lambda *refs: forward_kernel(nodes, fronts, *refs),
        "local_forward",
        [(pltpu.SMEM, parent), (V, rows), (V, sep), (pl.ANY, rhs), (pl.ANY, dinv), (pl.ANY, update)],
        [(half, F32), (half, BF16), (half, BF16), (half, BF16), (half, BF16), (part, F32), (part, F32)],
        [pltpu.VMEM((nodes, size, cols), F32), big, big, pltpu.VMEM((size, cols), F32)]
        + [pltpu.VMEM((nodes + 1, cols // HALVES, size), F32)] * HALVES
        + [pltpu.SemaphoreType.DMA((3, nodes))],
    )


def backward_kernel(nodes, fronts, *refs):
    parent, solved, inv_hi, inv_lo, upd_hi, upd_lo = refs[:6]
    pieces = refs[6 : 6 + fronts]
    sol, sep_out = refs[6 + fronts : 8 + fronts]
    square = refs[8 + fronts]
    known = refs[9 + fronts :]
    front = lax.axis_index("front")
    chunk = pieces[0].shape[0]
    width = known[0].shape[1]
    for i in range(fronts):
        start = pl.multiple_of((front ^ i) * chunk, 8)
        square[pl.ds(start, chunk), :] = pieces[i][...]
    for h in range(HALVES):
        known[h][nodes] = square[h * width : (h + 1) * width]
    square[...] = square[...].T
    share = sep_out.shape[0]
    sep_out[...] = square[pl.ds(pl.multiple_of(front * share, 8), share), :]
    for k in reversed(range(nodes)):
        inverse = (inv_hi[k], inv_lo[k])
        update = (upd_hi[k], upd_lo[k])
        above = parent[k]
        for h in range(HALVES):
            rows = slice(h * width, (h + 1) * width)
            part = solved[k, rows] - dot3(split(known[h][above]), update, NN)
            value = dot3(split(part), inverse, NN)
            known[h][k] = value
            sol[k, :, rows] = value.T


def local_backward(parent, solved, inv_hi, inv_lo, upd_hi, upd_lo, pieces):
    nodes, cols, size = solved.shape
    fronts = len(pieces)
    return call(
        lambda *refs: backward_kernel(nodes, fronts, *refs),
        "local_backward",
        [(pltpu.SMEM, parent)]
        + [(V, a) for a in (solved, inv_hi, inv_lo, upd_hi, upd_lo)]
        + [(V, a) for a in pieces],
        [((nodes, size, cols), F32), ((size // fronts, cols), F32)],
        [pltpu.VMEM((size, cols), F32)]
        + [pltpu.VMEM((nodes + 1, cols // HALVES, size), F32)] * HALVES,
    )


def block_map_kernel(fronts, *refs):
    inverse_parts, coupling_parts = refs[:fronts], refs[fronts : 2 * fronts]
    total, inverse_halves, square = refs[2 * fronts :]
    front = lax.axis_index("front")
    share = inverse_parts[0].shape[0]
    for parts, slot in ((inverse_parts, 0), (coupling_parts, 1)):
        for i in range(fronts):
            start = pl.multiple_of((front ^ i) * share, 8)
            square[slot, pl.ds(start, share), :] = parts[i][...]
    inverse = split(square[0])
    inverse_halves[0], inverse_halves[1] = inverse
    total[...] = -dot3(inverse, split(square[1]), NN)


def block_map(inverse_parts, coupling_parts):
    fronts = len(inverse_parts)
    share, size = inverse_parts[0].shape
    return call(
        lambda *refs: block_map_kernel(fronts, *refs),
        "block_map",
        [(V, a) for a in (*inverse_parts, *coupling_parts)],
        [((size, size), F32), ((2, size, size), BF16)],
        [pltpu.VMEM((2, size, size), F32)],
    )


def first_merge_kernel(*refs):
    own, other, total, curve, mixed, halves, curve_u, total_u, total_l = refs
    upper = bit_of("leaf", 0) == 1
    low = jnp.where(upper, other[...], own[...])
    up = jnp.where(upper, own[...], other[...])
    low_s, up_s = split(low), split(up)
    for ref, value in ((total_u, up_s), (total_l, low_s)):
        ref[0], ref[1] = value
    k_up = dot3(up_s, up_s, TN)
    k_up_s = split(k_up)
    curve_u[0], curve_u[1] = k_up_s
    x = dot3(k_up_s, low_s, NN)
    t = dot3(up_s, low_s, NN)
    total[...] = t
    curve[...] = dot3(low_s, low_s, TN) + dot3(low_s, split(x), TN)
    size = low.shape[0]
    row = lax.broadcasted_iota(jnp.int32, (size, size), 0)
    col = lax.broadcasted_iota(jnp.int32, (size, size), 1)
    unit = (row == col).astype(F32)
    keep_split(halves, jnp.where(upper, up.T, unit))
    mixed[0] = jnp.where(upper, t, low + x)
    mixed[1] = jnp.where(upper, unit, up)


def merge_kernel(bit, last, *refs):
    own_t, own_k, other_t, other_k, mixed = refs[:5]
    upper = bit_of("leaf", bit) == 1
    total, curve, mixed_n, halves, curve_u, total_u, total_l = refs[5:]
    low_s = split(jnp.where(upper, other_t[...], own_t[...]))
    up_s = split(jnp.where(upper, own_t[...], other_t[...]))
    k_low = jnp.where(upper, other_k[...], own_k[...])
    k_up_s = split(jnp.where(upper, own_k[...], other_k[...]))
    for ref, value in ((total_u, up_s), (total_l, low_s), (curve_u, k_up_s)):
        ref[0], ref[1] = value
    x = dot3(k_up_s, low_s, NN)
    x_s = split(x)
    if not last:
        total[...] = dot3(up_s, low_s, NN)
    curve[...] = k_low + dot3(low_s, x_s, TN)
    a, e = mixed[0], mixed[1]
    keep_split(halves, jnp.where(upper, a.T, e))
    a_s, e_s = split(a), split(e)
    mixed_n[0] = jnp.where(upper, dot3(a_s, low_s, NN), a + dot3(e_s, x_s, TN))
    mixed_n[1] = jnp.where(upper, e, dot3(up_s, e_s, NN))


def maps(size):
    square, both = ((size, size), F32), ((2, size, size), BF16)
    return [square, square, ((2, size, size), F32), both, both, both, both]


def last_map_kernel(bit, mixed, other_k, halves, curve_u):
    upper = bit_of("leaf", bit) == 1
    keep_split(halves, jnp.where(upper, mixed[0].T, mixed[1]))
    keep_split(curve_u, other_k[...])


def fold_kernel(bit, own, other, send, keep):
    total = send.shape[0]
    chunk = total
    value = own[...] + other[...]
    first, second = value[:chunk], value[chunk:]
    high = bit_of("front", bit) == 1
    send[...] = jnp.where(high, first, second)
    keep[...] = jnp.where(high, second, first)


def enter_kernel(own, other, inverse, own_map, sol, message):
    drive = own[...] + other[...]
    value = dot3(split(drive), pair(inverse), NT)
    sol[...] = value
    rows = value.shape[0]
    message[:rows] = value
    message[rows:] = dot3(split(value), split(own_map[...]), NN)


def step_kernel(bit, last, *refs):
    sol, own, other, halves, curve_u, total_u, total_l, sol_n, message = refs
    upper = bit_of("leaf", bit) == 1
    rows = sol.shape[0]
    z_own, p_own, z_other, p_other = own[:rows], own[rows:], other[:rows], other[rows:]
    z_low = jnp.where(upper, z_other, z_own)
    z_up = jnp.where(upper, z_own, z_other)
    p_low = jnp.where(upper, p_other, p_own)
    p_up = jnp.where(upper, p_own, p_other)
    z_low_s = split(z_low)
    middle = p_up + dot3(z_low_s, pair(curve_u), NN)
    middle_s = split(middle)
    z_new = z_up + dot3(z_low_s, pair(total_u), NT)
    p_new = p_low + dot3(middle_s, pair(total_l), NN)
    given = split(jnp.where(upper, z_low, middle))
    sol_n[...] = sol[...] + dot3(given, pair(halves), NN)
    if last:
        upper_next = bit_of("leaf", bit + 1) == 1
        message[0] = jnp.where(upper_next, p_new, z_new)
        message[1] = z_new
    else:
        message[:rows] = z_new
        message[rows:] = p_new


def leave_kernel(bit, sol, own_z, other, halves, curve_u, inverse, top):
    upper = bit_of("leaf", bit) == 1
    came = other[...]
    middle = came + dot3(split(own_z[...]), pair(curve_u), NN)
    given = split(jnp.where(upper, came, middle))
    value = sol[...] + dot3(given, pair(halves), NN)
    top[...] = dot3(split(value), pair(inverse), NN)


def gather_front(x, bits):
    pieces = {0: x}
    for bit in reversed(range(bits)):
        for i in list(pieces):
            pieces[i | (1 << bit)] = exchange(pieces[i], "front", bit)
    return [pieces[i] for i in range(1 << bits)]


def local(rhs_local, dinv_local, update_local, parent, row_blocks, sep_rhs, sep_dinv, sep_coupling):
    fronts, leaves = lax.axis_size("front"), lax.axis_size("leaf")
    front_bits, rounds = fronts.bit_length() - 1, leaves.bit_length() - 1
    size = sep_dinv.shape[1]
    cols = sep_rhs.shape[1]
    chunk = cols // fronts

    inverse_parts = gather_front(sep_dinv, front_bits)
    coupling_parts = gather_front(sep_coupling, front_bits)
    own_map, inverse = block_map(inverse_parts, coupling_parts)

    solved, inv_hi, inv_lo, upd_hi, upd_lo, send, keep = local_forward(
        rhs_local, dinv_local, update_local, parent, row_blocks, sep_rhs, fronts
    )

    other_map = exchange(own_map, "leaf", 0)
    square = maps(size)
    total, curve, mixed, *tools = call(
        first_merge_kernel, "merge_0", [(V, own_map), (V, other_map)], square
    )
    steps = [tools]
    for bit in range(1, rounds - 1):
        other_t, other_k = exchange(total, "leaf", bit), exchange(curve, "leaf", bit)
        total, curve, mixed, *tools = call(
            lambda *refs, bit=bit: merge_kernel(bit, bit == rounds - 2, *refs),
            f"merge_{bit}",
            [(V, a) for a in (total, curve, other_t, other_k, mixed)],
            square,
        )
        steps.append(tools)
    other_k = exchange(curve, "leaf", rounds - 1)
    last_halves, last_curve = call(
        lambda *refs: last_map_kernel(rounds - 1, *refs),
        "merge_last",
        [(V, mixed), (V, other_k)],
        [((2, size, size), BF16)] * 2,
    )

    for bit in range(front_bits):
        received = exchange(send, "front", bit)
        if bit + 1 < front_bits:
            half = ((keep.shape[0] // 2, size), F32)
            send, keep = call(
                lambda *refs, bit=bit: fold_kernel(bit + 1, *refs),
                "fold",
                [(V, keep), (V, received)],
                [half, half],
            )
    sol, message = call(
        enter_kernel,
        "enter",
        [(V, keep), (V, received), (V, inverse), (V, own_map)],
        [((chunk, size), F32), ((2 * chunk, size), F32)],
    )
    for bit in range(rounds - 1):
        received = exchange(message, "leaf", bit)
        last = bit == rounds - 2
        shape = (2, chunk, size) if last else (2 * chunk, size)
        sol, message = call(
            lambda *refs, bit=bit, last=last: step_kernel(bit, last, *refs),
            f"step_{bit}",
            [(V, a) for a in (sol, message, received, *steps[bit])],
            [((chunk, size), F32), (shape, F32)],
        )
    received = exchange(message[0], "leaf", rounds - 1)
    (top,) = call(
        lambda *refs: leave_kernel(rounds - 1, *refs),
        "leave",
        [(V, a) for a in (sol, message[1], received, last_halves, last_curve, inverse)],
        [((chunk, size), F32)],
    )
    pieces = gather_front(top, front_bits)
    sol_local, sep_solution = local_backward(
        parent, solved, inv_hi, inv_lo, upd_hi, upd_lo, pieces
    )
    return (sol_local, sep_solution)


def solution(mesh):
    spread3 = P(("leaf", "front"), None, None)
    spread2 = P(("leaf", "front"), None)
    spread1 = P(("leaf", "front"))
    return jax.shard_map(
        local,
        mesh=mesh,
        in_specs=(spread3, spread3, spread3, spread1, spread2, spread2, spread2, spread2),
        out_specs=(spread3, spread2),
        check_vma=False,
    )
```

time: 394 us -> 75 us (0.19)
  waiting for transfers between devices: 174 us -> 32.7 us
  matrix products: 78.4 us -> 0 us
  local copies, waits for them, and re-layouts: 37.6 us -> 3.89 us
  other arithmetic: 30.3 us -> 0 us
  loops' own time: 29.8 us -> 0 us
  blocking collectives: 25.6 us -> 0 us
  Pallas kernels: 0 us -> 21 us
  starting transfers between devices: 0.21 us -> 16.4 us
  between operations: 15.8 us -> 0.75 us
    all_gather x3 -> x0, waiting for transfers between devices: 136 us -> none  [entering(): gathered = jax.tree.map(lambda a: lax.all_gather(a, axis), part)]
    dot_general x44 -> x0, matrix products: 78.4 us -> none  [the longest x25 44.3 us: matmul_t(): lax.dot_general(left, right, (((0,), (0,)), ((), ())), precision=lax.Prec...]
    ppermute x0 -> x18, waiting for transfers between devices: none -> 32.7 us  [exchange(): return lax.ppermute(x, axis, [(i, i ^ 1 << bit) for i in range(n)])]
    another operation x4 -> x0, loops' own time: 29.8 us -> none  [the longest x1 15.5 us: forward_block(): lax.fori_loop(0, count_nodes, advance, (pending, finished_solution))]
    psum x1 -> x0, waiting for transfers between devices: 29.3 us -> none  [local(): top_value = lax.psum(matmul_t(sep_dinv, own_residue), 'front')]
    all_gather x4 -> x0, blocking collectives: 25.6 us -> none  [the longest x1 7.19 us: local(): lax.all_gather(sep_coupling, 'front', axis=0, tiled=True)]
    pallas_call x0 -> x11, Pallas kernels: none -> 21 us  [call(): pl.pallas_call(kernel, name=name, in_specs=specs, out_specs=tuple((pl.Blo...]
    ppermute x0 -> x18, starting transfers between devices: none -> 16.4 us  [exchange(): return lax.ppermute(x, axis, [(i, i ^ 1 << bit) for i in range(n)])]
  transfers between devices with their start and end apart: 5 -> 18, of which waited for: 5 -> 12; matrix products, arithmetic and copies ran while one was open for 0% -> 0% of each run, Pallas kernels for 0% -> 18%
where the time goes in v1:
time: 75 us; the launch traced here: 74.7 us
  waiting for transfers between devices  32.7 us (44%)
  Pallas kernels  21 us (28%)
  starting transfers between devices  16.4 us (22%)
  local copies, waits for them, and re-layouts  3.89 us (5%)
  between operations  0.75 us (1%)
    ppermute x18, waiting for transfers between devices, exchange(): return lax.ppermute(x, axis, [(i, i ^ 1 << bit) for i in range(n)])  32.7 us
    pallas_call x11, Pallas kernels, call(): pl.pallas_call(kernel, name=name, in_specs=specs, out_specs=tuple((pl.Blo...  21 us
    ppermute x18, starting transfers between devices, exchange(): return lax.ppermute(x, axis, [(i, i ^ 1 << bit) for i in range(n)])  16.4 us
    unnamed x12, local copies, waits for them, and re-layouts  3.87 us
  transfers between devices with their start and end apart: 18, of which 12 were waited for; matrix products, arithmetic and copies ran while one was open for 0% of the time, Pallas kernels for 18%

profile of v1, /device:TPU:0, one launch (start us, length us, event | category | flops | bytes accessed | tf_op | source)
XLA Modules:
  0.0 74.7 jit_solution(7295245454690660895)
XLA Ops:
  0.6 3.0 %collective-permute-start.3 = (f32[64,256]{1,0:T(8,128)}, f32[64,256]{1,0:T(8,128)S(1)}, u32[]{:S(2)}, u32[]{:S(2)}) collective-permute-start(f32[64,256]{1,0:T(8,128)} %refs_0_.4), channel_id=1, source_target_pairs={{0,2},{1,3},{2,0},{3,1},{4,6},{5,7},{6,4},{7,5},{8,10},{9,11},{10,... | collective-permute-start | bytes 196616 | tf_op jit(solution)/shard_map/ppermute | solution.py:60
  4.2 2.0 %collective-permute-done.3.refs_2_ = f32[64,256]{1,0:T(8,128)S(1)} collective-permute-done((f32[64,256]{1,0:T(8,128)}, f32[64,256]{1,0:T(8,128)S(1)}, u32[]{:S(2)}, u32[]{:S(2)}) %collective-permute-start.3) | collective-permute-done | bytes 65568 | tf_op jit(solution)/shard_map/ppermute | solution.py:60
  6.2 1.9 %collective-permute-done.6.refs_6_ = f32[64,256]{1,0:T(8,128)S(1)} collective-permute-done((f32[64,256]{1,0:T(8,128)}, f32[64,256]{1,0:T(8,128)S(1)}, u32[]{:S(2)}, u32[]{:S(2)}) %collective-permute-start.6) | collective-permute-done | bytes 65568 | tf_op jit(solution)/shard_map/ppermute | solution.py:60
  8.1 1.2 %collective-permute-done.7.refs_7_ = f32[64,256]{1,0:T(8,128)S(1)} collective-permute-done((f32[64,256]{1,0:T(8,128)S(1)}, f32[64,256]{1,0:T(8,128)S(1)}, u32[]{:S(2)}, u32[]{:S(2)}) %collective-permute-start.7) | collective-permute-done | bytes 65568 | tf_op jit(solution)/shard_map/ppermute | solution.py:60
  9.4 0.8 %copy-done.1 = f32[64,256]{1,0:T(8,128)S(1)} copy-done((f32[64,256]{1,0:T(8,128)S(1)}, f32[64,256]{1,0:T(8,128)}, u32[]{:S(2)}) %copy-start.1) | copy-done | bytes 65560
  10.2 0.8 %copy-done.2 = f32[64,256]{1,0:T(8,128)S(1)} copy-done((f32[64,256]{1,0:T(8,128)S(1)}, f32[64,256]{1,0:T(8,128)}, u32[]{:S(2)}) %copy-start.2) | copy-done | bytes 65560
  11.4 1.6 %collective-permute-start.9 = (f32[256,256]{1,0:T(8,128)S(1)}, f32[256,256]{1,0:T(8,128)S(1)}, u32[]{:S(2)}, u32[]{:S(2)}) collective-permute-start(f32[256,256]{1,0:T(8,128)S(1)} %get-tuple-element.44.own_map.refs_0_), channel_id=1, source_target_pairs={{0,4},{4,0},{8,12},{12,8},{16,20},{20,16},{24,28},{28,24},{1,5},{5... | collective-permute-start | bytes 786440 | tf_op jit(solution)/shard_map/ppermute | solution.py:60
  15.1 10.2 %local_forward.1 = (f32[8,256,256]{2,1,0:T(8,128)}, bf16[8,256,256]{2,1,0:T(8,128)(2,1)S(1)}, bf16[8,256,256]{2,1,0:T(8,128)(2,1)S(1)}, bf16[8,256,256]{2,1,0:T(...) custom-call(s32[8]{0:T(128)S(1)} %copy-done.4, ...), custom_call_target="tpu_custom_call" | custom-call | tf_op jit(solution)/shard_map/local_forward/pallas_call | solution.py:44
  25.4 1.3 %collective-permute-done.refs_1_ = f32[128,256]{1,0:T(8,128)S(1)} collective-permute-done((f32[128,256]{1,0:T(8,128)S(1)}, f32[128,256]{1,0:T(8,128)S(1)}, u32[]{:S(2)}, u32[]{:S(2)}) %collective-permute-start) | collective-permute-done | bytes 131104 | tf_op jit(solution)/shard_map/ppermute | solution.py:60
  26.8 1.0 %collective-permute-start.1 = (f32[64,256]{1,0:T(8,128)S(1)}, f32[64,256]{1,0:T(8,128)S(1)}, u32[]{:S(2)}, u32[]{:S(2)}) collective-permute-start(f32[64,256]{1,0:T(8,128)S(1)} %get-tuple-element.42), channel_id=1, source_target_pairs={{0,2},{1,3},{2,0},{3,1},{4,6},{5,7},{6,4},{7,5},{8,10},{9,11},{10,... | collective-permute-start | bytes 196616 | tf_op jit(solution)/shard_map/ppermute | solution.py:60
  27.8 3.3 %collective-permute-done.1.other = f32[64,256]{1,0:T(8,128)S(1)} collective-permute-done((f32[64,256]{1,0:T(8,128)S(1)}, f32[64,256]{1,0:T(8,128)S(1)}, u32[]{:S(2)}, u32[]{:S(2)}) %collective-permute-start.1) | collective-permute-done | bytes 65568 | tf_op jit(solution)/shard_map/ppermute | solution.py:60
  32.1 1.0 %merge_0.1 = (f32[256,256]{1,0:T(8,128)S(1)}, f32[256,256]{1,0:T(8,128)S(1)}, f32[2,256,256]{2,1,0:T(8,128)S(1)}, bf16[2,256,256]{2,1,0:T(8,128)(2,1)S(1)}, bf16...) custom-call(f32[256,256]{1,0:T(8,128)S(1)} %get-tuple-element.44.own_map.refs_0_, ...), custom_call_target="tpu_custom_call" | custom-call | tf_op jit(solution)/shard_map/merge_0/pallas_call | solution.py:44
  33.1 1.6 %collective-permute-start.11 = (f32[256,256]{1,0:T(8,128)S(1)}, f32[256,256]{1,0:T(8,128)S(1)}, u32[]{:S(2)}, u32[]{:S(2)}) collective-permute-start(f32[256,256]{1,0:T(8,128)S(1)} %get-tuple-element.53.refs_0_), channel_id=1, source_target_pairs={{0,8},{4,12},{8,0},{12,4},{16,24},{20,28},{24,16},{28,20},{1,9},{5... | collective-permute-start | bytes 786440 | tf_op jit(solution)/shard_map/ppermute | solution.py:60
  35.2 1.3 %collective-permute-done.8.refs_2_ = f32[128,256]{1,0:T(8,128)S(1)} collective-permute-done((f32[128,256]{1,0:T(8,128)S(1)}, f32[128,256]{1,0:T(8,128)S(1)}, u32[]{:S(2)}, u32[]{:S(2)}) %collective-permute-start.8) | collective-permute-done | bytes 131104 | tf_op jit(solution)/shard_map/ppermute | solution.py:60
  37.1 1.6 %collective-permute-start.10 = (f32[128,256]{1,0:T(8,128)S(1)}, f32[128,256]{1,0:T(8,128)S(1)}, u32[]{:S(2)}, u32[]{:S(2)}) collective-permute-start(f32[128,256]{1,0:T(8,128)S(1)} %get-tuple-element.52.refs_1_), channel_id=1, source_target_pairs={{0,8},{4,12},{8,0},{12,4},{16,24},{20,28},{24,16},{28,20},{1,9},{5... | collective-permute-start | bytes 393224 | tf_op jit(solution)/shard_map/ppermute | solution.py:60
  38.7 3.7 %collective-permute-done.11.refs_2_ = f32[256,256]{1,0:T(8,128)S(1)} collective-permute-done((f32[256,256]{1,0:T(8,128)S(1)}, f32[256,256]{1,0:T(8,128)S(1)}, u32[]{:S(2)}, u32[]{:S(2)}) %collective-permute-start.11) | collective-permute-done | bytes 262176 | tf_op jit(solution)/shard_map/ppermute | solution.py:60
  42.4 4.7 %collective-permute-done.12.refs_3_ = f32[256,256]{1,0:T(8,128)S(1)} collective-permute-done((f32[256,256]{1,0:T(8,128)S(1)}, f32[256,256]{1,0:T(8,128)S(1)}, u32[]{:S(2)}, u32[]{:S(2)}) %collective-permute-start.12) | collective-permute-done | bytes 262176 | tf_op jit(solution)/shard_map/ppermute | solution.py:60
  48.0 2.8 %collective-permute-start.14 = (f32[256,256]{1,0:T(8,128)S(1)}, f32[256,256]{1,0:T(8,128)S(1)}, u32[]{:S(2)}, u32[]{:S(2)}) collective-permute-start(f32[256,256]{1,0:T(8,128)S(1)} %get-tuple-element.63), channel_id=1, source_target_pairs={{0,16},{4,20},{8,24},{12,28},{16,0},{20,4},{24,8},{28,12},{1,17},{... | collective-permute-start | bytes 786440 | tf_op jit(solution)/shard_map/ppermute | solution.py:60
  51.3 1.9 %collective-permute-start.13 = (f32[64,256]{1,0:T(8,128)S(1)}, f32[64,256]{1,0:T(8,128)S(1)}, u32[]{:S(2)}, u32[]{:S(2)}) collective-permute-start(f32[64,256]{1,0:T(8,128)S(1)} %get-tuple-element.66), channel_id=1, source_target_pairs={{0,16},{4,20},{8,24},{12,28},{16,0},{20,4},{24,8},{28,12},{1,17},{... | collective-permute-start | bytes 196616 | tf_op jit(solution)/shard_map/ppermute | solution.py:60
  53.3 8.1 %collective-permute-done.14.refs_1_ = f32[256,256]{1,0:T(8,128)S(1)} collective-permute-done((f32[256,256]{1,0:T(8,128)S(1)}, f32[256,256]{1,0:T(8,128)S(1)}, u32[]{:S(2)}, u32[]{:S(2)}) %collective-permute-start.14) | collective-permute-done | bytes 262176 | tf_op jit(solution)/shard_map/ppermute | solution.py:60
  62.6 1.0 %collective-permute-start.16 = (f32[64,256]{1,0:T(8,128)S(1)}, f32[64,256]{1,0:T(8,128)S(1)}, u32[]{:S(2)}, u32[]{:S(2)}) collective-permute-start(f32[64,256]{1,0:T(8,128)S(1)} %leave.1.refs_6_), channel_id=1, source_target_pairs={{0,2},{1,3},{2,0},{3,1},{4,6},{5,7},{6,4},{7,5},{8,10},{9,11},{10,... | collective-permute-start | bytes 196616 | tf_op jit(solution)/shard_map/ppermute | solution.py:60
  63.7 3.3 %collective-permute-done.16.refs_8_ = f32[64,256]{1,0:T(8,128)S(1)} collective-permute-done((f32[64,256]{1,0:T(8,128)S(1)}, f32[64,256]{1,0:T(8,128)S(1)}, u32[]{:S(2)}, u32[]{:S(2)}) %collective-permute-start.16) | collective-permute-done | bytes 65568 | tf_op jit(solution)/shard_map/ppermute | solution.py:60
  67.0 1.2 %collective-permute-done.17.refs_9_ = f32[64,256]{1,0:T(8,128)S(1)} collective-permute-done((f32[64,256]{1,0:T(8,128)S(1)}, f32[64,256]{1,0:T(8,128)S(1)}, u32[]{:S(2)}, u32[]{:S(2)}) %collective-permute-start.17) | collective-permute-done | bytes 65568 | tf_op jit(solution)/shard_map/ppermute | solution.py:60
  68.2 6.5 %local_backward.1 = (f32[8,256,256]{2,1,0:T(8,128)}, f32[64,256]{1,0:T(8,128)}) custom-call(s32[8]{0:T(128)S(1)} %copy-done.5, f32[8,256,256]{2,1,0:T(8,128)} %get-tuple-element.34.refs_1_, bf16[8,256,256]{2,1,0:T(8,128)(2,1)S(1)} %get-tuple-element.35.refs_2_, bf16[8,256,256]{2,1,0:T(8,128)(2,1)S(1)} %get-tuple-element.36.refs_3_, ...), custom_call_target="tpu_custom_call" | custom-call | tf_op jit(solution)/shard_map/local_backward/pallas_call | solution.py:44
  (36 shorter events, 7.8 us)
Async XLA Ops:
  0.6 5.6 %collective-permute-start.3 = (f32[64,256]{1,0:T(8,128)}, f32[64,256]{1,0:T(8,128)S(1)}, u32[]{:S(2)}, u32[]{:S(2)}) collective-permute-start(f32[64,256]{1,0:T(8,128)} %refs_0_.4), channel_id=1, source_target_pairs={{0,2},{1,3},{2,0},{3,1},{4,6},{5,7},{6,4},{7,5},{8,10},{9,11},{10,... | collective-permute-start | bytes 196616 | tf_op jit(solution)/shard_map/ppermute | solution.py:60
  3.6 4.5 %collective-permute-start.6 = (f32[64,256]{1,0:T(8,128)}, f32[64,256]{1,0:T(8,128)S(1)}, u32[]{:S(2)}, u32[]{:S(2)}) collective-permute-start(f32[64,256]{1,0:T(8,128)} %refs_4_.3), channel_id=1, source_target_pairs={{0,2},{1,3},{2,0},{3,1},{4,6},{5,7},{6,4},{7,5},{8,10},{9,11},{10,... | collective-permute-start | bytes 196616 | tf_op jit(solution)/shard_map/ppermute | solution.py:60
  3.7 4.4 %collective-permute-start.2 = (f32[64,256]{1,0:T(8,128)}, f32[64,256]{1,0:T(8,128)S(1)}, u32[]{:S(2)}, u32[]{:S(2)}) collective-permute-start(f32[64,256]{1,0:T(8,128)} %refs_0_.4), channel_id=1, source_target_pairs={{0,1},{1,0},{2,3},{3,2},{4,5},{5,4},{6,7},{7,6},{8,9},{9,8},{10,11... | collective-permute-start | bytes 196616 | tf_op jit(solution)/shard_map/ppermute | solution.py:60
  3.7 4.4 %collective-permute-start.5 = (f32[64,256]{1,0:T(8,128)}, f32[64,256]{1,0:T(8,128)S(1)}, u32[]{:S(2)}, u32[]{:S(2)}) collective-permute-start(f32[64,256]{1,0:T(8,128)} %refs_4_.3), channel_id=1, source_target_pairs={{0,1},{1,0},{2,3},{3,2},{4,5},{5,4},{6,7},{7,6},{8,9},{9,8},{10,11... | collective-permute-start | bytes 196616 | tf_op jit(solution)/shard_map/ppermute | solution.py:60
  6.2 1.9 %collective-permute-start.4 = (f32[64,256]{1,0:T(8,128)S(1)}, f32[64,256]{1,0:T(8,128)S(1)}, u32[]{:S(2)}, u32[]{:S(2)}) collective-permute-start(f32[64,256]{1,0:T(8,128)S(1)} %collective-permute-done.3.refs_2_), channel_id=1, source_target_pairs={{0,1},{1,0},{2,3},{3,2},{4,5},{5,4},{6,7},{7,6},{8,9},{9,8},{10,11... | collective-permute-start | bytes 196616 | tf_op jit(solution)/shard_map/ppermute | solution.py:60
  8.1 1.3 %collective-permute-start.7 = (f32[64,256]{1,0:T(8,128)S(1)}, f32[64,256]{1,0:T(8,128)S(1)}, u32[]{:S(2)}, u32[]{:S(2)}) collective-permute-start(f32[64,256]{1,0:T(8,128)S(1)} %collective-permute-done.6.refs_6_), channel_id=1, source_target_pairs={{0,1},{1,0},{2,3},{3,2},{4,5},{5,4},{6,7},{7,6},{8,9},{9,8},{10,11... | collective-permute-start | bytes 196616 | tf_op jit(solution)/shard_map/ppermute | solution.py:60
  9.4 0.8 %copy-start.1 = (f32[64,256]{1,0:T(8,128)S(1)}, f32[64,256]{1,0:T(8,128)}, u32[]{:S(2)}) copy-start(f32[64,256]{1,0:T(8,128)} %refs_0_.4) | copy-start | bytes 196612
  10.2 0.8 %copy-start.2 = (f32[64,256]{1,0:T(8,128)S(1)}, f32[64,256]{1,0:T(8,128)}, u32[]{:S(2)}) copy-start(f32[64,256]{1,0:T(8,128)} %refs_4_.3) | copy-start | bytes 196612
  11.4 20.7 %collective-permute-start.9 = (f32[256,256]{1,0:T(8,128)S(1)}, f32[256,256]{1,0:T(8,128)S(1)}, u32[]{:S(2)}, u32[]{:S(2)}) collective-permute-start(f32[256,256]{1,0:T(8,128)S(1)} %get-tuple-element.44.own_map.refs_0_), channel_id=1, source_target_pairs={{0,4},{4,0},{8,12},{12,8},{16,20},{20,16},{24,28},{28,24},{1,5},{5... | collective-permute-start | bytes 786440 | tf_op jit(solution)/shard_map/ppermute | solution.py:60
  13.0 0.8 %copy-start = (f32[64,256]{1,0:T(8,128)S(1)}, f32[64,256]{1,0:T(8,128)}, u32[]{:S(2)}) copy-start(f32[64,256]{1,0:T(8,128)} %refs_2_.1) | copy-start | bytes 196612
  13.8 0.7 copy-start.3
  14.5 0.7 copy-start.4
  25.3 1.4 %collective-permute-start = (f32[128,256]{1,0:T(8,128)S(1)}, f32[128,256]{1,0:T(8,128)S(1)}, u32[]{:S(2)}, u32[]{:S(2)}) collective-permute-start(f32[128,256]{1,0:T(8,128)S(1)} %get-tuple-element.40), channel_id=1, source_target_pairs={{0,1},{1,0},{2,3},{3,2},{4,5},{5,4},{6,7},{7,6},{8,9},{9,8},{10,11... | collective-permute-start | bytes 393224 | tf_op jit(solution)/shard_map/ppermute | solution.py:60
  26.8 4.3 %collective-permute-start.1 = (f32[64,256]{1,0:T(8,128)S(1)}, f32[64,256]{1,0:T(8,128)S(1)}, u32[]{:S(2)}, u32[]{:S(2)}) collective-permute-start(f32[64,256]{1,0:T(8,128)S(1)} %get-tuple-element.42), channel_id=1, source_target_pairs={{0,2},{1,3},{2,0},{3,1},{4,6},{5,7},{6,4},{7,5},{8,10},{9,11},{10,... | collective-permute-start | bytes 196616 | tf_op jit(solution)/shard_map/ppermute | solution.py:60
  31.5 5.0 %collective-permute-start.8 = (f32[128,256]{1,0:T(8,128)S(1)}, f32[128,256]{1,0:T(8,128)S(1)}, u32[]{:S(2)}, u32[]{:S(2)}) collective-permute-start(f32[128,256]{1,0:T(8,128)S(1)} %get-tuple-element.46.refs_1_), channel_id=1, source_target_pairs={{0,4},{4,0},{8,12},{12,8},{16,20},{20,16},{24,28},{28,24},{1,5},{5... | collective-permute-start | bytes 393224 | tf_op jit(solution)/shard_map/ppermute | solution.py:60
  33.1 9.3 %collective-permute-start.11 = (f32[256,256]{1,0:T(8,128)S(1)}, f32[256,256]{1,0:T(8,128)S(1)}, u32[]{:S(2)}, u32[]{:S(2)}) collective-permute-start(f32[256,256]{1,0:T(8,128)S(1)} %get-tuple-element.53.refs_0_), channel_id=1, source_target_pairs={{0,8},{4,12},{8,0},{12,4},{16,24},{20,28},{24,16},{28,20},{1,9},{5... | collective-permute-start | bytes 786440 | tf_op jit(solution)/shard_map/ppermute | solution.py:60
  34.8 12.4 %collective-permute-start.12 = (f32[256,256]{1,0:T(8,128)S(1)}, f32[256,256]{1,0:T(8,128)S(1)}, u32[]{:S(2)}, u32[]{:S(2)}) collective-permute-start(f32[256,256]{1,0:T(8,128)S(1)} %get-tuple-element.54.refs_1_), channel_id=1, source_target_pairs={{0,8},{4,12},{8,0},{12,4},{16,24},{20,28},{24,16},{28,20},{1,9},{5... | collective-permute-start | bytes 786440 | tf_op jit(solution)/shard_map/ppermute | solution.py:60
  37.1 13.7 %collective-permute-start.10 = (f32[128,256]{1,0:T(8,128)S(1)}, f32[128,256]{1,0:T(8,128)S(1)}, u32[]{:S(2)}, u32[]{:S(2)}) collective-permute-start(f32[128,256]{1,0:T(8,128)S(1)} %get-tuple-element.52.refs_1_), channel_id=1, source_target_pairs={{0,8},{4,12},{8,0},{12,4},{16,24},{20,28},{24,16},{28,20},{1,9},{5... | collective-permute-start | bytes 393224 | tf_op jit(solution)/shard_map/ppermute | solution.py:60
  48.0 20.2 %copy-start.5 = (s32[8]{0:T(128)S(1)}, s32[8]{0:T(128)}, u32[]{:S(2)}) copy-start(s32[8]{0:T(128)} %refs_0_.5) | copy-start | bytes 100
  48.0 13.3 %collective-permute-start.14 = (f32[256,256]{1,0:T(8,128)S(1)}, f32[256,256]{1,0:T(8,128)S(1)}, u32[]{:S(2)}, u32[]{:S(2)}) collective-permute-start(f32[256,256]{1,0:T(8,128)S(1)} %get-tuple-element.63), channel_id=1, source_target_pairs={{0,16},{4,20},{8,24},{12,28},{16,0},{20,4},{24,8},{28,12},{1,17},{... | collective-permute-start | bytes 786440 | tf_op jit(solution)/shard_map/ppermute | solution.py:60
  51.3 10.7 %collective-permute-start.13 = (f32[64,256]{1,0:T(8,128)S(1)}, f32[64,256]{1,0:T(8,128)S(1)}, u32[]{:S(2)}, u32[]{:S(2)}) collective-permute-start(f32[64,256]{1,0:T(8,128)S(1)} %get-tuple-element.66), channel_id=1, source_target_pairs={{0,16},{4,20},{8,24},{12,28},{16,0},{20,4},{24,8},{28,12},{1,17},{... | collective-permute-start | bytes 196616 | tf_op jit(solution)/shard_map/ppermute | solution.py:60
  62.6 4.3 %collective-permute-start.16 = (f32[64,256]{1,0:T(8,128)S(1)}, f32[64,256]{1,0:T(8,128)S(1)}, u32[]{:S(2)}, u32[]{:S(2)}) collective-permute-start(f32[64,256]{1,0:T(8,128)S(1)} %leave.1.refs_6_), channel_id=1, source_target_pairs={{0,2},{1,3},{2,0},{3,1},{4,6},{5,7},{6,4},{7,5},{8,10},{9,11},{10,... | collective-permute-start | bytes 196616 | tf_op jit(solution)/shard_map/ppermute | solution.py:60
  63.7 3.3 %collective-permute-start.15 = (f32[64,256]{1,0:T(8,128)S(1)}, f32[64,256]{1,0:T(8,128)S(1)}, u32[]{:S(2)}, u32[]{:S(2)}) collective-permute-start(f32[64,256]{1,0:T(8,128)S(1)} %leave.1.refs_6_), channel_id=1, source_target_pairs={{0,1},{1,0},{2,3},{3,2},{4,5},{5,4},{6,7},{7,6},{8,9},{9,8},{10,11... | collective-permute-start | bytes 196616 | tf_op jit(solution)/shard_map/ppermute | solution.py:60
  67.0 1.3 %collective-permute-start.17 = (f32[64,256]{1,0:T(8,128)S(1)}, f32[64,256]{1,0:T(8,128)S(1)}, u32[]{:S(2)}, u32[]{:S(2)}) collective-permute-start(f32[64,256]{1,0:T(8,128)S(1)} %collective-permute-done.16.refs_8_), channel_id=1, source_target_pairs={{0,1},{1,0},{2,3},{3,2},{4,5},{5,4},{6,7},{7,6},{8,9},{9,8},{10,11... | collective-permute-start | bytes 196616 | tf_op jit(solution)/shard_map/ppermute | solution.py:60

commit v2 on v1

--- a/solution.py
+++ b/solution.py
@@ -10,7 +10,7 @@
 NN = (((1,), (0,)), ((), ()))
 NT = (((1,), (1,)), ((), ()))
 TN = (((0,), (0,)), ((), ()))
-VMEM_BYTES = 48 << 20
+VMEM_BYTES = 24 << 20
 HALVES = 2
 
 
@@ -41,6 +41,10 @@
 
 def call(kernel, name, ins, outs, scratch=()):
     specs = [pl.BlockSpec(memory_space=space) for space, _ in ins]
+    ins = [
+        (space, pltpu.with_memory_space_constraint(a, HBM) if space == HBM else a)
+        for space, a in ins
+    ]
     return pl.pallas_call(
         kernel,
         name=name,
@@ -53,37 +57,51 @@
 
 
 V = pltpu.VMEM
+HBM = pltpu.HBM
+
+
+def swap(x, axis, mask):
+    n = lax.axis_size(axis)
+    return lax.ppermute(x, axis, [(i, i ^ mask) for i in range(n)])
 
 
 def exchange(x, axis, bit):
-    n = lax.axis_size(axis)
-    return lax.ppermute(x, axis, [(i, i ^ (1 << bit)) for i in range(n)])
-
-
-def forward_kernel(nodes, fronts, *refs):
-    (parent, rows, sep, rhs_h, dinv_h, upd_h), refs = refs[:6], refs[6:]
-    (solved, inv_hi, inv_lo, upd_hi, upd_lo, send, keep), refs = refs[:7], refs[7:]
-    (rhs_v, dinv_v, upd_v, square), refs = refs[:4], refs[4:]
-    accs, sems = refs[:HALVES], refs[HALVES]
+    return swap(x, axis, 1 << bit)
+
+
+def prepare_kernel(nodes, *refs):
+    (rows_h, sep_h, own_inv_h, own_cpl_h, rhs_h, dinv_h, upd_h), refs = refs[:7], refs[7:]
+    (acc, inv_hi, inv_lo, upd_hi, upd_lo, own_inv, own_cpl), refs = refs[:7], refs[7:]
+    rhs_v, dinv_v, upd_v, square, rows, sep, sems, small = refs
     size, cols = rhs_v.shape[1:]
     width = cols // HALVES
+    few = [
+        pltpu.make_async_copy(src, dst, small.at[i])
+        for i, (src, dst) in enumerate(
+            ((rows_h, rows), (sep_h, sep), (own_inv_h, own_inv), (own_cpl_h, own_cpl))
+        )
+    ]
+    for c in few:
+        c.start()
     copies = []
     for k in range(nodes):
         group = [
+            pltpu.make_async_copy(upd_h.at[k], upd_v.at[k], sems.at[2, k]),
             pltpu.make_async_copy(dinv_h.at[k], dinv_v.at[k], sems.at[0, k]),
             pltpu.make_async_copy(rhs_h.at[k], rhs_v.at[k], sems.at[1, k]),
-            pltpu.make_async_copy(upd_h.at[k], upd_v.at[k], sems.at[2, k]),
         ]
         for c in group:
             c.start()
         copies.append(group)
     front = lax.axis_index("front")
+    square[...] = jnp.zeros_like(square)
+    for c in few:
+        c.wait()
     share = sep.shape[0]
-    square[...] = jnp.zeros_like(square)
     square[pl.ds(pl.multiple_of(front * share, 8), share), :] = sep[...]
     turned = square[...].T
     for h in range(HALVES):
-        accs[h][nodes] = turned[h * width : (h + 1) * width]
+        acc[h, nodes] = turned[h * width : (h + 1) * width]
     row_columns = rows[...].astype(F32).T
     lane = lax.broadcasted_iota(jnp.int32, (size, size), 1).astype(F32)
     for k in range(nodes):
@@ -96,7 +114,36 @@
         upd_lo[k] = dot1(chosen, low, NN).astype(BF16)
         turned = rhs_v[k].T
         for h in range(HALVES):
-            accs[h][k] = turned[h * width : (h + 1) * width]
+            acc[h, k] = turned[h * width : (h + 1) * width]
+
+
+def prepare(rhs, dinv, update, rows, sep, sep_dinv, sep_coupling):
+    nodes, size, cols = rhs.shape
+    big = pltpu.VMEM((nodes, size, size), F32)
+    half = ((nodes, size, size), BF16)
+    acc = ((HALVES, nodes + 1, cols // HALVES, size), F32)
+    return call(
+        lambda *refs: prepare_kernel(nodes, *refs),
+        "prepare",
+        [(HBM, a) for a in (rows, sep, sep_dinv, sep_coupling, rhs, dinv, update)],
+        [acc, half, half, half, half, (sep_dinv.shape, F32), (sep_coupling.shape, F32)],
+        [pltpu.VMEM((nodes, size, cols), F32), big, big, pltpu.VMEM((size, cols), F32)]
+        + [pltpu.VMEM(rows.shape, jnp.int32), pltpu.VMEM(sep.shape, F32)]
+        + [pltpu.SemaphoreType.DMA((3, nodes)), pltpu.SemaphoreType.DMA((4,))],
+    )
+
+
+def forward_kernel(nodes, fronts, *refs):
+    parent_h, acc, inv_hi, inv_lo, upd_hi, upd_lo, _ = refs[:7]
+    solved, send, keep, square, parent, sem = refs[7:13]
+    accs = refs[13:]
+    copy = pltpu.make_async_copy(parent_h, parent, sem)
+    copy.start()
+    width, size = acc.shape[2:]
+    cols = width * HALVES
+    for h in range(HALVES):
+        accs[h][...] = acc[h]
+    copy.wait()
     for k in range(nodes):
         inverse = (inv_hi[k], inv_lo[k])
         update = (upd_hi[k], upd_lo[k])
@@ -105,6 +152,7 @@
             value = dot3(split(accs[h][k]), inverse, NT)
             solved[k, h * width : (h + 1) * width] = value
             accs[h][above] = accs[h][above] - dot3(split(value), update, NT)
+    front = lax.axis_index("front")
     chunk = cols // fronts
     for h in range(HALVES):
         square[h * width : (h + 1) * width] = accs[h][nodes]
@@ -115,28 +163,28 @@
             ref[i * chunk : (i + 1) * chunk] = square[pl.ds(start, chunk), :]
 
 
-def local_forward(rhs, dinv, update, parent, rows, sep, fronts):
-    nodes, size, cols = rhs.shape
-    big = pltpu.VMEM((nodes, size, size), F32)
-    half = (nodes, size, size)
-    part = (cols // 2, size)
+def local_forward(parent, acc, halves, after, fronts):
+    nodes, (width, size) = acc.shape[1] - 1, acc.shape[2:]
+    cols = width * HALVES
+    part = ((cols // 2, size), F32)
     return call(
         lambda *refs: forward_kernel(nodes, fronts, *refs),
         "local_forward",
-        [(pltpu.SMEM, parent), (V, rows), (V, sep), (pl.ANY, rhs), (pl.ANY, dinv), (pl.ANY, update)],
-        [(half, F32), (half, BF16), (half, BF16), (half, BF16), (half, BF16), (part, F32), (part, F32)],
-        [pltpu.VMEM((nodes, size, cols), F32), big, big, pltpu.VMEM((size, cols), F32)]
-        + [pltpu.VMEM((nodes + 1, cols // HALVES, size), F32)] * HALVES
-        + [pltpu.SemaphoreType.DMA((3, nodes))],
+        [(HBM, parent), (V, acc)] + [(V, a) for a in halves] + [(pl.ANY, after)],
+        [((nodes, cols, size), F32), part, part],
+        [pltpu.VMEM((cols, size), F32), pltpu.SMEM((nodes,), jnp.int32), pltpu.SemaphoreType.DMA]
+        + [pltpu.VMEM((nodes + 1, width, size), F32)] * HALVES,
     )
 
 
 def backward_kernel(nodes, fronts, *refs):
-    parent, solved, inv_hi, inv_lo, upd_hi, upd_lo = refs[:6]
+    parent_h, solved, inv_hi, inv_lo, upd_hi, upd_lo = refs[:6]
     pieces = refs[6 : 6 + fronts]
     sol, sep_out = refs[6 + fronts : 8 + fronts]
-    square = refs[8 + fronts]
-    known = refs[9 + fronts :]
+    square, parent, staged, sem, sems = refs[8 + fronts : 13 + fronts]
+    known = refs[13 + fronts :]
+    copy = pltpu.make_async_copy(parent_h, parent, sem)
+    copy.start()
     front = lax.axis_index("front")
     chunk = pieces[0].shape[0]
     width = known[0].shape[1]
@@ -148,6 +196,8 @@
     square[...] = square[...].T
     share = sep_out.shape[0]
     sep_out[...] = square[pl.ds(pl.multiple_of(front * share, 8), share), :]
+    copy.wait()
+    outs = []
     for k in reversed(range(nodes)):
         inverse = (inv_hi[k], inv_lo[k])
         update = (upd_hi[k], upd_lo[k])
@@ -157,22 +207,31 @@
             part = solved[k, rows] - dot3(split(known[h][above]), update, NN)
             value = dot3(split(part), inverse, NN)
             known[h][k] = value
-            sol[k, :, rows] = value.T
-
-
-def local_backward(parent, solved, inv_hi, inv_lo, upd_hi, upd_lo, pieces):
+            staged[k, :, rows] = value.T
+        out = pltpu.make_async_copy(staged.at[k], sol.at[k], sems.at[k])
+        out.start()
+        outs.append(out)
+    for out in outs:
+        out.wait()
+
+
+def local_backward(parent, solved, halves, pieces):
     nodes, cols, size = solved.shape
     fronts = len(pieces)
-    return call(
+    sol, sep = jax.ShapeDtypeStruct((nodes, size, cols), F32), ((size // fronts, cols), F32)
+    ins = [(HBM, parent)] + [(V, a) for a in (solved, *halves, *pieces)]
+    return pl.pallas_call(
         lambda *refs: backward_kernel(nodes, fronts, *refs),
-        "local_backward",
-        [(pltpu.SMEM, parent)]
-        + [(V, a) for a in (solved, inv_hi, inv_lo, upd_hi, upd_lo)]
-        + [(V, a) for a in pieces],
-        [((nodes, size, cols), F32), ((size // fronts, cols), F32)],
-        [pltpu.VMEM((size, cols), F32)]
+        name="local_backward",
+        in_specs=[pl.BlockSpec(memory_space=space) for space, _ in ins],
+        out_specs=(pl.BlockSpec(memory_space=HBM), pl.BlockSpec(memory_space=V)),
+        out_shape=(sol, jax.ShapeDtypeStruct(*sep)),
+        scratch_shapes=[pltpu.VMEM((size, cols), F32), pltpu.SMEM((nodes,), jnp.int32)]
+        + [pltpu.VMEM((nodes, size, cols), F32), pltpu.SemaphoreType.DMA]
+        + [pltpu.SemaphoreType.DMA((nodes,))]
         + [pltpu.VMEM((nodes + 1, cols // HALVES, size), F32)] * HALVES,
-    )
+        compiler_params=pltpu.CompilerParams(vmem_limit_bytes=VMEM_BYTES),
+    )(pltpu.with_memory_space_constraint(parent, HBM), *[a for _, a in ins[1:]])
 
 
 def block_map_kernel(fronts, *refs):
@@ -201,8 +260,21 @@
     )
 
 
-def first_merge_kernel(*refs):
-    own, other, total, curve, mixed, halves, curve_u, total_u, total_l = refs
+def half_rows(part, values):
+    rows = values[0].shape[0] // 2
+    low = bit_of("front", 0) == 0
+    for i, value in enumerate(values):
+        part[i] = jnp.where(low, value[:rows], value[rows:])
+
+
+def whole(mine, pairs):
+    low = bit_of("front", 0) == 0
+    first, second = jnp.where(low, mine, pairs), jnp.where(low, pairs, mine)
+    return jnp.concatenate([first, second], axis=0)
+
+
+def first_merge_kernel(last, *refs):
+    own, other, _, total, curve, mixed, halves, curve_u, total_u, total_l, part = refs
     upper = bit_of("leaf", 0) == 1
     low = jnp.where(upper, other[...], own[...])
     up = jnp.where(upper, own[...], other[...])
@@ -215,7 +287,9 @@
     x = dot3(k_up_s, low_s, NN)
     t = dot3(up_s, low_s, NN)
     total[...] = t
-    curve[...] = dot3(low_s, low_s, TN) + dot3(low_s, split(x), TN)
+    k = dot3(low_s, low_s, TN) + dot3(low_s, split(x), TN)
+    curve[...] = k
+    half_rows(part, (k,) if last else (k, t))
     size = low.shape[0]
     row = lax.broadcasted_iota(jnp.int32, (size, size), 0)
     col = lax.broadcasted_iota(jnp.int32, (size, size), 1)
@@ -226,20 +300,26 @@
 
 
 def merge_kernel(bit, last, *refs):
-    own_t, own_k, other_t, other_k, mixed = refs[:5]
+    own_t, own_k, mine, pairs, mixed = refs[:5]
     upper = bit_of("leaf", bit) == 1
-    total, curve, mixed_n, halves, curve_u, total_u, total_l = refs[5:]
-    low_s = split(jnp.where(upper, other_t[...], own_t[...]))
-    up_s = split(jnp.where(upper, own_t[...], other_t[...]))
-    k_low = jnp.where(upper, other_k[...], own_k[...])
-    k_up_s = split(jnp.where(upper, own_k[...], other_k[...]))
+    total, curve, mixed_n, halves, curve_u, total_u, total_l, part = refs[5:]
+    other_k, other_t = whole(mine[0], pairs[0]), whole(mine[1], pairs[1])
+    low_s = split(jnp.where(upper, other_t, own_t[...]))
+    up_s = split(jnp.where(upper, own_t[...], other_t))
+    k_low = jnp.where(upper, other_k, own_k[...])
+    k_up_s = split(jnp.where(upper, own_k[...], other_k))
     for ref, value in ((total_u, up_s), (total_l, low_s), (curve_u, k_up_s)):
         ref[0], ref[1] = value
     x = dot3(k_up_s, low_s, NN)
     x_s = split(x)
-    if not last:
-        total[...] = dot3(up_s, low_s, NN)
-    curve[...] = k_low + dot3(low_s, x_s, TN)
+    k = k_low + dot3(low_s, x_s, TN)
+    curve[...] = k
+    if last:
+        half_rows(part, (k,))
+    else:
+        t = dot3(up_s, low_s, NN)
+        total[...] = t
+        half_rows(part, (k, t))
     a, e = mixed[0], mixed[1]
     keep_split(halves, jnp.where(upper, a.T, e))
     a_s, e_s = split(a), split(e)
@@ -247,15 +327,16 @@
     mixed_n[1] = jnp.where(upper, e, dot3(up_s, e_s, NN))
 
 
-def maps(size):
+def maps(size, last):
     square, both = ((size, size), F32), ((2, size, size), BF16)
-    return [square, square, ((2, size, size), F32), both, both, both, both]
-
-
-def last_map_kernel(bit, mixed, other_k, halves, curve_u):
+    part = ((1 if last else 2, size // 2, size), F32)
+    return [square, square, ((2, size, size), F32), both, both, both, both, part]
+
+
+def last_map_kernel(bit, mixed, mine, pairs, halves, curve_u):
     upper = bit_of("leaf", bit) == 1
     keep_split(halves, jnp.where(upper, mixed[0].T, mixed[1]))
-    keep_split(curve_u, other_k[...])
+    keep_split(curve_u, whole(mine[0], pairs[0]))
 
 
 def fold_kernel(bit, own, other, send, keep):
@@ -326,36 +407,17 @@
     cols = sep_rhs.shape[1]
     chunk = cols // fronts
 
-    inverse_parts = gather_front(sep_dinv, front_bits)
-    coupling_parts = gather_front(sep_coupling, front_bits)
-    own_map, inverse = block_map(inverse_parts, coupling_parts)
-
-    solved, inv_hi, inv_lo, upd_hi, upd_lo, send, keep = local_forward(
-        rhs_local, dinv_local, update_local, parent, row_blocks, sep_rhs, fronts
-    )
-
+    masks = range(1, fronts)
+    came_inverse = [swap(sep_dinv, "front", m) for m in masks]
+    came_coupling = [swap(sep_coupling, "front", m) for m in masks]
+    acc, *rest = prepare(
+        rhs_local, dinv_local, update_local, row_blocks, sep_rhs, sep_dinv, sep_coupling
+    )
+    local_halves, own_inverse, own_coupling = rest[:4], rest[4], rest[5]
+    own_map, inverse = block_map([own_inverse, *came_inverse], [own_coupling, *came_coupling])
     other_map = exchange(own_map, "leaf", 0)
-    square = maps(size)
-    total, curve, mixed, *tools = call(
-        first_merge_kernel, "merge_0", [(V, own_map), (V, other_map)], square
-    )
-    steps = [tools]
-    for bit in range(1, rounds - 1):
-        other_t, other_k = exchange(total, "leaf", bit), exchange(curve, "leaf", bit)
-        total, curve, mixed, *tools = call(
-            lambda *refs, bit=bit: merge_kernel(bit, bit == rounds - 2, *refs),
-            f"merge_{bit}",
-            [(V, a) for a in (total, curve, other_t, other_k, mixed)],
-            square,
-        )
-        steps.append(tools)
-    other_k = exchange(curve, "leaf", rounds - 1)
-    last_halves, last_curve = call(
-        lambda *refs: last_map_kernel(rounds - 1, *refs),
-        "merge_last",
-        [(V, mixed), (V, other_k)],
-        [((2, size, size), BF16)] * 2,
-    )
+
+    solved, send, keep = local_forward(parent, acc, local_halves, own_map, fronts)
 
     for bit in range(front_bits):
         received = exchange(send, "front", bit)
@@ -367,6 +429,12 @@
                 [(V, keep), (V, received)],
                 [half, half],
             )
+    total, curve, mixed, *tools, part = call(
+        lambda *refs: first_merge_kernel(rounds == 2, *refs),
+        "merge_0",
+        [(V, own_map), (V, other_map), (pl.ANY, send)],
+        maps(size, rounds == 2),
+    )
     sol, message = call(
         enter_kernel,
         "enter",
@@ -374,15 +442,32 @@
         [((chunk, size), F32), ((2 * chunk, size), F32)],
     )
     for bit in range(rounds - 1):
+        last = bit == rounds - 2
+        mine = exchange(part, "leaf", bit + 1)
         received = exchange(message, "leaf", bit)
-        last = bit == rounds - 2
         shape = (2, chunk, size) if last else (2 * chunk, size)
         sol, message = call(
             lambda *refs, bit=bit, last=last: step_kernel(bit, last, *refs),
             f"step_{bit}",
-            [(V, a) for a in (sol, message, received, *steps[bit])],
+            [(V, a) for a in (sol, message, received, *tools)],
             [((chunk, size), F32), (shape, F32)],
         )
+        mine, _ = lax.optimization_barrier((mine, sol))
+        pairs = exchange(mine, "front", 0)
+        if not last:
+            last = bit == rounds - 3
+            total, curve, mixed, *tools, part = call(
+                lambda *refs, bit=bit, last=last: merge_kernel(bit + 1, last, *refs),
+                f"merge_{bit + 1}",
+                [(V, a) for a in (total, curve, mine, pairs, mixed)],
+                maps(size, last),
+            )
+    last_halves, last_curve = call(
+        lambda *refs: last_map_kernel(rounds - 1, *refs),
+        "merge_last",
+        [(V, mixed), (V, mine), (V, pairs)],
+        [((2, size, size), BF16)] * 2,
+    )
     received = exchange(message[0], "leaf", rounds - 1)
     (top,) = call(
         lambda *refs: leave_kernel(rounds - 1, *refs),
@@ -392,7 +477,7 @@
     )
     pieces = gather_front(top, front_bits)
     sol_local, sep_solution = local_backward(
-        parent, solved, inv_hi, inv_lo, upd_hi, upd_lo, pieces
+        parent, solved, local_halves, pieces
     )
     return (sol_local, sep_solution)
 

time: 75 us -> 64.7 us (0.86)
  waiting for transfers between devices: 32.7 us -> 25.3 us
  local copies, waits for them, and re-layouts: 3.89 us -> 0.01 us
    ppermute x18 -> x19, waiting for transfers between devices: 32.7 us -> 25.3 us  [swap(): return lax.ppermute(x, axis, [(i, i ^ mask) for i in range(n)])]
    pallas_call x0 -> x1, Pallas kernels: none -> 5.59 us  [local_backward(): pl.pallas_call(lambda *refs: backward_kernel(nodes, fronts, *refs), name=...]
    pallas_call x11, Pallas kernels: 21 us -> 16.1 us  [call(): pl.pallas_call(kernel, name=name, in_specs=specs, out_specs=tuple((pl.Blo...]
    unnamed x12 -> x0, local copies, waits for them, and re-layouts: 3.87 us -> none
    ppermute x18 -> x19, starting transfers between devices: 16.4 us -> 16.8 us  [swap(): return lax.ppermute(x, axis, [(i, i ^ mask) for i in range(n)])]
  transfers between devices with their start and end apart: 18 -> 19, of which waited for: 12 -> 10; matrix products, arithmetic and copies ran while one was open for 0% -> 0% of each run, Pallas kernels for 18% -> 22%
where the time goes in v2:
time: 64.7 us; the launch traced here: 64.6 us
  waiting for transfers between devices  25.3 us (39%)
  Pallas kernels  21.7 us (34%)
  starting transfers between devices  16.8 us (26%)
  between operations  0.78 us (1%)
    ppermute x19, waiting for transfers between devices, swap(): return lax.ppermute(x, axis, [(i, i ^ mask) for i in range(n)])  25.3 us
    ppermute x19, starting transfers between devices, swap(): return lax.ppermute(x, axis, [(i, i ^ mask) for i in range(n)])  16.8 us
    pallas_call x11, Pallas kernels, call(): pl.pallas_call(kernel, name=name, in_specs=specs, out_specs=tuple((pl.Blo...  16.1 us
    pallas_call x1, Pallas kernels, local_backward(): pl.pallas_call(lambda *refs: backward_kernel(nodes, fronts, *refs), name=...  5.59 us
  transfers between devices with their start and end apart: 19, of which 10 were waited for; matrix products, arithmetic and copies ran while one was open for 0% of the time, Pallas kernels for 22%

profile of v2, /device:TPU:0, one launch (start us, length us, event | category | flops | bytes accessed | tf_op | source)
XLA Modules:
  0.0 64.6 jit_solution(2569984010107431823)
XLA Ops:
  0.6 0.5 collective-permute-start
  1.1 2.6 %collective-permute-start.1 = (f32[64,256]{1,0:T(8,128)}, f32[64,256]{1,0:T(8,128)S(1)}, u32[]{:S(2)}, u32[]{:S(2)}) collective-permute-start(f32[64,256]{1,0:T(8,128)} %refs_2_.1), channel_id=1, source_target_pairs={{0,2},{1,3},{2,0},{3,1},{4,6},{5,7},{6,4},{7,5},{8,10},{9,11},{10,... | collective-permute-start | bytes 196616 | tf_op jit(solution)/shard_map/ppermute | solution.py:65
  3.9 1.9 %collective-permute-start.4 = (f32[64,256]{1,0:T(8,128)}, f32[64,256]{1,0:T(8,128)S(1)}, u32[]{:S(2)}, u32[]{:S(2)}) collective-permute-start(f32[64,256]{1,0:T(8,128)} %refs_3_.1), channel_id=1, source_target_pairs={{0,2},{1,3},{2,0},{3,1},{4,6},{5,7},{6,4},{7,5},{8,10},{9,11},{10,... | collective-permute-start | bytes 196616 | tf_op jit(solution)/shard_map/ppermute | solution.py:65
  5.9 5.5 %prepare.1 = (f32[2,9,128,256]{3,2,1,0:T(8,128)S(1)}, bf16[8,256,256]{2,1,0:T(8,128)(2,1)S(1)}, bf16[8,256,256]{2,1,0:T(8,128)(2,1)S(1)}, bf16[8,256,256]{2,1,0:...) custom-call(s32[8,256]{1,0:T(8,128)} %refs_0_.3, ...), custom_call_target="tpu_custom_call" | custom-call | tf_op jit(solution)/shard_map/prepare/pallas_call | solution.py:48
  11.8 1.6 %collective-permute-start.9 = (f32[256,256]{1,0:T(8,128)S(1)}, f32[256,256]{1,0:T(8,128)S(1)}, u32[]{:S(2)}, u32[]{:S(2)}) collective-permute-start(f32[256,256]{1,0:T(8,128)S(1)} %get-tuple-element.47.refs_6_.own_map.refs_0_), channel_id=1, source_target_pairs={{0,4},{4,0},{8,12},{12,8},{16,20},{20,16},{24,28},{28,24},{1,5},{5... | collective-permute-start | bytes 786440 | tf_op jit(solution)/shard_map/ppermute | solution.py:65
  13.4 5.6 %local_forward.1 = (f32[8,256,256]{2,1,0:T(8,128)S(1)}, f32[128,256]{1,0:T(8,128)S(1)}, f32[128,256]{1,0:T(8,128)S(1)}) custom-call(s32[8]{0:T(128)} %refs_0_.5, f32[2,9,128,256]{3,2,1,0:T(8,128)S(1)} %get-tuple-element.40.refs_1_, bf16[8,256,256]{2,1,0:T(8,128)(2,1)S(1)} %get-tuple-element.41.refs_2_, bf16[8,256,256]{2,1,0:T(8,128)(2,1)S(1)} %get-tuple-element.42.refs_3_, ...), custom_call_target="tpu_custom_call" | custom-call | tf_op jit(solution)/shard_map/local_forward/pallas_call | solution.py:48
  19.4 1.0 %collective-permute-done.6.refs_1_ = f32[128,256]{1,0:T(8,128)S(1)} collective-permute-done((f32[128,256]{1,0:T(8,128)S(1)}, f32[128,256]{1,0:T(8,128)S(1)}, u32[]{:S(2)}, u32[]{:S(2)}) %collective-permute-start.6) | collective-permute-done | bytes 131104 | tf_op jit(solution)/shard_map/ppermute | solution.py:65
  20.5 1.0 %merge_0.1 = (f32[256,256]{1,0:T(8,128)S(1)}, f32[256,256]{1,0:T(8,128)S(1)}, f32[2,256,256]{2,1,0:T(8,128)S(1)}, bf16[2,256,256]{2,1,0:T(8,128)(2,1)S(1)}, bf16...) custom-call(f32[256,256]{1,0:T(8,128)S(1)} %get-tuple-element.47.ref, ...), custom_call_target="tpu_custom_call" | custom-call | tf_op jit(solution)/shard_map/merge_0/pallas_call | solution.py:48
  21.5 1.9 %collective-permute-start.11 = (f32[2,128,256]{2,1,0:T(8,128)S(1)}, f32[2,128,256]{2,1,0:T(8,128)S(1)}, u32[]{:S(2)}, u32[]{:S(2)}) collective-permute-start(f32[2,128,256]{2,1,0:T(8,128)S(1)} %get-tuple-element.64), channel_id=1, source_target_pairs={{0,8},{4,12},{8,0},{12,4},{16,24},{20,28},{24,16},{28,20},{1,9},{5... | collective-permute-start | bytes 786440 | tf_op jit(solution)/shard_map/ppermute | solution.py:65
  23.4 1.5 %collective-permute-start.7 = (f32[64,256]{1,0:T(8,128)S(1)}, f32[64,256]{1,0:T(8,128)S(1)}, u32[]{:S(2)}, u32[]{:S(2)}) collective-permute-start(f32[64,256]{1,0:T(8,128)S(1)} %get-tuple-element.52.refs_2_), channel_id=1, source_target_pairs={{0,2},{1,3},{2,0},{3,1},{4,6},{5,7},{6,4},{7,5},{8,10},{9,11},{10,... | collective-permute-start | bytes 196616 | tf_op jit(solution)/shard_map/ppermute | solution.py:65
  24.8 2.8 %collective-permute-done.7.other = f32[64,256]{1,0:T(8,128)S(1)} collective-permute-done((f32[64,256]{1,0:T(8,128)S(1)}, f32[64,256]{1,0:T(8,128)S(1)}, u32[]{:S(2)}, u32[]{:S(2)}) %collective-permute-start.7) | collective-permute-done | bytes 65568 | tf_op jit(solution)/shard_map/ppermute | solution.py:65
  28.1 1.6 %collective-permute-start.8 = (f32[128,256]{1,0:T(8,128)S(1)}, f32[128,256]{1,0:T(8,128)S(1)}, u32[]{:S(2)}, u32[]{:S(2)}) collective-permute-start(f32[128,256]{1,0:T(8,128)S(1)} %get-tuple-element.55.refs_1_), channel_id=1, source_target_pairs={{0,4},{4,0},{8,12},{12,8},{16,20},{20,16},{24,28},{28,24},{1,5},{5... | collective-permute-start | bytes 393224 | tf_op jit(solution)/shard_map/ppermute | solution.py:65
  29.6 3.4 %collective-permute-done.8.refs_2_ = f32[128,256]{1,0:T(8,128)S(1)} collective-permute-done((f32[128,256]{1,0:T(8,128)S(1)}, f32[128,256]{1,0:T(8,128)S(1)}, u32[]{:S(2)}, u32[]{:S(2)}) %collective-permute-start.8) | collective-permute-done | bytes 131104 | tf_op jit(solution)/shard_map/ppermute | solution.py:65
  34.0 1.2 %collective-permute-done.12.refs_3_ = f32[2,128,256]{2,1,0:T(8,128)S(1)} collective-permute-done((f32[2,128,256]{2,1,0:T(8,128)S(1)}, f32[2,128,256]{2,1,0:T(8,128)S(1)}, u32[]{:S(2)}, u32[]{:S(2)}) %collective-permute-start.12) | collective-permute-done | bytes 262176 | tf_op jit(solution)/shard_map/ppermute | solution.py:65
  35.2 1.4 %merge_1.1 = (f32[256,256]{1,0:T(8,128)}, f32[256,256]{1,0:T(8,128)}, f32[2,256,256]{2,1,0:T(8,128)S(1)}, bf16[2,256,256]{2,1,0:T(8,128)(2,1)S(1)}, bf16[2,256,2...) custom-call(f32[256,256]{1,0:T(8,128)S(1)} %get-tuple-element.62.ref, ...), custom_call_target="tpu_custom_call" | custom-call | tf_op jit(solution)/shard_map/merge_1/pallas_call | solution.py:48
  36.7 2.6 %collective-permute-start.14 = (f32[1,128,256]{2,1,0:T(8,128)S(1)}, f32[1,128,256]{2,1,0:T(8,128)S(1)}, u32[]{:S(2)}, u32[]{:S(2)}) collective-permute-start(f32[1,128,256]{2,1,0:T(8,128)S(1)} %get-tuple-element.74), channel_id=1, source_target_pairs={{0,16},{4,20},{8,24},{12,28},{16,0},{20,4},{24,8},{28,12},{1,17},{... | collective-permute-start | bytes 393224 | tf_op jit(solution)/shard_map/ppermute | solution.py:65
  40.1 5.8 %collective-permute-done.14.refs_1_ = f32[1,128,256]{2,1,0:T(8,128)S(1)} collective-permute-done((f32[1,128,256]{2,1,0:T(8,128)S(1)}, f32[1,128,256]{2,1,0:T(8,128)S(1)}, u32[]{:S(2)}, u32[]{:S(2)}) %collective-permute-start.14) | collective-permute-done | bytes 131104 | tf_op jit(solution)/shard_map/ppermute | solution.py:65
  46.0 1.3 %collective-permute-done.15.refs_2_ = f32[1,128,256]{2,1,0:T(8,128)S(1)} collective-permute-done((f32[1,128,256]{2,1,0:T(8,128)S(1)}, f32[1,128,256]{2,1,0:T(8,128)S(1)}, u32[]{:S(2)}, u32[]{:S(2)}) %collective-permute-start.15) | collective-permute-done | bytes 131104 | tf_op jit(solution)/shard_map/ppermute | solution.py:65
  47.4 5.4 %collective-permute-done.13.refs_2_ = f32[64,256]{1,0:T(8,128)S(1)} collective-permute-done((f32[64,256]{1,0:T(8,128)S(1)}, f32[64,256]{1,0:T(8,128)S(1)}, u32[]{:S(2)}, u32[]{:S(2)}) %collective-permute-start.13) | collective-permute-done | bytes 65568 | tf_op jit(solution)/shard_map/ppermute | solution.py:65
  52.8 0.6 leave.1.refs_6_
  53.4 1.6 %collective-permute-start.17 = (f32[64,256]{1,0:T(8,128)S(1)}, f32[64,256]{1,0:T(8,128)S(1)}, u32[]{:S(2)}, u32[]{:S(2)}) collective-permute-start(f32[64,256]{1,0:T(8,128)S(1)} %leave.1.refs_6_), channel_id=1, source_target_pairs={{0,2},{1,3},{2,0},{3,1},{4,6},{5,7},{6,4},{7,5},{8,10},{9,11},{10,... | collective-permute-start | bytes 196616 | tf_op jit(solution)/shard_map/ppermute | solution.py:65
  54.9 2.8 %collective-permute-done.17.refs_8_ = f32[64,256]{1,0:T(8,128)S(1)} collective-permute-done((f32[64,256]{1,0:T(8,128)S(1)}, f32[64,256]{1,0:T(8,128)S(1)}, u32[]{:S(2)}, u32[]{:S(2)}) %collective-permute-start.17) | collective-permute-done | bytes 65568 | tf_op jit(solution)/shard_map/ppermute | solution.py:65
  57.7 1.2 %collective-permute-done.18.refs_9_ = f32[64,256]{1,0:T(8,128)S(1)} collective-permute-done((f32[64,256]{1,0:T(8,128)S(1)}, f32[64,256]{1,0:T(8,128)S(1)}, u32[]{:S(2)}, u32[]{:S(2)}) %collective-permute-start.18) | collective-permute-done | bytes 65568 | tf_op jit(solution)/shard_map/ppermute | solution.py:65
  59.0 5.6 %local_backward.1 = (f32[8,256,256]{2,1,0:T(8,128)}, f32[64,256]{1,0:T(8,128)}) custom-call(s32[8]{0:T(128)} %refs_0_.5, f32[8,256,256]{2,1,0:T(8,128)S(1)} %get-tuple-element.48.refs_1_, bf16[8,256,256]{2,1,0:T(8,128)(2,1)S(1)} %get-tuple-element.41.refs_2_, bf16[8,256,256]{2,1,0:T(8,128)(2,1)S(1)} %get-tuple-element.42.refs_3_, ...), custom_call_target="tpu_custom_call" | custom-call | tf_op jit(solution)/shard_map/local_backward/pallas_call | solution.py:223
  (27 shorter events, 3.4 us)
Async XLA Ops:
  0.6 5.2 %collective-permute-start = (f32[64,256]{1,0:T(8,128)}, f32[64,256]{1,0:T(8,128)S(1)}, u32[]{:S(2)}, u32[]{:S(2)}) collective-permute-start(f32[64,256]{1,0:T(8,128)} %refs_2_.1), channel_id=1, source_target_pairs={{0,1},{1,0},{2,3},{3,2},{4,5},{5,4},{6,7},{7,6},{8,9},{9,8},{10,11... | collective-permute-start | bytes 196616 | tf_op jit(solution)/shard_map/ppermute | solution.py:65
  1.1 10.2 %collective-permute-start.1 = (f32[64,256]{1,0:T(8,128)}, f32[64,256]{1,0:T(8,128)S(1)}, u32[]{:S(2)}, u32[]{:S(2)}) collective-permute-start(f32[64,256]{1,0:T(8,128)} %refs_2_.1), channel_id=1, source_target_pairs={{0,2},{1,3},{2,0},{3,1},{4,6},{5,7},{6,4},{7,5},{8,10},{9,11},{10,... | collective-permute-start | bytes 196616 | tf_op jit(solution)/shard_map/ppermute | solution.py:65
  3.7 7.7 %collective-permute-start.2 = (f32[64,256]{1,0:T(8,128)}, f32[64,256]{1,0:T(8,128)S(1)}, u32[]{:S(2)}, u32[]{:S(2)}) collective-permute-start(f32[64,256]{1,0:T(8,128)} %refs_2_.1), channel_id=1, source_target_pairs={{0,3},{1,2},{2,1},{3,0},{4,7},{5,6},{6,5},{7,4},{8,11},{9,10},{10,... | collective-permute-start | bytes 196616 | tf_op jit(solution)/shard_map/ppermute | solution.py:65
  3.8 7.6 %collective-permute-start.3 = (f32[64,256]{1,0:T(8,128)}, f32[64,256]{1,0:T(8,128)S(1)}, u32[]{:S(2)}, u32[]{:S(2)}) collective-permute-start(f32[64,256]{1,0:T(8,128)} %refs_3_.1), channel_id=1, source_target_pairs={{0,1},{1,0},{2,3},{3,2},{4,5},{5,4},{6,7},{7,6},{8,9},{9,8},{10,11... | collective-permute-start | bytes 196616 | tf_op jit(solution)/shard_map/ppermute | solution.py:65
  3.9 7.5 %collective-permute-start.4 = (f32[64,256]{1,0:T(8,128)}, f32[64,256]{1,0:T(8,128)S(1)}, u32[]{:S(2)}, u32[]{:S(2)}) collective-permute-start(f32[64,256]{1,0:T(8,128)} %refs_3_.1), channel_id=1, source_target_pairs={{0,2},{1,3},{2,0},{3,1},{4,6},{5,7},{6,4},{7,5},{8,10},{9,11},{10,... | collective-permute-start | bytes 196616 | tf_op jit(solution)/shard_map/ppermute | solution.py:65
  5.9 5.6 %collective-permute-start.5 = (f32[64,256]{1,0:T(8,128)}, f32[64,256]{1,0:T(8,128)S(1)}, u32[]{:S(2)}, u32[]{:S(2)}) collective-permute-start(f32[64,256]{1,0:T(8,128)} %refs_3_.1), channel_id=1, source_target_pairs={{0,3},{1,2},{2,1},{3,0},{4,7},{5,6},{6,5},{7,4},{8,11},{9,10},{10,... | collective-permute-start | bytes 196616 | tf_op jit(solution)/shard_map/ppermute | solution.py:65
  11.8 8.7 %collective-permute-start.9 = (f32[256,256]{1,0:T(8,128)S(1)}, f32[256,256]{1,0:T(8,128)S(1)}, u32[]{:S(2)}, u32[]{:S(2)}) collective-permute-start(f32[256,256]{1,0:T(8,128)S(1)} %get-tuple-element.47.refs_6_.own_map.refs_0_), channel_id=1, source_target_pairs={{0,4},{4,0},{8,12},{12,8},{16,20},{20,16},{24,28},{28,24},{1,5},{5... | collective-permute-start | bytes 786440 | tf_op jit(solution)/shard_map/ppermute | solution.py:65
  19.0 1.4 %collective-permute-start.6 = (f32[128,256]{1,0:T(8,128)S(1)}, f32[128,256]{1,0:T(8,128)S(1)}, u32[]{:S(2)}, u32[]{:S(2)}) collective-permute-start(f32[128,256]{1,0:T(8,128)S(1)} %get-tuple-element.50), channel_id=1, source_target_pairs={{0,1},{1,0},{2,3},{3,2},{4,5},{5,4},{6,7},{7,6},{8,9},{9,8},{10,11... | collective-permute-start | bytes 393224 | tf_op jit(solution)/shard_map/ppermute | solution.py:65
  21.5 12.1 %collective-permute-start.11 = (f32[2,128,256]{2,1,0:T(8,128)S(1)}, f32[2,128,256]{2,1,0:T(8,128)S(1)}, u32[]{:S(2)}, u32[]{:S(2)}) collective-permute-start(f32[2,128,256]{2,1,0:T(8,128)S(1)} %get-tuple-element.64), channel_id=1, source_target_pairs={{0,8},{4,12},{8,0},{12,4},{16,24},{20,28},{24,16},{28,20},{1,9},{5... | collective-permute-start | bytes 786440 | tf_op jit(solution)/shard_map/ppermute | solution.py:65
  23.4 4.3 %collective-permute-start.7 = (f32[64,256]{1,0:T(8,128)S(1)}, f32[64,256]{1,0:T(8,128)S(1)}, u32[]{:S(2)}, u32[]{:S(2)}) collective-permute-start(f32[64,256]{1,0:T(8,128)S(1)} %get-tuple-element.52.refs_2_), channel_id=1, source_target_pairs={{0,2},{1,3},{2,0},{3,1},{4,6},{5,7},{6,4},{7,5},{8,10},{9,11},{10,... | collective-permute-start | bytes 196616 | tf_op jit(solution)/shard_map/ppermute | solution.py:65
  28.1 5.0 %collective-permute-start.8 = (f32[128,256]{1,0:T(8,128)S(1)}, f32[128,256]{1,0:T(8,128)S(1)}, u32[]{:S(2)}, u32[]{:S(2)}) collective-permute-start(f32[128,256]{1,0:T(8,128)S(1)} %get-tuple-element.55.refs_1_), channel_id=1, source_target_pairs={{0,4},{4,0},{8,12},{12,8},{16,20},{20,16},{24,28},{28,24},{1,5},{5... | collective-permute-start | bytes 393224 | tf_op jit(solution)/shard_map/ppermute | solution.py:65
  33.6 1.6 %collective-permute-start.12 = (f32[2,128,256]{2,1,0:T(8,128)S(1)}, f32[2,128,256]{2,1,0:T(8,128)S(1)}, u32[]{:S(2)}, u32[]{:S(2)}) collective-permute-start(f32[2,128,256]{2,1,0:T(8,128)S(1)} %collective-permute-done.11.refs_2_), channel_id=1, source_target_pairs={{0,1},{1,0},{2,3},{3,2},{4,5},{5,4},{6,7},{7,6},{8,9},{9,8},{10,11... | collective-permute-start | bytes 786440 | tf_op jit(solution)/shard_map/ppermute | solution.py:65
  33.7 5.9 %collective-permute-start.10 = (f32[128,256]{1,0:T(8,128)S(1)}, f32[128,256]{1,0:T(8,128)S(1)}, u32[]{:S(2)}, u32[]{:S(2)}) collective-permute-start(f32[128,256]{1,0:T(8,128)S(1)} %get-tuple-element.61.refs_1_), channel_id=1, source_target_pairs={{0,8},{4,12},{8,0},{12,4},{16,24},{20,28},{24,16},{28,20},{1,9},{5... | collective-permute-start | bytes 393224 | tf_op jit(solution)/shard_map/ppermute | solution.py:65
  36.7 9.2 %collective-permute-start.14 = (f32[1,128,256]{2,1,0:T(8,128)S(1)}, f32[1,128,256]{2,1,0:T(8,128)S(1)}, u32[]{:S(2)}, u32[]{:S(2)}) collective-permute-start(f32[1,128,256]{2,1,0:T(8,128)S(1)} %get-tuple-element.74), channel_id=1, source_target_pairs={{0,16},{4,20},{8,24},{12,28},{16,0},{20,4},{24,8},{28,12},{1,17},{... | collective-permute-start | bytes 393224 | tf_op jit(solution)/shard_map/ppermute | solution.py:65
  45.9 1.3 %collective-permute-start.15 = (f32[1,128,256]{2,1,0:T(8,128)S(1)}, f32[1,128,256]{2,1,0:T(8,128)S(1)}, u32[]{:S(2)}, u32[]{:S(2)}) collective-permute-start(f32[1,128,256]{2,1,0:T(8,128)S(1)} %collective-permute-done.14.refs_1_), channel_id=1, source_target_pairs={{0,1},{1,0},{2,3},{3,2},{4,5},{5,4},{6,7},{7,6},{8,9},{9,8},{10,11... | collective-permute-start | bytes 393224 | tf_op jit(solution)/shard_map/ppermute | solution.py:65
  45.9 6.9 %collective-permute-start.13 = (f32[64,256]{1,0:T(8,128)S(1)}, f32[64,256]{1,0:T(8,128)S(1)}, u32[]{:S(2)}, u32[]{:S(2)}) collective-permute-start(f32[64,256]{1,0:T(8,128)S(1)} %get-tuple-element.78), channel_id=1, source_target_pairs={{0,16},{4,20},{8,24},{12,28},{16,0},{20,4},{24,8},{28,12},{1,17},{... | collective-permute-start | bytes 196616 | tf_op jit(solution)/shard_map/ppermute | solution.py:65
  53.4 4.3 %collective-permute-start.17 = (f32[64,256]{1,0:T(8,128)S(1)}, f32[64,256]{1,0:T(8,128)S(1)}, u32[]{:S(2)}, u32[]{:S(2)}) collective-permute-start(f32[64,256]{1,0:T(8,128)S(1)} %leave.1.refs_6_), channel_id=1, source_target_pairs={{0,2},{1,3},{2,0},{3,1},{4,6},{5,7},{6,4},{7,5},{8,10},{9,11},{10,... | collective-permute-start | bytes 196616 | tf_op jit(solution)/shard_map/ppermute | solution.py:65
  54.9 2.8 %collective-permute-start.16 = (f32[64,256]{1,0:T(8,128)S(1)}, f32[64,256]{1,0:T(8,128)S(1)}, u32[]{:S(2)}, u32[]{:S(2)}) collective-permute-start(f32[64,256]{1,0:T(8,128)S(1)} %leave.1.refs_6_), channel_id=1, source_target_pairs={{0,1},{1,0},{2,3},{3,2},{4,5},{5,4},{6,7},{7,6},{8,9},{9,8},{10,11... | collective-permute-start | bytes 196616 | tf_op jit(solution)/shard_map/ppermute | solution.py:65
  57.7 1.3 %collective-permute-start.18 = (f32[64,256]{1,0:T(8,128)S(1)}, f32[64,256]{1,0:T(8,128)S(1)}, u32[]{:S(2)}, u32[]{:S(2)}) collective-permute-start(f32[64,256]{1,0:T(8,128)S(1)} %collective-permute-done.17.refs_8_), channel_id=1, source_target_pairs={{0,1},{1,0},{2,3},{3,2},{4,5},{5,4},{6,7},{7,6},{8,9},{9,8},{10,11... | collective-permute-start | bytes 196616 | tf_op jit(solution)/shard_map/ppermute | solution.py:65

commit v3 on v2

--- a/solution.py
+++ b/solution.py
@@ -70,16 +70,14 @@
 
 
 def prepare_kernel(nodes, *refs):
-    (rows_h, sep_h, own_inv_h, own_cpl_h, rhs_h, dinv_h, upd_h), refs = refs[:7], refs[7:]
-    (acc, inv_hi, inv_lo, upd_hi, upd_lo, own_inv, own_cpl), refs = refs[:7], refs[7:]
+    (rows_h, sep_h, rhs_h, dinv_h, upd_h, _), refs = refs[:6], refs[6:]
+    (acc, inv_hi, inv_lo, upd_hi, upd_lo), refs = refs[:5], refs[5:]
     rhs_v, dinv_v, upd_v, square, rows, sep, sems, small = refs
     size, cols = rhs_v.shape[1:]
     width = cols // HALVES
     few = [
         pltpu.make_async_copy(src, dst, small.at[i])
-        for i, (src, dst) in enumerate(
-            ((rows_h, rows), (sep_h, sep), (own_inv_h, own_inv), (own_cpl_h, own_cpl))
-        )
+        for i, (src, dst) in enumerate(((rows_h, rows), (sep_h, sep)))
     ]
     for c in few:
         c.start()
@@ -117,7 +115,7 @@
             acc[h, k] = turned[h * width : (h + 1) * width]
 
 
-def prepare(rhs, dinv, update, rows, sep, sep_dinv, sep_coupling):
+def prepare(rhs, dinv, update, rows, sep, after):
     nodes, size, cols = rhs.shape
     big = pltpu.VMEM((nodes, size, size), F32)
     half = ((nodes, size, size), BF16)
@@ -125,11 +123,11 @@
     return call(
         lambda *refs: prepare_kernel(nodes, *refs),
         "prepare",
-        [(HBM, a) for a in (rows, sep, sep_dinv, sep_coupling, rhs, dinv, update)],
-        [acc, half, half, half, half, (sep_dinv.shape, F32), (sep_coupling.shape, F32)],
+        [(HBM, a) for a in (rows, sep, rhs, dinv, update)] + [(pl.ANY, after)],
+        [acc, half, half, half, half],
         [pltpu.VMEM((nodes, size, cols), F32), big, big, pltpu.VMEM((size, cols), F32)]
         + [pltpu.VMEM(rows.shape, jnp.int32), pltpu.VMEM(sep.shape, F32)]
-        + [pltpu.SemaphoreType.DMA((3, nodes)), pltpu.SemaphoreType.DMA((4,))],
+        + [pltpu.SemaphoreType.DMA((3, nodes)), pltpu.SemaphoreType.DMA((2,))],
     )
 
 
@@ -234,47 +232,41 @@
     )(pltpu.with_memory_space_constraint(parent, HBM), *[a for _, a in ins[1:]])
 
 
+def stack_kernel(first, second, out, sems):
+    copies = [pltpu.make_async_copy(a, out.at[i], sems.at[i]) for i, a in enumerate((first, second))]
+    for c in copies:
+        c.start()
+    for c in copies:
+        c.wait()
+
+
 def block_map_kernel(fronts, *refs):
-    inverse_parts, coupling_parts = refs[:fronts], refs[fronts : 2 * fronts]
-    total, inverse_halves, square = refs[2 * fronts :]
+    parts = refs[:fronts]
+    _, total, inverse_halves, square = refs[fronts:]
     front = lax.axis_index("front")
-    share = inverse_parts[0].shape[0]
-    for parts, slot in ((inverse_parts, 0), (coupling_parts, 1)):
-        for i in range(fronts):
-            start = pl.multiple_of((front ^ i) * share, 8)
-            square[slot, pl.ds(start, share), :] = parts[i][...]
+    share = parts[0].shape[1]
+    for i in range(fronts):
+        start = pl.multiple_of((front ^ i) * share, 8)
+        square[:, pl.ds(start, share), :] = parts[i][...]
     inverse = split(square[0])
     inverse_halves[0], inverse_halves[1] = inverse
     total[...] = -dot3(inverse, split(square[1]), NN)
 
 
-def block_map(inverse_parts, coupling_parts):
-    fronts = len(inverse_parts)
-    share, size = inverse_parts[0].shape
+def block_map(parts, after):
+    fronts = len(parts)
+    size = parts[0].shape[2]
     return call(
         lambda *refs: block_map_kernel(fronts, *refs),
         "block_map",
-        [(V, a) for a in (*inverse_parts, *coupling_parts)],
+        [(V, a) for a in parts] + [(pl.ANY, after)],
         [((size, size), F32), ((2, size, size), BF16)],
         [pltpu.VMEM((2, size, size), F32)],
     )
 
 
-def half_rows(part, values):
-    rows = values[0].shape[0] // 2
-    low = bit_of("front", 0) == 0
-    for i, value in enumerate(values):
-        part[i] = jnp.where(low, value[:rows], value[rows:])
-
-
-def whole(mine, pairs):
-    low = bit_of("front", 0) == 0
-    first, second = jnp.where(low, mine, pairs), jnp.where(low, pairs, mine)
-    return jnp.concatenate([first, second], axis=0)
-
-
-def first_merge_kernel(last, *refs):
-    own, other, _, total, curve, mixed, halves, curve_u, total_u, total_l, part = refs
+def first_merge_kernel(*refs):
+    own, other, _, pack, mixed, halves, curve_u, total_u, total_l = refs
     upper = bit_of("leaf", 0) == 1
     low = jnp.where(upper, other[...], own[...])
     up = jnp.where(upper, own[...], other[...])
@@ -286,10 +278,8 @@
     curve_u[0], curve_u[1] = k_up_s
     x = dot3(k_up_s, low_s, NN)
     t = dot3(up_s, low_s, NN)
-    total[...] = t
-    k = dot3(low_s, low_s, TN) + dot3(low_s, split(x), TN)
-    curve[...] = k
-    half_rows(part, (k,) if last else (k, t))
+    pack[1] = t
+    pack[0] = dot3(low_s, low_s, TN) + dot3(low_s, split(x), TN)
     size = low.shape[0]
     row = lax.broadcasted_iota(jnp.int32, (size, size), 0)
     col = lax.broadcasted_iota(jnp.int32, (size, size), 1)
@@ -300,43 +290,36 @@
 
 
 def merge_kernel(bit, last, *refs):
-    own_t, own_k, mine, pairs, mixed = refs[:5]
+    own, other, mixed = refs[:3]
     upper = bit_of("leaf", bit) == 1
-    total, curve, mixed_n, halves, curve_u, total_u, total_l, part = refs[5:]
-    other_k, other_t = whole(mine[0], pairs[0]), whole(mine[1], pairs[1])
-    low_s = split(jnp.where(upper, other_t, own_t[...]))
-    up_s = split(jnp.where(upper, own_t[...], other_t))
-    k_low = jnp.where(upper, other_k, own_k[...])
-    k_up_s = split(jnp.where(upper, own_k[...], other_k))
+    pack, mixed_n, halves, curve_u, total_u, total_l = refs[3:]
+    low_s = split(jnp.where(upper, other[1], own[1]))
+    up_s = split(jnp.where(upper, own[1], other[1]))
+    k_low = jnp.where(upper, other[0], own[0])
+    k_up_s = split(jnp.where(upper, own[0], other[0]))
     for ref, value in ((total_u, up_s), (total_l, low_s), (curve_u, k_up_s)):
         ref[0], ref[1] = value
     x = dot3(k_up_s, low_s, NN)
     x_s = split(x)
     k = k_low + dot3(low_s, x_s, TN)
-    curve[...] = k
-    if last:
-        half_rows(part, (k,))
-    else:
-        t = dot3(up_s, low_s, NN)
-        total[...] = t
-        half_rows(part, (k, t))
     a, e = mixed[0], mixed[1]
     keep_split(halves, jnp.where(upper, a.T, e))
     a_s, e_s = split(a), split(e)
-    mixed_n[0] = jnp.where(upper, dot3(a_s, low_s, NN), a + dot3(e_s, x_s, TN))
-    mixed_n[1] = jnp.where(upper, e, dot3(up_s, e_s, NN))
+    a_n = jnp.where(upper, dot3(a_s, low_s, NN), a + dot3(e_s, x_s, TN))
+    e_n = jnp.where(upper, e, dot3(up_s, e_s, NN))
+    if last:
+        keep_split(pack, k)
+        keep_split(mixed_n, jnp.where(bit_of("leaf", bit + 1) == 1, a_n.T, e_n))
+    else:
+        pack[0] = k
+        pack[1] = dot3(up_s, low_s, NN)
+        mixed_n[0], mixed_n[1] = a_n, e_n
 
 
 def maps(size, last):
-    square, both = ((size, size), F32), ((2, size, size), BF16)
-    part = ((1 if last else 2, size // 2, size), F32)
-    return [square, square, ((2, size, size), F32), both, both, both, both, part]
-
-
-def last_map_kernel(bit, mixed, mine, pairs, halves, curve_u):
-    upper = bit_of("leaf", bit) == 1
-    keep_split(halves, jnp.where(upper, mixed[0].T, mixed[1]))
-    keep_split(curve_u, whole(mine[0], pairs[0]))
+    both = ((2, size, size), BF16)
+    kept = both if last else ((2, size, size), F32)
+    return [kept, kept, both, both, both, both]
 
 
 def fold_kernel(bit, own, other, send, keep):
@@ -359,7 +342,8 @@
 
 
 def step_kernel(bit, last, *refs):
-    sol, own, other, halves, curve_u, total_u, total_l, sol_n, message = refs
+    sol, own, other, halves, curve_u, total_u, total_l, sol_n = refs[:8]
+    message = refs[8:]
     upper = bit_of("leaf", bit) == 1
     rows = sol.shape[0]
     z_own, p_own, z_other, p_other = own[:rows], own[rows:], other[:rows], other[rows:]
@@ -375,19 +359,18 @@
     given = split(jnp.where(upper, z_low, middle))
     sol_n[...] = sol[...] + dot3(given, pair(halves), NN)
     if last:
-        upper_next = bit_of("leaf", bit + 1) == 1
-        message[0] = jnp.where(upper_next, p_new, z_new)
-        message[1] = z_new
+        message[0][...], message[1][...] = z_new, p_new
     else:
-        message[:rows] = z_new
-        message[rows:] = p_new
-
-
-def leave_kernel(bit, sol, own_z, other, halves, curve_u, inverse, top):
+        message[0][:rows], message[0][rows:] = z_new, p_new
+
+
+def turn_kernel(message, came, curve, back):
+    back[...] = message[...] + dot3(split(came[...]), pair(curve), NN)
+
+
+def leave_kernel(bit, sol, came, back, halves, inverse, top):
     upper = bit_of("leaf", bit) == 1
-    came = other[...]
-    middle = came + dot3(split(own_z[...]), pair(curve_u), NN)
-    given = split(jnp.where(upper, came, middle))
+    given = split(jnp.where(upper, came[...], back[...]))
     value = sol[...] + dot3(given, pair(halves), NN)
     top[...] = dot3(split(value), pair(inverse), NN)
 
@@ -407,18 +390,28 @@
     cols = sep_rhs.shape[1]
     chunk = cols // fronts
 
-    masks = range(1, fronts)
-    came_inverse = [swap(sep_dinv, "front", m) for m in masks]
-    came_coupling = [swap(sep_coupling, "front", m) for m in masks]
-    acc, *rest = prepare(
-        rhs_local, dinv_local, update_local, row_blocks, sep_rhs, sep_dinv, sep_coupling
-    )
-    local_halves, own_inverse, own_coupling = rest[:4], rest[4], rest[5]
-    own_map, inverse = block_map([own_inverse, *came_inverse], [own_coupling, *came_coupling])
+    (stacked,) = call(
+        stack_kernel,
+        "stack",
+        [(HBM, sep_dinv), (HBM, sep_coupling)],
+        [((2, *sep_dinv.shape), F32)],
+        [pltpu.SemaphoreType.DMA((2,))],
+    )
+    came = [swap(stacked, "front", m) for m in range(1, fronts)]
+    acc, *local_halves = prepare(
+        rhs_local, dinv_local, update_local, row_blocks, sep_rhs, stacked
+    )
+    own_map, inverse = block_map([stacked, *came], acc)
     other_map = exchange(own_map, "leaf", 0)
 
     solved, send, keep = local_forward(parent, acc, local_halves, own_map, fronts)
 
+    pack, mixed, *tools = call(
+        first_merge_kernel,
+        "merge_0",
+        [(V, own_map), (V, other_map), (pl.ANY, send)],
+        maps(size, False),
+    )
     for bit in range(front_bits):
         received = exchange(send, "front", bit)
         if bit + 1 < front_bits:
@@ -429,51 +422,41 @@
                 [(V, keep), (V, received)],
                 [half, half],
             )
-    total, curve, mixed, *tools, part = call(
-        lambda *refs: first_merge_kernel(rounds == 2, *refs),
-        "merge_0",
-        [(V, own_map), (V, other_map), (pl.ANY, send)],
-        maps(size, rounds == 2),
-    )
     sol, message = call(
         enter_kernel,
         "enter",
         [(V, keep), (V, received), (V, inverse), (V, own_map)],
         [((chunk, size), F32), ((2 * chunk, size), F32)],
     )
+    part = ((chunk, size), F32)
     for bit in range(rounds - 1):
         last = bit == rounds - 2
-        mine = exchange(part, "leaf", bit + 1)
         received = exchange(message, "leaf", bit)
-        shape = (2, chunk, size) if last else (2 * chunk, size)
-        sol, message = call(
+        if not last:
+            other_pack = exchange(pack, "leaf", bit + 1)
+        sol, *message = call(
             lambda *refs, bit=bit, last=last: step_kernel(bit, last, *refs),
             f"step_{bit}",
             [(V, a) for a in (sol, message, received, *tools)],
-            [((chunk, size), F32), (shape, F32)],
+            [part] + ([part, part] if last else [((2 * chunk, size), F32)]),
         )
-        mine, _ = lax.optimization_barrier((mine, sol))
-        pairs = exchange(mine, "front", 0)
         if not last:
+            (message,) = message
             last = bit == rounds - 3
-            total, curve, mixed, *tools, part = call(
+            pack, mixed, *tools = call(
                 lambda *refs, bit=bit, last=last: merge_kernel(bit + 1, last, *refs),
                 f"merge_{bit + 1}",
-                [(V, a) for a in (total, curve, mine, pairs, mixed)],
+                [(V, a) for a in (pack, other_pack, mixed)],
                 maps(size, last),
             )
-    last_halves, last_curve = call(
-        lambda *refs: last_map_kernel(rounds - 1, *refs),
-        "merge_last",
-        [(V, mixed), (V, mine), (V, pairs)],
-        [((2, size, size), BF16)] * 2,
-    )
-    received = exchange(message[0], "leaf", rounds - 1)
+    came = exchange(message[0], "leaf", rounds - 1)
+    (back,) = call(turn_kernel, "turn", [(V, a) for a in (message[1], came, pack)], [part])
+    back = exchange(back, "leaf", rounds - 1)
     (top,) = call(
         lambda *refs: leave_kernel(rounds - 1, *refs),
         "leave",
-        [(V, a) for a in (sol, message[1], received, last_halves, last_curve, inverse)],
-        [((chunk, size), F32)],
+        [(V, a) for a in (sol, came, back, mixed, inverse)],
+        [part],
     )
     pieces = gather_front(top, front_bits)
     sol_local, sep_solution = local_backward(

time: 64.7 us -> 63.6 us (0.983)
  waiting for transfers between devices: 25.3 us -> 21.2 us
  starting transfers between devices: 16.8 us -> 19.7 us
    ppermute x19 -> x14, waiting for transfers between devices: 25.3 us -> 21.2 us  [swap(): return lax.ppermute(x, axis, [(i, i ^ mask) for i in range(n)])]
    ppermute x19 -> x14, starting transfers between devices: 16.8 us -> 19.7 us  [swap(): return lax.ppermute(x, axis, [(i, i ^ mask) for i in range(n)])]
    pallas_call x11 -> x12, Pallas kernels: 16.1 us -> 16.3 us  [call(): pl.pallas_call(kernel, name=name, in_specs=specs, out_specs=tuple((pl.Blo...]
  transfers between devices with their start and end apart: 19 -> 14, of which waited for: 10 -> 10; matrix products, arithmetic and copies ran while one was open for 0% -> 0% of each run, Pallas kernels for 22% -> 20%
where the time goes in v3:
time: 63.6 us; the launch traced here: 63.4 us
  Pallas kernels  21.9 us (34%)
  waiting for transfers between devices  21.2 us (33%)
  starting transfers between devices  19.7 us (31%)
  between operations  0.73 us (1%)
    ppermute x14, waiting for transfers between devices, swap(): return lax.ppermute(x, axis, [(i, i ^ mask) for i in range(n)])  21.2 us
    ppermute x14, starting transfers between devices, swap(): return lax.ppermute(x, axis, [(i, i ^ mask) for i in range(n)])  19.7 us
    pallas_call x12, Pallas kernels, call(): pl.pallas_call(kernel, name=name, in_specs=specs, out_specs=tuple((pl.Blo...  16.3 us
    pallas_call x1, Pallas kernels, local_backward(): pl.pallas_call(lambda *refs: backward_kernel(nodes, fronts, *refs), name=...  5.6 us
  transfers between devices with their start and end apart: 14, of which 10 were waited for; matrix products, arithmetic and copies ran while one was open for 0% of the time, Pallas kernels for 20%

profile of v3, /device:TPU:0, one launch (start us, length us, event | category | flops | bytes accessed | tf_op | source)
XLA Modules:
  0.0 63.4 jit_solution(16388902023544650140)
XLA Ops:
  0.6 0.9 %stack.1.refs_5_.refs_0_ = f32[2,64,256]{2,1,0:T(8,128)S(1)} custom-call(f32[64,256]{1,0:T(8,128)} %first.1, f32[64,256]{1,0:T(8,128)} %second.1), custom_call_target="tpu_custom_call" | custom-call | tf_op jit(solution)/shard_map/stack/pallas_call | solution.py:48
  1.5 2.4 %collective-permute-start.2 = (f32[2,64,256]{2,1,0:T(8,128)S(1)}, f32[2,64,256]{2,1,0:T(8,128)S(1)}, u32[]{:S(2)}, u32[]{:S(2)}) collective-permute-start(f32[2,64,256]{2,1,0:T(8,128)S(1)} %stack.1.refs_5_.refs_0_), channel_id=1, source_target_pairs={{0,3},{1,2},{2,1},{3,0},{4,7},{5,6},{6,5},{7,4},{8,11},{9,10},{10,... | collective-permute-start | bytes 393224 | tf_op jit(solution)/shard_map/ppermute | solution.py:65
  4.7 5.5 %prepare.1 = (f32[2,9,128,256]{3,2,1,0:T(8,128)S(1)}, bf16[8,256,256]{2,1,0:T(8,128)(2,1)S(1)}, bf16[8,256,256]{2,1,0:T(8,128)(2,1)S(1)}, bf16[8,256,256]{2,1,0:T(8,128)(2,1)S(1)}, bf16[8,256,256]{2,1,0:T(8,128)(2,1)S(1)}) custom-call(s32[8,256]{1,0:T(8,128)} %refs_0_.3, f32[64,256]{1,0:T(8,128)} %refs_1_.1, f32[8,256,256]{2,1,0:T(8,128)} %refs_2_.1, ...), custom_call_target="tpu_custom_call" | custom-call | tf_op jit(solution)/shard_map/prepare/pallas_call | solution.py:48
  10.1 0.7 %collective-permute-done.1.refs_2_ = f32[2,64,256]{2,1,0:T(8,128)S(1)} collective-permute-done((f32[2,64,256]{2,1,0:T(8,128)S(1)}, f32[2,64,256]{2,1,0:T(8,128)S(1)}, u32[]{:S(2)}, u32[]{:S(2)}) %collective-permute-start.1) | collective-permute-done | bytes 131104 | tf_op jit(solution)/shard_map/ppermute | solution.py:65
  11.2 2.4 %collective-permute-start.6 = (f32[256,256]{1,0:T(8,128)S(1)}, f32[256,256]{1,0:T(8,128)S(1)}, u32[]{:S(2)}, u32[]{:S(2)}) collective-permute-start(f32[256,256]{1,0:T(8,128)S(1)} %get-tuple-element.38.refs_6_.own_map.refs_0_), channel_id=1, source_target_pairs={{0,4},{4,0},{8,12},{12,8},{16,20},{20,16},{24,28},{28,24},{1,5},{5... | collective-permute-start | bytes 786440 | tf_op jit(solution)/shard_map/ppermute | solution.py:65
  13.6 5.6 %local_forward.1 = (f32[8,256,256]{2,1,0:T(8,128)S(1)}, f32[128,256]{1,0:T(8,128)S(1)}, f32[128,256]{1,0:T(8,128)S(1)}) custom-call(s32[8]{0:T(128)} %refs_0_.5, f32[2,9,128,256]{3,2,1,0:T(8,128)S(1)} %get-tuple-element.33.refs_4_.refs_1_, bf16[8,256,256]{2,1,0:T(8,128)(2,1)S(1)} %get-tuple-element.34.refs_2_, ...), custom_call_target="tpu_custom_call" | custom-call | tf_op jit(solution)/shard_map/local_forward/pallas_call | solution.py:48
  19.2 0.9 %collective-permute-done.6.refs_1_ = f32[256,256]{1,0:T(8,128)S(1)} collective-permute-done((f32[256,256]{1,0:T(8,128)S(1)}, f32[256,256]{1,0:T(8,128)S(1)}, u32[]{:S(2)}, u32[]{:S(2)}) %collective-permute-start.6) | collective-permute-done | bytes 262176 | tf_op jit(solution)/shard_map/ppermute | solution.py:65
  20.1 1.0 %merge_0.1 = (f32[2,256,256]{2,1,0:T(8,128)S(1)}, f32[2,256,256]{2,1,0:T(8,128)S(1)}, bf16[2,256,256]{2,1,0:T(8,128)(2,1)S(1)}, bf16[2,256,256]{2,1,0:T(8,128)(2...) custom-call(f32[256,256]{1,0:T(8,128)S(1)} %get-tuple-element.38.refs_6_.own_map.refs_0_, ...), custom_call_target="tpu_custom_call" | custom-call | tf_op jit(solution)/shard_map/merge_0/pallas_call | solution.py:48
  21.1 1.9 %collective-permute-start.8 = (f32[2,256,256]{2,1,0:T(8,128)S(1)}, f32[2,256,256]{2,1,0:T(8,128)S(1)}, u32[]{:S(2)}, u32[]{:S(2)}) collective-permute-start(f32[2,256,256]{2,1,0:T(8,128)S(1)} %get-tuple-element.53.refs_0_), channel_id=1, source_target_pairs={{0,8},{4,12},{8,0},{12,4},{16,24},{20,28},{24,16},{28,20},{1,9},{5... | collective-permute-start | bytes 1572872 | tf_op jit(solution)/shard_map/ppermute | solution.py:65
  23.0 1.3 %collective-permute-done.3.refs_1_ = f32[128,256]{1,0:T(8,128)S(1)} collective-permute-done((f32[128,256]{1,0:T(8,128)S(1)}, f32[128,256]{1,0:T(8,128)S(1)}, u32[]{:S(2)}, u32[]{:S(2)}) %collective-permute-start.3) | collective-permute-done | bytes 131104 | tf_op jit(solution)/shard_map/ppermute | solution.py:65
  24.4 1.6 %collective-permute-start.4 = (f32[64,256]{1,0:T(8,128)S(1)}, f32[64,256]{1,0:T(8,128)S(1)}, u32[]{:S(2)}, u32[]{:S(2)}) collective-permute-start(f32[64,256]{1,0:T(8,128)S(1)} %get-tuple-element.43), channel_id=1, source_target_pairs={{0,2},{1,3},{2,0},{3,1},{4,6},{5,7},{6,4},{7,5},{8,10},{9,11},{10,... | collective-permute-start | bytes 196616 | tf_op jit(solution)/shard_map/ppermute | solution.py:65
  26.0 2.7 %collective-permute-done.4.other = f32[64,256]{1,0:T(8,128)S(1)} collective-permute-done((f32[64,256]{1,0:T(8,128)S(1)}, f32[64,256]{1,0:T(8,128)S(1)}, u32[]{:S(2)}, u32[]{:S(2)}) %collective-permute-start.4) | collective-permute-done | bytes 65568 | tf_op jit(solution)/shard_map/ppermute | solution.py:65
  29.1 1.6 %collective-permute-start.5 = (f32[128,256]{1,0:T(8,128)S(1)}, f32[128,256]{1,0:T(8,128)S(1)}, u32[]{:S(2)}, u32[]{:S(2)}) collective-permute-start(f32[128,256]{1,0:T(8,128)S(1)} %get-tuple-element.46.refs_1_), channel_id=1, source_target_pairs={{0,4},{4,0},{8,12},{12,8},{16,20},{20,16},{24,28},{28,24},{1,5},{5... | collective-permute-start | bytes 393224 | tf_op jit(solution)/shard_map/ppermute | solution.py:65
  30.7 3.4 %collective-permute-done.5.refs_2_ = f32[128,256]{1,0:T(8,128)S(1)} collective-permute-done((f32[128,256]{1,0:T(8,128)S(1)}, f32[128,256]{1,0:T(8,128)S(1)}, u32[]{:S(2)}, u32[]{:S(2)}) %collective-permute-start.5) | collective-permute-done | bytes 131104 | tf_op jit(solution)/shard_map/ppermute | solution.py:65
  35.0 0.9 %merge_1.1 = (bf16[2,256,256]{2,1,0:T(8,128)(2,1)S(1)}, bf16[2,256,256]{2,1,0:T(8,128)(2,1)S(1)}, bf16[2,256,256]{2,1,0:T(8,128)(2,1)S(1)}, bf16[2,256,256]{2,1,...) custom-call(f32[2,256,256]{2,1,0:T(8,128)S(1)} %get-tuple-element.53.refs_0_, ...), custom_call_target="tpu_custom_call" | custom-call | tf_op jit(solution)/shard_map/merge_1/pallas_call | solution.py:48
  35.9 3.8 %collective-permute-done.7.refs_2_ = f32[128,256]{1,0:T(8,128)S(1)} collective-permute-done((f32[128,256]{1,0:T(8,128)S(1)}, f32[128,256]{1,0:T(8,128)S(1)}, u32[]{:S(2)}, u32[]{:S(2)}) %collective-permute-start.7) | collective-permute-done | bytes 131104 | tf_op jit(solution)/shard_map/ppermute | solution.py:65
  40.2 3.4 %collective-permute-start.9 = (f32[64,256]{1,0:T(8,128)S(1)}, f32[64,256]{1,0:T(8,128)S(1)}, u32[]{:S(2)}, u32[]{:S(2)}) collective-permute-start(f32[64,256]{1,0:T(8,128)S(1)} %get-tuple-element.60), channel_id=1, source_target_pairs={{0,16},{4,20},{8,24},{12,28},{16,0},{20,4},{24,8},{28,12},{1,17},{... | collective-permute-start | bytes 196616 | tf_op jit(solution)/shard_map/ppermute | solution.py:65
  43.6 2.4 %collective-permute-done.9.came.refs_1_ = f32[64,256]{1,0:T(8,128)S(1)} collective-permute-done((f32[64,256]{1,0:T(8,128)S(1)}, f32[64,256]{1,0:T(8,128)S(1)}, u32[]{:S(2)}, u32[]{:S(2)}) %collective-permute-start.9) | collective-permute-done | bytes 65568 | tf_op jit(solution)/shard_map/ppermute | solution.py:65
  46.1 3.4 %collective-permute-start.10 = (f32[64,256]{1,0:T(8,128)S(1)}, f32[64,256]{1,0:T(8,128)S(1)}, u32[]{:S(2)}, u32[]{:S(2)}) collective-permute-start(f32[64,256]{1,0:T(8,128)S(1)} %turn.1), channel_id=1, source_target_pairs={{0,16},{4,20},{8,24},{12,28},{16,0},{20,4},{24,8},{28,12},{1,17},{... | collective-permute-start | bytes 196616 | tf_op jit(solution)/shard_map/ppermute | solution.py:65
  49.6 2.2 %collective-permute-done.10.refs_2_ = f32[64,256]{1,0:T(8,128)S(1)} collective-permute-done((f32[64,256]{1,0:T(8,128)S(1)}, f32[64,256]{1,0:T(8,128)S(1)}, u32[]{:S(2)}, u32[]{:S(2)}) %collective-permute-start.10) | collective-permute-done | bytes 65568 | tf_op jit(solution)/shard_map/ppermute | solution.py:65
  52.3 2.0 %collective-permute-start.12 = (f32[64,256]{1,0:T(8,128)S(1)}, f32[64,256]{1,0:T(8,128)S(1)}, u32[]{:S(2)}, u32[]{:S(2)}) collective-permute-start(f32[64,256]{1,0:T(8,128)S(1)} %leave.1.refs_6_), channel_id=1, source_target_pairs={{0,2},{1,3},{2,0},{3,1},{4,6},{5,7},{6,4},{7,5},{8,10},{9,11},{10,... | collective-permute-start | bytes 196616 | tf_op jit(solution)/shard_map/ppermute | solution.py:65
  54.3 2.3 %collective-permute-done.12.refs_8_ = f32[64,256]{1,0:T(8,128)S(1)} collective-permute-done((f32[64,256]{1,0:T(8,128)S(1)}, f32[64,256]{1,0:T(8,128)S(1)}, u32[]{:S(2)}, u32[]{:S(2)}) %collective-permute-start.12) | collective-permute-done | bytes 65568 | tf_op jit(solution)/shard_map/ppermute | solution.py:65
  56.6 1.2 %collective-permute-done.13.refs_9_ = f32[64,256]{1,0:T(8,128)S(1)} collective-permute-done((f32[64,256]{1,0:T(8,128)S(1)}, f32[64,256]{1,0:T(8,128)S(1)}, u32[]{:S(2)}, u32[]{:S(2)}) %collective-permute-start.13) | collective-permute-done | bytes 65568 | tf_op jit(solution)/shard_map/ppermute | solution.py:65
  57.8 5.6 %local_backward.1 = (f32[8,256,256]{2,1,0:T(8,128)}, f32[64,256]{1,0:T(8,128)}) custom-call(s32[8]{0:T(128)} %refs_0_.5, f32[8,256,256]{2,1,0:T(8,128)S(1)} %get-tuple-element.39.refs_1_, bf16[8,256,256]{2,1,0:T(8,128)(2,1)S(1)} %get-tuple-element.34.refs_2_, bf16[8,256,256]{2,1,0:T(8,128)(2,1)S(1)} %get-tuple-element.35.refs_3_, ...), custom_call_target="tpu_custom_call" | custom-call | tf_op jit(solution)/shard_map/local_backward/pallas_call | solution.py:221
  (17 shorter events, 3.4 us)
Async XLA Ops:
  1.5 8.6 %collective-permute-start.2 = (f32[2,64,256]{2,1,0:T(8,128)S(1)}, f32[2,64,256]{2,1,0:T(8,128)S(1)}, u32[]{:S(2)}, u32[]{:S(2)}) collective-permute-start(f32[2,64,256]{2,1,0:T(8,128)S(1)} %stack.1.refs_5_.refs_0_), channel_id=1, source_target_pairs={{0,3},{1,2},{2,1},{3,0},{4,7},{5,6},{6,5},{7,4},{8,11},{9,10},{10,... | collective-permute-start | bytes 393224 | tf_op jit(solution)/shard_map/ppermute | solution.py:65
  4.0 6.9 %collective-permute-start.1 = (f32[2,64,256]{2,1,0:T(8,128)S(1)}, f32[2,64,256]{2,1,0:T(8,128)S(1)}, u32[]{:S(2)}, u32[]{:S(2)}) collective-permute-start(f32[2,64,256]{2,1,0:T(8,128)S(1)} %stack.1.refs_5_.refs_0_), channel_id=1, source_target_pairs={{0,2},{1,3},{2,0},{3,1},{4,6},{5,7},{6,4},{7,5},{8,10},{9,11},{10,... | collective-permute-start | bytes 393224 | tf_op jit(solution)/shard_map/ppermute | solution.py:65
  4.6 6.2 %collective-permute-start = (f32[2,64,256]{2,1,0:T(8,128)S(1)}, f32[2,64,256]{2,1,0:T(8,128)S(1)}, u32[]{:S(2)}, u32[]{:S(2)}) collective-permute-start(f32[2,64,256]{2,1,0:T(8,128)S(1)} %stack.1.refs_5_.refs_0_), channel_id=1, source_target_pairs={{0,1},{1,0},{2,3},{3,2},{4,5},{5,4},{6,7},{7,6},{8,9},{9,8},{10,11... | collective-permute-start | bytes 393224 | tf_op jit(solution)/shard_map/ppermute | solution.py:65
  11.2 8.9 %collective-permute-start.6 = (f32[256,256]{1,0:T(8,128)S(1)}, f32[256,256]{1,0:T(8,128)S(1)}, u32[]{:S(2)}, u32[]{:S(2)}) collective-permute-start(f32[256,256]{1,0:T(8,128)S(1)} %get-tuple-element.38.refs_6_.own_map.refs_0_), channel_id=1, source_target_pairs={{0,4},{4,0},{8,12},{12,8},{16,20},{20,16},{24,28},{28,24},{1,5},{5... | collective-permute-start | bytes 786440 | tf_op jit(solution)/shard_map/ppermute | solution.py:65
  21.1 13.8 %collective-permute-start.8 = (f32[2,256,256]{2,1,0:T(8,128)S(1)}, f32[2,256,256]{2,1,0:T(8,128)S(1)}, u32[]{:S(2)}, u32[]{:S(2)}) collective-permute-start(f32[2,256,256]{2,1,0:T(8,128)S(1)} %get-tuple-element.53.refs_0_), channel_id=1, source_target_pairs={{0,8},{4,12},{8,0},{12,4},{16,24},{20,28},{24,16},{28,20},{1,9},{5... | collective-permute-start | bytes 1572872 | tf_op jit(solution)/shard_map/ppermute | solution.py:65
  23.0 1.3 %collective-permute-start.3 = (f32[128,256]{1,0:T(8,128)S(1)}, f32[128,256]{1,0:T(8,128)S(1)}, u32[]{:S(2)}, u32[]{:S(2)}) collective-permute-start(f32[128,256]{1,0:T(8,128)S(1)} %get-tuple-element.41.refs_2_), channel_id=1, source_target_pairs={{0,1},{1,0},{2,3},{3,2},{4,5},{5,4},{6,7},{7,6},{8,9},{9,8},{10,11... | collective-permute-start | bytes 393224 | tf_op jit(solution)/shard_map/ppermute | solution.py:65
  24.4 4.3 %collective-permute-start.4 = (f32[64,256]{1,0:T(8,128)S(1)}, f32[64,256]{1,0:T(8,128)S(1)}, u32[]{:S(2)}, u32[]{:S(2)}) collective-permute-start(f32[64,256]{1,0:T(8,128)S(1)} %get-tuple-element.43), channel_id=1, source_target_pairs={{0,2},{1,3},{2,0},{3,1},{4,6},{5,7},{6,4},{7,5},{8,10},{9,11},{10,... | collective-permute-start | bytes 196616 | tf_op jit(solution)/shard_map/ppermute | solution.py:65
  29.1 5.0 %collective-permute-start.5 = (f32[128,256]{1,0:T(8,128)S(1)}, f32[128,256]{1,0:T(8,128)S(1)}, u32[]{:S(2)}, u32[]{:S(2)}) collective-permute-start(f32[128,256]{1,0:T(8,128)S(1)} %get-tuple-element.46.refs_1_), channel_id=1, source_target_pairs={{0,4},{4,0},{8,12},{12,8},{16,20},{20,16},{24,28},{28,24},{1,5},{5... | collective-permute-start | bytes 393224 | tf_op jit(solution)/shard_map/ppermute | solution.py:65
  34.7 5.0 %collective-permute-start.7 = (f32[128,256]{1,0:T(8,128)S(1)}, f32[128,256]{1,0:T(8,128)S(1)}, u32[]{:S(2)}, u32[]{:S(2)}) collective-permute-start(f32[128,256]{1,0:T(8,128)S(1)} %get-tuple-element.52.refs_1_), channel_id=1, source_target_pairs={{0,8},{4,12},{8,0},{12,4},{16,24},{20,28},{24,16},{28,20},{1,9},{5... | collective-permute-start | bytes 393224 | tf_op jit(solution)/shard_map/ppermute | solution.py:65
  40.2 5.7 %collective-permute-start.9 = (f32[64,256]{1,0:T(8,128)S(1)}, f32[64,256]{1,0:T(8,128)S(1)}, u32[]{:S(2)}, u32[]{:S(2)}) collective-permute-start(f32[64,256]{1,0:T(8,128)S(1)} %get-tuple-element.60), channel_id=1, source_target_pairs={{0,16},{4,20},{8,24},{12,28},{16,0},{20,4},{24,8},{28,12},{1,17},{... | collective-permute-start | bytes 196616 | tf_op jit(solution)/shard_map/ppermute | solution.py:65
  46.1 5.7 %collective-permute-start.10 = (f32[64,256]{1,0:T(8,128)S(1)}, f32[64,256]{1,0:T(8,128)S(1)}, u32[]{:S(2)}, u32[]{:S(2)}) collective-permute-start(f32[64,256]{1,0:T(8,128)S(1)} %turn.1), channel_id=1, source_target_pairs={{0,16},{4,20},{8,24},{12,28},{16,0},{20,4},{24,8},{28,12},{1,17},{... | collective-permute-start | bytes 196616 | tf_op jit(solution)/shard_map/ppermute | solution.py:65
  52.3 4.3 %collective-permute-start.12 = (f32[64,256]{1,0:T(8,128)S(1)}, f32[64,256]{1,0:T(8,128)S(1)}, u32[]{:S(2)}, u32[]{:S(2)}) collective-permute-start(f32[64,256]{1,0:T(8,128)S(1)} %leave.1.refs_6_), channel_id=1, source_target_pairs={{0,2},{1,3},{2,0},{3,1},{4,6},{5,7},{6,4},{7,5},{8,10},{9,11},{10,... | collective-permute-start | bytes 196616 | tf_op jit(solution)/shard_map/ppermute | solution.py:65
  54.3 2.3 %collective-permute-start.11 = (f32[64,256]{1,0:T(8,128)S(1)}, f32[64,256]{1,0:T(8,128)S(1)}, u32[]{:S(2)}, u32[]{:S(2)}) collective-permute-start(f32[64,256]{1,0:T(8,128)S(1)} %leave.1.refs_6_), channel_id=1, source_target_pairs={{0,1},{1,0},{2,3},{3,2},{4,5},{5,4},{6,7},{7,6},{8,9},{9,8},{10,11... | collective-permute-start | bytes 196616 | tf_op jit(solution)/shard_map/ppermute | solution.py:65
  56.6 1.3 %collective-permute-start.13 = (f32[64,256]{1,0:T(8,128)S(1)}, f32[64,256]{1,0:T(8,128)S(1)}, u32[]{:S(2)}, u32[]{:S(2)}) collective-permute-start(f32[64,256]{1,0:T(8,128)S(1)} %collective-permute-done.12.refs_8_), channel_id=1, source_target_pairs={{0,1},{1,0},{2,3},{3,2},{4,5},{5,4},{6,7},{7,6},{8,9},{9,8},{10,11... | collective-permute-start | bytes 196616 | tf_op jit(solution)/shard_map/ppermute | solution.py:65

commit v4 on v3

--- a/solution.py
+++ b/solution.py
@@ -69,12 +69,31 @@
     return swap(x, axis, 1 << bit)
 
 
-def prepare_kernel(nodes, *refs):
+def prepare_nodes(count, rows_at, row_columns, dinv, upd, rhs, outs, waits):
+    acc, inv_hi, inv_lo, upd_hi, upd_lo = outs
+    size = dinv.shape[1]
+    width = acc.shape[2]
+    lane = lax.broadcasted_iota(jnp.int32, (size, size), 1).astype(F32)
+    for k in range(count):
+        for c in waits[k]:
+            c.wait()
+        inv_hi[k], inv_lo[k] = split(dinv[k])
+        high, low = split(upd[k])
+        chosen = (lane == row_columns[:, rows_at + k : rows_at + k + 1]).astype(BF16)
+        upd_hi[k] = dot1(chosen, high, NN).astype(BF16)
+        upd_lo[k] = dot1(chosen, low, NN).astype(BF16)
+        turned = rhs[k].T
+        for h in range(HALVES):
+            acc[h, k] = turned[h * width : (h + 1) * width]
+
+
+def prepare_first_kernel(nodes, *refs):
     (rows_h, sep_h, rhs_h, dinv_h, upd_h, _), refs = refs[:6], refs[6:]
-    (acc, inv_hi, inv_lo, upd_hi, upd_lo), refs = refs[:5], refs[5:]
+    outs, (top, row_columns, rhs_n, dinv_n, upd_n), refs = refs[:5], refs[5:10], refs[10:]
     rhs_v, dinv_v, upd_v, square, rows, sep, sems, small = refs
-    size, cols = rhs_v.shape[1:]
+    cols = rhs_v.shape[2]
     width = cols // HALVES
+    first = nodes // 2
     few = [
         pltpu.make_async_copy(src, dst, small.at[i])
         for i, (src, dst) in enumerate(((rows_h, rows), (sep_h, sep)))
@@ -83,10 +102,10 @@
         c.start()
     copies = []
     for k in range(nodes):
+        ins = (upd_v, dinv_v, rhs_v) if k < first else (upd_n, dinv_n, rhs_n)
         group = [
-            pltpu.make_async_copy(upd_h.at[k], upd_v.at[k], sems.at[2, k]),
-            pltpu.make_async_copy(dinv_h.at[k], dinv_v.at[k], sems.at[0, k]),
-            pltpu.make_async_copy(rhs_h.at[k], rhs_v.at[k], sems.at[1, k]),
+            pltpu.make_async_copy(src.at[k], dst.at[k % first], sems.at[i, k])
+            for i, (src, dst) in enumerate(zip((upd_h, dinv_h, rhs_h), ins))
         ]
         for c in group:
             c.start()
@@ -99,61 +118,118 @@
     square[pl.ds(pl.multiple_of(front * share, 8), share), :] = sep[...]
     turned = square[...].T
     for h in range(HALVES):
-        acc[h, nodes] = turned[h * width : (h + 1) * width]
-    row_columns = rows[...].astype(F32).T
-    lane = lax.broadcasted_iota(jnp.int32, (size, size), 1).astype(F32)
-    for k in range(nodes):
-        for c in copies[k]:
+        top[h] = turned[h * width : (h + 1) * width]
+    row_columns[...] = rows[...].astype(F32).T
+    prepare_nodes(first, 0, row_columns, dinv_v, upd_v, rhs_v, outs, copies[:first])
+    for group in copies[first:]:
+        for c in group:
             c.wait()
-        inv_hi[k], inv_lo[k] = split(dinv_v[k])
-        high, low = split(upd_v[k])
-        chosen = (lane == row_columns[:, k : k + 1]).astype(BF16)
-        upd_hi[k] = dot1(chosen, high, NN).astype(BF16)
-        upd_lo[k] = dot1(chosen, low, NN).astype(BF16)
-        turned = rhs_v[k].T
-        for h in range(HALVES):
-            acc[h, k] = turned[h * width : (h + 1) * width]
-
-
-def prepare(rhs, dinv, update, rows, sep, after):
+
+
+def prepare_second_kernel(first, row_columns, rhs, dinv, upd, _, *outs):
+    count = rhs.shape[0]
+    waits = [()] * count
+    prepare_nodes(count, first, row_columns, dinv, upd, rhs, outs, waits)
+
+
+def prepared(count, size, cols):
+    half = ((count, size, size), BF16)
+    return [((HALVES, count, cols // HALVES, size), F32), half, half, half, half]
+
+
+def prepare_first(rhs, dinv, update, rows, sep, after):
     nodes, size, cols = rhs.shape
-    big = pltpu.VMEM((nodes, size, size), F32)
-    half = ((nodes, size, size), BF16)
-    acc = ((HALVES, nodes + 1, cols // HALVES, size), F32)
+    first = nodes // 2
+    some = (first, size, cols)
+    big = pltpu.VMEM(some, F32)
     return call(
-        lambda *refs: prepare_kernel(nodes, *refs),
-        "prepare",
+        lambda *refs: prepare_first_kernel(nodes, *refs),
+        "prepare_first",
         [(HBM, a) for a in (rows, sep, rhs, dinv, update)] + [(pl.ANY, after)],
-        [acc, half, half, half, half],
-        [pltpu.VMEM((nodes, size, cols), F32), big, big, pltpu.VMEM((size, cols), F32)]
+        prepared(first, size, cols)
+        + [((HALVES, cols // HALVES, size), F32), ((size, nodes), F32)]
+        + [((nodes - first, *some[1:]), F32)] * 3,
+        [big, big, big, pltpu.VMEM((size, cols), F32)]
         + [pltpu.VMEM(rows.shape, jnp.int32), pltpu.VMEM(sep.shape, F32)]
         + [pltpu.SemaphoreType.DMA((3, nodes)), pltpu.SemaphoreType.DMA((2,))],
     )
 
 
-def forward_kernel(nodes, fronts, *refs):
-    parent_h, acc, inv_hi, inv_lo, upd_hi, upd_lo, _ = refs[:7]
-    solved, send, keep, square, parent, sem = refs[7:13]
+def prepare_second(row_columns, rhs, dinv, update, after):
+    count, size, cols = rhs.shape
+    first = row_columns.shape[1] - count
+    return call(
+        lambda *refs: prepare_second_kernel(first, *refs),
+        "prepare_second",
+        [(V, a) for a in (row_columns, rhs, dinv, update)] + [(pl.ANY, after)],
+        prepared(count, size, cols),
+    )
+
+
+def chain_up(begin, end, nodes, copy, parent, accs, halves, solved, offset):
+    inv_hi, inv_lo, upd_hi, upd_lo = halves
+    width = accs[0].shape[1]
+    for k in range(begin, end):
+        i = k - begin
+        inverse = (inv_hi[i], inv_lo[i])
+        update = (upd_hi[i], upd_lo[i])
+        for h in range(HALVES):
+            value = dot3(split(accs[h][k - offset]), inverse, NT)
+            solved[i, h * width : (h + 1) * width] = value
+            moved = dot3(split(value), update, NT)
+            if copy is not None:
+                copy.wait()
+                copy = None
+            above = (nodes if k == nodes - 1 else parent[k]) - offset
+            accs[h][above] = accs[h][above] - moved
+
+
+def chain_first_kernel(nodes, *refs):
+    parent_h, acc_a, acc_b, top = refs[:4]
+    halves, solved, rest, parent, sem = refs[4:8], refs[8], refs[9], refs[10], refs[11]
+    accs = refs[12:]
+    copy = pltpu.make_async_copy(parent_h, parent, sem)
+    copy.start()
+    first = acc_a.shape[1]
+    for h in range(HALVES):
+        for k in range(nodes):
+            accs[h][k] = acc_a[h, k] if k < first else acc_b[h, k - first]
+        accs[h][nodes] = top[h]
+    chain_up(0, first, nodes, copy, parent, accs, halves, solved, 0)
+    for h in range(HALVES):
+        for k in range(first, nodes + 1):
+            rest[h, k - first] = accs[h][k]
+
+
+def chain_first(parent, acc_a, acc_b, top, halves):
+    first, (width, size) = acc_a.shape[1], acc_a.shape[2:]
+    nodes = first + acc_b.shape[1]
+    return call(
+        lambda *refs: chain_first_kernel(nodes, *refs),
+        "chain_first",
+        [(HBM, parent)] + [(V, a) for a in (acc_a, acc_b, top, *halves)],
+        [((first, width * HALVES, size), F32), ((HALVES, nodes - first + 1, width, size), F32)],
+        [pltpu.SMEM((nodes,), jnp.int32), pltpu.SemaphoreType.DMA]
+        + [pltpu.VMEM((nodes + 1, width, size), F32)] * HALVES,
+    )
+
+
+def chain_second_kernel(nodes, fronts, *refs):
+    parent_h, rest = refs[:2]
+    halves, solved, send, keep, square, parent, sem = refs[2:6], *refs[7:13]
     accs = refs[13:]
     copy = pltpu.make_async_copy(parent_h, parent, sem)
     copy.start()
-    width, size = acc.shape[2:]
-    cols = width * HALVES
+    count = rest.shape[1]
+    width = rest.shape[2]
     for h in range(HALVES):
-        accs[h][...] = acc[h]
-    copy.wait()
-    for k in range(nodes):
-        inverse = (inv_hi[k], inv_lo[k])
-        update = (upd_hi[k], upd_lo[k])
-        above = parent[k]
-        for h in range(HALVES):
-            value = dot3(split(accs[h][k]), inverse, NT)
-            solved[k, h * width : (h + 1) * width] = value
-            accs[h][above] = accs[h][above] - dot3(split(value), update, NT)
+        accs[h][...] = rest[h]
+    first = nodes + 1 - count
+    chain_up(first, nodes, nodes, copy, parent, accs, halves, solved, first)
     front = lax.axis_index("front")
-    chunk = cols // fronts
+    chunk = width * HALVES // fronts
     for h in range(HALVES):
-        square[h * width : (h + 1) * width] = accs[h][nodes]
+        square[h * width : (h + 1) * width] = accs[h][nodes - first]
     low_bit = front % 2
     for i in range(fronts // 2):
         for ref, own in ((keep, low_bit), (send, 1 - low_bit)):
@@ -161,26 +237,28 @@
             ref[i * chunk : (i + 1) * chunk] = square[pl.ds(start, chunk), :]
 
 
-def local_forward(parent, acc, halves, after, fronts):
-    nodes, (width, size) = acc.shape[1] - 1, acc.shape[2:]
+def chain_second(parent, rest, halves, after, fronts):
+    nodes = parent.shape[0]
+    count, width, size = rest.shape[1:]
     cols = width * HALVES
     part = ((cols // 2, size), F32)
     return call(
-        lambda *refs: forward_kernel(nodes, fronts, *refs),
-        "local_forward",
-        [(HBM, parent), (V, acc)] + [(V, a) for a in halves] + [(pl.ANY, after)],
-        [((nodes, cols, size), F32), part, part],
+        lambda *refs: chain_second_kernel(nodes, fronts, *refs),
+        "chain_second",
+        [(HBM, parent)] + [(V, a) for a in (rest, *halves)] + [(pl.ANY, after)],
+        [((count - 1, cols, size), F32), part, part],
         [pltpu.VMEM((cols, size), F32), pltpu.SMEM((nodes,), jnp.int32), pltpu.SemaphoreType.DMA]
-        + [pltpu.VMEM((nodes + 1, width, size), F32)] * HALVES,
+        + [pltpu.VMEM((count, width, size), F32)] * HALVES,
     )
 
 
 def backward_kernel(nodes, fronts, *refs):
-    parent_h, solved, inv_hi, inv_lo, upd_hi, upd_lo = refs[:6]
-    pieces = refs[6 : 6 + fronts]
-    sol, sep_out = refs[6 + fronts : 8 + fronts]
-    square, parent, staged, sem, sems = refs[8 + fronts : 13 + fronts]
-    known = refs[13 + fronts :]
+    parent_h, parts, refs = refs[0], (refs[1:6], refs[6:11]), refs[11:]
+    pieces = refs[:fronts]
+    sol, sep_out = refs[fronts : 2 + fronts]
+    square, parent, staged, sem, sems = refs[2 + fronts : 7 + fronts]
+    known = refs[7 + fronts :]
+    first = parts[0][0].shape[0]
     copy = pltpu.make_async_copy(parent_h, parent, sem)
     copy.start()
     front = lax.axis_index("front")
@@ -194,15 +272,18 @@
     square[...] = square[...].T
     share = sep_out.shape[0]
     sep_out[...] = square[pl.ds(pl.multiple_of(front * share, 8), share), :]
-    copy.wait()
     outs = []
     for k in reversed(range(nodes)):
-        inverse = (inv_hi[k], inv_lo[k])
-        update = (upd_hi[k], upd_lo[k])
-        above = parent[k]
+        i = k % first
+        solved, inv_hi, inv_lo, upd_hi, upd_lo = parts[k // first]
+        inverse = (inv_hi[i], inv_lo[i])
+        update = (upd_hi[i], upd_lo[i])
+        if k == nodes - 2:
+            copy.wait()
+        above = nodes if k == nodes - 1 else parent[k]
         for h in range(HALVES):
             rows = slice(h * width, (h + 1) * width)
-            part = solved[k, rows] - dot3(split(known[h][above]), update, NN)
+            part = solved[i, rows] - dot3(split(known[h][above]), update, NN)
             value = dot3(split(part), inverse, NN)
             known[h][k] = value
             staged[k, :, rows] = value.T
@@ -213,11 +294,12 @@
         out.wait()
 
 
-def local_backward(parent, solved, halves, pieces):
-    nodes, cols, size = solved.shape
+def local_backward(parent, parts, pieces):
+    nodes = parent.shape[0]
+    cols, size = parts[0][0].shape[1:]
     fronts = len(pieces)
     sol, sep = jax.ShapeDtypeStruct((nodes, size, cols), F32), ((size // fronts, cols), F32)
-    ins = [(HBM, parent)] + [(V, a) for a in (solved, *halves, *pieces)]
+    ins = [(HBM, parent)] + [(V, a) for a in (*parts[0], *parts[1], *pieces)]
     return pl.pallas_call(
         lambda *refs: backward_kernel(nodes, fronts, *refs),
         name="local_backward",
@@ -263,6 +345,26 @@
         [((size, size), F32), ((2, size, size), BF16)],
         [pltpu.VMEM((2, size, size), F32)],
     )
+
+
+def pack_maps(pack, k, t):
+    half = k.shape[0] // 2
+    pack[0], pack[1], pack[2] = k[:half, :half], k[:half, half:], k[half:, half:]
+    if t is not None:
+        for i in range(4):
+            r, c = (i // 2) * half, (i % 2) * half
+            pack[3 + i] = t[r : r + half, c : c + half]
+
+
+def pack_k(pack):
+    first = jnp.concatenate([pack[0], pack[1]], axis=1)
+    second = jnp.concatenate([pack[1].T, pack[2]], axis=1)
+    return jnp.concatenate([first, second], axis=0)
+
+
+def pack_t(pack):
+    rows = [jnp.concatenate([pack[3 + i], pack[4 + i]], axis=1) for i in (0, 2)]
+    return jnp.concatenate(rows, axis=0)
 
 
 def first_merge_kernel(*refs):
@@ -278,8 +380,7 @@
     curve_u[0], curve_u[1] = k_up_s
     x = dot3(k_up_s, low_s, NN)
     t = dot3(up_s, low_s, NN)
-    pack[1] = t
-    pack[0] = dot3(low_s, low_s, TN) + dot3(low_s, split(x), TN)
+    pack_maps(pack, dot3(low_s, low_s, TN) + dot3(low_s, split(x), TN), t)
     size = low.shape[0]
     row = lax.broadcasted_iota(jnp.int32, (size, size), 0)
     col = lax.broadcasted_iota(jnp.int32, (size, size), 1)
@@ -293,10 +394,11 @@
     own, other, mixed = refs[:3]
     upper = bit_of("leaf", bit) == 1
     pack, mixed_n, halves, curve_u, total_u, total_l = refs[3:]
-    low_s = split(jnp.where(upper, other[1], own[1]))
-    up_s = split(jnp.where(upper, own[1], other[1]))
-    k_low = jnp.where(upper, other[0], own[0])
-    k_up_s = split(jnp.where(upper, own[0], other[0]))
+    own_k, own_t, other_k, other_t = pack_k(own), pack_t(own), pack_k(other), pack_t(other)
+    low_s = split(jnp.where(upper, other_t, own_t))
+    up_s = split(jnp.where(upper, own_t, other_t))
+    k_low = jnp.where(upper, other_k, own_k)
+    k_up_s = split(jnp.where(upper, own_k, other_k))
     for ref, value in ((total_u, up_s), (total_l, low_s), (curve_u, k_up_s)):
         ref[0], ref[1] = value
     x = dot3(k_up_s, low_s, NN)
@@ -308,18 +410,18 @@
     a_n = jnp.where(upper, dot3(a_s, low_s, NN), a + dot3(e_s, x_s, TN))
     e_n = jnp.where(upper, e, dot3(up_s, e_s, NN))
     if last:
-        keep_split(pack, k)
+        pack_maps(pack, k, None)
         keep_split(mixed_n, jnp.where(bit_of("leaf", bit + 1) == 1, a_n.T, e_n))
     else:
-        pack[0] = k
-        pack[1] = dot3(up_s, low_s, NN)
+        pack_maps(pack, k, dot3(up_s, low_s, NN))
         mixed_n[0], mixed_n[1] = a_n, e_n
 
 
 def maps(size, last):
     both = ((2, size, size), BF16)
-    kept = both if last else ((2, size, size), F32)
-    return [kept, kept, both, both, both, both]
+    half = size // 2
+    pack = ((3 if last else 7, half, half), F32)
+    return [pack, both if last else ((2, size, size), F32), both, both, both, both]
 
 
 def fold_kernel(bit, own, other, send, keep):
@@ -359,18 +461,17 @@
     given = split(jnp.where(upper, z_low, middle))
     sol_n[...] = sol[...] + dot3(given, pair(halves), NN)
     if last:
-        message[0][...], message[1][...] = z_new, p_new
+        message[0][...] = jnp.where(bit_of("leaf", bit + 1) == 1, p_new, z_new)
+        message[1][...] = z_new
     else:
         message[0][:rows], message[0][rows:] = z_new, p_new
 
 
-def turn_kernel(message, came, curve, back):
-    back[...] = message[...] + dot3(split(came[...]), pair(curve), NN)
-
-
-def leave_kernel(bit, sol, came, back, halves, inverse, top):
+def leave_kernel(bit, sol, own_z, came, halves, pack, inverse, top):
     upper = bit_of("leaf", bit) == 1
-    given = split(jnp.where(upper, came[...], back[...]))
+    value = came[...]
+    middle = value + dot3(split(own_z[...]), split(pack_k(pack)), NN)
+    given = split(jnp.where(upper, value, middle))
     value = sol[...] + dot3(given, pair(halves), NN)
     top[...] = dot3(split(value), pair(inverse), NN)
 
@@ -398,20 +499,22 @@
         [pltpu.SemaphoreType.DMA((2,))],
     )
     came = [swap(stacked, "front", m) for m in range(1, fronts)]
-    acc, *local_halves = prepare(
+    acc_a, *first_halves = prepare_first(
         rhs_local, dinv_local, update_local, row_blocks, sep_rhs, stacked
     )
-    own_map, inverse = block_map([stacked, *came], acc)
+    first_halves, (top, row_columns, *raw) = first_halves[:4], first_halves[4:]
+    own_map, inverse = block_map([stacked, *came], acc_a)
     other_map = exchange(own_map, "leaf", 0)
-
-    solved, send, keep = local_forward(parent, acc, local_halves, own_map, fronts)
-
+    acc_b, *second_halves = prepare_second(row_columns, *raw, own_map)
+    first_solved, rest = chain_first(parent, acc_a, acc_b, top, first_halves)
     pack, mixed, *tools = call(
         first_merge_kernel,
         "merge_0",
-        [(V, own_map), (V, other_map), (pl.ANY, send)],
+        [(V, own_map), (V, other_map), (pl.ANY, rest)],
         maps(size, False),
     )
+    other_pack = exchange(pack, "leaf", 1)
+    second_solved, send, keep = chain_second(parent, rest, second_halves, mixed, fronts)
     for bit in range(front_bits):
         received = exchange(send, "front", bit)
         if bit + 1 < front_bits:
@@ -432,8 +535,6 @@
     for bit in range(rounds - 1):
         last = bit == rounds - 2
         received = exchange(message, "leaf", bit)
-        if not last:
-            other_pack = exchange(pack, "leaf", bit + 1)
         sol, *message = call(
             lambda *refs, bit=bit, last=last: step_kernel(bit, last, *refs),
             f"step_{bit}",
@@ -449,18 +550,17 @@
                 [(V, a) for a in (pack, other_pack, mixed)],
                 maps(size, last),
             )
+            other_pack = exchange(pack, "leaf", bit + 2)
     came = exchange(message[0], "leaf", rounds - 1)
-    (back,) = call(turn_kernel, "turn", [(V, a) for a in (message[1], came, pack)], [part])
-    back = exchange(back, "leaf", rounds - 1)
     (top,) = call(
         lambda *refs: leave_kernel(rounds - 1, *refs),
         "leave",
-        [(V, a) for a in (sol, came, back, mixed, inverse)],
+        [(V, a) for a in (sol, message[1], came, mixed, other_pack, inverse)],
         [part],
     )
     pieces = gather_front(top, front_bits)
     sol_local, sep_solution = local_backward(
-        parent, solved, local_halves, pieces
+        parent, [(first_solved, *first_halves), (second_solved, *second_halves)], pieces
     )
     return (sol_local, sep_solution)
 

time: 63.6 us -> 63.9 us (level)
  waiting for transfers between devices: 21.2 us -> 22.2 us
  starting transfers between devices: 19.7 us -> 18.8 us
    ppermute x14, waiting for transfers between devices: 21.2 us -> 22.2 us  [swap(): return lax.ppermute(x, axis, [(i, i ^ mask) for i in range(n)])]
    ppermute x14, starting transfers between devices: 19.7 us -> 18.8 us  [swap(): return lax.ppermute(x, axis, [(i, i ^ mask) for i in range(n)])]
    pallas_call x12 -> x13, Pallas kernels: 16.3 us -> 16.4 us  [call(): pl.pallas_call(kernel, name=name, in_specs=specs, out_specs=tuple((pl.Blo...]
  transfers between devices with their start and end apart: 14 -> 14, of which waited for: 10 -> 9; matrix products, arithmetic and copies ran while one was open for 0% -> 0% of each run, Pallas kernels for 20% -> 21%
where the time goes in v4:
time: 63.9 us; the launch traced here: 63.7 us
  waiting for transfers between devices  22.2 us (35%)
  Pallas kernels  22 us (34%)
  starting transfers between devices  18.8 us (29%)
  between operations  0.74 us (1%)
    ppermute x14, waiting for transfers between devices, swap(): return lax.ppermute(x, axis, [(i, i ^ mask) for i in range(n)])  22.2 us
    ppermute x14, starting transfers between devices, swap(): return lax.ppermute(x, axis, [(i, i ^ mask) for i in range(n)])  18.8 us
    pallas_call x13, Pallas kernels, call(): pl.pallas_call(kernel, name=name, in_specs=specs, out_specs=tuple((pl.Blo...  16.4 us
    pallas_call x1, Pallas kernels, local_backward(): pl.pallas_call(lambda *refs: backward_kernel(nodes, fronts, *refs), name=...  5.61 us
  transfers between devices with their start and end apart: 14, of which 9 were waited for; matrix products, arithmetic and copies ran while one was open for 0% of the time, Pallas kernels for 21%

profile of v4, /device:TPU:0, one launch (start us, length us, event | category | flops | bytes accessed | tf_op | source)
XLA Modules:
  0.0 63.7 jit_solution(11363788493526042923)
XLA Ops:
  0.6 0.9 %stack.1.refs_5_.refs_0_ = f32[2,64,256]{2,1,0:T(8,128)S(1)} custom-call(f32[64,256]{1,0:T(8,128)} %first.1, f32[64,256]{1,0:T(8,128)} %second.1), custom_call_target="tpu_custom_call" | custom-call | tf_op jit(solution)/shard_map/stack/pallas_call | solution.py:48
  1.5 2.4 %collective-permute-start.2 = (f32[2,64,256]{2,1,0:T(8,128)S(1)}, f32[2,64,256]{2,1,0:T(8,128)S(1)}, u32[]{:S(2)}, u32[]{:S(2)}) collective-permute-start(f32[2,64,256]{2,1,0:T(8,128)S(1)} %stack.1.refs_5_.refs_0_), channel_id=1, source_target_pairs={{0,3},{1,2},{2,1},{3,0},{4,7},{5,6},{6,5},{7,4},{8,11},{9,10},{10,... | collective-permute-start | bytes 393224 | tf_op jit(solution)/shard_map/ppermute | solution.py:65
  4.7 4.3 %prepare_first.1 = (f32[2,4,128,256]{3,2,1,0:T(8,128)S(1)}, bf16[4,256,256]{2,1,0:T(8,128)(2,1)S(1)}, bf16[4,256,256]{2,1,0:T(8,128)(2,1)S(1)}, bf16[4,256,256]{...) custom-call(s32[8,256]{1,0:T(8,128)} %refs_0_.4, ...), custom_call_target="tpu_custom_call" | custom-call | tf_op jit(solution)/shard_map/prepare_first/pallas_call | solution.py:48
  8.9 1.9 %collective-permute-done.1.refs_2_ = f32[2,64,256]{2,1,0:T(8,128)S(1)} collective-permute-done((f32[2,64,256]{2,1,0:T(8,128)S(1)}, f32[2,64,256]{2,1,0:T(8,128)S(1)}, u32[]{:S(2)}, u32[]{:S(2)}) %collective-permute-start.1) | collective-permute-done | bytes 131104 | tf_op jit(solution)/shard_map/ppermute | solution.py:65
  11.2 2.4 %collective-permute-start.3 = (f32[256,256]{1,0:T(8,128)S(1)}, f32[256,256]{1,0:T(8,128)S(1)}, u32[]{:S(2)}, u32[]{:S(2)}) collective-permute-start(f32[256,256]{1,0:T(8,128)S(1)} %get-tuple-element.50.refs_4_.refs_0_.own_map), channel_id=1, source_target_pairs={{0,4},{4,0},{8,12},{12,8},{16,20},{20,16},{24,28},{28,24},{1,5},{5... | collective-permute-start | bytes 786440 | tf_op jit(solution)/shard_map/ppermute | solution.py:65
  14.2 3.1 %chain_first.1 = (f32[4,256,256]{2,1,0:T(8,128)S(1)}, f32[2,5,128,256]{3,2,1,0:T(8,128)S(1)}) custom-call(s32[8]{0:T(128)} %refs_0_.7, f32[2,4,128,256]{3,2,1,0:T(8,128)S(1)} %get-tuple-element.45.refs_4_.refs_1_, f32[2,4,128,256]{3,2,1,0:T(8,128)S(1)} %get-tuple-element.51.refs_2_, f32[2,128,256]{2,1,0:T(8,128)S(1)} %get-tuple-element.52.refs_3_, ...), custom_call_target="tpu_custom_call" | custom-call | tf_op jit(solution)/shard_map/chain_first/pallas_call | solution.py:48
  17.3 2.8 %collective-permute-done.3.refs_1_ = f32[256,256]{1,0:T(8,128)S(1)} collective-permute-done((f32[256,256]{1,0:T(8,128)S(1)}, f32[256,256]{1,0:T(8,128)S(1)}, u32[]{:S(2)}, u32[]{:S(2)}) %collective-permute-start.3) | collective-permute-done | bytes 262176 | tf_op jit(solution)/shard_map/ppermute | solution.py:65
  20.1 1.0 %merge_0.1 = (f32[7,128,128]{2,1,0:T(8,128)S(1)}, f32[2,256,256]{2,1,0:T(8,128)S(1)}, bf16[2,256,256]{2,1,0:T(8,128)(2,1)S(1)}, bf16[2,256,256]{2,1,0:T(8,128)(2...) custom-call(f32[256,256]{1,0:T(8,128)S(1)} %get-tuple-element.50.refs_4_.refs_0_.own_map, ...), custom_call_target="tpu_custom_call" | custom-call | tf_op jit(solution)/shard_map/merge_0/pallas_call | solution.py:48
  21.1 1.9 %collective-permute-start.8 = (f32[7,128,128]{2,1,0:T(8,128)S(1)}, f32[7,128,128]{2,1,0:T(8,128)S(1)}, u32[]{:S(2)}, u32[]{:S(2)}) collective-permute-start(f32[7,128,128]{2,1,0:T(8,128)S(1)} %get-tuple-element.78.refs_0_), channel_id=1, source_target_pairs={{0,8},{4,12},{8,0},{12,4},{16,24},{20,28},{24,16},{28,20},{1,9},{5... | collective-permute-start | bytes 1376264 | tf_op jit(solution)/shard_map/ppermute | solution.py:65
  23.0 3.1 %chain_second.1 = (f32[4,256,256]{2,1,0:T(8,128)S(1)}, f32[128,256]{1,0:T(8,128)S(1)}, f32[128,256]{1,0:T(8,128)S(1)}) custom-call(s32[8]{0:T(128)} %refs_0_.7, f32[2,5,128,256]{3,2,1,0:T(8,128)S(1)} %get-tuple-element.58.refs_2_.refs_1_, bf16[4,256,256]{2,1,0:T(8,128)(2,1)S(1)} %get-tuple-element.59.refs_2_.refs_7_, ...), custom_call_target="tpu_custom_call" | custom-call | tf_op jit(solution)/shard_map/chain_second/pallas_call | solution.py:48
  26.1 1.3 %collective-permute-done.4.refs_1_ = f32[128,256]{1,0:T(8,128)S(1)} collective-permute-done((f32[128,256]{1,0:T(8,128)S(1)}, f32[128,256]{1,0:T(8,128)S(1)}, u32[]{:S(2)}, u32[]{:S(2)}) %collective-permute-start.4) | collective-permute-done | bytes 131104 | tf_op jit(solution)/shard_map/ppermute | solution.py:65
  27.5 1.6 %collective-permute-start.5 = (f32[64,256]{1,0:T(8,128)S(1)}, f32[64,256]{1,0:T(8,128)S(1)}, u32[]{:S(2)}, u32[]{:S(2)}) collective-permute-start(f32[64,256]{1,0:T(8,128)S(1)} %get-tuple-element.68), channel_id=1, source_target_pairs={{0,2},{1,3},{2,0},{3,1},{4,6},{5,7},{6,4},{7,5},{8,10},{9,11},{10,... | collective-permute-start | bytes 196616 | tf_op jit(solution)/shard_map/ppermute | solution.py:65
  29.1 2.7 %collective-permute-done.5.other = f32[64,256]{1,0:T(8,128)S(1)} collective-permute-done((f32[64,256]{1,0:T(8,128)S(1)}, f32[64,256]{1,0:T(8,128)S(1)}, u32[]{:S(2)}, u32[]{:S(2)}) %collective-permute-start.5) | collective-permute-done | bytes 65568 | tf_op jit(solution)/shard_map/ppermute | solution.py:65
  32.3 1.6 %collective-permute-start.6 = (f32[128,256]{1,0:T(8,128)S(1)}, f32[128,256]{1,0:T(8,128)S(1)}, u32[]{:S(2)}, u32[]{:S(2)}) collective-permute-start(f32[128,256]{1,0:T(8,128)S(1)} %get-tuple-element.71.refs_1_), channel_id=1, source_target_pairs={{0,4},{4,0},{8,12},{12,8},{16,20},{20,16},{24,28},{28,24},{1,5},{5... | collective-permute-start | bytes 393224 | tf_op jit(solution)/shard_map/ppermute | solution.py:65
  33.9 3.4 %collective-permute-done.6.refs_2_ = f32[128,256]{1,0:T(8,128)S(1)} collective-permute-done((f32[128,256]{1,0:T(8,128)S(1)}, f32[128,256]{1,0:T(8,128)S(1)}, u32[]{:S(2)}, u32[]{:S(2)}) %collective-permute-start.6) | collective-permute-done | bytes 131104 | tf_op jit(solution)/shard_map/ppermute | solution.py:65
  38.1 0.9 %merge_1.1 = (f32[3,128,128]{2,1,0:T(8,128)S(1)}, bf16[2,256,256]{2,1,0:T(8,128)(2,1)S(1)}, bf16[2,256,256]{2,1,0:T(8,128)(2,1)S(1)}, bf16[2,256,256]{2,1,0:T(8,...) custom-call(f32[7,128,128]{2,1,0:T(8,128)S(1)} %get-tuple-element.78.refs_0_, ...), custom_call_target="tpu_custom_call" | custom-call | tf_op jit(solution)/shard_map/merge_1/pallas_call | solution.py:48
  39.1 2.9 %collective-permute-start.10 = (f32[3,128,128]{2,1,0:T(8,128)S(1)}, f32[3,128,128]{2,1,0:T(8,128)S(1)}, u32[]{:S(2)}, u32[]{:S(2)}) collective-permute-start(f32[3,128,128]{2,1,0:T(8,128)S(1)} %get-tuple-element.87), channel_id=1, source_target_pairs={{0,16},{4,20},{8,24},{12,28},{16,0},{20,4},{24,8},{28,12},{1,17},{... | collective-permute-start | bytes 589832 | tf_op jit(solution)/shard_map/ppermute | solution.py:65
  41.9 1.6 %collective-permute-done.7.refs_2_ = f32[128,256]{1,0:T(8,128)S(1)} collective-permute-done((f32[128,256]{1,0:T(8,128)S(1)}, f32[128,256]{1,0:T(8,128)S(1)}, u32[]{:S(2)}, u32[]{:S(2)}) %collective-permute-start.7) | collective-permute-done | bytes 131104 | tf_op jit(solution)/shard_map/ppermute | solution.py:65
  44.1 3.4 %collective-permute-start.9 = (f32[64,256]{1,0:T(8,128)S(1)}, f32[64,256]{1,0:T(8,128)S(1)}, u32[]{:S(2)}, u32[]{:S(2)}) collective-permute-start(f32[64,256]{1,0:T(8,128)S(1)} %get-tuple-element.85), channel_id=1, source_target_pairs={{0,16},{4,20},{8,24},{12,28},{16,0},{20,4},{24,8},{28,12},{1,17},{... | collective-permute-start | bytes 196616 | tf_op jit(solution)/shard_map/ppermute | solution.py:65
  47.4 4.5 %collective-permute-done.9.refs_2_ = f32[64,256]{1,0:T(8,128)S(1)} collective-permute-done((f32[64,256]{1,0:T(8,128)S(1)}, f32[64,256]{1,0:T(8,128)S(1)}, u32[]{:S(2)}, u32[]{:S(2)}) %collective-permute-start.9) | collective-permute-done | bytes 65568 | tf_op jit(solution)/shard_map/ppermute | solution.py:65
  52.5 1.6 %collective-permute-start.12 = (f32[64,256]{1,0:T(8,128)S(1)}, f32[64,256]{1,0:T(8,128)S(1)}, u32[]{:S(2)}, u32[]{:S(2)}) collective-permute-start(f32[64,256]{1,0:T(8,128)S(1)} %leave.1.refs_11_), channel_id=1, source_target_pairs={{0,2},{1,3},{2,0},{3,1},{4,6},{5,7},{6,4},{7,5},{8,10},{9,11},{10,... | collective-permute-start | bytes 196616 | tf_op jit(solution)/shard_map/ppermute | solution.py:65
  54.2 2.7 %collective-permute-done.12.refs_13_ = f32[64,256]{1,0:T(8,128)S(1)} collective-permute-done((f32[64,256]{1,0:T(8,128)S(1)}, f32[64,256]{1,0:T(8,128)S(1)}, u32[]{:S(2)}, u32[]{:S(2)}) %collective-permute-start.12) | collective-permute-done | bytes 65568 | tf_op jit(solution)/shard_map/ppermute | solution.py:65
  56.9 1.2 %collective-permute-done.13.refs_14_ = f32[64,256]{1,0:T(8,128)S(1)} collective-permute-done((f32[64,256]{1,0:T(8,128)S(1)}, f32[64,256]{1,0:T(8,128)S(1)}, u32[]{:S(2)}, u32[]{:S(2)}) %collective-permute-start.13) | collective-permute-done | bytes 65568 | tf_op jit(solution)/shard_map/ppermute | solution.py:65
  58.1 5.6 %local_backward.1 = (f32[8,256,256]{2,1,0:T(8,128)}, f32[64,256]{1,0:T(8,128)}) custom-call(s32[8]{0:T(128)} %refs_0_.7, f32[4,256,256]{2,1,0:T(8,128)S(1)} %get-tuple-element.57.refs_1_, bf16[4,256,256]{2,1,0:T(8,128)(2,1)S(1)} %get-tuple-element.53.refs_4_.refs_2_, bf16[4,256,256]{2,1,0:T(8,128)(2,1)S(1)} %get-tuple-element.54.refs_5_.refs_3_, ...), custom_call_target="tpu_custom_call" | custom-call | tf_op jit(solution)/shard_map/local_backward/pallas_call | solution.py:303
  (18 shorter events, 4.1 us)
Async XLA Ops:
  1.5 7.4 %collective-permute-start.2 = (f32[2,64,256]{2,1,0:T(8,128)S(1)}, f32[2,64,256]{2,1,0:T(8,128)S(1)}, u32[]{:S(2)}, u32[]{:S(2)}) collective-permute-start(f32[2,64,256]{2,1,0:T(8,128)S(1)} %stack.1.refs_5_.refs_0_), channel_id=1, source_target_pairs={{0,3},{1,2},{2,1},{3,0},{4,7},{5,6},{6,5},{7,4},{8,11},{9,10},{10,... | collective-permute-start | bytes 393224 | tf_op jit(solution)/shard_map/ppermute | solution.py:65
  4.0 6.9 %collective-permute-start.1 = (f32[2,64,256]{2,1,0:T(8,128)S(1)}, f32[2,64,256]{2,1,0:T(8,128)S(1)}, u32[]{:S(2)}, u32[]{:S(2)}) collective-permute-start(f32[2,64,256]{2,1,0:T(8,128)S(1)} %stack.1.refs_5_.refs_0_), channel_id=1, source_target_pairs={{0,2},{1,3},{2,0},{3,1},{4,6},{5,7},{6,4},{7,5},{8,10},{9,11},{10,... | collective-permute-start | bytes 393224 | tf_op jit(solution)/shard_map/ppermute | solution.py:65
  4.6 6.2 %collective-permute-start = (f32[2,64,256]{2,1,0:T(8,128)S(1)}, f32[2,64,256]{2,1,0:T(8,128)S(1)}, u32[]{:S(2)}, u32[]{:S(2)}) collective-permute-start(f32[2,64,256]{2,1,0:T(8,128)S(1)} %stack.1.refs_5_.refs_0_), channel_id=1, source_target_pairs={{0,1},{1,0},{2,3},{3,2},{4,5},{5,4},{6,7},{7,6},{8,9},{9,8},{10,11... | collective-permute-start | bytes 393224 | tf_op jit(solution)/shard_map/ppermute | solution.py:65
  11.2 8.9 %collective-permute-start.3 = (f32[256,256]{1,0:T(8,128)S(1)}, f32[256,256]{1,0:T(8,128)S(1)}, u32[]{:S(2)}, u32[]{:S(2)}) collective-permute-start(f32[256,256]{1,0:T(8,128)S(1)} %get-tuple-element.50.refs_4_.refs_0_.own_map), channel_id=1, source_target_pairs={{0,4},{4,0},{8,12},{12,8},{16,20},{20,16},{24,28},{28,24},{1,5},{5... | collective-permute-start | bytes 786440 | tf_op jit(solution)/shard_map/ppermute | solution.py:65
  21.1 17.0 %collective-permute-start.8 = (f32[7,128,128]{2,1,0:T(8,128)S(1)}, f32[7,128,128]{2,1,0:T(8,128)S(1)}, u32[]{:S(2)}, u32[]{:S(2)}) collective-permute-start(f32[7,128,128]{2,1,0:T(8,128)S(1)} %get-tuple-element.78.refs_0_), channel_id=1, source_target_pairs={{0,8},{4,12},{8,0},{12,4},{16,24},{20,28},{24,16},{28,20},{1,9},{5... | collective-permute-start | bytes 1376264 | tf_op jit(solution)/shard_map/ppermute | solution.py:65
  26.1 1.4 %collective-permute-start.4 = (f32[128,256]{1,0:T(8,128)S(1)}, f32[128,256]{1,0:T(8,128)S(1)}, u32[]{:S(2)}, u32[]{:S(2)}) collective-permute-start(f32[128,256]{1,0:T(8,128)S(1)} %get-tuple-element.66), channel_id=1, source_target_pairs={{0,1},{1,0},{2,3},{3,2},{4,5},{5,4},{6,7},{7,6},{8,9},{9,8},{10,11... | collective-permute-start | bytes 393224 | tf_op jit(solution)/shard_map/ppermute | solution.py:65
  27.5 4.3 %collective-permute-start.5 = (f32[64,256]{1,0:T(8,128)S(1)}, f32[64,256]{1,0:T(8,128)S(1)}, u32[]{:S(2)}, u32[]{:S(2)}) collective-permute-start(f32[64,256]{1,0:T(8,128)S(1)} %get-tuple-element.68), channel_id=1, source_target_pairs={{0,2},{1,3},{2,0},{3,1},{4,6},{5,7},{6,4},{7,5},{8,10},{9,11},{10,... | collective-permute-start | bytes 196616 | tf_op jit(solution)/shard_map/ppermute | solution.py:65
  32.3 5.0 %collective-permute-start.6 = (f32[128,256]{1,0:T(8,128)S(1)}, f32[128,256]{1,0:T(8,128)S(1)}, u32[]{:S(2)}, u32[]{:S(2)}) collective-permute-start(f32[128,256]{1,0:T(8,128)S(1)} %get-tuple-element.71.refs_1_), channel_id=1, source_target_pairs={{0,4},{4,0},{8,12},{12,8},{16,20},{20,16},{24,28},{28,24},{1,5},{5... | collective-permute-start | bytes 393224 | tf_op jit(solution)/shard_map/ppermute | solution.py:65
  37.8 5.7 %collective-permute-start.7 = (f32[128,256]{1,0:T(8,128)S(1)}, f32[128,256]{1,0:T(8,128)S(1)}, u32[]{:S(2)}, u32[]{:S(2)}) collective-permute-start(f32[128,256]{1,0:T(8,128)S(1)} %get-tuple-element.77.refs_1_), channel_id=1, source_target_pairs={{0,8},{4,12},{8,0},{12,4},{16,24},{20,28},{24,16},{28,20},{1,9},{5... | collective-permute-start | bytes 393224 | tf_op jit(solution)/shard_map/ppermute | solution.py:65
  39.1 12.8 %collective-permute-start.10 = (f32[3,128,128]{2,1,0:T(8,128)S(1)}, f32[3,128,128]{2,1,0:T(8,128)S(1)}, u32[]{:S(2)}, u32[]{:S(2)}) collective-permute-start(f32[3,128,128]{2,1,0:T(8,128)S(1)} %get-tuple-element.87), channel_id=1, source_target_pairs={{0,16},{4,20},{8,24},{12,28},{16,0},{20,4},{24,8},{28,12},{1,17},{... | collective-permute-start | bytes 589832 | tf_op jit(solution)/shard_map/ppermute | solution.py:65
  44.1 7.8 %collective-permute-start.9 = (f32[64,256]{1,0:T(8,128)S(1)}, f32[64,256]{1,0:T(8,128)S(1)}, u32[]{:S(2)}, u32[]{:S(2)}) collective-permute-start(f32[64,256]{1,0:T(8,128)S(1)} %get-tuple-element.85), channel_id=1, source_target_pairs={{0,16},{4,20},{8,24},{12,28},{16,0},{20,4},{24,8},{28,12},{1,17},{... | collective-permute-start | bytes 196616 | tf_op jit(solution)/shard_map/ppermute | solution.py:65
  52.5 4.3 %collective-permute-start.12 = (f32[64,256]{1,0:T(8,128)S(1)}, f32[64,256]{1,0:T(8,128)S(1)}, u32[]{:S(2)}, u32[]{:S(2)}) collective-permute-start(f32[64,256]{1,0:T(8,128)S(1)} %leave.1.refs_11_), channel_id=1, source_target_pairs={{0,2},{1,3},{2,0},{3,1},{4,6},{5,7},{6,4},{7,5},{8,10},{9,11},{10,... | collective-permute-start | bytes 196616 | tf_op jit(solution)/shard_map/ppermute | solution.py:65
  54.2 2.7 %collective-permute-start.11 = (f32[64,256]{1,0:T(8,128)S(1)}, f32[64,256]{1,0:T(8,128)S(1)}, u32[]{:S(2)}, u32[]{:S(2)}) collective-permute-start(f32[64,256]{1,0:T(8,128)S(1)} %leave.1.refs_11_), channel_id=1, source_target_pairs={{0,1},{1,0},{2,3},{3,2},{4,5},{5,4},{6,7},{7,6},{8,9},{9,8},{10,11... | collective-permute-start | bytes 196616 | tf_op jit(solution)/shard_map/ppermute | solution.py:65
  56.9 1.3 %collective-permute-start.13 = (f32[64,256]{1,0:T(8,128)S(1)}, f32[64,256]{1,0:T(8,128)S(1)}, u32[]{:S(2)}, u32[]{:S(2)}) collective-permute-start(f32[64,256]{1,0:T(8,128)S(1)} %collective-permute-done.12.refs_13_), channel_id=1, source_target_pairs={{0,1},{1,0},{2,3},{3,2},{4,5},{5,4},{6,7},{7,6},{8,9},{9,8},{10,11... | collective-permute-start | bytes 196616 | tf_op jit(solution)/shard_map/ppermute | solution.py:65

commit v5 on v4

--- a/solution.py
+++ b/solution.py
@@ -24,7 +24,10 @@
 
 
 def dot3(a, b, dims):
-    return dot1(a[0], b[0], dims) + (dot1(a[0], b[1], dims) + dot1(a[1], b[0], dims))
+    axis = 1 - dims[0][0][0]
+    rows = a[0].shape[axis]
+    both = dot1(jnp.concatenate(a, axis=axis), b[0], dims)
+    return both[:rows] + (both[rows:] + dot1(a[0], b[1], dims))
 
 
 def keep_split(ref, value):
@@ -166,70 +169,34 @@
     )
 
 
-def chain_up(begin, end, nodes, copy, parent, accs, halves, solved, offset):
-    inv_hi, inv_lo, upd_hi, upd_lo = halves
-    width = accs[0].shape[1]
-    for k in range(begin, end):
-        i = k - begin
-        inverse = (inv_hi[i], inv_lo[i])
-        update = (upd_hi[i], upd_lo[i])
-        for h in range(HALVES):
-            value = dot3(split(accs[h][k - offset]), inverse, NT)
-            solved[i, h * width : (h + 1) * width] = value
-            moved = dot3(split(value), update, NT)
-            if copy is not None:
-                copy.wait()
-                copy = None
-            above = (nodes if k == nodes - 1 else parent[k]) - offset
-            accs[h][above] = accs[h][above] - moved
-
-
-def chain_first_kernel(nodes, *refs):
-    parent_h, acc_a, acc_b, top = refs[:4]
-    halves, solved, rest, parent, sem = refs[4:8], refs[8], refs[9], refs[10], refs[11]
-    accs = refs[12:]
+def forward_kernel(nodes, fronts, *refs):
+    (parent_h, acc_a, acc_b, top), parts, refs = refs[:4], (refs[4:8], refs[8:12]), refs[13:]
+    solved, send, keep, square, parent, sem = refs[:6]
+    accs = refs[6:]
     copy = pltpu.make_async_copy(parent_h, parent, sem)
     copy.start()
-    first = acc_a.shape[1]
+    first, width = acc_a.shape[1:3]
     for h in range(HALVES):
         for k in range(nodes):
             accs[h][k] = acc_a[h, k] if k < first else acc_b[h, k - first]
         accs[h][nodes] = top[h]
-    chain_up(0, first, nodes, copy, parent, accs, halves, solved, 0)
-    for h in range(HALVES):
-        for k in range(first, nodes + 1):
-            rest[h, k - first] = accs[h][k]
-
-
-def chain_first(parent, acc_a, acc_b, top, halves):
-    first, (width, size) = acc_a.shape[1], acc_a.shape[2:]
-    nodes = first + acc_b.shape[1]
-    return call(
-        lambda *refs: chain_first_kernel(nodes, *refs),
-        "chain_first",
-        [(HBM, parent)] + [(V, a) for a in (acc_a, acc_b, top, *halves)],
-        [((first, width * HALVES, size), F32), ((HALVES, nodes - first + 1, width, size), F32)],
-        [pltpu.SMEM((nodes,), jnp.int32), pltpu.SemaphoreType.DMA]
-        + [pltpu.VMEM((nodes + 1, width, size), F32)] * HALVES,
-    )
-
-
-def chain_second_kernel(nodes, fronts, *refs):
-    parent_h, rest = refs[:2]
-    halves, solved, send, keep, square, parent, sem = refs[2:6], *refs[7:13]
-    accs = refs[13:]
-    copy = pltpu.make_async_copy(parent_h, parent, sem)
-    copy.start()
-    count = rest.shape[1]
-    width = rest.shape[2]
-    for h in range(HALVES):
-        accs[h][...] = rest[h]
-    first = nodes + 1 - count
-    chain_up(first, nodes, nodes, copy, parent, accs, halves, solved, first)
+    for k in range(nodes):
+        inv_hi, inv_lo, upd_hi, upd_lo = parts[k // first]
+        i = k % first
+        inverse = (inv_hi[i], inv_lo[i])
+        update = (upd_hi[i], upd_lo[i])
+        for h in range(HALVES):
+            value = dot3(split(accs[h][k]), inverse, NT)
+            solved[k, h * width : (h + 1) * width] = value
+            moved = dot3(split(value), update, NT)
+            if k + h == 0:
+                copy.wait()
+            above = nodes if k == nodes - 1 else parent[k]
+            accs[h][above] = accs[h][above] - moved
     front = lax.axis_index("front")
     chunk = width * HALVES // fronts
     for h in range(HALVES):
-        square[h * width : (h + 1) * width] = accs[h][nodes - first]
+        square[h * width : (h + 1) * width] = accs[h][nodes]
     low_bit = front % 2
     for i in range(fronts // 2):
         for ref, own in ((keep, low_bit), (send, 1 - low_bit)):
@@ -237,23 +204,25 @@
             ref[i * chunk : (i + 1) * chunk] = square[pl.ds(start, chunk), :]
 
 
-def chain_second(parent, rest, halves, after, fronts):
-    nodes = parent.shape[0]
-    count, width, size = rest.shape[1:]
+def local_forward(parent, acc_a, acc_b, top, first_halves, second_halves, after, fronts):
+    first, (width, size) = acc_a.shape[1], acc_a.shape[2:]
+    nodes = first + acc_b.shape[1]
     cols = width * HALVES
     part = ((cols // 2, size), F32)
     return call(
-        lambda *refs: chain_second_kernel(nodes, fronts, *refs),
-        "chain_second",
-        [(HBM, parent)] + [(V, a) for a in (rest, *halves)] + [(pl.ANY, after)],
-        [((count - 1, cols, size), F32), part, part],
+        lambda *refs: forward_kernel(nodes, fronts, *refs),
+        "local_forward",
+        [(HBM, parent)]
+        + [(V, a) for a in (acc_a, acc_b, top, *first_halves, *second_halves)]
+        + [(pl.ANY, after)],
+        [((nodes, cols, size), F32), part, part],
         [pltpu.VMEM((cols, size), F32), pltpu.SMEM((nodes,), jnp.int32), pltpu.SemaphoreType.DMA]
-        + [pltpu.VMEM((count, width, size), F32)] * HALVES,
+        + [pltpu.VMEM((nodes + 1, width, size), F32)] * HALVES,
     )
 
 
 def backward_kernel(nodes, fronts, *refs):
-    parent_h, parts, refs = refs[0], (refs[1:6], refs[6:11]), refs[11:]
+    (parent_h, solved), parts, refs = refs[:2], (refs[2:6], refs[6:10]), refs[10:]
     pieces = refs[:fronts]
     sol, sep_out = refs[fronts : 2 + fronts]
     square, parent, staged, sem, sems = refs[2 + fronts : 7 + fronts]
@@ -261,21 +230,19 @@
     first = parts[0][0].shape[0]
     copy = pltpu.make_async_copy(parent_h, parent, sem)
     copy.start()
-    front = lax.axis_index("front")
     chunk = pieces[0].shape[0]
     width = known[0].shape[1]
-    for i in range(fronts):
-        start = pl.multiple_of((front ^ i) * chunk, 8)
-        square[pl.ds(start, chunk), :] = pieces[i][...]
-    for h in range(HALVES):
-        known[h][nodes] = square[h * width : (h + 1) * width]
-    square[...] = square[...].T
-    share = sep_out.shape[0]
-    sep_out[...] = square[pl.ds(pl.multiple_of(front * share, 8), share), :]
+    order = [p[...] for p in pieces]
+    for bit in range(fronts.bit_length() - 1):
+        flip = bit_of("front", bit) == 1
+        order = [jnp.where(flip, order[i ^ (1 << bit)], order[i]) for i in range(fronts)]
+    for i, value in enumerate(order):
+        at = i * chunk
+        known[at // width][nodes, at % width : at % width + chunk] = value
     outs = []
     for k in reversed(range(nodes)):
         i = k % first
-        solved, inv_hi, inv_lo, upd_hi, upd_lo = parts[k // first]
+        inv_hi, inv_lo, upd_hi, upd_lo = parts[k // first]
         inverse = (inv_hi[i], inv_lo[i])
         update = (upd_hi[i], upd_lo[i])
         if k == nodes - 2:
@@ -283,27 +250,31 @@
         above = nodes if k == nodes - 1 else parent[k]
         for h in range(HALVES):
             rows = slice(h * width, (h + 1) * width)
-            part = solved[i, rows] - dot3(split(known[h][above]), update, NN)
+            part = solved[k, rows] - dot3(split(known[h][above]), update, NN)
             value = dot3(split(part), inverse, NN)
             known[h][k] = value
             staged[k, :, rows] = value.T
         out = pltpu.make_async_copy(staged.at[k], sol.at[k], sems.at[k])
         out.start()
         outs.append(out)
+    for h in range(HALVES):
+        square[:, h * width : (h + 1) * width] = known[h][nodes].T
+    share = sep_out.shape[0]
+    start = pl.multiple_of(lax.axis_index("front") * share, 8)
+    sep_out[...] = square[pl.ds(start, share), :]
     for out in outs:
         out.wait()
 
 
-def local_backward(parent, parts, pieces):
-    nodes = parent.shape[0]
-    cols, size = parts[0][0].shape[1:]
+def local_backward(parent, solved, first_halves, second_halves, pieces):
+    nodes, cols, size = solved.shape
     fronts = len(pieces)
     sol, sep = jax.ShapeDtypeStruct((nodes, size, cols), F32), ((size // fronts, cols), F32)
-    ins = [(HBM, parent)] + [(V, a) for a in (*parts[0], *parts[1], *pieces)]
+    ins = (solved, *first_halves, *second_halves, *pieces)
     return pl.pallas_call(
         lambda *refs: backward_kernel(nodes, fronts, *refs),
         name="local_backward",
-        in_specs=[pl.BlockSpec(memory_space=space) for space, _ in ins],
+        in_specs=[pl.BlockSpec(memory_space=HBM)] + [pl.BlockSpec(memory_space=V)] * len(ins),
         out_specs=(pl.BlockSpec(memory_space=HBM), pl.BlockSpec(memory_space=V)),
         out_shape=(sol, jax.ShapeDtypeStruct(*sep)),
         scratch_shapes=[pltpu.VMEM((size, cols), F32), pltpu.SMEM((nodes,), jnp.int32)]
@@ -311,7 +282,7 @@
         + [pltpu.SemaphoreType.DMA((nodes,))]
         + [pltpu.VMEM((nodes + 1, cols // HALVES, size), F32)] * HALVES,
         compiler_params=pltpu.CompilerParams(vmem_limit_bytes=VMEM_BYTES),
-    )(pltpu.with_memory_space_constraint(parent, HBM), *[a for _, a in ins[1:]])
+    )(pltpu.with_memory_space_constraint(parent, HBM), *ins)
 
 
 def stack_kernel(first, second, out, sems):
@@ -324,7 +295,7 @@
 
 def block_map_kernel(fronts, *refs):
     parts = refs[:fronts]
-    _, total, inverse_halves, square = refs[fronts:]
+    _, total, part, inverse_halves, square = refs[fronts:]
     front = lax.axis_index("front")
     share = parts[0].shape[1]
     for i in range(fronts):
@@ -332,7 +303,10 @@
         square[:, pl.ds(start, share), :] = parts[i][...]
     inverse = split(square[0])
     inverse_halves[0], inverse_halves[1] = inverse
-    total[...] = -dot3(inverse, split(square[1]), NN)
+    value = -dot3(inverse, split(square[1]), NN)
+    total[...] = value
+    half = part.shape[1]
+    send_blocks(part, [value[:half], value[half:]])
 
 
 def block_map(parts, after):
@@ -342,36 +316,58 @@
         lambda *refs: block_map_kernel(fronts, *refs),
         "block_map",
         [(V, a) for a in parts] + [(pl.ANY, after)],
-        [((size, size), F32), ((2, size, size), BF16)],
+        [((size, size), F32), ((1, size // 2, size), F32), ((2, size, size), BF16)],
         [pltpu.VMEM((2, size, size), F32)],
     )
 
 
-def pack_maps(pack, k, t):
-    half = k.shape[0] // 2
-    pack[0], pack[1], pack[2] = k[:half, :half], k[:half, half:], k[half:, half:]
-    if t is not None:
-        for i in range(4):
-            r, c = (i // 2) * half, (i % 2) * half
-            pack[3 + i] = t[r : r + half, c : c + half]
-
-
-def pack_k(pack):
-    first = jnp.concatenate([pack[0], pack[1]], axis=1)
-    second = jnp.concatenate([pack[1].T, pack[2]], axis=1)
+def quarters(x):
+    half = x.shape[0] // 2
+    return [x[i : i + half, j : j + half] for i in (0, half) for j in (0, half)]
+
+
+def joined(a, b, c, d):
+    first, second = jnp.concatenate([a, b], axis=1), jnp.concatenate([c, d], axis=1)
     return jnp.concatenate([first, second], axis=0)
 
 
-def pack_t(pack):
-    rows = [jnp.concatenate([pack[3 + i], pack[4 + i]], axis=1) for i in (0, 2)]
-    return jnp.concatenate(rows, axis=0)
+def low_core():
+    return bit_of("front", 0) == 0
+
+
+def send_blocks(part, blocks):
+    count = part.shape[0]
+    low = low_core()
+    for i in range(count):
+        part[i] = jnp.where(low, blocks[i], blocks[len(blocks) - count + i])
+
+
+def came_blocks(mine, pairs, total):
+    low = low_core()
+    count = mine.shape[0]
+    blocks = [jnp.where(low, mine[i], pairs[i]) for i in range(count)]
+    for i in range(count, total):
+        j = i - total + count
+        blocks.append(jnp.where(low, pairs[j], mine[j]))
+    return blocks
+
+
+def k_blocks(k):
+    a, b, _, d = quarters(k)
+    return [a, b, d]
+
+
+def k_of(blocks):
+    return joined(blocks[0], blocks[1], blocks[1].T, blocks[2])
 
 
 def first_merge_kernel(*refs):
-    own, other, _, pack, mixed, halves, curve_u, total_u, total_l = refs
+    own, mine, pairs, _, kept, part, mixed, halves, curve_u, total_u, total_l = refs
     upper = bit_of("leaf", 0) == 1
-    low = jnp.where(upper, other[...], own[...])
-    up = jnp.where(upper, own[...], other[...])
+    came = jnp.concatenate(came_blocks(mine, pairs, 2), axis=0)
+    mine = own[...]
+    low = jnp.where(upper, came, mine)
+    up = jnp.where(upper, mine, came)
     low_s, up_s = split(low), split(up)
     for ref, value in ((total_u, up_s), (total_l, low_s)):
         ref[0], ref[1] = value
@@ -380,7 +376,9 @@
     curve_u[0], curve_u[1] = k_up_s
     x = dot3(k_up_s, low_s, NN)
     t = dot3(up_s, low_s, NN)
-    pack_maps(pack, dot3(low_s, low_s, TN) + dot3(low_s, split(x), TN), t)
+    k = dot3(low_s, low_s, TN) + dot3(low_s, split(x), TN)
+    kept[0], kept[1] = k, t
+    send_blocks(part, k_blocks(k) + quarters(t))
     size = low.shape[0]
     row = lax.broadcasted_iota(jnp.int32, (size, size), 0)
     col = lax.broadcasted_iota(jnp.int32, (size, size), 1)
@@ -391,10 +389,12 @@
 
 
 def merge_kernel(bit, last, *refs):
-    own, other, mixed = refs[:3]
+    own, mine, pairs, mixed = refs[:4]
     upper = bit_of("leaf", bit) == 1
-    pack, mixed_n, halves, curve_u, total_u, total_l = refs[3:]
-    own_k, own_t, other_k, other_t = pack_k(own), pack_t(own), pack_k(other), pack_t(other)
+    kept, part, mixed_n, halves, curve_u, total_u, total_l = refs[4:]
+    own_k, own_t = own[0], own[1]
+    blocks = came_blocks(mine, pairs, 7)
+    other_k, other_t = k_of(blocks), joined(*blocks[3:])
     low_s = split(jnp.where(upper, other_t, own_t))
     up_s = split(jnp.where(upper, own_t, other_t))
     k_low = jnp.where(upper, other_k, own_k)
@@ -410,18 +410,21 @@
     a_n = jnp.where(upper, dot3(a_s, low_s, NN), a + dot3(e_s, x_s, TN))
     e_n = jnp.where(upper, e, dot3(up_s, e_s, NN))
     if last:
-        pack_maps(pack, k, None)
+        send_blocks(part, k_blocks(k))
         keep_split(mixed_n, jnp.where(bit_of("leaf", bit + 1) == 1, a_n.T, e_n))
     else:
-        pack_maps(pack, k, dot3(up_s, low_s, NN))
+        t = dot3(up_s, low_s, NN)
+        kept[0], kept[1] = k, t
+        send_blocks(part, k_blocks(k) + quarters(t))
         mixed_n[0], mixed_n[1] = a_n, e_n
 
 
 def maps(size, last):
-    both = ((2, size, size), BF16)
+    both, whole = ((2, size, size), BF16), ((2, size, size), F32)
     half = size // 2
-    pack = ((3 if last else 7, half, half), F32)
-    return [pack, both if last else ((2, size, size), F32), both, both, both, both]
+    part = ((2 if last else 4, half, half), F32)
+    kept = ((8, 128), F32) if last else whole
+    return [kept, part, both if last else whole, both, both, both, both]
 
 
 def fold_kernel(bit, own, other, send, keep):
@@ -467,10 +470,10 @@
         message[0][:rows], message[0][rows:] = z_new, p_new
 
 
-def leave_kernel(bit, sol, own_z, came, halves, pack, inverse, top):
+def leave_kernel(bit, sol, own_z, came, halves, mine, pairs, inverse, top):
     upper = bit_of("leaf", bit) == 1
     value = came[...]
-    middle = value + dot3(split(own_z[...]), split(pack_k(pack)), NN)
+    middle = value + dot3(split(own_z[...]), split(k_of(came_blocks(mine, pairs, 3))), NN)
     given = split(jnp.where(upper, value, middle))
     value = sol[...] + dot3(given, pair(halves), NN)
     top[...] = dot3(split(value), pair(inverse), NN)
@@ -498,23 +501,26 @@
         [((2, *sep_dinv.shape), F32)],
         [pltpu.SemaphoreType.DMA((2,))],
     )
-    came = [swap(stacked, "front", m) for m in range(1, fronts)]
+    came = {0: stacked}
+    for bit in reversed(range(1, front_bits)):
+        for i in list(came):
+            came[i | (1 << bit)] = exchange(came[i], "front", bit)
+    came[1] = exchange(stacked, "front", 0)
     acc_a, *first_halves = prepare_first(
         rhs_local, dinv_local, update_local, row_blocks, sep_rhs, stacked
     )
     first_halves, (top, row_columns, *raw) = first_halves[:4], first_halves[4:]
-    own_map, inverse = block_map([stacked, *came], acc_a)
-    other_map = exchange(own_map, "leaf", 0)
-    acc_b, *second_halves = prepare_second(row_columns, *raw, own_map)
-    first_solved, rest = chain_first(parent, acc_a, acc_b, top, first_halves)
-    pack, mixed, *tools = call(
-        first_merge_kernel,
-        "merge_0",
-        [(V, own_map), (V, other_map), (pl.ANY, rest)],
-        maps(size, False),
-    )
-    other_pack = exchange(pack, "leaf", 1)
-    second_solved, send, keep = chain_second(parent, rest, second_halves, mixed, fronts)
+    for i in range(2, fronts, 2):
+        held, _ = lax.optimization_barrier((came[i], acc_a))
+        came[i + 1] = exchange(held, "front", 0)
+    acc_b, *second_halves = prepare_second(row_columns, *raw, acc_a)
+    own_map, part, inverse = block_map([came[i] for i in range(fronts)], acc_b)
+    mine = exchange(part, "leaf", 0)
+    solved, send, keep = local_forward(
+        parent, acc_a, acc_b, top, first_halves, second_halves, own_map, fronts
+    )
+    mine, _ = lax.optimization_barrier((mine, send))
+    pairs = exchange(mine, "front", 0)
     for bit in range(front_bits):
         received = exchange(send, "front", bit)
         if bit + 1 < front_bits:
@@ -531,36 +537,47 @@
         [(V, keep), (V, received), (V, inverse), (V, own_map)],
         [((chunk, size), F32), ((2 * chunk, size), F32)],
     )
-    part = ((chunk, size), F32)
+    kept, part, mixed, *tools = call(
+        first_merge_kernel,
+        "merge_0",
+        [(V, own_map), (V, mine), (V, pairs), (pl.ANY, message)],
+        maps(size, False),
+    )
+    share = ((chunk, size), F32)
     for bit in range(rounds - 1):
         last = bit == rounds - 2
         received = exchange(message, "leaf", bit)
+        mine = exchange(part, "leaf", bit + 1)
         sol, *message = call(
             lambda *refs, bit=bit, last=last: step_kernel(bit, last, *refs),
             f"step_{bit}",
             [(V, a) for a in (sol, message, received, *tools)],
-            [part] + ([part, part] if last else [((2 * chunk, size), F32)]),
+            [share] + ([share, share] if last else [((2 * chunk, size), F32)]),
         )
-        if not last:
+        if last:
+            came = exchange(message[0], "leaf", bit + 1)
+            mine, _ = lax.optimization_barrier((mine, came))
+            pairs = exchange(mine, "front", 0)
+        else:
+            mine, _ = lax.optimization_barrier((mine, sol))
+            pairs = exchange(mine, "front", 0)
             (message,) = message
             last = bit == rounds - 3
-            pack, mixed, *tools = call(
+            kept, part, mixed, *tools = call(
                 lambda *refs, bit=bit, last=last: merge_kernel(bit + 1, last, *refs),
                 f"merge_{bit + 1}",
-                [(V, a) for a in (pack, other_pack, mixed)],
+                [(V, a) for a in (kept, mine, pairs, mixed)],
                 maps(size, last),
             )
-            other_pack = exchange(pack, "leaf", bit + 2)
-    came = exchange(message[0], "leaf", rounds - 1)
     (top,) = call(
         lambda *refs: leave_kernel(rounds - 1, *refs),
         "leave",
-        [(V, a) for a in (sol, message[1], came, mixed, other_pack, inverse)],
-        [part],
+        [(V, a) for a in (sol, message[1], came, mixed, mine, pairs, inverse)],
+        [share],
     )
     pieces = gather_front(top, front_bits)
     sol_local, sep_solution = local_backward(
-        parent, [(first_solved, *first_halves), (second_solved, *second_halves)], pieces
+        parent, solved, first_halves, second_halves, pieces
     )
     return (sol_local, sep_solution)
 

time: 63.9 us -> 59 us (0.923)
  Pallas kernels: 22 us -> 19.7 us
  starting transfers between devices: 18.8 us -> 16.6 us
    ppermute x14 -> x17, starting transfers between devices: 18.8 us -> 16.6 us  [swap(): return lax.ppermute(x, axis, [(i, i ^ mask) for i in range(n)])]
    pallas_call x13 -> x12, Pallas kernels: 16.4 us -> 14.5 us  [call(): pl.pallas_call(kernel, name=name, in_specs=specs, out_specs=tuple((pl.Blo...]
    ppermute x14 -> x17, waiting for transfers between devices: 22.2 us -> 21.7 us  [swap(): return lax.ppermute(x, axis, [(i, i ^ mask) for i in range(n)])]
  transfers between devices with their start and end apart: 14 -> 17, of which waited for: 9 -> 10; matrix products, arithmetic and copies ran while one was open for 0% -> 0% of each run, Pallas kernels for 21% -> 20%
where the time goes in v5:
time: 59 us; the launch traced here: 58.8 us
  waiting for transfers between devices  21.7 us (37%)
  Pallas kernels  19.7 us (33%)
  starting transfers between devices  16.6 us (28%)
  between operations  0.75 us (1%)
    ppermute x17, waiting for transfers between devices, swap(): return lax.ppermute(x, axis, [(i, i ^ mask) for i in range(n)])  21.7 us
    ppermute x17, starting transfers between devices, swap(): return lax.ppermute(x, axis, [(i, i ^ mask) for i in range(n)])  16.6 us
    pallas_call x12, Pallas kernels, call(): pl.pallas_call(kernel, name=name, in_specs=specs, out_specs=tuple((pl.Blo...  14.5 us
    pallas_call x1, Pallas kernels, local_backward(): pl.pallas_call(lambda *refs: backward_kernel(nodes, fronts, *refs), name=...  5.19 us
  transfers between devices with their start and end apart: 17, of which 10 were waited for; matrix products, arithmetic and copies ran while one was open for 0% of the time, Pallas kernels for 20%

profile of v5, /device:TPU:0, one launch (start us, length us, event | category | flops | bytes accessed | tf_op | source)
XLA Modules:
  0.0 58.8 jit_solution(17204617131479984721)
XLA Ops:
  0.6 0.9 %stack.1.refs_5_.refs_0_ = f32[2,64,256]{2,1,0:T(8,128)S(1)} custom-call(f32[64,256]{1,0:T(8,128)} %first.1, f32[64,256]{1,0:T(8,128)} %second.1), custom_call_target="tpu_custom_call" | custom-call | tf_op jit(solution)/shard_map/stack/pallas_call | solution.py:51
  1.5 3.0 %collective-permute-start.1 = (f32[2,64,256]{2,1,0:T(8,128)S(1)}, f32[2,64,256]{2,1,0:T(8,128)S(1)}, u32[]{:S(2)}, u32[]{:S(2)}) collective-permute-start(f32[2,64,256]{2,1,0:T(8,128)S(1)} %stack.1.refs_5_.refs_0_), channel_id=1, source_target_pairs={{0,2},{1,3},{2,0},{3,1},{4,6},{5,7},{6,4},{7,5},{8,10},{9,11},{10,... | collective-permute-start | bytes 393224 | tf_op jit(solution)/shard_map/ppermute | solution.py:68
  4.5 4.3 %prepare_first.1 = (f32[2,4,128,256]{3,2,1,0:T(8,128)S(1)}, bf16[4,256,256]{2,1,0:T(8,128)(2,1)S(1)}, bf16[4,256,256]{2,1,0:T(8,128)(2,1)S(1)}, bf16[4,256,256]{...) custom-call(s32[8,256]{1,0:T(8,128)} %refs_0_.3, ...), custom_call_target="tpu_custom_call" | custom-call | tf_op jit(solution)/shard_map/prepare_first/pallas_call | solution.py:51
  8.8 0.6 collective-permute-start.2
  9.4 0.7 %prepare_second.1 = (f32[2,4,128,256]{3,2,1,0:T(8,128)S(1)}, bf16[4,256,256]{2,1,0:T(8,128)(2,1)S(1)}, bf16[4,256,256]{2,1,0:T(8,128)(2,1)S(1)}, bf16[4,256,256]...) custom-call(f32[256,8]{1,0:T(8,128)S(1)} %get-tuple-element.50.refs_0_, f32[4,256,256]{2,1,0:T(8,128)S(1)} %get-tuple-element.51.refs_1_, ...), custom_call_target="tpu_custom_call" | custom-call | tf_op jit(solution)/shard_map/prepare_second/pallas_call | solution.py:51
  10.7 1.6 %collective-permute-start.6 = (f32[1,128,256]{2,1,0:T(8,128)S(1)}, f32[1,128,256]{2,1,0:T(8,128)S(1)}, u32[]{:S(2)}, u32[]{:S(2)}) collective-permute-start(f32[1,128,256]{2,1,0:T(8,128)S(1)} %get-tuple-element.74), channel_id=1, source_target_pairs={{0,4},{4,0},{8,12},{12,8},{16,20},{20,16},{24,28},{28,24},{1,5},{5... | collective-permute-start | bytes 393224 | tf_op jit(solution)/shard_map/ppermute | solution.py:68
  12.3 4.1 %local_forward.1 = (f32[8,256,256]{2,1,0:T(8,128)S(1)}, f32[128,256]{1,0:T(8,128)S(1)}, f32[128,256]{1,0:T(8,128)S(1)}) custom-call(s32[8]{0:T(128)} %refs_0_.5, f32[2,4,128,256]{3,2,1,0:T(8,128)S(1)} %get-tuple-element.49.refs_4_.refs_1_, f32[2,4,128,256]{3,2,1,0:T(8,128)S(1)} %get-tuple-element.54.refs_4_.refs_2_, ...), custom_call_target="tpu_custom_call" | custom-call | tf_op jit(solution)/shard_map/local_forward/pallas_call | solution.py:51
  17.0 0.8 %collective-permute-done.3.refs_1_ = f32[128,256]{1,0:T(8,128)S(1)} collective-permute-done((f32[128,256]{1,0:T(8,128)S(1)}, f32[128,256]{1,0:T(8,128)S(1)}, u32[]{:S(2)}, u32[]{:S(2)}) %collective-permute-start.3) | collective-permute-done | bytes 131104 | tf_op jit(solution)/shard_map/ppermute | solution.py:68
  17.8 0.8 %collective-permute-start.4 = (f32[64,256]{1,0:T(8,128)S(1)}, f32[64,256]{1,0:T(8,128)S(1)}, u32[]{:S(2)}, u32[]{:S(2)}) collective-permute-start(f32[64,256]{1,0:T(8,128)S(1)} %get-tuple-element.70), channel_id=1, source_target_pairs={{0,2},{1,3},{2,0},{3,1},{4,6},{5,7},{6,4},{7,5},{8,10},{9,11},{10,... | collective-permute-start | bytes 196616 | tf_op jit(solution)/shard_map/ppermute | solution.py:68
  18.6 3.5 %collective-permute-done.4.other = f32[64,256]{1,0:T(8,128)S(1)} collective-permute-done((f32[64,256]{1,0:T(8,128)S(1)}, f32[64,256]{1,0:T(8,128)S(1)}, u32[]{:S(2)}, u32[]{:S(2)}) %collective-permute-start.4) | collective-permute-done | bytes 65568 | tf_op jit(solution)/shard_map/ppermute | solution.py:68
  22.6 1.0 %merge_0.1 = (f32[2,256,256]{2,1,0:T(8,128)S(1)}, f32[4,128,128]{2,1,0:T(8,128)S(1)}, f32[2,256,256]{2,1,0:T(8,128)S(1)}, bf16[2,256,256]{2,1,0:T(8,128)(2,1)S(1...) custom-call(f32[256,256]{1,0:T(8,128)S(1)} %get-tuple-element.65.refs_12_.ow, ...), custom_call_target="tpu_custom_call" | custom-call | tf_op jit(solution)/shard_map/merge_0/pallas_call | solution.py:51
  23.6 1.6 %collective-permute-start.9 = (f32[4,128,128]{2,1,0:T(8,128)S(1)}, f32[4,128,128]{2,1,0:T(8,128)S(1)}, u32[]{:S(2)}, u32[]{:S(2)}) collective-permute-start(f32[4,128,128]{2,1,0:T(8,128)S(1)} %get-tuple-element.83), channel_id=1, source_target_pairs={{0,8},{4,12},{8,0},{12,4},{16,24},{20,28},{24,16},{28,20},{1,9},{5... | collective-permute-start | bytes 786440 | tf_op jit(solution)/shard_map/ppermute | solution.py:68
  25.8 4.5 %collective-permute-done.5.refs_2_ = f32[128,256]{1,0:T(8,128)S(1)} collective-permute-done((f32[128,256]{1,0:T(8,128)S(1)}, f32[128,256]{1,0:T(8,128)S(1)}, u32[]{:S(2)}, u32[]{:S(2)}) %collective-permute-start.5) | collective-permute-done | bytes 131104 | tf_op jit(solution)/shard_map/ppermute | solution.py:68
  30.9 1.6 %collective-permute-start.8 = (f32[128,256]{1,0:T(8,128)S(1)}, f32[128,256]{1,0:T(8,128)S(1)}, u32[]{:S(2)}, u32[]{:S(2)}) collective-permute-start(f32[128,256]{1,0:T(8,128)S(1)} %get-tuple-element.81.refs_1_), channel_id=1, source_target_pairs={{0,8},{4,12},{8,0},{12,4},{16,24},{20,28},{24,16},{28,20},{1,9},{5... | collective-permute-start | bytes 393224 | tf_op jit(solution)/shard_map/ppermute | solution.py:68
  32.5 1.4 %merge_1.1 = (f32[8,128]{1,0:T(8,128)}, f32[2,128,128]{2,1,0:T(8,128)S(1)}, bf16[2,256,256]{2,1,0:T(8,128)(2,1)S(1)}, bf16[2,256,256]{2,1,0:T(8,128)(2,1)S(1)}, ...) custom-call(f32[2,256,256]{2,1,0:T(8,128)S(1)} %get-tuple-element.82.refs_0_, ...), custom_call_target="tpu_custom_call" | custom-call | tf_op jit(solution)/shard_map/merge_1/pallas_call | solution.py:51
  33.9 2.6 %collective-permute-start.12 = (f32[2,128,128]{2,1,0:T(8,128)S(1)}, f32[2,128,128]{2,1,0:T(8,128)S(1)}, u32[]{:S(2)}, u32[]{:S(2)}) collective-permute-start(f32[2,128,128]{2,1,0:T(8,128)S(1)} %get-tuple-element.94), channel_id=1, source_target_pairs={{0,16},{4,20},{8,24},{12,28},{16,0},{20,4},{24,8},{28,12},{1,17},{... | collective-permute-start | bytes 393224 | tf_op jit(solution)/shard_map/ppermute | solution.py:68
  37.3 2.9 %collective-permute-start.11 = (f32[64,256]{1,0:T(8,128)S(1)}, f32[64,256]{1,0:T(8,128)S(1)}, u32[]{:S(2)}, u32[]{:S(2)}) collective-permute-start(f32[64,256]{1,0:T(8,128)S(1)} %get-tuple-element.92), channel_id=1, source_target_pairs={{0,16},{4,20},{8,24},{12,28},{16,0},{20,4},{24,8},{28,12},{1,17},{... | collective-permute-start | bytes 196616 | tf_op jit(solution)/shard_map/ppermute | solution.py:68
  40.2 5.9 %collective-permute-done.11.refs_2_ = f32[64,256]{1,0:T(8,128)S(1)} collective-permute-done((f32[64,256]{1,0:T(8,128)S(1)}, f32[64,256]{1,0:T(8,128)S(1)}, u32[]{:S(2)}, u32[]{:S(2)}) %collective-permute-start.11) | collective-permute-done | bytes 65568 | tf_op jit(solution)/shard_map/ppermute | solution.py:68
  46.1 1.3 %collective-permute-done.13.refs_5_ = f32[2,128,128]{2,1,0:T(8,128)S(1)} collective-permute-done((f32[2,128,128]{2,1,0:T(8,128)S(1)}, f32[2,128,128]{2,1,0:T(8,128)S(1)}, u32[]{:S(2)}, u32[]{:S(2)}) %collective-permute-start.13) | collective-permute-done | bytes 131104 | tf_op jit(solution)/shard_map/ppermute | solution.py:68
  47.4 0.6 leave.1.refs_10_
  48.0 0.8 %collective-permute-start.15 = (f32[64,256]{1,0:T(8,128)S(1)}, f32[64,256]{1,0:T(8,128)S(1)}, u32[]{:S(2)}, u32[]{:S(2)}) collective-permute-start(f32[64,256]{1,0:T(8,128)S(1)} %leave.1.refs_10_), channel_id=1, source_target_pairs={{0,2},{1,3},{2,0},{3,1},{4,6},{5,7},{6,4},{7,5},{8,10},{9,11},{10,... | collective-permute-start | bytes 196616 | tf_op jit(solution)/shard_map/ppermute | solution.py:68
  48.8 3.5 %collective-permute-done.15.refs_12_ = f32[64,256]{1,0:T(8,128)S(1)} collective-permute-done((f32[64,256]{1,0:T(8,128)S(1)}, f32[64,256]{1,0:T(8,128)S(1)}, u32[]{:S(2)}, u32[]{:S(2)}) %collective-permute-start.15) | collective-permute-done | bytes 65568 | tf_op jit(solution)/shard_map/ppermute | solution.py:68
  52.3 1.2 %collective-permute-done.16.refs_13_ = f32[64,256]{1,0:T(8,128)S(1)} collective-permute-done((f32[64,256]{1,0:T(8,128)S(1)}, f32[64,256]{1,0:T(8,128)S(1)}, u32[]{:S(2)}, u32[]{:S(2)}) %collective-permute-start.16) | collective-permute-done | bytes 65568 | tf_op jit(solution)/shard_map/ppermute | solution.py:68
  53.6 5.2 %local_backward.1 = (f32[8,256,256]{2,1,0:T(8,128)}, f32[64,256]{1,0:T(8,128)}) custom-call(s32[8]{0:T(128)} %refs_0_.5, f32[8,256,256]{2,1,0:T(8,128)S(1)} %get-tuple-element.66.refs_1_, bf16[4,256,256]{2,1,0:T(8,128)(2,1)S(1)} %get-tuple-element.56.refs_4_.refs_2_, bf16[4,256,256]{2,1,0:T(8,128)(2,1)S(1)} %get-tuple-element.57.refs_5_.refs_3_, ...), custom_call_target="tpu_custom_call" | custom-call | tf_op jit(solution)/shard_map/local_backward/pallas_call | solution.py:274
  (23 shorter events, 3.6 us)
Async XLA Ops:
  1.5 7.3 %collective-permute-start.1 = (f32[2,64,256]{2,1,0:T(8,128)S(1)}, f32[2,64,256]{2,1,0:T(8,128)S(1)}, u32[]{:S(2)}, u32[]{:S(2)}) collective-permute-start(f32[2,64,256]{2,1,0:T(8,128)S(1)} %stack.1.refs_5_.refs_0_), channel_id=1, source_target_pairs={{0,2},{1,3},{2,0},{3,1},{4,6},{5,7},{6,4},{7,5},{8,10},{9,11},{10,... | collective-permute-start | bytes 393224 | tf_op jit(solution)/shard_map/ppermute | solution.py:68
  4.5 5.5 %collective-permute-start = (f32[2,64,256]{2,1,0:T(8,128)S(1)}, f32[2,64,256]{2,1,0:T(8,128)S(1)}, u32[]{:S(2)}, u32[]{:S(2)}) collective-permute-start(f32[2,64,256]{2,1,0:T(8,128)S(1)} %stack.1.refs_5_.refs_0_), channel_id=1, source_target_pairs={{0,1},{1,0},{2,3},{3,2},{4,5},{5,4},{6,7},{7,6},{8,9},{9,8},{10,11... | collective-permute-start | bytes 393224 | tf_op jit(solution)/shard_map/ppermute | solution.py:68
  8.8 1.6 %collective-permute-start.2 = (f32[2,64,256]{2,1,0:T(8,128)S(1)}, f32[2,64,256]{2,1,0:T(8,128)S(1)}, u32[]{:S(2)}, u32[]{:S(2)}) collective-permute-start(f32[2,64,256]{2,1,0:T(8,128)S(1)} %collective-permute-done.1.refs_2_), channel_id=1, source_target_pairs={{0,1},{1,0},{2,3},{3,2},{4,5},{5,4},{6,7},{7,6},{8,9},{9,8},{10,11... | collective-permute-start | bytes 393224 | tf_op jit(solution)/shard_map/ppermute | solution.py:68
  10.7 5.8 %collective-permute-start.6 = (f32[1,128,256]{2,1,0:T(8,128)S(1)}, f32[1,128,256]{2,1,0:T(8,128)S(1)}, u32[]{:S(2)}, u32[]{:S(2)}) collective-permute-start(f32[1,128,256]{2,1,0:T(8,128)S(1)} %get-tuple-element.74), channel_id=1, source_target_pairs={{0,4},{4,0},{8,12},{12,8},{16,20},{20,16},{24,28},{28,24},{1,5},{5... | collective-permute-start | bytes 393224 | tf_op jit(solution)/shard_map/ppermute | solution.py:68
  16.4 1.4 %collective-permute-start.3 = (f32[128,256]{1,0:T(8,128)S(1)}, f32[128,256]{1,0:T(8,128)S(1)}, u32[]{:S(2)}, u32[]{:S(2)}) collective-permute-start(f32[128,256]{1,0:T(8,128)S(1)} %get-tuple-element.68), channel_id=1, source_target_pairs={{0,1},{1,0},{2,3},{3,2},{4,5},{5,4},{6,7},{7,6},{8,9},{9,8},{10,11... | collective-permute-start | bytes 393224 | tf_op jit(solution)/shard_map/ppermute | solution.py:68
  16.5 6.1 %collective-permute-start.7 = (f32[1,128,256]{2,1,0:T(8,128)S(1)}, f32[1,128,256]{2,1,0:T(8,128)S(1)}, u32[]{:S(2)}, u32[]{:S(2)}) collective-permute-start(f32[1,128,256]{2,1,0:T(8,128)S(1)} %collective-permute-done.6.refs_1_), channel_id=1, source_target_pairs={{0,1},{1,0},{2,3},{3,2},{4,5},{5,4},{6,7},{7,6},{8,9},{9,8},{10,11... | collective-permute-start | bytes 393224 | tf_op jit(solution)/shard_map/ppermute | solution.py:68
  17.8 4.3 %collective-permute-start.4 = (f32[64,256]{1,0:T(8,128)S(1)}, f32[64,256]{1,0:T(8,128)S(1)}, u32[]{:S(2)}, u32[]{:S(2)}) collective-permute-start(f32[64,256]{1,0:T(8,128)S(1)} %get-tuple-element.70), channel_id=1, source_target_pairs={{0,2},{1,3},{2,0},{3,1},{4,6},{5,7},{6,4},{7,5},{8,10},{9,11},{10,... | collective-permute-start | bytes 196616 | tf_op jit(solution)/shard_map/ppermute | solution.py:68
  23.6 7.3 %collective-permute-start.9 = (f32[4,128,128]{2,1,0:T(8,128)S(1)}, f32[4,128,128]{2,1,0:T(8,128)S(1)}, u32[]{:S(2)}, u32[]{:S(2)}) collective-permute-start(f32[4,128,128]{2,1,0:T(8,128)S(1)} %get-tuple-element.83), channel_id=1, source_target_pairs={{0,8},{4,12},{8,0},{12,4},{16,24},{20,28},{24,16},{28,20},{1,9},{5... | collective-permute-start | bytes 786440 | tf_op jit(solution)/shard_map/ppermute | solution.py:68
  25.3 5.0 %collective-permute-start.5 = (f32[128,256]{1,0:T(8,128)S(1)}, f32[128,256]{1,0:T(8,128)S(1)}, u32[]{:S(2)}, u32[]{:S(2)}) collective-permute-start(f32[128,256]{1,0:T(8,128)S(1)} %get-tuple-element.73.refs_3_.refs_1_), channel_id=1, source_target_pairs={{0,4},{4,0},{8,12},{12,8},{16,20},{20,16},{24,28},{28,24},{1,5},{5... | collective-permute-start | bytes 393224 | tf_op jit(solution)/shard_map/ppermute | solution.py:68
  30.9 1.6 %collective-permute-start.10 = (f32[4,128,128]{2,1,0:T(8,128)S(1)}, f32[4,128,128]{2,1,0:T(8,128)S(1)}, u32[]{:S(2)}, u32[]{:S(2)}) collective-permute-start(f32[4,128,128]{2,1,0:T(8,128)S(1)} %collective-permute-done.9.refs_1_), channel_id=1, source_target_pairs={{0,1},{1,0},{2,3},{3,2},{4,5},{5,4},{6,7},{7,6},{8,9},{9,8},{10,11... | collective-permute-start | bytes 786440 | tf_op jit(solution)/shard_map/ppermute | solution.py:68
  30.9 5.9 %collective-permute-start.8 = (f32[128,256]{1,0:T(8,128)S(1)}, f32[128,256]{1,0:T(8,128)S(1)}, u32[]{:S(2)}, u32[]{:S(2)}) collective-permute-start(f32[128,256]{1,0:T(8,128)S(1)} %get-tuple-element.81.refs_1_), channel_id=1, source_target_pairs={{0,8},{4,12},{8,0},{12,4},{16,24},{20,28},{24,16},{28,20},{1,9},{5... | collective-permute-start | bytes 393224 | tf_op jit(solution)/shard_map/ppermute | solution.py:68
  33.9 12.1 %collective-permute-start.12 = (f32[2,128,128]{2,1,0:T(8,128)S(1)}, f32[2,128,128]{2,1,0:T(8,128)S(1)}, u32[]{:S(2)}, u32[]{:S(2)}) collective-permute-start(f32[2,128,128]{2,1,0:T(8,128)S(1)} %get-tuple-element.94), channel_id=1, source_target_pairs={{0,16},{4,20},{8,24},{12,28},{16,0},{20,4},{24,8},{28,12},{1,17},{... | collective-permute-start | bytes 393224 | tf_op jit(solution)/shard_map/ppermute | solution.py:68
  37.3 8.8 %collective-permute-start.11 = (f32[64,256]{1,0:T(8,128)S(1)}, f32[64,256]{1,0:T(8,128)S(1)}, u32[]{:S(2)}, u32[]{:S(2)}) collective-permute-start(f32[64,256]{1,0:T(8,128)S(1)} %get-tuple-element.92), channel_id=1, source_target_pairs={{0,16},{4,20},{8,24},{12,28},{16,0},{20,4},{24,8},{28,12},{1,17},{... | collective-permute-start | bytes 196616 | tf_op jit(solution)/shard_map/ppermute | solution.py:68
  46.1 1.3 %collective-permute-start.13 = (f32[2,128,128]{2,1,0:T(8,128)S(1)}, f32[2,128,128]{2,1,0:T(8,128)S(1)}, u32[]{:S(2)}, u32[]{:S(2)}) collective-permute-start(f32[2,128,128]{2,1,0:T(8,128)S(1)} %collective-permute-done.12.refs_4_), channel_id=1, source_target_pairs={{0,1},{1,0},{2,3},{3,2},{4,5},{5,4},{6,7},{7,6},{8,9},{9,8},{10,11... | collective-permute-start | bytes 393224 | tf_op jit(solution)/shard_map/ppermute | solution.py:68
  48.0 4.3 %collective-permute-start.15 = (f32[64,256]{1,0:T(8,128)S(1)}, f32[64,256]{1,0:T(8,128)S(1)}, u32[]{:S(2)}, u32[]{:S(2)}) collective-permute-start(f32[64,256]{1,0:T(8,128)S(1)} %leave.1.refs_10_), channel_id=1, source_target_pairs={{0,2},{1,3},{2,0},{3,1},{4,6},{5,7},{6,4},{7,5},{8,10},{9,11},{10,... | collective-permute-start | bytes 196616 | tf_op jit(solution)/shard_map/ppermute | solution.py:68
  48.8 3.5 %collective-permute-start.14 = (f32[64,256]{1,0:T(8,128)S(1)}, f32[64,256]{1,0:T(8,128)S(1)}, u32[]{:S(2)}, u32[]{:S(2)}) collective-permute-start(f32[64,256]{1,0:T(8,128)S(1)} %leave.1.refs_10_), channel_id=1, source_target_pairs={{0,1},{1,0},{2,3},{3,2},{4,5},{5,4},{6,7},{7,6},{8,9},{9,8},{10,11... | collective-permute-start | bytes 196616 | tf_op jit(solution)/shard_map/ppermute | solution.py:68
  52.3 1.3 %collective-permute-start.16 = (f32[64,256]{1,0:T(8,128)S(1)}, f32[64,256]{1,0:T(8,128)S(1)}, u32[]{:S(2)}, u32[]{:S(2)}) collective-permute-start(f32[64,256]{1,0:T(8,128)S(1)} %collective-permute-done.15.refs_12_), channel_id=1, source_target_pairs={{0,1},{1,0},{2,3},{3,2},{4,5},{5,4},{6,7},{7,6},{8,9},{9,8},{10,11... | collective-permute-start | bytes 196616 | tf_op jit(solution)/shard_map/ppermute | solution.py:68

commit v6 on v5

--- a/solution.py
+++ b/solution.py
@@ -305,8 +305,8 @@
     inverse_halves[0], inverse_halves[1] = inverse
     value = -dot3(inverse, split(square[1]), NN)
     total[...] = value
-    half = part.shape[1]
-    send_blocks(part, [value[:half], value[half:]])
+    half = part.shape[0]
+    send_blocks([part], [value[:half], value[half:]])
 
 
 def block_map(parts, after):
@@ -316,7 +316,7 @@
         lambda *refs: block_map_kernel(fronts, *refs),
         "block_map",
         [(V, a) for a in parts] + [(pl.ANY, after)],
-        [((size, size), F32), ((1, size // 2, size), F32), ((2, size, size), BF16)],
+        [((size, size), F32), ((size // 2, size), F32), ((2, size, size), BF16)],
         [pltpu.VMEM((2, size, size), F32)],
     )
 
@@ -335,16 +335,17 @@
     return bit_of("front", 0) == 0
 
 
-def send_blocks(part, blocks):
-    count = part.shape[0]
+def send_blocks(parts, blocks):
+    count = len(parts)
     low = low_core()
-    for i in range(count):
-        part[i] = jnp.where(low, blocks[i], blocks[len(blocks) - count + i])
+    for i, part in enumerate(parts):
+        part[...] = jnp.where(low, blocks[i], blocks[len(blocks) - count + i])
 
 
 def came_blocks(mine, pairs, total):
     low = low_core()
-    count = mine.shape[0]
+    count = len(mine)
+    mine, pairs = [m[...] for m in mine], [p[...] for p in pairs]
     blocks = [jnp.where(low, mine[i], pairs[i]) for i in range(count)]
     for i in range(count, total):
         j = i - total + count
@@ -362,9 +363,9 @@
 
 
 def first_merge_kernel(*refs):
-    own, mine, pairs, _, kept, part, mixed, halves, curve_u, total_u, total_l = refs
+    own, mine, pairs, _, kept, mixed, halves, curve_u, total_u, total_l, *parts = refs
     upper = bit_of("leaf", 0) == 1
-    came = jnp.concatenate(came_blocks(mine, pairs, 2), axis=0)
+    came = jnp.concatenate(came_blocks([mine], [pairs], 2), axis=0)
     mine = own[...]
     low = jnp.where(upper, came, mine)
     up = jnp.where(upper, mine, came)
@@ -378,7 +379,7 @@
     t = dot3(up_s, low_s, NN)
     k = dot3(low_s, low_s, TN) + dot3(low_s, split(x), TN)
     kept[0], kept[1] = k, t
-    send_blocks(part, k_blocks(k) + quarters(t))
+    send_blocks(parts, k_blocks(k) + quarters(t))
     size = low.shape[0]
     row = lax.broadcasted_iota(jnp.int32, (size, size), 0)
     col = lax.broadcasted_iota(jnp.int32, (size, size), 1)
@@ -389,9 +390,9 @@
 
 
 def merge_kernel(bit, last, *refs):
-    own, mine, pairs, mixed = refs[:4]
+    own, mine, pairs, mixed = refs[0], refs[1:5], refs[5:9], refs[9]
     upper = bit_of("leaf", bit) == 1
-    kept, part, mixed_n, halves, curve_u, total_u, total_l = refs[4:]
+    kept, mixed_n, halves, curve_u, total_u, total_l, *parts = refs[10:]
     own_k, own_t = own[0], own[1]
     blocks = came_blocks(mine, pairs, 7)
     other_k, other_t = k_of(blocks), joined(*blocks[3:])
@@ -410,21 +411,20 @@
     a_n = jnp.where(upper, dot3(a_s, low_s, NN), a + dot3(e_s, x_s, TN))
     e_n = jnp.where(upper, e, dot3(up_s, e_s, NN))
     if last:
-        send_blocks(part, k_blocks(k))
+        keep_split(kept, k)
         keep_split(mixed_n, jnp.where(bit_of("leaf", bit + 1) == 1, a_n.T, e_n))
     else:
         t = dot3(up_s, low_s, NN)
         kept[0], kept[1] = k, t
-        send_blocks(part, k_blocks(k) + quarters(t))
+        send_blocks(parts, k_blocks(k) + quarters(t))
         mixed_n[0], mixed_n[1] = a_n, e_n
 
 
 def maps(size, last):
     both, whole = ((2, size, size), BF16), ((2, size, size), F32)
-    half = size // 2
-    part = ((2 if last else 4, half, half), F32)
-    kept = ((8, 128), F32) if last else whole
-    return [kept, part, both if last else whole, both, both, both, both]
+    if last:
+        return [both] * 6
+    return [whole, whole, both, both, both, both] + [((size // 2, size // 2), F32)] * 4
 
 
 def fold_kernel(bit, own, other, send, keep):
@@ -464,17 +464,18 @@
     given = split(jnp.where(upper, z_low, middle))
     sol_n[...] = sol[...] + dot3(given, pair(halves), NN)
     if last:
-        message[0][...] = jnp.where(bit_of("leaf", bit + 1) == 1, p_new, z_new)
-        message[1][...] = z_new
+        message[0][...], message[1][...] = z_new, p_new
     else:
         message[0][:rows], message[0][rows:] = z_new, p_new
 
 
-def leave_kernel(bit, sol, own_z, came, halves, mine, pairs, inverse, top):
+def turn_kernel(message, came, curve, back):
+    back[...] = message[...] + dot3(split(came[...]), pair(curve), NN)
+
+
+def leave_kernel(bit, sol, came, back, halves, inverse, top):
     upper = bit_of("leaf", bit) == 1
-    value = came[...]
-    middle = value + dot3(split(own_z[...]), split(k_of(came_blocks(mine, pairs, 3))), NN)
-    given = split(jnp.where(upper, value, middle))
+    given = split(jnp.where(upper, came[...], back[...]))
     value = sol[...] + dot3(given, pair(halves), NN)
     top[...] = dot3(split(value), pair(inverse), NN)
 
@@ -519,7 +520,7 @@
     solved, send, keep = local_forward(
         parent, acc_a, acc_b, top, first_halves, second_halves, own_map, fronts
     )
-    mine, _ = lax.optimization_barrier((mine, send))
+    mine, send = lax.optimization_barrier((mine, send))
     pairs = exchange(mine, "front", 0)
     for bit in range(front_bits):
         received = exchange(send, "front", bit)
@@ -531,48 +532,50 @@
                 [(V, keep), (V, received)],
                 [half, half],
             )
+    kept, mixed, *tools = call(
+        first_merge_kernel,
+        "merge_0",
+        [(V, own_map), (V, mine), (V, pairs), (pl.ANY, send)],
+        maps(size, False),
+    )
+    tools, parts = tools[:4], tools[4:]
     sol, message = call(
         enter_kernel,
         "enter",
         [(V, keep), (V, received), (V, inverse), (V, own_map)],
         [((chunk, size), F32), ((2 * chunk, size), F32)],
     )
-    kept, part, mixed, *tools = call(
-        first_merge_kernel,
-        "merge_0",
-        [(V, own_map), (V, mine), (V, pairs), (pl.ANY, message)],
-        maps(size, False),
-    )
     share = ((chunk, size), F32)
     for bit in range(rounds - 1):
         last = bit == rounds - 2
         received = exchange(message, "leaf", bit)
-        mine = exchange(part, "leaf", bit + 1)
+        if not last:
+            mine = [exchange(part, "leaf", bit + 1) for part in parts]
         sol, *message = call(
             lambda *refs, bit=bit, last=last: step_kernel(bit, last, *refs),
             f"step_{bit}",
             [(V, a) for a in (sol, message, received, *tools)],
             [share] + ([share, share] if last else [((2 * chunk, size), F32)]),
         )
-        if last:
-            came = exchange(message[0], "leaf", bit + 1)
-            mine, _ = lax.optimization_barrier((mine, came))
-            pairs = exchange(mine, "front", 0)
-        else:
+        if not last:
+            (message,) = message
             mine, _ = lax.optimization_barrier((mine, sol))
-            pairs = exchange(mine, "front", 0)
-            (message,) = message
+            pairs = [exchange(m, "front", 0) for m in mine]
             last = bit == rounds - 3
-            kept, part, mixed, *tools = call(
+            kept, mixed, *tools = call(
                 lambda *refs, bit=bit, last=last: merge_kernel(bit + 1, last, *refs),
                 f"merge_{bit + 1}",
-                [(V, a) for a in (kept, mine, pairs, mixed)],
+                [(V, a) for a in (kept, *mine, *pairs, mixed)],
                 maps(size, last),
             )
+            tools, parts = tools[:4], tools[4:]
+    came = exchange(message[0], "leaf", rounds - 1)
+    (back,) = call(turn_kernel, "turn", [(V, a) for a in (message[1], came, kept)], [share])
+    back = exchange(back, "leaf", rounds - 1)
     (top,) = call(
         lambda *refs: leave_kernel(rounds - 1, *refs),
         "leave",
-        [(V, a) for a in (sol, message[1], came, mixed, mine, pairs, inverse)],
+        [(V, a) for a in (sol, came, back, mixed, inverse)],
         [share],
     )
     pieces = gather_front(top, front_bits)

time: 59 us -> 61.8 us (1.047)
  starting transfers between devices: 16.6 us -> 18.9 us
  waiting for transfers between devices: 21.7 us -> 22.7 us
    ppermute x17 -> x22, starting transfers between devices: 16.6 us -> 18.9 us  [swap(): return lax.ppermute(x, axis, [(i, i ^ mask) for i in range(n)])]
    ppermute x17 -> x22, waiting for transfers between devices: 21.7 us -> 22.7 us  [swap(): return lax.ppermute(x, axis, [(i, i ^ mask) for i in range(n)])]
    pallas_call x12 -> x13, Pallas kernels: 14.5 us -> 14 us  [call(): pl.pallas_call(kernel, name=name, in_specs=specs, out_specs=tuple((pl.Blo...]
  transfers between devices with their start and end apart: 17 -> 22, of which waited for: 10 -> 15; matrix products, arithmetic and copies ran while one was open for 0% -> 0% of each run, Pallas kernels for 20% -> 19%
where the time goes in v6:
time: 61.8 us; the launch traced here: 61.6 us
  waiting for transfers between devices  22.7 us (37%)
  Pallas kernels  19.2 us (31%)
  starting transfers between devices  18.9 us (31%)
  between operations  0.77 us (1%)
    ppermute x22, waiting for transfers between devices, swap(): return lax.ppermute(x, axis, [(i, i ^ mask) for i in range(n)])  22.7 us
    ppermute x22, starting transfers between devices, swap(): return lax.ppermute(x, axis, [(i, i ^ mask) for i in range(n)])  18.9 us
    pallas_call x13, Pallas kernels, call(): pl.pallas_call(kernel, name=name, in_specs=specs, out_specs=tuple((pl.Blo...  14 us
    pallas_call x1, Pallas kernels, local_backward(): pl.pallas_call(lambda *refs: backward_kernel(nodes, fronts, *refs), name=...  5.19 us
  transfers between devices with their start and end apart: 22, of which 15 were waited for; matrix products, arithmetic and copies ran while one was open for 0% of the time, Pallas kernels for 19%

profile of v6, /device:TPU:0, one launch (start us, length us, event | category | flops | bytes accessed | tf_op | source)
XLA Modules:
  0.0 61.6 jit_solution(5534206438898884735)
XLA Ops:
  0.6 0.9 %stack.1.refs_5_.refs_0_ = f32[2,64,256]{2,1,0:T(8,128)S(1)} custom-call(f32[64,256]{1,0:T(8,128)} %first.1, f32[64,256]{1,0:T(8,128)} %second.1), custom_call_target="tpu_custom_call" | custom-call | tf_op jit(solution)/shard_map/stack/pallas_call | solution.py:51
  1.5 3.0 %collective-permute-start.1 = (f32[2,64,256]{2,1,0:T(8,128)S(1)}, f32[2,64,256]{2,1,0:T(8,128)S(1)}, u32[]{:S(2)}, u32[]{:S(2)}) collective-permute-start(f32[2,64,256]{2,1,0:T(8,128)S(1)} %stack.1.refs_5_.refs_0_), channel_id=1, source_target_pairs={{0,2},{1,3},{2,0},{3,1},{4,6},{5,7},{6,4},{7,5},{8,10},{9,11},{10,... | collective-permute-start | bytes 393224 | tf_op jit(solution)/shard_map/ppermute | solution.py:68
  4.5 4.3 %prepare_first.1 = (f32[2,4,128,256]{3,2,1,0:T(8,128)S(1)}, bf16[4,256,256]{2,1,0:T(8,128)(2,1)S(1)}, bf16[4,256,256]{2,1,0:T(8,128)(2,1)S(1)}, bf16[4,256,256]{...) custom-call(s32[8,256]{1,0:T(8,128)} %refs_0_.3, ...), custom_call_target="tpu_custom_call" | custom-call | tf_op jit(solution)/shard_map/prepare_first/pallas_call | solution.py:51
  9.4 0.7 %prepare_second.1 = (f32[2,4,128,256]{3,2,1,0:T(8,128)S(1)}, bf16[4,256,256]{2,1,0:T(8,128)(2,1)S(1)}, bf16[4,256,256]{2,1,0:T(8,128)(2,1)S(1)}, bf16[4,256,256]...) custom-call(f32[256,8]{1,0:T(8,128)S(1)} %get-tuple-element.56.refs_0_, f32[4,256,256]{2,1,0:T(8,128)S(1)} %get-tuple-element.57.refs_1_, ...), custom_call_target="tpu_custom_call" | custom-call | tf_op jit(solution)/shard_map/prepare_second/pallas_call | solution.py:51
  10.7 1.6 %collective-permute-start.3 = (f32[128,256]{1,0:T(8,128)S(1)}, f32[128,256]{1,0:T(8,128)S(1)}, u32[]{:S(2)}, u32[]{:S(2)}) collective-permute-start(f32[128,256]{1,0:T(8,128)S(1)} %get-tuple-element.74), channel_id=1, source_target_pairs={{0,4},{4,0},{8,12},{12,8},{16,20},{20,16},{24,28},{28,24},{1,5},{5... | collective-permute-start | bytes 393224 | tf_op jit(solution)/shard_map/ppermute | solution.py:68
  12.3 4.1 %local_forward.1 = (f32[8,256,256]{2,1,0:T(8,128)S(1)}, f32[128,256]{1,0:T(8,128)S(1)}, f32[128,256]{1,0:T(8,128)S(1)}) custom-call(s32[8]{0:T(128)} %refs_0_.5, f32[2,4,128,256]{3,2,1,0:T(8,128)S(1)} %get-tuple-element.55.refs_4_.refs_1_, f32[2,4,128,256]{3,2,1,0:T(8,128)S(1)} %get-tuple-element.60.refs_4_.refs_2_, ...), custom_call_target="tpu_custom_call" | custom-call | tf_op jit(solution)/shard_map/local_forward/pallas_call | solution.py:51
  16.5 1.3 %collective-permute-done.4.refs_1_ = f32[128,256]{1,0:T(8,128)S(1)} collective-permute-done((f32[128,256]{1,0:T(8,128)S(1)}, f32[128,256]{1,0:T(8,128)S(1)}, u32[]{:S(2)}, u32[]{:S(2)}) %collective-permute-start.4) | collective-permute-done | bytes 131104 | tf_op jit(solution)/shard_map/ppermute | solution.py:68
  17.9 0.7 %collective-permute-start.5 = (f32[64,256]{1,0:T(8,128)S(1)}, f32[64,256]{1,0:T(8,128)S(1)}, u32[]{:S(2)}, u32[]{:S(2)}) collective-permute-start(f32[64,256]{1,0:T(8,128)S(1)} %get-tuple-element.78.refs_3_), channel_id=1, source_target_pairs={{0,2},{1,3},{2,0},{3,1},{4,6},{5,7},{6,4},{7,5},{8,10},{9,11},{10,... | collective-permute-start | bytes 196616 | tf_op jit(solution)/shard_map/ppermute | solution.py:68
  18.7 3.6 %collective-permute-done.5.other = f32[64,256]{1,0:T(8,128)S(1)} collective-permute-done((f32[64,256]{1,0:T(8,128)S(1)}, f32[64,256]{1,0:T(8,128)S(1)}, u32[]{:S(2)}, u32[]{:S(2)}) %collective-permute-start.5) | collective-permute-done | bytes 65568 | tf_op jit(solution)/shard_map/ppermute | solution.py:68
  22.7 1.6 %collective-permute-start.6 = (f32[128,256]{1,0:T(8,128)S(1)}, f32[128,256]{1,0:T(8,128)S(1)}, u32[]{:S(2)}, u32[]{:S(2)}) collective-permute-start(f32[128,256]{1,0:T(8,128)S(1)} %get-tuple-element.81.refs_1_), channel_id=1, source_target_pairs={{0,4},{4,0},{8,12},{12,8},{16,20},{20,16},{24,28},{28,24},{1,5},{5... | collective-permute-start | bytes 393224 | tf_op jit(solution)/shard_map/ppermute | solution.py:68
  24.2 1.0 %merge_0.1 = (f32[2,256,256]{2,1,0:T(8,128)S(1)}, f32[2,256,256]{2,1,0:T(8,128)S(1)}, bf16[2,256,256]{2,1,0:T(8,128)(2,1)S(1)}, bf16[2,256,256]{2,1,0:T(8,128)(2...) custom-call(f32[256,256]{1,0:T(8,128)S(1)} %get-tuple-element.71.ref, ...), custom_call_target="tpu_custom_call" | custom-call | tf_op jit(solution)/shard_map/merge_0/pallas_call | solution.py:51
  25.3 1.6 %collective-permute-start.10 = (f32[128,128]{1,0:T(8,128)S(1)}, f32[128,128]{1,0:T(8,128)S(1)}, u32[]{:S(2)}, u32[]{:S(2)}) collective-permute-start(f32[128,128]{1,0:T(8,128)S(1)} %get-tuple-element.91), channel_id=1, source_target_pairs={{0,8},{4,12},{8,0},{12,4},{16,24},{20,28},{24,16},{28,20},{1,9},{5... | collective-permute-start | bytes 196616 | tf_op jit(solution)/shard_map/ppermute | solution.py:68
  27.4 1.6 %collective-permute-start.12 = (f32[128,128]{1,0:T(8,128)S(1)}, f32[128,128]{1,0:T(8,128)S(1)}, u32[]{:S(2)}, u32[]{:S(2)}) collective-permute-start(f32[128,128]{1,0:T(8,128)S(1)} %get-tuple-element.93), channel_id=1, source_target_pairs={{0,8},{4,12},{8,0},{12,4},{16,24},{20,28},{24,16},{28,20},{1,9},{5... | collective-permute-start | bytes 196616 | tf_op jit(solution)/shard_map/ppermute | solution.py:68
  29.8 1.6 %collective-permute-start.8 = (f32[128,256]{1,0:T(8,128)S(1)}, f32[128,256]{1,0:T(8,128)S(1)}, u32[]{:S(2)}, u32[]{:S(2)}) collective-permute-start(f32[128,256]{1,0:T(8,128)S(1)} %get-tuple-element.88.refs_1_), channel_id=1, source_target_pairs={{0,8},{4,12},{8,0},{12,4},{16,24},{20,28},{24,16},{28,20},{1,9},{5... | collective-permute-start | bytes 393224 | tf_op jit(solution)/shard_map/ppermute | solution.py:68
  32.0 1.4 %collective-permute-done.12.refs_4_ = f32[128,128]{1,0:T(8,128)S(1)} collective-permute-done((f32[128,128]{1,0:T(8,128)S(1)}, f32[128,128]{1,0:T(8,128)S(1)}, u32[]{:S(2)}, u32[]{:S(2)}) %collective-permute-start.12) | collective-permute-done | bytes 65568 | tf_op jit(solution)/shard_map/ppermute | solution.py:68
  33.4 0.9 %collective-permute-done.9.refs_1_ = f32[128,128]{1,0:T(8,128)S(1)} collective-permute-done((f32[128,128]{1,0:T(8,128)S(1)}, f32[128,128]{1,0:T(8,128)S(1)}, u32[]{:S(2)}, u32[]{:S(2)}) %collective-permute-start.9) | collective-permute-done | bytes 65568 | tf_op jit(solution)/shard_map/ppermute | solution.py:68
  36.2 0.9 %merge_1.1 = (bf16[2,256,256]{2,1,0:T(8,128)(2,1)S(1)}, bf16[2,256,256]{2,1,0:T(8,128)(2,1)S(1)}, bf16[2,256,256]{2,1,0:T(8,128)(2,1)S(1)}, bf16[2,256,256]{2,1,...) custom-call(f32[2,256,256]{2,1,0:T(8,128)S(1)} %get-tuple-element.89.refs_0_, ...), custom_call_target="tpu_custom_call" | custom-call | tf_op jit(solution)/shard_map/merge_1/pallas_call | solution.py:51
  37.6 2.7 %collective-permute-start.17 = (f32[64,256]{1,0:T(8,128)S(1)}, f32[64,256]{1,0:T(8,128)S(1)}, u32[]{:S(2)}, u32[]{:S(2)}) collective-permute-start(f32[64,256]{1,0:T(8,128)S(1)} %get-tuple-element.104), channel_id=1, source_target_pairs={{0,16},{4,20},{8,24},{12,28},{16,0},{20,4},{24,8},{28,12},{1,17},{... | collective-permute-start | bytes 196616 | tf_op jit(solution)/shard_map/ppermute | solution.py:68
  40.3 4.1 %collective-permute-done.17.came.refs_1_ = f32[64,256]{1,0:T(8,128)S(1)} collective-permute-done((f32[64,256]{1,0:T(8,128)S(1)}, f32[64,256]{1,0:T(8,128)S(1)}, u32[]{:S(2)}, u32[]{:S(2)}) %collective-permute-start.17) | collective-permute-done | bytes 65568 | tf_op jit(solution)/shard_map/ppermute | solution.py:68
  44.5 1.3 %collective-permute-start.18 = (f32[64,256]{1,0:T(8,128)S(1)}, f32[64,256]{1,0:T(8,128)S(1)}, u32[]{:S(2)}, u32[]{:S(2)}) collective-permute-start(f32[64,256]{1,0:T(8,128)S(1)} %turn.1), channel_id=1, source_target_pairs={{0,16},{4,20},{8,24},{12,28},{16,0},{20,4},{24,8},{28,12},{1,17},{... | collective-permute-start | bytes 196616 | tf_op jit(solution)/shard_map/ppermute | solution.py:68
  45.9 4.6 %collective-permute-done.18.refs_2_ = f32[64,256]{1,0:T(8,128)S(1)} collective-permute-done((f32[64,256]{1,0:T(8,128)S(1)}, f32[64,256]{1,0:T(8,128)S(1)}, u32[]{:S(2)}, u32[]{:S(2)}) %collective-permute-start.18) | collective-permute-done | bytes 65568 | tf_op jit(solution)/shard_map/ppermute | solution.py:68
  51.4 3.7 %collective-permute-done.20.refs_12_ = f32[64,256]{1,0:T(8,128)S(1)} collective-permute-done((f32[64,256]{1,0:T(8,128)S(1)}, f32[64,256]{1,0:T(8,128)S(1)}, u32[]{:S(2)}, u32[]{:S(2)}) %collective-permute-start.20) | collective-permute-done | bytes 65568 | tf_op jit(solution)/shard_map/ppermute | solution.py:68
  55.2 1.2 %collective-permute-done.21.refs_13_ = f32[64,256]{1,0:T(8,128)S(1)} collective-permute-done((f32[64,256]{1,0:T(8,128)S(1)}, f32[64,256]{1,0:T(8,128)S(1)}, u32[]{:S(2)}, u32[]{:S(2)}) %collective-permute-start.21) | collective-permute-done | bytes 65568 | tf_op jit(solution)/shard_map/ppermute | solution.py:68
  56.4 5.2 %local_backward.1 = (f32[8,256,256]{2,1,0:T(8,128)}, f32[64,256]{1,0:T(8,128)}) custom-call(s32[8]{0:T(128)} %refs_0_.5, f32[8,256,256]{2,1,0:T(8,128)S(1)} %get-tuple-element.72.refs_1_, bf16[4,256,256]{2,1,0:T(8,128)(2,1)S(1)} %get-tuple-element.62.refs_4_.refs_2_, bf16[4,256,256]{2,1,0:T(8,128)(2,1)S(1)} %get-tuple-element.63.refs_5_.refs_3_, ...), custom_call_target="tpu_custom_call" | custom-call | tf_op jit(solution)/shard_map/local_backward/pallas_call | solution.py:274
  (34 shorter events, 7.1 us)
Async XLA Ops:
  1.5 7.3 %collective-permute-start.1 = (f32[2,64,256]{2,1,0:T(8,128)S(1)}, f32[2,64,256]{2,1,0:T(8,128)S(1)}, u32[]{:S(2)}, u32[]{:S(2)}) collective-permute-start(f32[2,64,256]{2,1,0:T(8,128)S(1)} %stack.1.refs_5_.refs_0_), channel_id=1, source_target_pairs={{0,2},{1,3},{2,0},{3,1},{4,6},{5,7},{6,4},{7,5},{8,10},{9,11},{10,... | collective-permute-start | bytes 393224 | tf_op jit(solution)/shard_map/ppermute | solution.py:68
  4.5 5.5 %collective-permute-start = (f32[2,64,256]{2,1,0:T(8,128)S(1)}, f32[2,64,256]{2,1,0:T(8,128)S(1)}, u32[]{:S(2)}, u32[]{:S(2)}) collective-permute-start(f32[2,64,256]{2,1,0:T(8,128)S(1)} %stack.1.refs_5_.refs_0_), channel_id=1, source_target_pairs={{0,1},{1,0},{2,3},{3,2},{4,5},{5,4},{6,7},{7,6},{8,9},{9,8},{10,11... | collective-permute-start | bytes 393224 | tf_op jit(solution)/shard_map/ppermute | solution.py:68
  8.8 1.6 %collective-permute-start.2 = (f32[2,64,256]{2,1,0:T(8,128)S(1)}, f32[2,64,256]{2,1,0:T(8,128)S(1)}, u32[]{:S(2)}, u32[]{:S(2)}) collective-permute-start(f32[2,64,256]{2,1,0:T(8,128)S(1)} %collective-permute-done.1.refs_2_), channel_id=1, source_target_pairs={{0,1},{1,0},{2,3},{3,2},{4,5},{5,4},{6,7},{7,6},{8,9},{9,8},{10,11... | collective-permute-start | bytes 393224 | tf_op jit(solution)/shard_map/ppermute | solution.py:68
  10.7 5.8 %collective-permute-start.3 = (f32[128,256]{1,0:T(8,128)S(1)}, f32[128,256]{1,0:T(8,128)S(1)}, u32[]{:S(2)}, u32[]{:S(2)}) collective-permute-start(f32[128,256]{1,0:T(8,128)S(1)} %get-tuple-element.74), channel_id=1, source_target_pairs={{0,4},{4,0},{8,12},{12,8},{16,20},{20,16},{24,28},{28,24},{1,5},{5... | collective-permute-start | bytes 393224 | tf_op jit(solution)/shard_map/ppermute | solution.py:68
  16.5 1.3 %collective-permute-start.4 = (f32[128,256]{1,0:T(8,128)S(1)}, f32[128,256]{1,0:T(8,128)S(1)}, u32[]{:S(2)}, u32[]{:S(2)}) collective-permute-start(f32[128,256]{1,0:T(8,128)S(1)} %get-tuple-element.76), channel_id=1, source_target_pairs={{0,1},{1,0},{2,3},{3,2},{4,5},{5,4},{6,7},{7,6},{8,9},{9,8},{10,11... | collective-permute-start | bytes 393224 | tf_op jit(solution)/shard_map/ppermute | solution.py:68
  17.9 4.3 %collective-permute-start.5 = (f32[64,256]{1,0:T(8,128)S(1)}, f32[64,256]{1,0:T(8,128)S(1)}, u32[]{:S(2)}, u32[]{:S(2)}) collective-permute-start(f32[64,256]{1,0:T(8,128)S(1)} %get-tuple-element.78.refs_3_), channel_id=1, source_target_pairs={{0,2},{1,3},{2,0},{3,1},{4,6},{5,7},{6,4},{7,5},{8,10},{9,11},{10,... | collective-permute-start | bytes 196616 | tf_op jit(solution)/shard_map/ppermute | solution.py:68
  18.7 5.6 %collective-permute-start.7 = (f32[128,256]{1,0:T(8,128)S(1)}, f32[128,256]{1,0:T(8,128)S(1)}, u32[]{:S(2)}, u32[]{:S(2)}) collective-permute-start(f32[128,256]{1,0:T(8,128)S(1)} %collective-permute-done.3.refs_1_), channel_id=1, source_target_pairs={{0,1},{1,0},{2,3},{3,2},{4,5},{5,4},{6,7},{7,6},{8,9},{9,8},{10,11... | collective-permute-start | bytes 393224 | tf_op jit(solution)/shard_map/ppermute | solution.py:68
  22.7 6.7 %collective-permute-start.6 = (f32[128,256]{1,0:T(8,128)S(1)}, f32[128,256]{1,0:T(8,128)S(1)}, u32[]{:S(2)}, u32[]{:S(2)}) collective-permute-start(f32[128,256]{1,0:T(8,128)S(1)} %get-tuple-element.81.refs_1_), channel_id=1, source_target_pairs={{0,4},{4,0},{8,12},{12,8},{16,20},{20,16},{24,28},{28,24},{1,5},{5... | collective-permute-start | bytes 393224 | tf_op jit(solution)/shard_map/ppermute | solution.py:68
  25.3 6.2 %collective-permute-start.10 = (f32[128,128]{1,0:T(8,128)S(1)}, f32[128,128]{1,0:T(8,128)S(1)}, u32[]{:S(2)}, u32[]{:S(2)}) collective-permute-start(f32[128,128]{1,0:T(8,128)S(1)} %get-tuple-element.91), channel_id=1, source_target_pairs={{0,8},{4,12},{8,0},{12,4},{16,24},{20,28},{24,16},{28,20},{1,9},{5... | collective-permute-start | bytes 196616 | tf_op jit(solution)/shard_map/ppermute | solution.py:68
  26.9 5.0 %collective-permute-start.11 = (f32[128,128]{1,0:T(8,128)S(1)}, f32[128,128]{1,0:T(8,128)S(1)}, u32[]{:S(2)}, u32[]{:S(2)}) collective-permute-start(f32[128,128]{1,0:T(8,128)S(1)} %get-tuple-element.92), channel_id=1, source_target_pairs={{0,8},{4,12},{8,0},{12,4},{16,24},{20,28},{24,16},{28,20},{1,9},{5... | collective-permute-start | bytes 196616 | tf_op jit(solution)/shard_map/ppermute | solution.py:68
  27.4 6.0 %collective-permute-start.12 = (f32[128,128]{1,0:T(8,128)S(1)}, f32[128,128]{1,0:T(8,128)S(1)}, u32[]{:S(2)}, u32[]{:S(2)}) collective-permute-start(f32[128,128]{1,0:T(8,128)S(1)} %get-tuple-element.93), channel_id=1, source_target_pairs={{0,8},{4,12},{8,0},{12,4},{16,24},{20,28},{24,16},{28,20},{1,9},{5... | collective-permute-start | bytes 196616 | tf_op jit(solution)/shard_map/ppermute | solution.py:68
  29.0 5.3 %collective-permute-start.9 = (f32[128,128]{1,0:T(8,128)S(1)}, f32[128,128]{1,0:T(8,128)S(1)}, u32[]{:S(2)}, u32[]{:S(2)}) collective-permute-start(f32[128,128]{1,0:T(8,128)S(1)} %get-tuple-element.90), channel_id=1, source_target_pairs={{0,8},{4,12},{8,0},{12,4},{16,24},{20,28},{24,16},{28,20},{1,9},{5... | collective-permute-start | bytes 196616 | tf_op jit(solution)/shard_map/ppermute | solution.py:68
  29.8 7.3 %collective-permute-start.8 = (f32[128,256]{1,0:T(8,128)S(1)}, f32[128,256]{1,0:T(8,128)S(1)}, u32[]{:S(2)}, u32[]{:S(2)}) collective-permute-start(f32[128,256]{1,0:T(8,128)S(1)} %get-tuple-element.88.refs_1_), channel_id=1, source_target_pairs={{0,8},{4,12},{8,0},{12,4},{16,24},{20,28},{24,16},{28,20},{1,9},{5... | collective-permute-start | bytes 393224 | tf_op jit(solution)/shard_map/ppermute | solution.py:68
  34.3 1.3 %collective-permute-start.13 = (f32[128,128]{1,0:T(8,128)S(1)}, f32[128,128]{1,0:T(8,128)S(1)}, u32[]{:S(2)}, u32[]{:S(2)}) collective-permute-start(f32[128,128]{1,0:T(8,128)S(1)} %collective-permute-done.9.refs_1_), channel_id=1, source_target_pairs={{0,1},{1,0},{2,3},{3,2},{4,5},{5,4},{6,7},{7,6},{8,9},{9,8},{10,11... | collective-permute-start | bytes 196616 | tf_op jit(solution)/shard_map/ppermute | solution.py:68
  34.3 1.4 %collective-permute-start.14 = (f32[128,128]{1,0:T(8,128)S(1)}, f32[128,128]{1,0:T(8,128)S(1)}, u32[]{:S(2)}, u32[]{:S(2)}) collective-permute-start(f32[128,128]{1,0:T(8,128)S(1)} %collective-permute-done.10.refs_2_), channel_id=1, source_target_pairs={{0,1},{1,0},{2,3},{3,2},{4,5},{5,4},{6,7},{7,6},{8,9},{9,8},{10,11... | collective-permute-start | bytes 196616 | tf_op jit(solution)/shard_map/ppermute | solution.py:68
  34.8 1.3 %collective-permute-start.15 = (f32[128,128]{1,0:T(8,128)S(1)}, f32[128,128]{1,0:T(8,128)S(1)}, u32[]{:S(2)}, u32[]{:S(2)}) collective-permute-start(f32[128,128]{1,0:T(8,128)S(1)} %collective-permute-done.11.refs_3_), channel_id=1, source_target_pairs={{0,1},{1,0},{2,3},{3,2},{4,5},{5,4},{6,7},{7,6},{8,9},{9,8},{10,11... | collective-permute-start | bytes 196616 | tf_op jit(solution)/shard_map/ppermute | solution.py:68
  34.8 1.4 %collective-permute-start.16 = (f32[128,128]{1,0:T(8,128)S(1)}, f32[128,128]{1,0:T(8,128)S(1)}, u32[]{:S(2)}, u32[]{:S(2)}) collective-permute-start(f32[128,128]{1,0:T(8,128)S(1)} %collective-permute-done.12.refs_4_), channel_id=1, source_target_pairs={{0,1},{1,0},{2,3},{3,2},{4,5},{5,4},{6,7},{7,6},{8,9},{9,8},{10,11... | collective-permute-start | bytes 196616 | tf_op jit(solution)/shard_map/ppermute | solution.py:68
  37.6 6.7 %collective-permute-start.17 = (f32[64,256]{1,0:T(8,128)S(1)}, f32[64,256]{1,0:T(8,128)S(1)}, u32[]{:S(2)}, u32[]{:S(2)}) collective-permute-start(f32[64,256]{1,0:T(8,128)S(1)} %get-tuple-element.104), channel_id=1, source_target_pairs={{0,16},{4,20},{8,24},{12,28},{16,0},{20,4},{24,8},{28,12},{1,17},{... | collective-permute-start | bytes 196616 | tf_op jit(solution)/shard_map/ppermute | solution.py:68
  44.5 6.0 %collective-permute-start.18 = (f32[64,256]{1,0:T(8,128)S(1)}, f32[64,256]{1,0:T(8,128)S(1)}, u32[]{:S(2)}, u32[]{:S(2)}) collective-permute-start(f32[64,256]{1,0:T(8,128)S(1)} %turn.1), channel_id=1, source_target_pairs={{0,16},{4,20},{8,24},{12,28},{16,0},{20,4},{24,8},{28,12},{1,17},{... | collective-permute-start | bytes 196616 | tf_op jit(solution)/shard_map/ppermute | solution.py:68
  50.8 4.3 %collective-permute-start.20 = (f32[64,256]{1,0:T(8,128)S(1)}, f32[64,256]{1,0:T(8,128)S(1)}, u32[]{:S(2)}, u32[]{:S(2)}) collective-permute-start(f32[64,256]{1,0:T(8,128)S(1)} %leave.1.refs_10_), channel_id=1, source_target_pairs={{0,2},{1,3},{2,0},{3,1},{4,6},{5,7},{6,4},{7,5},{8,10},{9,11},{10,... | collective-permute-start | bytes 196616 | tf_op jit(solution)/shard_map/ppermute | solution.py:68
  51.4 3.7 %collective-permute-start.19 = (f32[64,256]{1,0:T(8,128)S(1)}, f32[64,256]{1,0:T(8,128)S(1)}, u32[]{:S(2)}, u32[]{:S(2)}) collective-permute-start(f32[64,256]{1,0:T(8,128)S(1)} %leave.1.refs_10_), channel_id=1, source_target_pairs={{0,1},{1,0},{2,3},{3,2},{4,5},{5,4},{6,7},{7,6},{8,9},{9,8},{10,11... | collective-permute-start | bytes 196616 | tf_op jit(solution)/shard_map/ppermute | solution.py:68
  55.2 1.3 %collective-permute-start.21 = (f32[64,256]{1,0:T(8,128)S(1)}, f32[64,256]{1,0:T(8,128)S(1)}, u32[]{:S(2)}, u32[]{:S(2)}) collective-permute-start(f32[64,256]{1,0:T(8,128)S(1)} %collective-permute-done.20.refs_12_), channel_id=1, source_target_pairs={{0,1},{1,0},{2,3},{3,2},{4,5},{5,4},{6,7},{7,6},{8,9},{9,8},{10,11... | collective-permute-start | bytes 196616 | tf_op jit(solution)/shard_map/ppermute | solution.py:68

commit v7 on v6

--- a/solution.py
+++ b/solution.py
@@ -12,6 +12,7 @@
 TN = (((0,), (0,)), ((), ()))
 VMEM_BYTES = 24 << 20
 HALVES = 2
+SENDS = 2
 
 
 def split(x):
@@ -305,7 +306,7 @@
     inverse_halves[0], inverse_halves[1] = inverse
     value = -dot3(inverse, split(square[1]), NN)
     total[...] = value
-    half = part.shape[0]
+    half = part.shape[1]
     send_blocks([part], [value[:half], value[half:]])
 
 
@@ -316,7 +317,7 @@
         lambda *refs: block_map_kernel(fronts, *refs),
         "block_map",
         [(V, a) for a in parts] + [(pl.ANY, after)],
-        [((size, size), F32), ((size // 2, size), F32), ((2, size, size), BF16)],
+        [((size, size), F32), ((1, size // 2, size), F32), ((2, size, size), BF16)],
         [pltpu.VMEM((2, size, size), F32)],
     )
 
@@ -336,16 +337,20 @@
 
 
 def send_blocks(parts, blocks):
-    count = len(parts)
+    count = sum(part.shape[0] for part in parts)
     low = low_core()
-    for i, part in enumerate(parts):
-        part[...] = jnp.where(low, blocks[i], blocks[len(blocks) - count + i])
+    i = 0
+    for part in parts:
+        for j in range(part.shape[0]):
+            part[j] = jnp.where(low, blocks[i], blocks[len(blocks) - count + i])
+            i += 1
 
 
 def came_blocks(mine, pairs, total):
     low = low_core()
+    mine = [m[j] for m in mine for j in range(m.shape[0])]
+    pairs = [p[j] for p in pairs for j in range(p.shape[0])]
     count = len(mine)
-    mine, pairs = [m[...] for m in mine], [p[...] for p in pairs]
     blocks = [jnp.where(low, mine[i], pairs[i]) for i in range(count)]
     for i in range(count, total):
         j = i - total + count
@@ -390,9 +395,9 @@
 
 
 def merge_kernel(bit, last, *refs):
-    own, mine, pairs, mixed = refs[0], refs[1:5], refs[5:9], refs[9]
+    own, mine, pairs, mixed = refs[0], refs[1 : 1 + SENDS], refs[1 + SENDS : 1 + 2 * SENDS], refs[1 + 2 * SENDS]
     upper = bit_of("leaf", bit) == 1
-    kept, mixed_n, halves, curve_u, total_u, total_l, *parts = refs[10:]
+    kept, mixed_n, halves, curve_u, total_u, total_l, *parts = refs[2 + 2 * SENDS :]
     own_k, own_t = own[0], own[1]
     blocks = came_blocks(mine, pairs, 7)
     other_k, other_t = k_of(blocks), joined(*blocks[3:])
@@ -411,7 +416,8 @@
     a_n = jnp.where(upper, dot3(a_s, low_s, NN), a + dot3(e_s, x_s, TN))
     e_n = jnp.where(upper, e, dot3(up_s, e_s, NN))
     if last:
-        keep_split(kept, k)
+        kept[...] = jnp.zeros_like(kept)
+        send_blocks(parts, k_blocks(k))
         keep_split(mixed_n, jnp.where(bit_of("leaf", bit + 1) == 1, a_n.T, e_n))
     else:
         t = dot3(up_s, low_s, NN)
@@ -422,9 +428,11 @@
 
 def maps(size, last):
     both, whole = ((2, size, size), BF16), ((2, size, size), F32)
+    half = size // 2
     if last:
-        return [both] * 6
-    return [whole, whole, both, both, both, both] + [((size // 2, size // 2), F32)] * 4
+        return [((8, 128), F32)] + [both] * 5 + [((2, half, half), F32)]
+    sends = [((4 // SENDS, half, half), F32)] * SENDS
+    return [whole, whole, both, both, both, both] + sends
 
 
 def fold_kernel(bit, own, other, send, keep):
@@ -446,9 +454,9 @@
     message[rows:] = dot3(split(value), split(own_map[...]), NN)
 
 
-def step_kernel(bit, last, *refs):
-    sol, own, other, halves, curve_u, total_u, total_l, sol_n = refs[:8]
-    message = refs[8:]
+def step_kernel(bit, last, held, *refs):
+    sol, own, other, halves, curve_u, total_u, total_l = refs[:7]
+    sol_n, message = refs[7 + held], refs[8 + held :]
     upper = bit_of("leaf", bit) == 1
     rows = sol.shape[0]
     z_own, p_own, z_other, p_other = own[:rows], own[rows:], other[:rows], other[rows:]
@@ -464,18 +472,18 @@
     given = split(jnp.where(upper, z_low, middle))
     sol_n[...] = sol[...] + dot3(given, pair(halves), NN)
     if last:
-        message[0][...], message[1][...] = z_new, p_new
+        message[0][...] = jnp.where(bit_of("leaf", bit + 1) == 1, p_new, z_new)
+        message[1][...] = z_new
     else:
         message[0][:rows], message[0][rows:] = z_new, p_new
 
 
-def turn_kernel(message, came, curve, back):
-    back[...] = message[...] + dot3(split(came[...]), pair(curve), NN)
-
-
-def leave_kernel(bit, sol, came, back, halves, inverse, top):
+def leave_kernel(bit, sol, own_z, came, halves, mine, pairs, inverse, top):
     upper = bit_of("leaf", bit) == 1
-    given = split(jnp.where(upper, came[...], back[...]))
+    value = came[...]
+    curve = k_of(came_blocks([mine], [pairs], 3))
+    middle = value + dot3(split(own_z[...]), split(curve), NN)
+    given = split(jnp.where(upper, value, middle))
     value = sol[...] + dot3(given, pair(halves), NN)
     top[...] = dot3(split(value), pair(inverse), NN)
 
@@ -549,15 +557,19 @@
     for bit in range(rounds - 1):
         last = bit == rounds - 2
         received = exchange(message, "leaf", bit)
-        if not last:
-            mine = [exchange(part, "leaf", bit + 1) for part in parts]
+        mine = [exchange(part, "leaf", bit + 1) for part in parts]
+        held = [] if last else mine
         sol, *message = call(
-            lambda *refs, bit=bit, last=last: step_kernel(bit, last, *refs),
+            lambda *refs, bit=bit, last=last: step_kernel(bit, last, len(held), *refs),
             f"step_{bit}",
-            [(V, a) for a in (sol, message, received, *tools)],
+            [(V, a) for a in (sol, message, received, *tools)] + [(pl.ANY, a) for a in held],
             [share] + ([share, share] if last else [((2 * chunk, size), F32)]),
         )
-        if not last:
+        if last:
+            came = exchange(message[0], "leaf", bit + 1)
+            mine, _ = lax.optimization_barrier((mine, came))
+            pairs = [exchange(m, "front", 0) for m in mine]
+        else:
             (message,) = message
             mine, _ = lax.optimization_barrier((mine, sol))
             pairs = [exchange(m, "front", 0) for m in mine]
@@ -569,13 +581,10 @@
                 maps(size, last),
             )
             tools, parts = tools[:4], tools[4:]
-    came = exchange(message[0], "leaf", rounds - 1)
-    (back,) = call(turn_kernel, "turn", [(V, a) for a in (message[1], came, kept)], [share])
-    back = exchange(back, "leaf", rounds - 1)
     (top,) = call(
         lambda *refs: leave_kernel(rounds - 1, *refs),
         "leave",
-        [(V, a) for a in (sol, came, back, mixed, inverse)],
+        [(V, a) for a in (sol, message[1], came, mixed, mine[0], pairs[0], inverse)],
         [share],
     )
     pieces = gather_front(top, front_bits)

time: 61.8 us -> 56.5 us (0.914)
  waiting for transfers between devices: 22.7 us -> 17 us
    ppermute x22 -> x19, waiting for transfers between devices: 22.7 us -> 17 us  [swap(): return lax.ppermute(x, axis, [(i, i ^ mask) for i in range(n)])]
    pallas_call x13 -> x12, Pallas kernels: 14 us -> 14.6 us  [call(): pl.pallas_call(kernel, name=name, in_specs=specs, out_specs=tuple((pl.Blo...]
    ppermute x22 -> x19, starting transfers between devices: 18.9 us -> 18.8 us  [swap(): return lax.ppermute(x, axis, [(i, i ^ mask) for i in range(n)])]
  transfers between devices with their start and end apart: 22 -> 19, of which waited for: 15 -> 10; matrix products, arithmetic and copies ran while one was open for 0% -> 0% of each run, Pallas kernels for 19% -> 22%
where the time goes in v7:
time: 56.5 us; the launch traced here: 56.3 us
  Pallas kernels  19.8 us (35%)
  starting transfers between devices  18.8 us (33%)
  waiting for transfers between devices  17 us (30%)
  between operations  0.75 us (1%)
    ppermute x19, starting transfers between devices, swap(): return lax.ppermute(x, axis, [(i, i ^ mask) for i in range(n)])  18.8 us
    ppermute x19, waiting for transfers between devices, swap(): return lax.ppermute(x, axis, [(i, i ^ mask) for i in range(n)])  17 us
    pallas_call x12, Pallas kernels, call(): pl.pallas_call(kernel, name=name, in_specs=specs, out_specs=tuple((pl.Blo...  14.6 us
    pallas_call x1, Pallas kernels, local_backward(): pl.pallas_call(lambda *refs: backward_kernel(nodes, fronts, *refs), name=...  5.19 us
  transfers between devices with their start and end apart: 19, of which 10 were waited for; matrix products, arithmetic and copies ran while one was open for 0% of the time, Pallas kernels for 22%

profile of v7, /device:TPU:0, one launch (start us, length us, event | category | flops | bytes accessed | tf_op | source)
XLA Modules:
  0.0 56.3 jit_solution(6149888724998147217)
XLA Ops:
  0.6 0.9 %stack.1.refs_5_.refs_0_ = f32[2,64,256]{2,1,0:T(8,128)S(1)} custom-call(f32[64,256]{1,0:T(8,128)} %first.1, f32[64,256]{1,0:T(8,128)} %second.1), custom_call_target="tpu_custom_call" | custom-call | tf_op jit(solution)/shard_map/stack/pallas_call | solution.py:52
  1.5 3.0 %collective-permute-start.1 = (f32[2,64,256]{2,1,0:T(8,128)S(1)}, f32[2,64,256]{2,1,0:T(8,128)S(1)}, u32[]{:S(2)}, u32[]{:S(2)}) collective-permute-start(f32[2,64,256]{2,1,0:T(8,128)S(1)} %stack.1.refs_5_.refs_0_), channel_id=1, source_target_pairs={{0,2},{1,3},{2,0},{3,1},{4,6},{5,7},{6,4},{7,5},{8,10},{9,11},{10,... | collective-permute-start | bytes 393224 | tf_op jit(solution)/shard_map/ppermute | solution.py:69
  4.5 4.3 %prepare_first.1 = (f32[2,4,128,256]{3,2,1,0:T(8,128)S(1)}, bf16[4,256,256]{2,1,0:T(8,128)(2,1)S(1)}, bf16[4,256,256]{2,1,0:T(8,128)(2,1)S(1)}, bf16[4,256,256]{...) custom-call(s32[8,256]{1,0:T(8,128)} %refs_0_.3, ...), custom_call_target="tpu_custom_call" | custom-call | tf_op jit(solution)/shard_map/prepare_first/pallas_call | solution.py:52
  8.8 0.6 %collective-permute-start.2 = (f32[2,64,256]{2,1,0:T(8,128)S(1)}, f32[2,64,256]{2,1,0:T(8,128)S(1)}, u32[]{:S(2)}, u32[]{:S(2)}) collective-permute-start(f32[2,64,256]{2,1,0:T(8,128)S(1)} %collective-permute-done.1.refs_2_), channel_id=1, source_target_pairs={{0,1},{1,0},{2,3},{3,2},{4,5},{5,4},{6,7},{7,6},{8,9},{9,8},{10,11... | collective-permute-start | bytes 393224 | tf_op jit(solution)/shard_map/ppermute | solution.py:69
  9.4 0.7 %prepare_second.1 = (f32[2,4,128,256]{3,2,1,0:T(8,128)S(1)}, bf16[4,256,256]{2,1,0:T(8,128)(2,1)S(1)}, bf16[4,256,256]{2,1,0:T(8,128)(2,1)S(1)}, bf16[4,256,256]...) custom-call(f32[256,8]{1,0:T(8,128)S(1)} %get-tuple-element.53.refs_0_, f32[4,256,256]{2,1,0:T(8,128)S(1)} %get-tuple-element.54.refs_1_, ...), custom_call_target="tpu_custom_call" | custom-call | tf_op jit(solution)/shard_map/prepare_second/pallas_call | solution.py:52
  10.7 1.6 %collective-permute-start.3 = (f32[1,128,256]{2,1,0:T(8,128)S(1)}, f32[1,128,256]{2,1,0:T(8,128)S(1)}, u32[]{:S(2)}, u32[]{:S(2)}) collective-permute-start(f32[1,128,256]{2,1,0:T(8,128)S(1)} %get-tuple-element.71), channel_id=1, source_target_pairs={{0,4},{4,0},{8,12},{12,8},{16,20},{20,16},{24,28},{28,24},{1,5},{5... | collective-permute-start | bytes 393224 | tf_op jit(solution)/shard_map/ppermute | solution.py:69
  12.3 4.1 %local_forward.1 = (f32[8,256,256]{2,1,0:T(8,128)S(1)}, f32[128,256]{1,0:T(8,128)S(1)}, f32[128,256]{1,0:T(8,128)S(1)}) custom-call(s32[8]{0:T(128)} %refs_0_.5, f32[2,4,128,256]{3,2,1,0:T(8,128)S(1)} %get-tuple-element.52.refs_4_.refs_1_, f32[2,4,128,256]{3,2,1,0:T(8,128)S(1)} %get-tuple-element.57.refs_4_.refs_2_, ...), custom_call_target="tpu_custom_call" | custom-call | tf_op jit(solution)/shard_map/local_forward/pallas_call | solution.py:52
  17.0 0.8 %collective-permute-done.4.refs_1_ = f32[128,256]{1,0:T(8,128)S(1)} collective-permute-done((f32[128,256]{1,0:T(8,128)S(1)}, f32[128,256]{1,0:T(8,128)S(1)}, u32[]{:S(2)}, u32[]{:S(2)}) %collective-permute-start.4) | collective-permute-done | bytes 131104 | tf_op jit(solution)/shard_map/ppermute | solution.py:69
  17.9 0.7 %collective-permute-start.5 = (f32[64,256]{1,0:T(8,128)S(1)}, f32[64,256]{1,0:T(8,128)S(1)}, u32[]{:S(2)}, u32[]{:S(2)}) collective-permute-start(f32[64,256]{1,0:T(8,128)S(1)} %get-tuple-element.75.refs_3_), channel_id=1, source_target_pairs={{0,2},{1,3},{2,0},{3,1},{4,6},{5,7},{6,4},{7,5},{8,10},{9,11},{10,... | collective-permute-start | bytes 196616 | tf_op jit(solution)/shard_map/ppermute | solution.py:69
  18.7 1.0 %merge_0.1 = (f32[2,256,256]{2,1,0:T(8,128)S(1)}, f32[2,256,256]{2,1,0:T(8,128)S(1)}, bf16[2,256,256]{2,1,0:T(8,128)(2,1)S(1)}, bf16[2,256,256]{2,1,0:T(8,128)(2...) custom-call(f32[256,256]{1,0:T(8,128)S(1)} %get-tuple-element.68.ref, ...), custom_call_target="tpu_custom_call" | custom-call | tf_op jit(solution)/shard_map/merge_0/pallas_call | solution.py:52
  19.7 1.6 %collective-permute-start.8 = (f32[2,128,128]{2,1,0:T(8,128)S(1)}, f32[2,128,128]{2,1,0:T(8,128)S(1)}, u32[]{:S(2)}, u32[]{:S(2)}) collective-permute-start(f32[2,128,128]{2,1,0:T(8,128)S(1)} %get-tuple-element.84), channel_id=1, source_target_pairs={{0,8},{4,12},{8,0},{12,4},{16,24},{20,28},{24,16},{28,20},{1,9},{5... | collective-permute-start | bytes 393224 | tf_op jit(solution)/shard_map/ppermute | solution.py:69
  22.7 1.6 %collective-permute-start.6 = (f32[128,256]{1,0:T(8,128)S(1)}, f32[128,256]{1,0:T(8,128)S(1)}, u32[]{:S(2)}, u32[]{:S(2)}) collective-permute-start(f32[128,256]{1,0:T(8,128)S(1)} %get-tuple-element.78.refs_1_), channel_id=1, source_target_pairs={{0,4},{4,0},{8,12},{12,8},{16,20},{20,16},{24,28},{28,24},{1,5},{5... | collective-permute-start | bytes 393224 | tf_op jit(solution)/shard_map/ppermute | solution.py:69
  24.2 1.9 %collective-permute-done.8.refs_7_.refs_1_ = f32[2,128,128]{2,1,0:T(8,128)S(1)} collective-permute-done((f32[2,128,128]{2,1,0:T(8,128)S(1)}, f32[2,128,128]{2,1,0:T(8,128)S(1)}, u32[]{:S(2)}, u32[]{:S(2)}) %collective-permute-start.8) | collective-permute-done | bytes 131104 | tf_op jit(solution)/shard_map/ppermute | solution.py:69
  26.1 1.7 %collective-permute-done.9.refs_8_.refs_2_ = f32[2,128,128]{2,1,0:T(8,128)S(1)} collective-permute-done((f32[2,128,128]{2,1,0:T(8,128)S(1)}, f32[2,128,128]{2,1,0:T(8,128)S(1)}, u32[]{:S(2)}, u32[]{:S(2)}) %collective-permute-start.9) | collective-permute-done | bytes 131104 | tf_op jit(solution)/shard_map/ppermute | solution.py:69
  28.8 1.6 %collective-permute-start.10 = (f32[128,256]{1,0:T(8,128)S(1)}, f32[128,256]{1,0:T(8,128)S(1)}, u32[]{:S(2)}, u32[]{:S(2)}) collective-permute-start(f32[128,256]{1,0:T(8,128)S(1)} %get-tuple-element.87.refs_1_), channel_id=1, source_target_pairs={{0,8},{4,12},{8,0},{12,4},{16,24},{20,28},{24,16},{28,20},{1,9},{5... | collective-permute-start | bytes 393224 | tf_op jit(solution)/shard_map/ppermute | solution.py:69
  30.4 1.5 %merge_1.1 = (f32[8,128]{1,0:T(8,128)}, bf16[2,256,256]{2,1,0:T(8,128)(2,1)S(1)}, bf16[2,256,256]{2,1,0:T(8,128)(2,1)S(1)}, bf16[2,256,256]{2,1,0:T(8,128)(2,1)S...) custom-call(f32[2,256,256]{2,1,0:T(8,128)S(1)} %get-tuple-element.88.refs_0_, ...), custom_call_target="tpu_custom_call" | custom-call | tf_op jit(solution)/shard_map/merge_1/pallas_call | solution.py:52
  31.9 2.6 %collective-permute-start.14 = (f32[2,128,128]{2,1,0:T(8,128)S(1)}, f32[2,128,128]{2,1,0:T(8,128)S(1)}, u32[]{:S(2)}, u32[]{:S(2)}) collective-permute-start(f32[2,128,128]{2,1,0:T(8,128)S(1)} %get-tuple-element.100), channel_id=1, source_target_pairs={{0,16},{4,20},{8,24},{12,28},{16,0},{20,4},{24,8},{28,12},{1,17},{... | collective-permute-start | bytes 393224 | tf_op jit(solution)/shard_map/ppermute | solution.py:69
  34.9 2.6 %collective-permute-start.13 = (f32[64,256]{1,0:T(8,128)S(1)}, f32[64,256]{1,0:T(8,128)S(1)}, u32[]{:S(2)}, u32[]{:S(2)}) collective-permute-start(f32[64,256]{1,0:T(8,128)S(1)} %get-tuple-element.98), channel_id=1, source_target_pairs={{0,16},{4,20},{8,24},{12,28},{16,0},{20,4},{24,8},{28,12},{1,17},{... | collective-permute-start | bytes 196616 | tf_op jit(solution)/shard_map/ppermute | solution.py:69
  37.5 6.1 %collective-permute-done.13.refs_2_ = f32[64,256]{1,0:T(8,128)S(1)} collective-permute-done((f32[64,256]{1,0:T(8,128)S(1)}, f32[64,256]{1,0:T(8,128)S(1)}, u32[]{:S(2)}, u32[]{:S(2)}) %collective-permute-start.13) | collective-permute-done | bytes 65568 | tf_op jit(solution)/shard_map/ppermute | solution.py:69
  43.6 1.3 %collective-permute-done.15.refs_5_ = f32[2,128,128]{2,1,0:T(8,128)S(1)} collective-permute-done((f32[2,128,128]{2,1,0:T(8,128)S(1)}, f32[2,128,128]{2,1,0:T(8,128)S(1)}, u32[]{:S(2)}, u32[]{:S(2)}) %collective-permute-start.15) | collective-permute-done | bytes 131104 | tf_op jit(solution)/shard_map/ppermute | solution.py:69
  45.6 1.4 %collective-permute-start.17 = (f32[64,256]{1,0:T(8,128)S(1)}, f32[64,256]{1,0:T(8,128)S(1)}, u32[]{:S(2)}, u32[]{:S(2)}) collective-permute-start(f32[64,256]{1,0:T(8,128)S(1)} %leave.1.refs_10_), channel_id=1, source_target_pairs={{0,2},{1,3},{2,0},{3,1},{4,6},{5,7},{6,4},{7,5},{8,10},{9,11},{10,... | collective-permute-start | bytes 196616 | tf_op jit(solution)/shard_map/ppermute | solution.py:69
  47.0 2.9 %collective-permute-done.17.refs_12_ = f32[64,256]{1,0:T(8,128)S(1)} collective-permute-done((f32[64,256]{1,0:T(8,128)S(1)}, f32[64,256]{1,0:T(8,128)S(1)}, u32[]{:S(2)}, u32[]{:S(2)}) %collective-permute-start.17) | collective-permute-done | bytes 65568 | tf_op jit(solution)/shard_map/ppermute | solution.py:69
  49.9 1.2 %collective-permute-done.18.refs_13_ = f32[64,256]{1,0:T(8,128)S(1)} collective-permute-done((f32[64,256]{1,0:T(8,128)S(1)}, f32[64,256]{1,0:T(8,128)S(1)}, u32[]{:S(2)}, u32[]{:S(2)}) %collective-permute-start.18) | collective-permute-done | bytes 65568 | tf_op jit(solution)/shard_map/ppermute | solution.py:69
  51.2 5.2 %local_backward.1 = (f32[8,256,256]{2,1,0:T(8,128)}, f32[64,256]{1,0:T(8,128)}) custom-call(s32[8]{0:T(128)} %refs_0_.5, f32[8,256,256]{2,1,0:T(8,128)S(1)} %get-tuple-element.69.refs_1_, bf16[4,256,256]{2,1,0:T(8,128)(2,1)S(1)} %get-tuple-element.59.refs_4_.refs_2_, bf16[4,256,256]{2,1,0:T(8,128)(2,1)S(1)} %get-tuple-element.60.refs_5_.refs_3_, ...), custom_call_target="tpu_custom_call" | custom-call | tf_op jit(solution)/shard_map/local_backward/pallas_call | solution.py:275
  (27 shorter events, 4.6 us)
Async XLA Ops:
  1.5 7.3 %collective-permute-start.1 = (f32[2,64,256]{2,1,0:T(8,128)S(1)}, f32[2,64,256]{2,1,0:T(8,128)S(1)}, u32[]{:S(2)}, u32[]{:S(2)}) collective-permute-start(f32[2,64,256]{2,1,0:T(8,128)S(1)} %stack.1.refs_5_.refs_0_), channel_id=1, source_target_pairs={{0,2},{1,3},{2,0},{3,1},{4,6},{5,7},{6,4},{7,5},{8,10},{9,11},{10,... | collective-permute-start | bytes 393224 | tf_op jit(solution)/shard_map/ppermute | solution.py:69
  4.5 5.5 %collective-permute-start = (f32[2,64,256]{2,1,0:T(8,128)S(1)}, f32[2,64,256]{2,1,0:T(8,128)S(1)}, u32[]{:S(2)}, u32[]{:S(2)}) collective-permute-start(f32[2,64,256]{2,1,0:T(8,128)S(1)} %stack.1.refs_5_.refs_0_), channel_id=1, source_target_pairs={{0,1},{1,0},{2,3},{3,2},{4,5},{5,4},{6,7},{7,6},{8,9},{9,8},{10,11... | collective-permute-start | bytes 393224 | tf_op jit(solution)/shard_map/ppermute | solution.py:69
  8.8 1.6 %collective-permute-start.2 = (f32[2,64,256]{2,1,0:T(8,128)S(1)}, f32[2,64,256]{2,1,0:T(8,128)S(1)}, u32[]{:S(2)}, u32[]{:S(2)}) collective-permute-start(f32[2,64,256]{2,1,0:T(8,128)S(1)} %collective-permute-done.1.refs_2_), channel_id=1, source_target_pairs={{0,1},{1,0},{2,3},{3,2},{4,5},{5,4},{6,7},{7,6},{8,9},{9,8},{10,11... | collective-permute-start | bytes 393224 | tf_op jit(solution)/shard_map/ppermute | solution.py:69
  10.7 5.8 %collective-permute-start.3 = (f32[1,128,256]{2,1,0:T(8,128)S(1)}, f32[1,128,256]{2,1,0:T(8,128)S(1)}, u32[]{:S(2)}, u32[]{:S(2)}) collective-permute-start(f32[1,128,256]{2,1,0:T(8,128)S(1)} %get-tuple-element.71), channel_id=1, source_target_pairs={{0,4},{4,0},{8,12},{12,8},{16,20},{20,16},{24,28},{28,24},{1,5},{5... | collective-permute-start | bytes 393224 | tf_op jit(solution)/shard_map/ppermute | solution.py:69
  16.5 1.3 %collective-permute-start.4 = (f32[128,256]{1,0:T(8,128)S(1)}, f32[128,256]{1,0:T(8,128)S(1)}, u32[]{:S(2)}, u32[]{:S(2)}) collective-permute-start(f32[128,256]{1,0:T(8,128)S(1)} %get-tuple-element.73), channel_id=1, source_target_pairs={{0,1},{1,0},{2,3},{3,2},{4,5},{5,4},{6,7},{7,6},{8,9},{9,8},{10,11... | collective-permute-start | bytes 393224 | tf_op jit(solution)/shard_map/ppermute | solution.py:69
  16.5 2.1 %collective-permute-start.7 = (f32[1,128,256]{2,1,0:T(8,128)S(1)}, f32[1,128,256]{2,1,0:T(8,128)S(1)}, u32[]{:S(2)}, u32[]{:S(2)}) collective-permute-start(f32[1,128,256]{2,1,0:T(8,128)S(1)} %collective-permute-done.3.refs_1_), channel_id=1, source_target_pairs={{0,1},{1,0},{2,3},{3,2},{4,5},{5,4},{6,7},{7,6},{8,9},{9,8},{10,11... | collective-permute-start | bytes 393224 | tf_op jit(solution)/shard_map/ppermute | solution.py:69
  17.9 4.3 %collective-permute-start.5 = (f32[64,256]{1,0:T(8,128)S(1)}, f32[64,256]{1,0:T(8,128)S(1)}, u32[]{:S(2)}, u32[]{:S(2)}) collective-permute-start(f32[64,256]{1,0:T(8,128)S(1)} %get-tuple-element.75.refs_3_), channel_id=1, source_target_pairs={{0,2},{1,3},{2,0},{3,1},{4,6},{5,7},{6,4},{7,5},{8,10},{9,11},{10,... | collective-permute-start | bytes 196616 | tf_op jit(solution)/shard_map/ppermute | solution.py:69
  19.7 6.4 %collective-permute-start.8 = (f32[2,128,128]{2,1,0:T(8,128)S(1)}, f32[2,128,128]{2,1,0:T(8,128)S(1)}, u32[]{:S(2)}, u32[]{:S(2)}) collective-permute-start(f32[2,128,128]{2,1,0:T(8,128)S(1)} %get-tuple-element.84), channel_id=1, source_target_pairs={{0,8},{4,12},{8,0},{12,4},{16,24},{20,28},{24,16},{28,20},{1,9},{5... | collective-permute-start | bytes 393224 | tf_op jit(solution)/shard_map/ppermute | solution.py:69
  21.3 6.5 %collective-permute-start.9 = (f32[2,128,128]{2,1,0:T(8,128)S(1)}, f32[2,128,128]{2,1,0:T(8,128)S(1)}, u32[]{:S(2)}, u32[]{:S(2)}) collective-permute-start(f32[2,128,128]{2,1,0:T(8,128)S(1)} %get-tuple-element.85), channel_id=1, source_target_pairs={{0,8},{4,12},{8,0},{12,4},{16,24},{20,28},{24,16},{28,20},{1,9},{5... | collective-permute-start | bytes 393224 | tf_op jit(solution)/shard_map/ppermute | solution.py:69
  22.7 5.2 %collective-permute-start.6 = (f32[128,256]{1,0:T(8,128)S(1)}, f32[128,256]{1,0:T(8,128)S(1)}, u32[]{:S(2)}, u32[]{:S(2)}) collective-permute-start(f32[128,256]{1,0:T(8,128)S(1)} %get-tuple-element.78.refs_1_), channel_id=1, source_target_pairs={{0,4},{4,0},{8,12},{12,8},{16,20},{20,16},{24,28},{28,24},{1,5},{5... | collective-permute-start | bytes 393224 | tf_op jit(solution)/shard_map/ppermute | solution.py:69
  28.3 2.2 %collective-permute-start.11 = (f32[2,128,128]{2,1,0:T(8,128)S(1)}, f32[2,128,128]{2,1,0:T(8,128)S(1)}, u32[]{:S(2)}, u32[]{:S(2)}) collective-permute-start(f32[2,128,128]{2,1,0:T(8,128)S(1)} %collective-permute-done.8.refs_7_.refs_1_), channel_id=1, source_target_pairs={{0,1},{1,0},{2,3},{3,2},{4,5},{5,4},{6,7},{7,6},{8,9},{9,8},{10,11... | collective-permute-start | bytes 393224 | tf_op jit(solution)/shard_map/ppermute | solution.py:69
  28.3 2.1 %collective-permute-start.12 = (f32[2,128,128]{2,1,0:T(8,128)S(1)}, f32[2,128,128]{2,1,0:T(8,128)S(1)}, u32[]{:S(2)}, u32[]{:S(2)}) collective-permute-start(f32[2,128,128]{2,1,0:T(8,128)S(1)} %collective-permute-done.9.refs_8_.refs_2_), channel_id=1, source_target_pairs={{0,1},{1,0},{2,3},{3,2},{4,5},{5,4},{6,7},{7,6},{8,9},{9,8},{10,11... | collective-permute-start | bytes 393224 | tf_op jit(solution)/shard_map/ppermute | solution.py:69
  28.8 5.7 %collective-permute-start.10 = (f32[128,256]{1,0:T(8,128)S(1)}, f32[128,256]{1,0:T(8,128)S(1)}, u32[]{:S(2)}, u32[]{:S(2)}) collective-permute-start(f32[128,256]{1,0:T(8,128)S(1)} %get-tuple-element.87.refs_1_), channel_id=1, source_target_pairs={{0,8},{4,12},{8,0},{12,4},{16,24},{20,28},{24,16},{28,20},{1,9},{5... | collective-permute-start | bytes 393224 | tf_op jit(solution)/shard_map/ppermute | solution.py:69
  31.9 11.7 %collective-permute-start.14 = (f32[2,128,128]{2,1,0:T(8,128)S(1)}, f32[2,128,128]{2,1,0:T(8,128)S(1)}, u32[]{:S(2)}, u32[]{:S(2)}) collective-permute-start(f32[2,128,128]{2,1,0:T(8,128)S(1)} %get-tuple-element.100), channel_id=1, source_target_pairs={{0,16},{4,20},{8,24},{12,28},{16,0},{20,4},{24,8},{28,12},{1,17},{... | collective-permute-start | bytes 393224 | tf_op jit(solution)/shard_map/ppermute | solution.py:69
  34.9 8.7 %collective-permute-start.13 = (f32[64,256]{1,0:T(8,128)S(1)}, f32[64,256]{1,0:T(8,128)S(1)}, u32[]{:S(2)}, u32[]{:S(2)}) collective-permute-start(f32[64,256]{1,0:T(8,128)S(1)} %get-tuple-element.98), channel_id=1, source_target_pairs={{0,16},{4,20},{8,24},{12,28},{16,0},{20,4},{24,8},{28,12},{1,17},{... | collective-permute-start | bytes 196616 | tf_op jit(solution)/shard_map/ppermute | solution.py:69
  43.6 1.3 %collective-permute-start.15 = (f32[2,128,128]{2,1,0:T(8,128)S(1)}, f32[2,128,128]{2,1,0:T(8,128)S(1)}, u32[]{:S(2)}, u32[]{:S(2)}) collective-permute-start(f32[2,128,128]{2,1,0:T(8,128)S(1)} %collective-permute-done.14.refs_4_), channel_id=1, source_target_pairs={{0,1},{1,0},{2,3},{3,2},{4,5},{5,4},{6,7},{7,6},{8,9},{9,8},{10,11... | collective-permute-start | bytes 393224 | tf_op jit(solution)/shard_map/ppermute | solution.py:69
  45.6 4.3 %collective-permute-start.17 = (f32[64,256]{1,0:T(8,128)S(1)}, f32[64,256]{1,0:T(8,128)S(1)}, u32[]{:S(2)}, u32[]{:S(2)}) collective-permute-start(f32[64,256]{1,0:T(8,128)S(1)} %leave.1.refs_10_), channel_id=1, source_target_pairs={{0,2},{1,3},{2,0},{3,1},{4,6},{5,7},{6,4},{7,5},{8,10},{9,11},{10,... | collective-permute-start | bytes 196616 | tf_op jit(solution)/shard_map/ppermute | solution.py:69
  47.0 2.9 %collective-permute-start.16 = (f32[64,256]{1,0:T(8,128)S(1)}, f32[64,256]{1,0:T(8,128)S(1)}, u32[]{:S(2)}, u32[]{:S(2)}) collective-permute-start(f32[64,256]{1,0:T(8,128)S(1)} %leave.1.refs_10_), channel_id=1, source_target_pairs={{0,1},{1,0},{2,3},{3,2},{4,5},{5,4},{6,7},{7,6},{8,9},{9,8},{10,11... | collective-permute-start | bytes 196616 | tf_op jit(solution)/shard_map/ppermute | solution.py:69
  49.9 1.3 %collective-permute-start.18 = (f32[64,256]{1,0:T(8,128)S(1)}, f32[64,256]{1,0:T(8,128)S(1)}, u32[]{:S(2)}, u32[]{:S(2)}) collective-permute-start(f32[64,256]{1,0:T(8,128)S(1)} %collective-permute-done.17.refs_12_), channel_id=1, source_target_pairs={{0,1},{1,0},{2,3},{3,2},{4,5},{5,4},{6,7},{7,6},{8,9},{9,8},{10,11... | collective-permute-start | bytes 196616 | tf_op jit(solution)/shard_map/ppermute | solution.py:69

commit v8 on v7

--- a/solution.py
+++ b/solution.py
@@ -226,8 +226,8 @@
     (parent_h, solved), parts, refs = refs[:2], (refs[2:6], refs[6:10]), refs[10:]
     pieces = refs[:fronts]
     sol, sep_out = refs[fronts : 2 + fronts]
-    square, parent, staged, sem, sems = refs[2 + fronts : 7 + fronts]
-    known = refs[7 + fronts :]
+    square, parent, staged, sep_v, sem, sems = refs[2 + fronts : 8 + fronts]
+    known = refs[8 + fronts :]
     first = parts[0][0].shape[0]
     copy = pltpu.make_async_copy(parent_h, parent, sem)
     copy.start()
@@ -258,11 +258,15 @@
         out = pltpu.make_async_copy(staged.at[k], sol.at[k], sems.at[k])
         out.start()
         outs.append(out)
-    for h in range(HALVES):
-        square[:, h * width : (h + 1) * width] = known[h][nodes].T
-    share = sep_out.shape[0]
-    start = pl.multiple_of(lax.axis_index("front") * share, 8)
-    sep_out[...] = square[pl.ds(start, share), :]
+        if k == nodes - 1:
+            for h in range(HALVES):
+                square[:, h * width : (h + 1) * width] = known[h][nodes].T
+            share = sep_v.shape[0]
+            start = pl.multiple_of(lax.axis_index("front") * share, 8)
+            sep_v[...] = square[pl.ds(start, share), :]
+            out = pltpu.make_async_copy(sep_v, sep_out, sems.at[nodes])
+            out.start()
+            outs.append(out)
     for out in outs:
         out.wait()
 
@@ -276,11 +280,11 @@
         lambda *refs: backward_kernel(nodes, fronts, *refs),
         name="local_backward",
         in_specs=[pl.BlockSpec(memory_space=HBM)] + [pl.BlockSpec(memory_space=V)] * len(ins),
-        out_specs=(pl.BlockSpec(memory_space=HBM), pl.BlockSpec(memory_space=V)),
+        out_specs=(pl.BlockSpec(memory_space=HBM),) * 2,
         out_shape=(sol, jax.ShapeDtypeStruct(*sep)),
         scratch_shapes=[pltpu.VMEM((size, cols), F32), pltpu.SMEM((nodes,), jnp.int32)]
-        + [pltpu.VMEM((nodes, size, cols), F32), pltpu.SemaphoreType.DMA]
-        + [pltpu.SemaphoreType.DMA((nodes,))]
+        + [pltpu.VMEM((nodes, size, cols), F32), pltpu.VMEM(*sep), pltpu.SemaphoreType.DMA]
+        + [pltpu.SemaphoreType.DMA((nodes + 1,))]
         + [pltpu.VMEM((nodes + 1, cols // HALVES, size), F32)] * HALVES,
         compiler_params=pltpu.CompilerParams(vmem_limit_bytes=VMEM_BYTES),
     )(pltpu.with_memory_space_constraint(parent, HBM), *ins)
@@ -395,9 +399,10 @@
 
 
 def merge_kernel(bit, last, *refs):
-    own, mine, pairs, mixed = refs[0], refs[1 : 1 + SENDS], refs[1 + SENDS : 1 + 2 * SENDS], refs[1 + 2 * SENDS]
+    own, refs = refs[0], refs[1:]
+    mine, pairs, mixed = refs[:SENDS], refs[SENDS : 2 * SENDS], refs[2 * SENDS]
     upper = bit_of("leaf", bit) == 1
-    kept, mixed_n, halves, curve_u, total_u, total_l, *parts = refs[2 + 2 * SENDS :]
+    kept, mixed_n, halves, curve_u, total_u, total_l, *parts = refs[1 + 2 * SENDS :]
     own_k, own_t = own[0], own[1]
     blocks = came_blocks(mine, pairs, 7)
     other_k, other_t = k_of(blocks), joined(*blocks[3:])
@@ -417,7 +422,8 @@
     e_n = jnp.where(upper, e, dot3(up_s, e_s, NN))
     if last:
         kept[...] = jnp.zeros_like(kept)
-        send_blocks(parts, k_blocks(k))
+        for i, block in enumerate(k_blocks(k)):
+            parts[0][i] = block
         keep_split(mixed_n, jnp.where(bit_of("leaf", bit + 1) == 1, a_n.T, e_n))
     else:
         t = dot3(up_s, low_s, NN)
@@ -430,7 +436,7 @@
     both, whole = ((2, size, size), BF16), ((2, size, size), F32)
     half = size // 2
     if last:
-        return [((8, 128), F32)] + [both] * 5 + [((2, half, half), F32)]
+        return [((8, 128), F32)] + [both] * 5 + [((3, half, half), F32)]
     sends = [((4 // SENDS, half, half), F32)] * SENDS
     return [whole, whole, both, both, both, both] + sends
 
@@ -478,13 +484,20 @@
         message[0][:rows], message[0][rows:] = z_new, p_new
 
 
-def leave_kernel(bit, sol, own_z, came, halves, mine, pairs, inverse, top):
-    upper = bit_of("leaf", bit) == 1
+def turn_kernel(bit, own_z, came, blocks, given):
     value = came[...]
-    curve = k_of(came_blocks([mine], [pairs], 3))
-    middle = value + dot3(split(own_z[...]), split(curve), NN)
-    given = split(jnp.where(upper, value, middle))
-    value = sol[...] + dot3(given, pair(halves), NN)
+    middle = value + dot3(split(own_z[...]), split(k_of(blocks)), NN)
+    given[...] = jnp.where(bit_of("leaf", bit) == 1, value, middle)
+
+
+def passed_on(bit, last, given, received):
+    away = bit_of("leaf", bit) == bit_of("leaf", last)
+    return jnp.where(away, received, given)
+
+
+def leave_kernel(last, sol, given, received, halves, inverse, top):
+    came = passed_on(1, last, given[...], received[...])
+    value = sol[...] + dot3(split(came), pair(halves), NN)
     top[...] = dot3(split(value), pair(inverse), NN)
 
 
@@ -557,19 +570,14 @@
     for bit in range(rounds - 1):
         last = bit == rounds - 2
         received = exchange(message, "leaf", bit)
-        mine = [exchange(part, "leaf", bit + 1) for part in parts]
-        held = [] if last else mine
+        mine = [] if last else [exchange(part, "leaf", bit + 1) for part in parts]
         sol, *message = call(
-            lambda *refs, bit=bit, last=last: step_kernel(bit, last, len(held), *refs),
+            lambda *refs, bit=bit, last=last: step_kernel(bit, last, len(mine), *refs),
             f"step_{bit}",
-            [(V, a) for a in (sol, message, received, *tools)] + [(pl.ANY, a) for a in held],
+            [(V, a) for a in (sol, message, received, *tools)] + [(pl.ANY, a) for a in mine],
             [share] + ([share, share] if last else [((2 * chunk, size), F32)]),
         )
-        if last:
-            came = exchange(message[0], "leaf", bit + 1)
-            mine, _ = lax.optimization_barrier((mine, came))
-            pairs = [exchange(m, "front", 0) for m in mine]
-        else:
+        if not last:
             (message,) = message
             mine, _ = lax.optimization_barrier((mine, sol))
             pairs = [exchange(m, "front", 0) for m in mine]
@@ -581,10 +589,24 @@
                 maps(size, last),
             )
             tools, parts = tools[:4], tools[4:]
+    middle = leaves // 2
+    boundary = [(middle - 2 + i, middle + i) for i in range(2)]
+    boundary += [(j, i) for i, j in boundary]
+    blocks = lax.ppermute(parts[0], "leaf", boundary)
+    came = lax.ppermute(message[0], "leaf", boundary)
+    (given,) = call(
+        lambda *refs: turn_kernel(rounds - 1, *refs),
+        "turn",
+        [(V, a) for a in (message[1], came, blocks)],
+        [share],
+    )
+    for bit in reversed(range(2, rounds - 1)):
+        given = passed_on(bit, rounds - 1, given, exchange(given, "leaf", bit))
+    received = exchange(given, "leaf", 1)
     (top,) = call(
         lambda *refs: leave_kernel(rounds - 1, *refs),
         "leave",
-        [(V, a) for a in (sol, message[1], came, mixed, mine[0], pairs[0], inverse)],
+        [(V, a) for a in (sol, given, received, mixed, inverse)],
         [share],
     )
     pieces = gather_front(top, front_bits)

time: 56.5 us -> 56.9 us (level)
  starting transfers between devices: 18.8 us -> 23.2 us
  waiting for transfers between devices: 17 us -> 13.5 us
  Pallas kernels: 19.8 us -> 19.2 us
    ppermute x19 -> x17, waiting for transfers between devices: 17 us -> 13.5 us  [swap(): return lax.ppermute(x, axis, [(i, i ^ mask) for i in range(n)])]
    ppermute x19 -> x17, starting transfers between devices: 18.8 us -> 21.9 us  [swap(): return lax.ppermute(x, axis, [(i, i ^ mask) for i in range(n)])]
    ppermute x0 -> x2, starting transfers between devices: none -> 1.33 us  [the longest x1 0.66 us: local(): came = lax.ppermute(message[0], 'leaf', boundary)]
    pallas_call x1, Pallas kernels: 5.19 us -> 4.55 us  [local_backward(): pl.pallas_call(lambda *refs: backward_kernel(nodes, fronts, *refs), name=...]
    pallas_call x12 -> x13, Pallas kernels: 14.6 us -> 14.6 us  [call(): pl.pallas_call(kernel, name=name, in_specs=specs, out_specs=tuple((pl.Blo...]
where the time goes in v8:
time: 56.9 us; the launch traced here: 56.7 us
  starting transfers between devices  23.2 us (41%)
  Pallas kernels  19.2 us (34%)
  waiting for transfers between devices  13.5 us (24%)
  between operations  0.79 us (1%)
    ppermute x17, starting transfers between devices, swap(): return lax.ppermute(x, axis, [(i, i ^ mask) for i in range(n)])  21.9 us
    pallas_call x13, Pallas kernels, call(): pl.pallas_call(kernel, name=name, in_specs=specs, out_specs=tuple((pl.Blo...  14.6 us
    ppermute x17, waiting for transfers between devices, swap(): return lax.ppermute(x, axis, [(i, i ^ mask) for i in range(n)])  13.5 us
    pallas_call x1, Pallas kernels, local_backward(): pl.pallas_call(lambda *refs: backward_kernel(nodes, fronts, *refs), name=...  4.55 us
  transfers between devices with their start and end apart: 19, of which 10 were waited for; matrix products, arithmetic and copies ran while one was open for 0% of the time, Pallas kernels for 22%

profile of v8, /device:TPU:0, one launch (start us, length us, event | category | flops | bytes accessed | tf_op | source)
XLA Modules:
  0.0 56.7 jit_solution(659491256880296359)
XLA Ops:
  0.6 0.9 %stack.1.refs_5_.refs_0_ = f32[2,64,256]{2,1,0:T(8,128)S(1)} custom-call(f32[64,256]{1,0:T(8,128)} %first.1, f32[64,256]{1,0:T(8,128)} %second.1), custom_call_target="tpu_custom_call" | custom-call | tf_op jit(solution)/shard_map/stack/pallas_call | solution.py:52
  1.5 3.0 %collective-permute-start.1 = (f32[2,64,256]{2,1,0:T(8,128)S(1)}, f32[2,64,256]{2,1,0:T(8,128)S(1)}, u32[]{:S(2)}, u32[]{:S(2)}) collective-permute-start(f32[2,64,256]{2,1,0:T(8,128)S(1)} %stack.1.refs_5_.refs_0_), channel_id=1, source_target_pairs={{0,2},{1,3},{2,0},{3,1},{4,6},{5,7},{6,4},{7,5},{8,10},{9,11},{10,... | collective-permute-start | bytes 393224 | tf_op jit(solution)/shard_map/ppermute | solution.py:69
  4.5 4.3 %prepare_first.1 = (f32[2,4,128,256]{3,2,1,0:T(8,128)S(1)}, bf16[4,256,256]{2,1,0:T(8,128)(2,1)S(1)}, bf16[4,256,256]{2,1,0:T(8,128)(2,1)S(1)}, bf16[4,256,256]{...) custom-call(s32[8,256]{1,0:T(8,128)} %refs_0_.3, ...), custom_call_target="tpu_custom_call" | custom-call | tf_op jit(solution)/shard_map/prepare_first/pallas_call | solution.py:52
  9.4 0.7 %prepare_second.1 = (f32[2,4,128,256]{3,2,1,0:T(8,128)S(1)}, bf16[4,256,256]{2,1,0:T(8,128)(2,1)S(1)}, bf16[4,256,256]{2,1,0:T(8,128)(2,1)S(1)}, bf16[4,256,256]...) custom-call(f32[256,8]{1,0:T(8,128)S(1)} %get-tuple-element.52.refs_0_, f32[4,256,256]{2,1,0:T(8,128)S(1)} %get-tuple-element.53.refs_1_, ...), custom_call_target="tpu_custom_call" | custom-call | tf_op jit(solution)/shard_map/prepare_second/pallas_call | solution.py:52
  10.7 1.6 %collective-permute-start.3 = (f32[1,128,256]{2,1,0:T(8,128)S(1)}, f32[1,128,256]{2,1,0:T(8,128)S(1)}, u32[]{:S(2)}, u32[]{:S(2)}) collective-permute-start(f32[1,128,256]{2,1,0:T(8,128)S(1)} %get-tuple-element.70), channel_id=1, source_target_pairs={{0,4},{4,0},{8,12},{12,8},{16,20},{20,16},{24,28},{28,24},{1,5},{5... | collective-permute-start | bytes 393224 | tf_op jit(solution)/shard_map/ppermute | solution.py:69
  12.3 4.1 %local_forward.1 = (f32[8,256,256]{2,1,0:T(8,128)S(1)}, f32[128,256]{1,0:T(8,128)S(1)}, f32[128,256]{1,0:T(8,128)S(1)}) custom-call(s32[8]{0:T(128)} %refs_0_.5, f32[2,4,128,256]{3,2,1,0:T(8,128)S(1)} %get-tuple-element.51.refs_4_.refs_1_, f32[2,4,128,256]{3,2,1,0:T(8,128)S(1)} %get-tuple-element.56.refs_4_.refs_2_, ...), custom_call_target="tpu_custom_call" | custom-call | tf_op jit(solution)/shard_map/local_forward/pallas_call | solution.py:52
  17.0 0.8 %collective-permute-done.4.refs_1_ = f32[128,256]{1,0:T(8,128)S(1)} collective-permute-done((f32[128,256]{1,0:T(8,128)S(1)}, f32[128,256]{1,0:T(8,128)S(1)}, u32[]{:S(2)}, u32[]{:S(2)}) %collective-permute-start.4) | collective-permute-done | bytes 131104 | tf_op jit(solution)/shard_map/ppermute | solution.py:69
  17.9 0.7 %collective-permute-start.5 = (f32[64,256]{1,0:T(8,128)S(1)}, f32[64,256]{1,0:T(8,128)S(1)}, u32[]{:S(2)}, u32[]{:S(2)}) collective-permute-start(f32[64,256]{1,0:T(8,128)S(1)} %get-tuple-element.74.refs_3_), channel_id=1, source_target_pairs={{0,2},{1,3},{2,0},{3,1},{4,6},{5,7},{6,4},{7,5},{8,10},{9,11},{10,... | collective-permute-start | bytes 196616 | tf_op jit(solution)/shard_map/ppermute | solution.py:69
  18.7 1.0 %merge_0.1 = (f32[2,256,256]{2,1,0:T(8,128)S(1)}, f32[2,256,256]{2,1,0:T(8,128)S(1)}, bf16[2,256,256]{2,1,0:T(8,128)(2,1)S(1)}, bf16[2,256,256]{2,1,0:T(8,128)(2...) custom-call(f32[256,256]{1,0:T(8,128)S(1)} %get-tuple-element.67.ref, ...), custom_call_target="tpu_custom_call" | custom-call | tf_op jit(solution)/shard_map/merge_0/pallas_call | solution.py:52
  19.7 1.6 %collective-permute-start.8 = (f32[2,128,128]{2,1,0:T(8,128)S(1)}, f32[2,128,128]{2,1,0:T(8,128)S(1)}, u32[]{:S(2)}, u32[]{:S(2)}) collective-permute-start(f32[2,128,128]{2,1,0:T(8,128)S(1)} %get-tuple-element.83), channel_id=1, source_target_pairs={{0,8},{4,12},{8,0},{12,4},{16,24},{20,28},{24,16},{28,20},{1,9},{5... | collective-permute-start | bytes 393224 | tf_op jit(solution)/shard_map/ppermute | solution.py:69
  22.7 1.6 %collective-permute-start.6 = (f32[128,256]{1,0:T(8,128)S(1)}, f32[128,256]{1,0:T(8,128)S(1)}, u32[]{:S(2)}, u32[]{:S(2)}) collective-permute-start(f32[128,256]{1,0:T(8,128)S(1)} %get-tuple-element.77.refs_1_), channel_id=1, source_target_pairs={{0,4},{4,0},{8,12},{12,8},{16,20},{20,16},{24,28},{28,24},{1,5},{5... | collective-permute-start | bytes 393224 | tf_op jit(solution)/shard_map/ppermute | solution.py:69
  24.2 1.9 %collective-permute-done.8.refs_7_.refs_1_ = f32[2,128,128]{2,1,0:T(8,128)S(1)} collective-permute-done((f32[2,128,128]{2,1,0:T(8,128)S(1)}, f32[2,128,128]{2,1,0:T(8,128)S(1)}, u32[]{:S(2)}, u32[]{:S(2)}) %collective-permute-start.8) | collective-permute-done | bytes 131104 | tf_op jit(solution)/shard_map/ppermute | solution.py:69
  26.1 1.7 %collective-permute-done.9.refs_8_.refs_2_ = f32[2,128,128]{2,1,0:T(8,128)S(1)} collective-permute-done((f32[2,128,128]{2,1,0:T(8,128)S(1)}, f32[2,128,128]{2,1,0:T(8,128)S(1)}, u32[]{:S(2)}, u32[]{:S(2)}) %collective-permute-start.9) | collective-permute-done | bytes 131104 | tf_op jit(solution)/shard_map/ppermute | solution.py:69
  28.8 1.6 %collective-permute-start.10 = (f32[128,256]{1,0:T(8,128)S(1)}, f32[128,256]{1,0:T(8,128)S(1)}, u32[]{:S(2)}, u32[]{:S(2)}) collective-permute-start(f32[128,256]{1,0:T(8,128)S(1)} %get-tuple-element.86.refs_1_), channel_id=1, source_target_pairs={{0,8},{4,12},{8,0},{12,4},{16,24},{20,28},{24,16},{28,20},{1,9},{5... | collective-permute-start | bytes 393224 | tf_op jit(solution)/shard_map/ppermute | solution.py:69
  30.4 1.5 %merge_1.1 = (f32[8,128]{1,0:T(8,128)}, bf16[2,256,256]{2,1,0:T(8,128)(2,1)S(1)}, bf16[2,256,256]{2,1,0:T(8,128)(2,1)S(1)}, bf16[2,256,256]{2,1,0:T(8,128)(2,1)S...) custom-call(f32[2,256,256]{2,1,0:T(8,128)S(1)} %get-tuple-element.87.refs_0_, ...), custom_call_target="tpu_custom_call" | custom-call | tf_op jit(solution)/shard_map/merge_1/pallas_call | solution.py:52
  31.9 0.7 %collective-permute-start.14 = (f32[3,128,128]{2,1,0:T(8,128)S(1)}, f32[3,128,128]{2,1,0:T(8,128)S(1)}, u32[]{:S(2)}, u32[]{:S(2)}) collective-permute-start(f32[3,128,128]{2,1,0:T(8,128)S(1)} %get-tuple-element.98), channel_id=1, source_target_pairs={{8,16},{12,20},{16,8},{20,12},{9,17},{13,21},{17,9},{21,13},{10,18... | collective-permute-start | bytes 589832 | tf_op jit(solution)/shard_map/ppermute | solution.py:595
  32.6 1.7 %collective-permute-done.10.refs_2_ = f32[128,256]{1,0:T(8,128)S(1)} collective-permute-done((f32[128,256]{1,0:T(8,128)S(1)}, f32[128,256]{1,0:T(8,128)S(1)}, u32[]{:S(2)}, u32[]{:S(2)}) %collective-permute-start.10) | collective-permute-done | bytes 131104 | tf_op jit(solution)/shard_map/ppermute | solution.py:69
  34.8 0.7 %collective-permute-start.13 = (f32[64,256]{1,0:T(8,128)S(1)}, f32[64,256]{1,0:T(8,128)S(1)}, u32[]{:S(2)}, u32[]{:S(2)}) collective-permute-start(f32[64,256]{1,0:T(8,128)S(1)} %get-tuple-element.97), channel_id=1, source_target_pairs={{8,16},{12,20},{16,8},{20,12},{9,17},{13,21},{17,9},{21,13},{10,18... | collective-permute-start | bytes 196616 | tf_op jit(solution)/shard_map/ppermute | solution.py:596
  35.7 8.2 %collective-permute-start.15 = (f32[64,256]{1,0:T(8,128)S(1)}, f32[64,256]{1,0:T(8,128)S(1)}, u32[]{:S(2)}, u32[]{:S(2)}) collective-permute-start(f32[64,256]{1,0:T(8,128)S(1)} %turn.1.refs_1_), channel_id=1, source_target_pairs={{0,8},{4,12},{8,0},{12,4},{16,24},{20,28},{24,16},{28,20},{1,9},{5... | collective-permute-start | bytes 196616 | tf_op jit(solution)/shard_map/ppermute | solution.py:69
  43.9 2.2 %collective-permute-done.15.refs_2_ = f32[64,256]{1,0:T(8,128)S(1)} collective-permute-done((f32[64,256]{1,0:T(8,128)S(1)}, f32[64,256]{1,0:T(8,128)S(1)}, u32[]{:S(2)}, u32[]{:S(2)}) %collective-permute-start.15) | collective-permute-done | bytes 65568 | tf_op jit(solution)/shard_map/ppermute | solution.py:69
  46.5 1.4 %collective-permute-start.17 = (f32[64,256]{1,0:T(8,128)S(1)}, f32[64,256]{1,0:T(8,128)S(1)}, u32[]{:S(2)}, u32[]{:S(2)}) collective-permute-start(f32[64,256]{1,0:T(8,128)S(1)} %leave.1.refs_10_), channel_id=1, source_target_pairs={{0,2},{1,3},{2,0},{3,1},{4,6},{5,7},{6,4},{7,5},{8,10},{9,11},{10,... | collective-permute-start | bytes 196616 | tf_op jit(solution)/shard_map/ppermute | solution.py:69
  47.9 2.9 %collective-permute-done.17.refs_12_ = f32[64,256]{1,0:T(8,128)S(1)} collective-permute-done((f32[64,256]{1,0:T(8,128)S(1)}, f32[64,256]{1,0:T(8,128)S(1)}, u32[]{:S(2)}, u32[]{:S(2)}) %collective-permute-start.17) | collective-permute-done | bytes 65568 | tf_op jit(solution)/shard_map/ppermute | solution.py:69
  50.9 1.2 %collective-permute-done.18.refs_13_ = f32[64,256]{1,0:T(8,128)S(1)} collective-permute-done((f32[64,256]{1,0:T(8,128)S(1)}, f32[64,256]{1,0:T(8,128)S(1)}, u32[]{:S(2)}, u32[]{:S(2)}) %collective-permute-start.18) | collective-permute-done | bytes 65568 | tf_op jit(solution)/shard_map/ppermute | solution.py:69
  52.1 4.5 %local_backward.1 = (f32[8,256,256]{2,1,0:T(8,128)}, f32[64,256]{1,0:T(8,128)}) custom-call(s32[8]{0:T(128)} %refs_0_.5, f32[8,256,256]{2,1,0:T(8,128)S(1)} %get-tuple-element.68.refs_1_, bf16[4,256,256]{2,1,0:T(8,128)(2,1)S(1)} %get-tuple-element.58.refs_4_.refs_2_, bf16[4,256,256]{2,1,0:T(8,128)(2,1)S(1)} %get-tuple-element.59.refs_5_.refs_3_, ...), custom_call_target="tpu_custom_call" | custom-call | tf_op jit(solution)/shard_map/local_backward/pallas_call | solution.py:279
  (28 shorter events, 5.2 us)
Async XLA Ops:
  1.5 7.3 %collective-permute-start.1 = (f32[2,64,256]{2,1,0:T(8,128)S(1)}, f32[2,64,256]{2,1,0:T(8,128)S(1)}, u32[]{:S(2)}, u32[]{:S(2)}) collective-permute-start(f32[2,64,256]{2,1,0:T(8,128)S(1)} %stack.1.refs_5_.refs_0_), channel_id=1, source_target_pairs={{0,2},{1,3},{2,0},{3,1},{4,6},{5,7},{6,4},{7,5},{8,10},{9,11},{10,... | collective-permute-start | bytes 393224 | tf_op jit(solution)/shard_map/ppermute | solution.py:69
  4.5 5.5 %collective-permute-start = (f32[2,64,256]{2,1,0:T(8,128)S(1)}, f32[2,64,256]{2,1,0:T(8,128)S(1)}, u32[]{:S(2)}, u32[]{:S(2)}) collective-permute-start(f32[2,64,256]{2,1,0:T(8,128)S(1)} %stack.1.refs_5_.refs_0_), channel_id=1, source_target_pairs={{0,1},{1,0},{2,3},{3,2},{4,5},{5,4},{6,7},{7,6},{8,9},{9,8},{10,11... | collective-permute-start | bytes 393224 | tf_op jit(solution)/shard_map/ppermute | solution.py:69
  8.8 1.6 %collective-permute-start.2 = (f32[2,64,256]{2,1,0:T(8,128)S(1)}, f32[2,64,256]{2,1,0:T(8,128)S(1)}, u32[]{:S(2)}, u32[]{:S(2)}) collective-permute-start(f32[2,64,256]{2,1,0:T(8,128)S(1)} %collective-permute-done.1.refs_2_), channel_id=1, source_target_pairs={{0,1},{1,0},{2,3},{3,2},{4,5},{5,4},{6,7},{7,6},{8,9},{9,8},{10,11... | collective-permute-start | bytes 393224 | tf_op jit(solution)/shard_map/ppermute | solution.py:69
  10.7 5.8 %collective-permute-start.3 = (f32[1,128,256]{2,1,0:T(8,128)S(1)}, f32[1,128,256]{2,1,0:T(8,128)S(1)}, u32[]{:S(2)}, u32[]{:S(2)}) collective-permute-start(f32[1,128,256]{2,1,0:T(8,128)S(1)} %get-tuple-element.70), channel_id=1, source_target_pairs={{0,4},{4,0},{8,12},{12,8},{16,20},{20,16},{24,28},{28,24},{1,5},{5... | collective-permute-start | bytes 393224 | tf_op jit(solution)/shard_map/ppermute | solution.py:69
  16.5 1.3 %collective-permute-start.4 = (f32[128,256]{1,0:T(8,128)S(1)}, f32[128,256]{1,0:T(8,128)S(1)}, u32[]{:S(2)}, u32[]{:S(2)}) collective-permute-start(f32[128,256]{1,0:T(8,128)S(1)} %get-tuple-element.72), channel_id=1, source_target_pairs={{0,1},{1,0},{2,3},{3,2},{4,5},{5,4},{6,7},{7,6},{8,9},{9,8},{10,11... | collective-permute-start | bytes 393224 | tf_op jit(solution)/shard_map/ppermute | solution.py:69
  16.5 2.1 %collective-permute-start.7 = (f32[1,128,256]{2,1,0:T(8,128)S(1)}, f32[1,128,256]{2,1,0:T(8,128)S(1)}, u32[]{:S(2)}, u32[]{:S(2)}) collective-permute-start(f32[1,128,256]{2,1,0:T(8,128)S(1)} %collective-permute-done.3.refs_1_), channel_id=1, source_target_pairs={{0,1},{1,0},{2,3},{3,2},{4,5},{5,4},{6,7},{7,6},{8,9},{9,8},{10,11... | collective-permute-start | bytes 393224 | tf_op jit(solution)/shard_map/ppermute | solution.py:69
  17.9 4.3 %collective-permute-start.5 = (f32[64,256]{1,0:T(8,128)S(1)}, f32[64,256]{1,0:T(8,128)S(1)}, u32[]{:S(2)}, u32[]{:S(2)}) collective-permute-start(f32[64,256]{1,0:T(8,128)S(1)} %get-tuple-element.74.refs_3_), channel_id=1, source_target_pairs={{0,2},{1,3},{2,0},{3,1},{4,6},{5,7},{6,4},{7,5},{8,10},{9,11},{10,... | collective-permute-start | bytes 196616 | tf_op jit(solution)/shard_map/ppermute | solution.py:69
  19.7 6.4 %collective-permute-start.8 = (f32[2,128,128]{2,1,0:T(8,128)S(1)}, f32[2,128,128]{2,1,0:T(8,128)S(1)}, u32[]{:S(2)}, u32[]{:S(2)}) collective-permute-start(f32[2,128,128]{2,1,0:T(8,128)S(1)} %get-tuple-element.83), channel_id=1, source_target_pairs={{0,8},{4,12},{8,0},{12,4},{16,24},{20,28},{24,16},{28,20},{1,9},{5... | collective-permute-start | bytes 393224 | tf_op jit(solution)/shard_map/ppermute | solution.py:69
  21.3 6.5 %collective-permute-start.9 = (f32[2,128,128]{2,1,0:T(8,128)S(1)}, f32[2,128,128]{2,1,0:T(8,128)S(1)}, u32[]{:S(2)}, u32[]{:S(2)}) collective-permute-start(f32[2,128,128]{2,1,0:T(8,128)S(1)} %get-tuple-element.84), channel_id=1, source_target_pairs={{0,8},{4,12},{8,0},{12,4},{16,24},{20,28},{24,16},{28,20},{1,9},{5... | collective-permute-start | bytes 393224 | tf_op jit(solution)/shard_map/ppermute | solution.py:69
  22.7 5.2 %collective-permute-start.6 = (f32[128,256]{1,0:T(8,128)S(1)}, f32[128,256]{1,0:T(8,128)S(1)}, u32[]{:S(2)}, u32[]{:S(2)}) collective-permute-start(f32[128,256]{1,0:T(8,128)S(1)} %get-tuple-element.77.refs_1_), channel_id=1, source_target_pairs={{0,4},{4,0},{8,12},{12,8},{16,20},{20,16},{24,28},{28,24},{1,5},{5... | collective-permute-start | bytes 393224 | tf_op jit(solution)/shard_map/ppermute | solution.py:69
  28.3 2.2 %collective-permute-start.11 = (f32[2,128,128]{2,1,0:T(8,128)S(1)}, f32[2,128,128]{2,1,0:T(8,128)S(1)}, u32[]{:S(2)}, u32[]{:S(2)}) collective-permute-start(f32[2,128,128]{2,1,0:T(8,128)S(1)} %collective-permute-done.8.refs_7_.refs_1_), channel_id=1, source_target_pairs={{0,1},{1,0},{2,3},{3,2},{4,5},{5,4},{6,7},{7,6},{8,9},{9,8},{10,11... | collective-permute-start | bytes 393224 | tf_op jit(solution)/shard_map/ppermute | solution.py:69
  28.3 2.1 %collective-permute-start.12 = (f32[2,128,128]{2,1,0:T(8,128)S(1)}, f32[2,128,128]{2,1,0:T(8,128)S(1)}, u32[]{:S(2)}, u32[]{:S(2)}) collective-permute-start(f32[2,128,128]{2,1,0:T(8,128)S(1)} %collective-permute-done.9.refs_8_.refs_2_), channel_id=1, source_target_pairs={{0,1},{1,0},{2,3},{3,2},{4,5},{5,4},{6,7},{7,6},{8,9},{9,8},{10,11... | collective-permute-start | bytes 393224 | tf_op jit(solution)/shard_map/ppermute | solution.py:69
  28.8 5.5 %collective-permute-start.10 = (f32[128,256]{1,0:T(8,128)S(1)}, f32[128,256]{1,0:T(8,128)S(1)}, u32[]{:S(2)}, u32[]{:S(2)}) collective-permute-start(f32[128,256]{1,0:T(8,128)S(1)} %get-tuple-element.86.refs_1_), channel_id=1, source_target_pairs={{0,8},{4,12},{8,0},{12,4},{16,24},{20,28},{24,16},{28,20},{1,9},{5... | collective-permute-start | bytes 393224 | tf_op jit(solution)/shard_map/ppermute | solution.py:69
  31.9 3.5 %collective-permute-start.14 = (f32[3,128,128]{2,1,0:T(8,128)S(1)}, f32[3,128,128]{2,1,0:T(8,128)S(1)}, u32[]{:S(2)}, u32[]{:S(2)}) collective-permute-start(f32[3,128,128]{2,1,0:T(8,128)S(1)} %get-tuple-element.98), channel_id=1, source_target_pairs={{8,16},{12,20},{16,8},{20,12},{9,17},{13,21},{17,9},{21,13},{10,18... | collective-permute-start | bytes 589832 | tf_op jit(solution)/shard_map/ppermute | solution.py:595
  34.8 0.7 %collective-permute-start.13 = (f32[64,256]{1,0:T(8,128)S(1)}, f32[64,256]{1,0:T(8,128)S(1)}, u32[]{:S(2)}, u32[]{:S(2)}) collective-permute-start(f32[64,256]{1,0:T(8,128)S(1)} %get-tuple-element.97), channel_id=1, source_target_pairs={{8,16},{12,20},{16,8},{20,12},{9,17},{13,21},{17,9},{21,13},{10,18... | collective-permute-start | bytes 196616 | tf_op jit(solution)/shard_map/ppermute | solution.py:596
  35.7 10.4 %collective-permute-start.15 = (f32[64,256]{1,0:T(8,128)S(1)}, f32[64,256]{1,0:T(8,128)S(1)}, u32[]{:S(2)}, u32[]{:S(2)}) collective-permute-start(f32[64,256]{1,0:T(8,128)S(1)} %turn.1.refs_1_), channel_id=1, source_target_pairs={{0,8},{4,12},{8,0},{12,4},{16,24},{20,28},{24,16},{28,20},{1,9},{5... | collective-permute-start | bytes 196616 | tf_op jit(solution)/shard_map/ppermute | solution.py:69
  46.5 4.3 %collective-permute-start.17 = (f32[64,256]{1,0:T(8,128)S(1)}, f32[64,256]{1,0:T(8,128)S(1)}, u32[]{:S(2)}, u32[]{:S(2)}) collective-permute-start(f32[64,256]{1,0:T(8,128)S(1)} %leave.1.refs_10_), channel_id=1, source_target_pairs={{0,2},{1,3},{2,0},{3,1},{4,6},{5,7},{6,4},{7,5},{8,10},{9,11},{10,... | collective-permute-start | bytes 196616 | tf_op jit(solution)/shard_map/ppermute | solution.py:69
  47.9 2.9 %collective-permute-start.16 = (f32[64,256]{1,0:T(8,128)S(1)}, f32[64,256]{1,0:T(8,128)S(1)}, u32[]{:S(2)}, u32[]{:S(2)}) collective-permute-start(f32[64,256]{1,0:T(8,128)S(1)} %leave.1.refs_10_), channel_id=1, source_target_pairs={{0,1},{1,0},{2,3},{3,2},{4,5},{5,4},{6,7},{7,6},{8,9},{9,8},{10,11... | collective-permute-start | bytes 196616 | tf_op jit(solution)/shard_map/ppermute | solution.py:69
  50.9 1.3 %collective-permute-start.18 = (f32[64,256]{1,0:T(8,128)S(1)}, f32[64,256]{1,0:T(8,128)S(1)}, u32[]{:S(2)}, u32[]{:S(2)}) collective-permute-start(f32[64,256]{1,0:T(8,128)S(1)} %collective-permute-done.17.refs_12_), channel_id=1, source_target_pairs={{0,1},{1,0},{2,3},{3,2},{4,5},{5,4},{6,7},{7,6},{8,9},{9,8},{10,11... | collective-permute-start | bytes 196616 | tf_op jit(solution)/shard_map/ppermute | solution.py:69

commit v9 on v8

--- a/solution.py
+++ b/solution.py
@@ -12,7 +12,6 @@
 TN = (((0,), (0,)), ((), ()))
 VMEM_BYTES = 24 << 20
 HALVES = 2
-SENDS = 2
 
 
 def split(x):
@@ -371,6 +370,12 @@
     return joined(blocks[0], blocks[1], blocks[1].T, blocks[2])
 
 
+def send_maps(parts, k, t):
+    for i, block in enumerate(k_blocks(k)):
+        parts[0][i] = block
+    send_blocks(parts[1:], quarters(t))
+
+
 def first_merge_kernel(*refs):
     own, mine, pairs, _, kept, mixed, halves, curve_u, total_u, total_l, *parts = refs
     upper = bit_of("leaf", 0) == 1
@@ -388,7 +393,7 @@
     t = dot3(up_s, low_s, NN)
     k = dot3(low_s, low_s, TN) + dot3(low_s, split(x), TN)
     kept[0], kept[1] = k, t
-    send_blocks(parts, k_blocks(k) + quarters(t))
+    send_maps(parts, k, t)
     size = low.shape[0]
     row = lax.broadcasted_iota(jnp.int32, (size, size), 0)
     col = lax.broadcasted_iota(jnp.int32, (size, size), 1)
@@ -399,13 +404,11 @@
 
 
 def merge_kernel(bit, last, *refs):
-    own, refs = refs[0], refs[1:]
-    mine, pairs, mixed = refs[:SENDS], refs[SENDS : 2 * SENDS], refs[2 * SENDS]
+    own, other, mine, pairs, mixed = refs[:5]
+    kept, mixed_n, halves, curve_u, total_u, total_l, *parts = refs[5:]
     upper = bit_of("leaf", bit) == 1
-    kept, mixed_n, halves, curve_u, total_u, total_l, *parts = refs[1 + 2 * SENDS :]
     own_k, own_t = own[0], own[1]
-    blocks = came_blocks(mine, pairs, 7)
-    other_k, other_t = k_of(blocks), joined(*blocks[3:])
+    other_k, other_t = k_of(other), joined(*came_blocks([mine], [pairs], 4))
     low_s = split(jnp.where(upper, other_t, own_t))
     up_s = split(jnp.where(upper, own_t, other_t))
     k_low = jnp.where(upper, other_k, own_k)
@@ -414,7 +417,6 @@
         ref[0], ref[1] = value
     x = dot3(k_up_s, low_s, NN)
     x_s = split(x)
-    k = k_low + dot3(low_s, x_s, TN)
     a, e = mixed[0], mixed[1]
     keep_split(halves, jnp.where(upper, a.T, e))
     a_s, e_s = split(a), split(e)
@@ -422,22 +424,28 @@
     e_n = jnp.where(upper, e, dot3(up_s, e_s, NN))
     if last:
         kept[...] = jnp.zeros_like(kept)
-        for i, block in enumerate(k_blocks(k)):
-            parts[0][i] = block
         keep_split(mixed_n, jnp.where(bit_of("leaf", bit + 1) == 1, a_n.T, e_n))
     else:
+        k = k_low + dot3(low_s, x_s, TN)
         t = dot3(up_s, low_s, NN)
         kept[0], kept[1] = k, t
-        send_blocks(parts, k_blocks(k) + quarters(t))
+        send_maps(parts, k, t)
         mixed_n[0], mixed_n[1] = a_n, e_n
+
+
+def boundary_kernel(own, other, blocks):
+    k, t = own[0], split(own[1])
+    x = dot3(split(k_of(other)), t, NN)
+    for i, block in enumerate(k_blocks(k + dot3(t, split(x), TN))):
+        blocks[i] = block
 
 
 def maps(size, last):
     both, whole = ((2, size, size), BF16), ((2, size, size), F32)
     half = size // 2
     if last:
-        return [((8, 128), F32)] + [both] * 5 + [((3, half, half), F32)]
-    sends = [((4 // SENDS, half, half), F32)] * SENDS
+        return [((8, 128), F32)] + [both] * 5
+    sends = [((i, half, half), F32) for i in (3, 2)]
     return [whole, whole, both, both, both, both] + sends
 
 
@@ -567,32 +575,39 @@
         [((chunk, size), F32), ((2 * chunk, size), F32)],
     )
     share = ((chunk, size), F32)
+    middle = leaves // 2
+    boundary = [(middle - 2 + i, middle + i) for i in range(2)]
+    boundary += [(j, i) for i, j in boundary]
     for bit in range(rounds - 1):
         last = bit == rounds - 2
         received = exchange(message, "leaf", bit)
-        mine = [] if last else [exchange(part, "leaf", bit + 1) for part in parts]
+        ahead = []
+        if not last:
+            other, mine = [exchange(part, "leaf", bit + 1) for part in parts]
+            ahead = [other]
+        if bit == rounds - 3:
+            ahead = (blocks,) = call(
+                boundary_kernel, "boundary", [(V, kept), (V, other)], [(other.shape, F32)]
+            )
+            blocks = lax.ppermute(blocks, "leaf", boundary)
         sol, *message = call(
-            lambda *refs, bit=bit, last=last: step_kernel(bit, last, len(mine), *refs),
+            lambda *refs, bit=bit, last=last: step_kernel(bit, last, len(ahead), *refs),
             f"step_{bit}",
-            [(V, a) for a in (sol, message, received, *tools)] + [(pl.ANY, a) for a in mine],
+            [(V, a) for a in (sol, message, received, *tools)] + [(pl.ANY, a) for a in ahead],
             [share] + ([share, share] if last else [((2 * chunk, size), F32)]),
         )
         if not last:
             (message,) = message
             mine, _ = lax.optimization_barrier((mine, sol))
-            pairs = [exchange(m, "front", 0) for m in mine]
+            pairs = exchange(mine, "front", 0)
             last = bit == rounds - 3
             kept, mixed, *tools = call(
                 lambda *refs, bit=bit, last=last: merge_kernel(bit + 1, last, *refs),
                 f"merge_{bit + 1}",
-                [(V, a) for a in (kept, *mine, *pairs, mixed)],
+                [(V, a) for a in (kept, other, mine, pairs, mixed)],
                 maps(size, last),
             )
             tools, parts = tools[:4], tools[4:]
-    middle = leaves // 2
-    boundary = [(middle - 2 + i, middle + i) for i in range(2)]
-    boundary += [(j, i) for i, j in boundary]
-    blocks = lax.ppermute(parts[0], "leaf", boundary)
     came = lax.ppermute(message[0], "leaf", boundary)
     (given,) = call(
         lambda *refs: turn_kernel(rounds - 1, *refs),

time: 56.9 us -> 57.2 us (level)
    pallas_call x13 -> x14, Pallas kernels: 14.6 us -> 15.2 us  [call(): pl.pallas_call(kernel, name=name, in_specs=specs, out_specs=tuple((pl.Blo...]
    ppermute x17 -> x16, waiting for transfers between devices: 13.5 us -> 13.2 us  [swap(): return lax.ppermute(x, axis, [(i, i ^ mask) for i in range(n)])]
    ppermute x17 -> x16, starting transfers between devices: 21.9 us -> 21.7 us  [swap(): return lax.ppermute(x, axis, [(i, i ^ mask) for i in range(n)])]
  transfers between devices with their start and end apart: 19 -> 18, of which waited for: 10 -> 10; matrix products, arithmetic and copies ran while one was open for 0% -> 0% of each run, Pallas kernels for 22% -> 23%
where the time goes in v9:
time: 57.2 us; the launch traced here: 57 us
  starting transfers between devices  23.2 us (41%)
  Pallas kernels  19.7 us (34%)
  waiting for transfers between devices  13.2 us (23%)
  between operations  0.96 us (2%)
    ppermute x16, starting transfers between devices, swap(): return lax.ppermute(x, axis, [(i, i ^ mask) for i in range(n)])  21.7 us
    pallas_call x14, Pallas kernels, call(): pl.pallas_call(kernel, name=name, in_specs=specs, out_specs=tuple((pl.Blo...  15.2 us
    ppermute x16, waiting for transfers between devices, swap(): return lax.ppermute(x, axis, [(i, i ^ mask) for i in range(n)])  13.2 us
    pallas_call x1, Pallas kernels, local_backward(): pl.pallas_call(lambda *refs: backward_kernel(nodes, fronts, *refs), name=...  4.54 us
  transfers between devices with their start and end apart: 18, of which 10 were waited for; matrix products, arithmetic and copies ran while one was open for 0% of the time, Pallas kernels for 23%

profile of v9, /device:TPU:0, one launch (start us, length us, event | category | flops | bytes accessed | tf_op | source)
XLA Modules:
  0.0 57.0 jit_solution(5282450217470937731)
XLA Ops:
  0.6 0.9 %stack.1.refs_5_.refs_0_ = f32[2,64,256]{2,1,0:T(8,128)S(1)} custom-call(f32[64,256]{1,0:T(8,128)} %first.1, f32[64,256]{1,0:T(8,128)} %second.1), custom_call_target="tpu_custom_call" | custom-call | tf_op jit(solution)/shard_map/stack/pallas_call | solution.py:51
  1.5 3.0 %collective-permute-start.1 = (f32[2,64,256]{2,1,0:T(8,128)S(1)}, f32[2,64,256]{2,1,0:T(8,128)S(1)}, u32[]{:S(2)}, u32[]{:S(2)}) collective-permute-start(f32[2,64,256]{2,1,0:T(8,128)S(1)} %stack.1.refs_5_.refs_0_), channel_id=1, source_target_pairs={{0,2},{1,3},{2,0},{3,1},{4,6},{5,7},{6,4},{7,5},{8,10},{9,11},{10,... | collective-permute-start | bytes 393224 | tf_op jit(solution)/shard_map/ppermute | solution.py:68
  4.5 4.3 %prepare_first.1 = (f32[2,4,128,256]{3,2,1,0:T(8,128)S(1)}, bf16[4,256,256]{2,1,0:T(8,128)(2,1)S(1)}, bf16[4,256,256]{2,1,0:T(8,128)(2,1)S(1)}, bf16[4,256,256]{...) custom-call(s32[8,256]{1,0:T(8,128)} %refs_0_.3, ...), custom_call_target="tpu_custom_call" | custom-call | tf_op jit(solution)/shard_map/prepare_first/pallas_call | solution.py:51
  10.7 1.6 %collective-permute-start.3 = (f32[1,128,256]{2,1,0:T(8,128)S(1)}, f32[1,128,256]{2,1,0:T(8,128)S(1)}, u32[]{:S(2)}, u32[]{:S(2)}) collective-permute-start(f32[1,128,256]{2,1,0:T(8,128)S(1)} %get-tuple-element.68), channel_id=1, source_target_pairs={{0,4},{4,0},{8,12},{12,8},{16,20},{20,16},{24,28},{28,24},{1,5},{5... | collective-permute-start | bytes 393224 | tf_op jit(solution)/shard_map/ppermute | solution.py:68
  12.3 4.1 %local_forward.1 = (f32[8,256,256]{2,1,0:T(8,128)S(1)}, f32[128,256]{1,0:T(8,128)S(1)}, f32[128,256]{1,0:T(8,128)S(1)}) custom-call(s32[8]{0:T(128)} %refs_0_.5, f32[2,4,128,256]{3,2,1,0:T(8,128)S(1)} %get-tuple-element.49.refs_4_.refs_1_, f32[2,4,128,256]{3,2,1,0:T(8,128)S(1)} %get-tuple-element.54.refs_4_.refs_2_, ...), custom_call_target="tpu_custom_call" | custom-call | tf_op jit(solution)/shard_map/local_forward/pallas_call | solution.py:51
  17.0 0.8 %collective-permute-done.4.refs_1_ = f32[128,256]{1,0:T(8,128)S(1)} collective-permute-done((f32[128,256]{1,0:T(8,128)S(1)}, f32[128,256]{1,0:T(8,128)S(1)}, u32[]{:S(2)}, u32[]{:S(2)}) %collective-permute-start.4) | collective-permute-done | bytes 131104 | tf_op jit(solution)/shard_map/ppermute | solution.py:68
  17.9 0.7 %collective-permute-start.5 = (f32[64,256]{1,0:T(8,128)S(1)}, f32[64,256]{1,0:T(8,128)S(1)}, u32[]{:S(2)}, u32[]{:S(2)}) collective-permute-start(f32[64,256]{1,0:T(8,128)S(1)} %get-tuple-element.72.refs_3_), channel_id=1, source_target_pairs={{0,2},{1,3},{2,0},{3,1},{4,6},{5,7},{6,4},{7,5},{8,10},{9,11},{10,... | collective-permute-start | bytes 196616 | tf_op jit(solution)/shard_map/ppermute | solution.py:68
  18.7 1.0 %merge_0.1 = (f32[2,256,256]{2,1,0:T(8,128)S(1)}, f32[2,256,256]{2,1,0:T(8,128)S(1)}, bf16[2,256,256]{2,1,0:T(8,128)(2,1)S(1)}, bf16[2,256,256]{2,1,0:T(8,128)(2...) custom-call(f32[256,256]{1,0:T(8,128)S(1)} %get-tuple-element.65.ref, ...), custom_call_target="tpu_custom_call" | custom-call | tf_op jit(solution)/shard_map/merge_0/pallas_call | solution.py:51
  19.7 1.6 %collective-permute-start.8 = (f32[3,128,128]{2,1,0:T(8,128)S(1)}, f32[3,128,128]{2,1,0:T(8,128)S(1)}, u32[]{:S(2)}, u32[]{:S(2)}) collective-permute-start(f32[3,128,128]{2,1,0:T(8,128)S(1)} %get-tuple-element.82), channel_id=1, source_target_pairs={{0,8},{4,12},{8,0},{12,4},{16,24},{20,28},{24,16},{28,20},{1,9},{5... | collective-permute-start | bytes 589832 | tf_op jit(solution)/shard_map/ppermute | solution.py:68
  21.3 0.9 %collective-permute-done.5.other = f32[64,256]{1,0:T(8,128)S(1)} collective-permute-done((f32[64,256]{1,0:T(8,128)S(1)}, f32[64,256]{1,0:T(8,128)S(1)}, u32[]{:S(2)}, u32[]{:S(2)}) %collective-permute-start.5) | collective-permute-done | bytes 65568 | tf_op jit(solution)/shard_map/ppermute | solution.py:68
  22.7 1.6 %collective-permute-start.6 = (f32[128,256]{1,0:T(8,128)S(1)}, f32[128,256]{1,0:T(8,128)S(1)}, u32[]{:S(2)}, u32[]{:S(2)}) collective-permute-start(f32[128,256]{1,0:T(8,128)S(1)} %get-tuple-element.75.refs_1_), channel_id=1, source_target_pairs={{0,4},{4,0},{8,12},{12,8},{16,20},{20,16},{24,28},{28,24},{1,5},{5... | collective-permute-start | bytes 393224 | tf_op jit(solution)/shard_map/ppermute | solution.py:68
  24.2 1.6 %collective-permute-start.10 = (f32[2,128,128]{2,1,0:T(8,128)S(1)}, f32[2,128,128]{2,1,0:T(8,128)S(1)}, u32[]{:S(2)}, u32[]{:S(2)}) collective-permute-start(f32[2,128,128]{2,1,0:T(8,128)S(1)} %get-tuple-element.85), channel_id=1, source_target_pairs={{0,8},{4,12},{8,0},{12,4},{16,24},{20,28},{24,16},{28,20},{1,9},{5... | collective-permute-start | bytes 393224 | tf_op jit(solution)/shard_map/ppermute | solution.py:68
  25.8 1.4 %collective-permute-done.8.other.refs_1_ = f32[3,128,128]{2,1,0:T(8,128)S(1)} collective-permute-done((f32[3,128,128]{2,1,0:T(8,128)S(1)}, f32[3,128,128]{2,1,0:T(8,128)S(1)}, u32[]{:S(2)}, u32[]{:S(2)}) %collective-permute-start.8) | collective-permute-done | bytes 196640 | tf_op jit(solution)/shard_map/ppermute | solution.py:68
  28.4 0.9 %collective-permute-done.10.refs_2_ = f32[2,128,128]{2,1,0:T(8,128)S(1)} collective-permute-done((f32[2,128,128]{2,1,0:T(8,128)S(1)}, f32[2,128,128]{2,1,0:T(8,128)S(1)}, u32[]{:S(2)}, u32[]{:S(2)}) %collective-permute-start.10) | collective-permute-done | bytes 131104 | tf_op jit(solution)/shard_map/ppermute | solution.py:68
  29.2 1.6 %collective-permute-start.9 = (f32[128,256]{1,0:T(8,128)S(1)}, f32[128,256]{1,0:T(8,128)S(1)}, u32[]{:S(2)}, u32[]{:S(2)}) collective-permute-start(f32[128,256]{1,0:T(8,128)S(1)} %get-tuple-element.84.refs_1_), channel_id=1, source_target_pairs={{0,8},{4,12},{8,0},{12,4},{16,24},{20,28},{24,16},{28,20},{1,9},{5... | collective-permute-start | bytes 393224 | tf_op jit(solution)/shard_map/ppermute | solution.py:68
  31.5 1.3 %merge_1.1 = (f32[8,128]{1,0:T(8,128)}, bf16[2,256,256]{2,1,0:T(8,128)(2,1)S(1)}, bf16[2,256,256]{2,1,0:T(8,128)(2,1)S(1)}, bf16[2,256,256]{2,1,0:T(8,128)(2,1)S...) custom-call(f32[2,256,256]{2,1,0:T(8,128)S(1)} %get-tuple-element.81.own.refs_0_, ...), custom_call_target="tpu_custom_call" | custom-call | tf_op jit(solution)/shard_map/merge_1/pallas_call | solution.py:51
  32.8 2.3 %collective-permute-done.9.refs_2_ = f32[128,256]{1,0:T(8,128)S(1)} collective-permute-done((f32[128,256]{1,0:T(8,128)S(1)}, f32[128,256]{1,0:T(8,128)S(1)}, u32[]{:S(2)}, u32[]{:S(2)}) %collective-permute-start.9) | collective-permute-done | bytes 131104 | tf_op jit(solution)/shard_map/ppermute | solution.py:68
  35.6 0.8 %collective-permute-start.12 = (f32[64,256]{1,0:T(8,128)S(1)}, f32[64,256]{1,0:T(8,128)S(1)}, u32[]{:S(2)}, u32[]{:S(2)}) collective-permute-start(f32[64,256]{1,0:T(8,128)S(1)} %get-tuple-element.94), channel_id=1, source_target_pairs={{8,16},{12,20},{16,8},{20,12},{9,17},{13,21},{17,9},{21,13},{10,18... | collective-permute-start | bytes 196616 | tf_op jit(solution)/shard_map/ppermute | solution.py:611
  36.7 7.4 %collective-permute-start.14 = (f32[64,256]{1,0:T(8,128)S(1)}, f32[64,256]{1,0:T(8,128)S(1)}, u32[]{:S(2)}, u32[]{:S(2)}) collective-permute-start(f32[64,256]{1,0:T(8,128)S(1)} %turn.1.refs_1_), channel_id=1, source_target_pairs={{0,8},{4,12},{8,0},{12,4},{16,24},{20,28},{24,16},{28,20},{1,9},{5... | collective-permute-start | bytes 196616 | tf_op jit(solution)/shard_map/ppermute | solution.py:68
  44.1 2.2 %collective-permute-done.14.refs_2_ = f32[64,256]{1,0:T(8,128)S(1)} collective-permute-done((f32[64,256]{1,0:T(8,128)S(1)}, f32[64,256]{1,0:T(8,128)S(1)}, u32[]{:S(2)}, u32[]{:S(2)}) %collective-permute-start.14) | collective-permute-done | bytes 65568 | tf_op jit(solution)/shard_map/ppermute | solution.py:68
  46.7 1.4 %collective-permute-start.16 = (f32[64,256]{1,0:T(8,128)S(1)}, f32[64,256]{1,0:T(8,128)S(1)}, u32[]{:S(2)}, u32[]{:S(2)}) collective-permute-start(f32[64,256]{1,0:T(8,128)S(1)} %leave.1.refs_10_), channel_id=1, source_target_pairs={{0,2},{1,3},{2,0},{3,1},{4,6},{5,7},{6,4},{7,5},{8,10},{9,11},{10,... | collective-permute-start | bytes 196616 | tf_op jit(solution)/shard_map/ppermute | solution.py:68
  48.2 2.9 %collective-permute-done.16.refs_12_ = f32[64,256]{1,0:T(8,128)S(1)} collective-permute-done((f32[64,256]{1,0:T(8,128)S(1)}, f32[64,256]{1,0:T(8,128)S(1)}, u32[]{:S(2)}, u32[]{:S(2)}) %collective-permute-start.16) | collective-permute-done | bytes 65568 | tf_op jit(solution)/shard_map/ppermute | solution.py:68
  51.1 1.2 %collective-permute-done.17.refs_13_ = f32[64,256]{1,0:T(8,128)S(1)} collective-permute-done((f32[64,256]{1,0:T(8,128)S(1)}, f32[64,256]{1,0:T(8,128)S(1)}, u32[]{:S(2)}, u32[]{:S(2)}) %collective-permute-start.17) | collective-permute-done | bytes 65568 | tf_op jit(solution)/shard_map/ppermute | solution.py:68
  52.3 4.5 %local_backward.1 = (f32[8,256,256]{2,1,0:T(8,128)}, f32[64,256]{1,0:T(8,128)}) custom-call(s32[8]{0:T(128)} %refs_0_.5, f32[8,256,256]{2,1,0:T(8,128)S(1)} %get-tuple-element.66.refs_1_, bf16[4,256,256]{2,1,0:T(8,128)(2,1)S(1)} %get-tuple-element.56.refs_4_.refs_2_, bf16[4,256,256]{2,1,0:T(8,128)(2,1)S(1)} %get-tuple-element.57.refs_5_.refs_3_, ...), custom_call_target="tpu_custom_call" | custom-call | tf_op jit(solution)/shard_map/local_backward/pallas_call | solution.py:278
  (27 shorter events, 5.8 us)
Async XLA Ops:
  1.5 7.3 %collective-permute-start.1 = (f32[2,64,256]{2,1,0:T(8,128)S(1)}, f32[2,64,256]{2,1,0:T(8,128)S(1)}, u32[]{:S(2)}, u32[]{:S(2)}) collective-permute-start(f32[2,64,256]{2,1,0:T(8,128)S(1)} %stack.1.refs_5_.refs_0_), channel_id=1, source_target_pairs={{0,2},{1,3},{2,0},{3,1},{4,6},{5,7},{6,4},{7,5},{8,10},{9,11},{10,... | collective-permute-start | bytes 393224 | tf_op jit(solution)/shard_map/ppermute | solution.py:68
  4.5 5.5 %collective-permute-start = (f32[2,64,256]{2,1,0:T(8,128)S(1)}, f32[2,64,256]{2,1,0:T(8,128)S(1)}, u32[]{:S(2)}, u32[]{:S(2)}) collective-permute-start(f32[2,64,256]{2,1,0:T(8,128)S(1)} %stack.1.refs_5_.refs_0_), channel_id=1, source_target_pairs={{0,1},{1,0},{2,3},{3,2},{4,5},{5,4},{6,7},{7,6},{8,9},{9,8},{10,11... | collective-permute-start | bytes 393224 | tf_op jit(solution)/shard_map/ppermute | solution.py:68
  8.8 1.6 %collective-permute-start.2 = (f32[2,64,256]{2,1,0:T(8,128)S(1)}, f32[2,64,256]{2,1,0:T(8,128)S(1)}, u32[]{:S(2)}, u32[]{:S(2)}) collective-permute-start(f32[2,64,256]{2,1,0:T(8,128)S(1)} %collective-permute-done.1.refs_2_), channel_id=1, source_target_pairs={{0,1},{1,0},{2,3},{3,2},{4,5},{5,4},{6,7},{7,6},{8,9},{9,8},{10,11... | collective-permute-start | bytes 393224 | tf_op jit(solution)/shard_map/ppermute | solution.py:68
  10.7 5.8 %collective-permute-start.3 = (f32[1,128,256]{2,1,0:T(8,128)S(1)}, f32[1,128,256]{2,1,0:T(8,128)S(1)}, u32[]{:S(2)}, u32[]{:S(2)}) collective-permute-start(f32[1,128,256]{2,1,0:T(8,128)S(1)} %get-tuple-element.68), channel_id=1, source_target_pairs={{0,4},{4,0},{8,12},{12,8},{16,20},{20,16},{24,28},{28,24},{1,5},{5... | collective-permute-start | bytes 393224 | tf_op jit(solution)/shard_map/ppermute | solution.py:68
  16.5 1.3 %collective-permute-start.4 = (f32[128,256]{1,0:T(8,128)S(1)}, f32[128,256]{1,0:T(8,128)S(1)}, u32[]{:S(2)}, u32[]{:S(2)}) collective-permute-start(f32[128,256]{1,0:T(8,128)S(1)} %get-tuple-element.70), channel_id=1, source_target_pairs={{0,1},{1,0},{2,3},{3,2},{4,5},{5,4},{6,7},{7,6},{8,9},{9,8},{10,11... | collective-permute-start | bytes 393224 | tf_op jit(solution)/shard_map/ppermute | solution.py:68
  16.5 2.1 %collective-permute-start.7 = (f32[1,128,256]{2,1,0:T(8,128)S(1)}, f32[1,128,256]{2,1,0:T(8,128)S(1)}, u32[]{:S(2)}, u32[]{:S(2)}) collective-permute-start(f32[1,128,256]{2,1,0:T(8,128)S(1)} %collective-permute-done.3.refs_1_), channel_id=1, source_target_pairs={{0,1},{1,0},{2,3},{3,2},{4,5},{5,4},{6,7},{7,6},{8,9},{9,8},{10,11... | collective-permute-start | bytes 393224 | tf_op jit(solution)/shard_map/ppermute | solution.py:68
  17.9 4.3 %collective-permute-start.5 = (f32[64,256]{1,0:T(8,128)S(1)}, f32[64,256]{1,0:T(8,128)S(1)}, u32[]{:S(2)}, u32[]{:S(2)}) collective-permute-start(f32[64,256]{1,0:T(8,128)S(1)} %get-tuple-element.72.refs_3_), channel_id=1, source_target_pairs={{0,2},{1,3},{2,0},{3,1},{4,6},{5,7},{6,4},{7,5},{8,10},{9,11},{10,... | collective-permute-start | bytes 196616 | tf_op jit(solution)/shard_map/ppermute | solution.py:68
  19.7 7.5 %collective-permute-start.8 = (f32[3,128,128]{2,1,0:T(8,128)S(1)}, f32[3,128,128]{2,1,0:T(8,128)S(1)}, u32[]{:S(2)}, u32[]{:S(2)}) collective-permute-start(f32[3,128,128]{2,1,0:T(8,128)S(1)} %get-tuple-element.82), channel_id=1, source_target_pairs={{0,8},{4,12},{8,0},{12,4},{16,24},{20,28},{24,16},{28,20},{1,9},{5... | collective-permute-start | bytes 589832 | tf_op jit(solution)/shard_map/ppermute | solution.py:68
  22.7 5.3 %collective-permute-start.6 = (f32[128,256]{1,0:T(8,128)S(1)}, f32[128,256]{1,0:T(8,128)S(1)}, u32[]{:S(2)}, u32[]{:S(2)}) collective-permute-start(f32[128,256]{1,0:T(8,128)S(1)} %get-tuple-element.75.refs_1_), channel_id=1, source_target_pairs={{0,4},{4,0},{8,12},{12,8},{16,20},{20,16},{24,28},{28,24},{1,5},{5... | collective-permute-start | bytes 393224 | tf_op jit(solution)/shard_map/ppermute | solution.py:68
  24.2 5.0 %collective-permute-start.10 = (f32[2,128,128]{2,1,0:T(8,128)S(1)}, f32[2,128,128]{2,1,0:T(8,128)S(1)}, u32[]{:S(2)}, u32[]{:S(2)}) collective-permute-start(f32[2,128,128]{2,1,0:T(8,128)S(1)} %get-tuple-element.85), channel_id=1, source_target_pairs={{0,8},{4,12},{8,0},{12,4},{16,24},{20,28},{24,16},{28,20},{1,9},{5... | collective-permute-start | bytes 393224 | tf_op jit(solution)/shard_map/ppermute | solution.py:68
  29.2 2.3 %collective-permute-start.11 = (f32[2,128,128]{2,1,0:T(8,128)S(1)}, f32[2,128,128]{2,1,0:T(8,128)S(1)}, u32[]{:S(2)}, u32[]{:S(2)}) collective-permute-start(f32[2,128,128]{2,1,0:T(8,128)S(1)} %collective-permute-done.10.refs_2_), channel_id=1, source_target_pairs={{0,1},{1,0},{2,3},{3,2},{4,5},{5,4},{6,7},{7,6},{8,9},{9,8},{10,11... | collective-permute-start | bytes 393224 | tf_op jit(solution)/shard_map/ppermute | solution.py:68
  29.2 5.9 %collective-permute-start.9 = (f32[128,256]{1,0:T(8,128)S(1)}, f32[128,256]{1,0:T(8,128)S(1)}, u32[]{:S(2)}, u32[]{:S(2)}) collective-permute-start(f32[128,256]{1,0:T(8,128)S(1)} %get-tuple-element.84.refs_1_), channel_id=1, source_target_pairs={{0,8},{4,12},{8,0},{12,4},{16,24},{20,28},{24,16},{28,20},{1,9},{5... | collective-permute-start | bytes 393224 | tf_op jit(solution)/shard_map/ppermute | solution.py:68
  30.8 5.6 %collective-permute-start.13 = (f32[3,128,128]{2,1,0:T(8,128)S(1)}, f32[3,128,128]{2,1,0:T(8,128)S(1)}, u32[]{:S(2)}, u32[]{:S(2)}) collective-permute-start(f32[3,128,128]{2,1,0:T(8,128)S(1)} %boundary.1.refs_7_), channel_id=1, source_target_pairs={{8,16},{12,20},{16,8},{20,12},{9,17},{13,21},{17,9},{21,13},{10,18... | collective-permute-start | bytes 589832 | tf_op jit(solution)/shard_map/ppermute | solution.py:592
  35.6 0.9 %collective-permute-start.12 = (f32[64,256]{1,0:T(8,128)S(1)}, f32[64,256]{1,0:T(8,128)S(1)}, u32[]{:S(2)}, u32[]{:S(2)}) collective-permute-start(f32[64,256]{1,0:T(8,128)S(1)} %get-tuple-element.94), channel_id=1, source_target_pairs={{8,16},{12,20},{16,8},{20,12},{9,17},{13,21},{17,9},{21,13},{10,18... | collective-permute-start | bytes 196616 | tf_op jit(solution)/shard_map/ppermute | solution.py:611
  36.7 9.7 %collective-permute-start.14 = (f32[64,256]{1,0:T(8,128)S(1)}, f32[64,256]{1,0:T(8,128)S(1)}, u32[]{:S(2)}, u32[]{:S(2)}) collective-permute-start(f32[64,256]{1,0:T(8,128)S(1)} %turn.1.refs_1_), channel_id=1, source_target_pairs={{0,8},{4,12},{8,0},{12,4},{16,24},{20,28},{24,16},{28,20},{1,9},{5... | collective-permute-start | bytes 196616 | tf_op jit(solution)/shard_map/ppermute | solution.py:68
  46.7 4.3 %collective-permute-start.16 = (f32[64,256]{1,0:T(8,128)S(1)}, f32[64,256]{1,0:T(8,128)S(1)}, u32[]{:S(2)}, u32[]{:S(2)}) collective-permute-start(f32[64,256]{1,0:T(8,128)S(1)} %leave.1.refs_10_), channel_id=1, source_target_pairs={{0,2},{1,3},{2,0},{3,1},{4,6},{5,7},{6,4},{7,5},{8,10},{9,11},{10,... | collective-permute-start | bytes 196616 | tf_op jit(solution)/shard_map/ppermute | solution.py:68
  48.2 2.9 %collective-permute-start.15 = (f32[64,256]{1,0:T(8,128)S(1)}, f32[64,256]{1,0:T(8,128)S(1)}, u32[]{:S(2)}, u32[]{:S(2)}) collective-permute-start(f32[64,256]{1,0:T(8,128)S(1)} %leave.1.refs_10_), channel_id=1, source_target_pairs={{0,1},{1,0},{2,3},{3,2},{4,5},{5,4},{6,7},{7,6},{8,9},{9,8},{10,11... | collective-permute-start | bytes 196616 | tf_op jit(solution)/shard_map/ppermute | solution.py:68
  51.1 1.3 %collective-permute-start.17 = (f32[64,256]{1,0:T(8,128)S(1)}, f32[64,256]{1,0:T(8,128)S(1)}, u32[]{:S(2)}, u32[]{:S(2)}) collective-permute-start(f32[64,256]{1,0:T(8,128)S(1)} %collective-permute-done.16.refs_12_), channel_id=1, source_target_pairs={{0,1},{1,0},{2,3},{3,2},{4,5},{5,4},{6,7},{7,6},{8,9},{9,8},{10,11... | collective-permute-start | bytes 196616 | tf_op jit(solution)/shard_map/ppermute | solution.py:68

commit v10 on v9

--- a/solution.py
+++ b/solution.py
@@ -578,6 +578,8 @@
     middle = leaves // 2
     boundary = [(middle - 2 + i, middle + i) for i in range(2)]
     boundary += [(j, i) for i, j in boundary]
+    paired = {i for i, _ in boundary}
+    boundary += [(i, i ^ 1) for i in range(leaves) if i not in paired]
     for bit in range(rounds - 1):
         last = bit == rounds - 2
         received = exchange(message, "leaf", bit)

time: 57.2 us -> 55.2 us (0.965)
  starting transfers between devices: 23.2 us -> 18.7 us
  waiting for transfers between devices: 13.2 us -> 15.8 us
    ppermute x16, starting transfers between devices: 21.7 us -> 15.9 us  [swap(): return lax.ppermute(x, axis, [(i, i ^ mask) for i in range(n)])]
    ppermute x1, waiting for transfers between devices: 0.01 us -> 2.88 us  [local(): came = lax.ppermute(message[0], 'leaf', boundary)]
    ppermute x1, starting transfers between devices: 0.66 us -> 1.39 us  [local(): blocks = lax.ppermute(blocks, 'leaf', boundary)]
    ppermute x1, starting transfers between devices: 0.85 us -> 1.45 us  [local(): came = lax.ppermute(message[0], 'leaf', boundary)]
  transfers between devices with their start and end apart: 18 -> 18, of which waited for: 10 -> 11; matrix products, arithmetic and copies ran while one was open for 0% -> 0% of each run, Pallas kernels for 23% -> 24%
where the time goes in v10:
time: 55.2 us; the launch traced here: 55 us
  Pallas kernels  19.7 us (36%)
  starting transfers between devices  18.7 us (34%)
  waiting for transfers between devices  15.8 us (29%)
  between operations  0.76 us (1%)
    ppermute x16, starting transfers between devices, swap(): return lax.ppermute(x, axis, [(i, i ^ mask) for i in range(n)])  15.9 us
    pallas_call x14, Pallas kernels, call(): pl.pallas_call(kernel, name=name, in_specs=specs, out_specs=tuple((pl.Blo...  15.1 us
    ppermute x16, waiting for transfers between devices, swap(): return lax.ppermute(x, axis, [(i, i ^ mask) for i in range(n)])  12.9 us
    pallas_call x1, Pallas kernels, local_backward(): pl.pallas_call(lambda *refs: backward_kernel(nodes, fronts, *refs), name=...  4.55 us
    ppermute x1, waiting for transfers between devices, local(): came = lax.ppermute(message[0], 'leaf', boundary)  2.88 us
    ppermute x1, starting transfers between devices, local(): came = lax.ppermute(message[0], 'leaf', boundary)  1.45 us
    ppermute x1, starting transfers between devices, local(): blocks = lax.ppermute(blocks, 'leaf', boundary)  1.39 us
  transfers between devices with their start and end apart: 18, of which 11 were waited for; matrix products, arithmetic and copies ran while one was open for 0% of the time, Pallas kernels for 24%

profile of v10, /device:TPU:0, one launch (start us, length us, event | category | flops | bytes accessed | tf_op | source)
XLA Modules:
  0.0 55.0 jit_solution(553753169688459055)
XLA Ops:
  0.6 0.9 %stack.1.refs_5_.refs_0_ = f32[2,64,256]{2,1,0:T(8,128)S(1)} custom-call(f32[64,256]{1,0:T(8,128)} %first.1, f32[64,256]{1,0:T(8,128)} %second.1), custom_call_target="tpu_custom_call" | custom-call | tf_op jit(solution)/shard_map/stack/pallas_call | solution.py:51
  1.5 3.0 %collective-permute-start.1 = (f32[2,64,256]{2,1,0:T(8,128)S(1)}, f32[2,64,256]{2,1,0:T(8,128)S(1)}, u32[]{:S(2)}, u32[]{:S(2)}) collective-permute-start(f32[2,64,256]{2,1,0:T(8,128)S(1)} %stack.1.refs_5_.refs_0_), channel_id=1, source_target_pairs={{0,2},{1,3},{2,0},{3,1},{4,6},{5,7},{6,4},{7,5},{8,10},{9,11},{10,... | collective-permute-start | bytes 393224 | tf_op jit(solution)/shard_map/ppermute | solution.py:68
  4.5 4.3 %prepare_first.1 = (f32[2,4,128,256]{3,2,1,0:T(8,128)S(1)}, bf16[4,256,256]{2,1,0:T(8,128)(2,1)S(1)}, bf16[4,256,256]{2,1,0:T(8,128)(2,1)S(1)}, bf16[4,256,256]{...) custom-call(s32[8,256]{1,0:T(8,128)} %refs_0_.3, ...), custom_call_target="tpu_custom_call" | custom-call | tf_op jit(solution)/shard_map/prepare_first/pallas_call | solution.py:51
  10.7 1.6 %collective-permute-start.3 = (f32[1,128,256]{2,1,0:T(8,128)S(1)}, f32[1,128,256]{2,1,0:T(8,128)S(1)}, u32[]{:S(2)}, u32[]{:S(2)}) collective-permute-start(f32[1,128,256]{2,1,0:T(8,128)S(1)} %get-tuple-element.68), channel_id=1, source_target_pairs={{0,4},{4,0},{8,12},{12,8},{16,20},{20,16},{24,28},{28,24},{1,5},{5... | collective-permute-start | bytes 393224 | tf_op jit(solution)/shard_map/ppermute | solution.py:68
  12.3 4.1 %local_forward.1 = (f32[8,256,256]{2,1,0:T(8,128)S(1)}, f32[128,256]{1,0:T(8,128)S(1)}, f32[128,256]{1,0:T(8,128)S(1)}) custom-call(s32[8]{0:T(128)} %refs_0_.5, f32[2,4,128,256]{3,2,1,0:T(8,128)S(1)} %get-tuple-element.49.refs_4_.refs_1_, f32[2,4,128,256]{3,2,1,0:T(8,128)S(1)} %get-tuple-element.54.refs_4_.refs_2_, ...), custom_call_target="tpu_custom_call" | custom-call | tf_op jit(solution)/shard_map/local_forward/pallas_call | solution.py:51
  18.7 1.0 %merge_0.1 = (f32[2,256,256]{2,1,0:T(8,128)S(1)}, f32[2,256,256]{2,1,0:T(8,128)S(1)}, bf16[2,256,256]{2,1,0:T(8,128)(2,1)S(1)}, bf16[2,256,256]{2,1,0:T(8,128)(2...) custom-call(f32[256,256]{1,0:T(8,128)S(1)} %get-tuple-element.65.ref, ...), custom_call_target="tpu_custom_call" | custom-call | tf_op jit(solution)/shard_map/merge_0/pallas_call | solution.py:51
  19.7 1.6 %collective-permute-start.8 = (f32[3,128,128]{2,1,0:T(8,128)S(1)}, f32[3,128,128]{2,1,0:T(8,128)S(1)}, u32[]{:S(2)}, u32[]{:S(2)}) collective-permute-start(f32[3,128,128]{2,1,0:T(8,128)S(1)} %get-tuple-element.82), channel_id=1, source_target_pairs={{0,8},{4,12},{8,0},{12,4},{16,24},{20,28},{24,16},{28,20},{1,9},{5... | collective-permute-start | bytes 589832 | tf_op jit(solution)/shard_map/ppermute | solution.py:68
  21.3 0.9 %collective-permute-done.5.other = f32[64,256]{1,0:T(8,128)S(1)} collective-permute-done((f32[64,256]{1,0:T(8,128)S(1)}, f32[64,256]{1,0:T(8,128)S(1)}, u32[]{:S(2)}, u32[]{:S(2)}) %collective-permute-start.5) | collective-permute-done | bytes 65568 | tf_op jit(solution)/shard_map/ppermute | solution.py:68
  22.7 1.6 %collective-permute-start.6 = (f32[128,256]{1,0:T(8,128)S(1)}, f32[128,256]{1,0:T(8,128)S(1)}, u32[]{:S(2)}, u32[]{:S(2)}) collective-permute-start(f32[128,256]{1,0:T(8,128)S(1)} %get-tuple-element.75.refs_1_), channel_id=1, source_target_pairs={{0,4},{4,0},{8,12},{12,8},{16,20},{20,16},{24,28},{28,24},{1,5},{5... | collective-permute-start | bytes 393224 | tf_op jit(solution)/shard_map/ppermute | solution.py:68
  24.2 1.6 %collective-permute-start.10 = (f32[2,128,128]{2,1,0:T(8,128)S(1)}, f32[2,128,128]{2,1,0:T(8,128)S(1)}, u32[]{:S(2)}, u32[]{:S(2)}) collective-permute-start(f32[2,128,128]{2,1,0:T(8,128)S(1)} %get-tuple-element.85), channel_id=1, source_target_pairs={{0,8},{4,12},{8,0},{12,4},{16,24},{20,28},{24,16},{28,20},{1,9},{5... | collective-permute-start | bytes 393224 | tf_op jit(solution)/shard_map/ppermute | solution.py:68
  25.8 1.4 %collective-permute-done.8.other.refs_1_ = f32[3,128,128]{2,1,0:T(8,128)S(1)} collective-permute-done((f32[3,128,128]{2,1,0:T(8,128)S(1)}, f32[3,128,128]{2,1,0:T(8,128)S(1)}, u32[]{:S(2)}, u32[]{:S(2)}) %collective-permute-start.8) | collective-permute-done | bytes 196640 | tf_op jit(solution)/shard_map/ppermute | solution.py:68
  28.3 0.9 %collective-permute-done.10.refs_2_ = f32[2,128,128]{2,1,0:T(8,128)S(1)} collective-permute-done((f32[2,128,128]{2,1,0:T(8,128)S(1)}, f32[2,128,128]{2,1,0:T(8,128)S(1)}, u32[]{:S(2)}, u32[]{:S(2)}) %collective-permute-start.10) | collective-permute-done | bytes 131104 | tf_op jit(solution)/shard_map/ppermute | solution.py:68
  29.2 1.6 %collective-permute-start.9 = (f32[128,256]{1,0:T(8,128)S(1)}, f32[128,256]{1,0:T(8,128)S(1)}, u32[]{:S(2)}, u32[]{:S(2)}) collective-permute-start(f32[128,256]{1,0:T(8,128)S(1)} %get-tuple-element.84.refs_1_), channel_id=1, source_target_pairs={{0,8},{4,12},{8,0},{12,4},{16,24},{20,28},{24,16},{28,20},{1,9},{5... | collective-permute-start | bytes 393224 | tf_op jit(solution)/shard_map/ppermute | solution.py:68
  30.8 1.4 %collective-permute-start.13 = (f32[3,128,128]{2,1,0:T(8,128)S(1)}, f32[3,128,128]{2,1,0:T(8,128)S(1)}, u32[]{:S(2)}, u32[]{:S(2)}) collective-permute-start(f32[3,128,128]{2,1,0:T(8,128)S(1)} %boundary.1.refs_7_), channel_id=1, source_target_pairs={{8,16},{12,20},{16,8},{20,12},{0,4},{4,0},{24,28},{28,24},{9,17},{... | collective-permute-start | bytes 589832 | tf_op jit(solution)/shard_map/ppermute | solution.py:594
  32.2 1.3 %merge_1.1 = (f32[8,128]{1,0:T(8,128)}, bf16[2,256,256]{2,1,0:T(8,128)(2,1)S(1)}, bf16[2,256,256]{2,1,0:T(8,128)(2,1)S(1)}, bf16[2,256,256]{2,1,0:T(8,128)(2,1)S...) custom-call(f32[2,256,256]{2,1,0:T(8,128)S(1)} %get-tuple-element.81.own.refs_0_, ...), custom_call_target="tpu_custom_call" | custom-call | tf_op jit(solution)/shard_map/merge_1/pallas_call | solution.py:51
  33.5 1.6 %collective-permute-done.9.refs_2_ = f32[128,256]{1,0:T(8,128)S(1)} collective-permute-done((f32[128,256]{1,0:T(8,128)S(1)}, f32[128,256]{1,0:T(8,128)S(1)}, u32[]{:S(2)}, u32[]{:S(2)}) %collective-permute-start.9) | collective-permute-done | bytes 131104 | tf_op jit(solution)/shard_map/ppermute | solution.py:68
  35.6 1.4 %collective-permute-start.12 = (f32[64,256]{1,0:T(8,128)S(1)}, f32[64,256]{1,0:T(8,128)S(1)}, u32[]{:S(2)}, u32[]{:S(2)}) collective-permute-start(f32[64,256]{1,0:T(8,128)S(1)} %get-tuple-element.94), channel_id=1, source_target_pairs={{8,16},{12,20},{16,8},{20,12},{0,4},{4,0},{24,28},{28,24},{9,17},{... | collective-permute-start | bytes 196616 | tf_op jit(solution)/shard_map/ppermute | solution.py:613
  37.0 2.9 %collective-permute-done.12.refs_1_ = f32[64,256]{1,0:T(8,128)S(1)} collective-permute-done((f32[64,256]{1,0:T(8,128)S(1)}, f32[64,256]{1,0:T(8,128)S(1)}, u32[]{:S(2)}, u32[]{:S(2)}) %collective-permute-start.12) | collective-permute-done | bytes 65568 | tf_op jit(solution)/shard_map/ppermute | solution.py:613
  40.2 1.6 %collective-permute-start.14 = (f32[64,256]{1,0:T(8,128)S(1)}, f32[64,256]{1,0:T(8,128)S(1)}, u32[]{:S(2)}, u32[]{:S(2)}) collective-permute-start(f32[64,256]{1,0:T(8,128)S(1)} %turn.1.refs_1_), channel_id=1, source_target_pairs={{0,8},{4,12},{8,0},{12,4},{16,24},{20,28},{24,16},{28,20},{1,9},{5... | collective-permute-start | bytes 196616 | tf_op jit(solution)/shard_map/ppermute | solution.py:68
  41.8 2.7 %collective-permute-done.14.refs_2_ = f32[64,256]{1,0:T(8,128)S(1)} collective-permute-done((f32[64,256]{1,0:T(8,128)S(1)}, f32[64,256]{1,0:T(8,128)S(1)}, u32[]{:S(2)}, u32[]{:S(2)}) %collective-permute-start.14) | collective-permute-done | bytes 65568 | tf_op jit(solution)/shard_map/ppermute | solution.py:68
  44.9 1.4 %collective-permute-start.16 = (f32[64,256]{1,0:T(8,128)S(1)}, f32[64,256]{1,0:T(8,128)S(1)}, u32[]{:S(2)}, u32[]{:S(2)}) collective-permute-start(f32[64,256]{1,0:T(8,128)S(1)} %leave.1.refs_10_), channel_id=1, source_target_pairs={{0,2},{1,3},{2,0},{3,1},{4,6},{5,7},{6,4},{7,5},{8,10},{9,11},{10,... | collective-permute-start | bytes 196616 | tf_op jit(solution)/shard_map/ppermute | solution.py:68
  46.3 2.9 %collective-permute-done.16.refs_12_ = f32[64,256]{1,0:T(8,128)S(1)} collective-permute-done((f32[64,256]{1,0:T(8,128)S(1)}, f32[64,256]{1,0:T(8,128)S(1)}, u32[]{:S(2)}, u32[]{:S(2)}) %collective-permute-start.16) | collective-permute-done | bytes 65568 | tf_op jit(solution)/shard_map/ppermute | solution.py:68
  49.2 1.2 %collective-permute-done.17.refs_13_ = f32[64,256]{1,0:T(8,128)S(1)} collective-permute-done((f32[64,256]{1,0:T(8,128)S(1)}, f32[64,256]{1,0:T(8,128)S(1)}, u32[]{:S(2)}, u32[]{:S(2)}) %collective-permute-start.17) | collective-permute-done | bytes 65568 | tf_op jit(solution)/shard_map/ppermute | solution.py:68
  50.4 4.5 %local_backward.1 = (f32[8,256,256]{2,1,0:T(8,128)}, f32[64,256]{1,0:T(8,128)}) custom-call(s32[8]{0:T(128)} %refs_0_.5, f32[8,256,256]{2,1,0:T(8,128)S(1)} %get-tuple-element.66.refs_1_, bf16[4,256,256]{2,1,0:T(8,128)(2,1)S(1)} %get-tuple-element.56.refs_4_.refs_2_, bf16[4,256,256]{2,1,0:T(8,128)(2,1)S(1)} %get-tuple-element.57.refs_5_.refs_3_, ...), custom_call_target="tpu_custom_call" | custom-call | tf_op jit(solution)/shard_map/local_backward/pallas_call | solution.py:278
  (27 shorter events, 6.7 us)
Async XLA Ops:
  1.5 7.3 %collective-permute-start.1 = (f32[2,64,256]{2,1,0:T(8,128)S(1)}, f32[2,64,256]{2,1,0:T(8,128)S(1)}, u32[]{:S(2)}, u32[]{:S(2)}) collective-permute-start(f32[2,64,256]{2,1,0:T(8,128)S(1)} %stack.1.refs_5_.refs_0_), channel_id=1, source_target_pairs={{0,2},{1,3},{2,0},{3,1},{4,6},{5,7},{6,4},{7,5},{8,10},{9,11},{10,... | collective-permute-start | bytes 393224 | tf_op jit(solution)/shard_map/ppermute | solution.py:68
  4.5 5.5 %collective-permute-start = (f32[2,64,256]{2,1,0:T(8,128)S(1)}, f32[2,64,256]{2,1,0:T(8,128)S(1)}, u32[]{:S(2)}, u32[]{:S(2)}) collective-permute-start(f32[2,64,256]{2,1,0:T(8,128)S(1)} %stack.1.refs_5_.refs_0_), channel_id=1, source_target_pairs={{0,1},{1,0},{2,3},{3,2},{4,5},{5,4},{6,7},{7,6},{8,9},{9,8},{10,11... | collective-permute-start | bytes 393224 | tf_op jit(solution)/shard_map/ppermute | solution.py:68
  8.8 1.6 %collective-permute-start.2 = (f32[2,64,256]{2,1,0:T(8,128)S(1)}, f32[2,64,256]{2,1,0:T(8,128)S(1)}, u32[]{:S(2)}, u32[]{:S(2)}) collective-permute-start(f32[2,64,256]{2,1,0:T(8,128)S(1)} %collective-permute-done.1.refs_2_), channel_id=1, source_target_pairs={{0,1},{1,0},{2,3},{3,2},{4,5},{5,4},{6,7},{7,6},{8,9},{9,8},{10,11... | collective-permute-start | bytes 393224 | tf_op jit(solution)/shard_map/ppermute | solution.py:68
  10.7 5.8 %collective-permute-start.3 = (f32[1,128,256]{2,1,0:T(8,128)S(1)}, f32[1,128,256]{2,1,0:T(8,128)S(1)}, u32[]{:S(2)}, u32[]{:S(2)}) collective-permute-start(f32[1,128,256]{2,1,0:T(8,128)S(1)} %get-tuple-element.68), channel_id=1, source_target_pairs={{0,4},{4,0},{8,12},{12,8},{16,20},{20,16},{24,28},{28,24},{1,5},{5... | collective-permute-start | bytes 393224 | tf_op jit(solution)/shard_map/ppermute | solution.py:68
  16.5 1.3 %collective-permute-start.4 = (f32[128,256]{1,0:T(8,128)S(1)}, f32[128,256]{1,0:T(8,128)S(1)}, u32[]{:S(2)}, u32[]{:S(2)}) collective-permute-start(f32[128,256]{1,0:T(8,128)S(1)} %get-tuple-element.70), channel_id=1, source_target_pairs={{0,1},{1,0},{2,3},{3,2},{4,5},{5,4},{6,7},{7,6},{8,9},{9,8},{10,11... | collective-permute-start | bytes 393224 | tf_op jit(solution)/shard_map/ppermute | solution.py:68
  16.5 2.1 %collective-permute-start.7 = (f32[1,128,256]{2,1,0:T(8,128)S(1)}, f32[1,128,256]{2,1,0:T(8,128)S(1)}, u32[]{:S(2)}, u32[]{:S(2)}) collective-permute-start(f32[1,128,256]{2,1,0:T(8,128)S(1)} %collective-permute-done.3.refs_1_), channel_id=1, source_target_pairs={{0,1},{1,0},{2,3},{3,2},{4,5},{5,4},{6,7},{7,6},{8,9},{9,8},{10,11... | collective-permute-start | bytes 393224 | tf_op jit(solution)/shard_map/ppermute | solution.py:68
  17.9 4.3 %collective-permute-start.5 = (f32[64,256]{1,0:T(8,128)S(1)}, f32[64,256]{1,0:T(8,128)S(1)}, u32[]{:S(2)}, u32[]{:S(2)}) collective-permute-start(f32[64,256]{1,0:T(8,128)S(1)} %get-tuple-element.72.refs_3_), channel_id=1, source_target_pairs={{0,2},{1,3},{2,0},{3,1},{4,6},{5,7},{6,4},{7,5},{8,10},{9,11},{10,... | collective-permute-start | bytes 196616 | tf_op jit(solution)/shard_map/ppermute | solution.py:68
  19.7 7.5 %collective-permute-start.8 = (f32[3,128,128]{2,1,0:T(8,128)S(1)}, f32[3,128,128]{2,1,0:T(8,128)S(1)}, u32[]{:S(2)}, u32[]{:S(2)}) collective-permute-start(f32[3,128,128]{2,1,0:T(8,128)S(1)} %get-tuple-element.82), channel_id=1, source_target_pairs={{0,8},{4,12},{8,0},{12,4},{16,24},{20,28},{24,16},{28,20},{1,9},{5... | collective-permute-start | bytes 589832 | tf_op jit(solution)/shard_map/ppermute | solution.py:68
  22.7 5.2 %collective-permute-start.6 = (f32[128,256]{1,0:T(8,128)S(1)}, f32[128,256]{1,0:T(8,128)S(1)}, u32[]{:S(2)}, u32[]{:S(2)}) collective-permute-start(f32[128,256]{1,0:T(8,128)S(1)} %get-tuple-element.75.refs_1_), channel_id=1, source_target_pairs={{0,4},{4,0},{8,12},{12,8},{16,20},{20,16},{24,28},{28,24},{1,5},{5... | collective-permute-start | bytes 393224 | tf_op jit(solution)/shard_map/ppermute | solution.py:68
  24.2 5.0 %collective-permute-start.10 = (f32[2,128,128]{2,1,0:T(8,128)S(1)}, f32[2,128,128]{2,1,0:T(8,128)S(1)}, u32[]{:S(2)}, u32[]{:S(2)}) collective-permute-start(f32[2,128,128]{2,1,0:T(8,128)S(1)} %get-tuple-element.85), channel_id=1, source_target_pairs={{0,8},{4,12},{8,0},{12,4},{16,24},{20,28},{24,16},{28,20},{1,9},{5... | collective-permute-start | bytes 393224 | tf_op jit(solution)/shard_map/ppermute | solution.py:68
  29.2 3.0 %collective-permute-start.11 = (f32[2,128,128]{2,1,0:T(8,128)S(1)}, f32[2,128,128]{2,1,0:T(8,128)S(1)}, u32[]{:S(2)}, u32[]{:S(2)}) collective-permute-start(f32[2,128,128]{2,1,0:T(8,128)S(1)} %collective-permute-done.10.refs_2_), channel_id=1, source_target_pairs={{0,1},{1,0},{2,3},{3,2},{4,5},{5,4},{6,7},{7,6},{8,9},{9,8},{10,11... | collective-permute-start | bytes 393224 | tf_op jit(solution)/shard_map/ppermute | solution.py:68
  29.2 5.9 %collective-permute-start.9 = (f32[128,256]{1,0:T(8,128)S(1)}, f32[128,256]{1,0:T(8,128)S(1)}, u32[]{:S(2)}, u32[]{:S(2)}) collective-permute-start(f32[128,256]{1,0:T(8,128)S(1)} %get-tuple-element.84.refs_1_), channel_id=1, source_target_pairs={{0,8},{4,12},{8,0},{12,4},{16,24},{20,28},{24,16},{28,20},{1,9},{5... | collective-permute-start | bytes 393224 | tf_op jit(solution)/shard_map/ppermute | solution.py:68
  30.8 9.1 %collective-permute-start.13 = (f32[3,128,128]{2,1,0:T(8,128)S(1)}, f32[3,128,128]{2,1,0:T(8,128)S(1)}, u32[]{:S(2)}, u32[]{:S(2)}) collective-permute-start(f32[3,128,128]{2,1,0:T(8,128)S(1)} %boundary.1.refs_7_), channel_id=1, source_target_pairs={{8,16},{12,20},{16,8},{20,12},{0,4},{4,0},{24,28},{28,24},{9,17},{... | collective-permute-start | bytes 589832 | tf_op jit(solution)/shard_map/ppermute | solution.py:594
  35.6 4.3 %collective-permute-start.12 = (f32[64,256]{1,0:T(8,128)S(1)}, f32[64,256]{1,0:T(8,128)S(1)}, u32[]{:S(2)}, u32[]{:S(2)}) collective-permute-start(f32[64,256]{1,0:T(8,128)S(1)} %get-tuple-element.94), channel_id=1, source_target_pairs={{8,16},{12,20},{16,8},{20,12},{0,4},{4,0},{24,28},{28,24},{9,17},{... | collective-permute-start | bytes 196616 | tf_op jit(solution)/shard_map/ppermute | solution.py:613
  40.2 4.3 %collective-permute-start.14 = (f32[64,256]{1,0:T(8,128)S(1)}, f32[64,256]{1,0:T(8,128)S(1)}, u32[]{:S(2)}, u32[]{:S(2)}) collective-permute-start(f32[64,256]{1,0:T(8,128)S(1)} %turn.1.refs_1_), channel_id=1, source_target_pairs={{0,8},{4,12},{8,0},{12,4},{16,24},{20,28},{24,16},{28,20},{1,9},{5... | collective-permute-start | bytes 196616 | tf_op jit(solution)/shard_map/ppermute | solution.py:68
  44.9 4.3 %collective-permute-start.16 = (f32[64,256]{1,0:T(8,128)S(1)}, f32[64,256]{1,0:T(8,128)S(1)}, u32[]{:S(2)}, u32[]{:S(2)}) collective-permute-start(f32[64,256]{1,0:T(8,128)S(1)} %leave.1.refs_10_), channel_id=1, source_target_pairs={{0,2},{1,3},{2,0},{3,1},{4,6},{5,7},{6,4},{7,5},{8,10},{9,11},{10,... | collective-permute-start | bytes 196616 | tf_op jit(solution)/shard_map/ppermute | solution.py:68
  46.3 2.9 %collective-permute-start.15 = (f32[64,256]{1,0:T(8,128)S(1)}, f32[64,256]{1,0:T(8,128)S(1)}, u32[]{:S(2)}, u32[]{:S(2)}) collective-permute-start(f32[64,256]{1,0:T(8,128)S(1)} %leave.1.refs_10_), channel_id=1, source_target_pairs={{0,1},{1,0},{2,3},{3,2},{4,5},{5,4},{6,7},{7,6},{8,9},{9,8},{10,11... | collective-permute-start | bytes 196616 | tf_op jit(solution)/shard_map/ppermute | solution.py:68
  49.2 1.3 %collective-permute-start.17 = (f32[64,256]{1,0:T(8,128)S(1)}, f32[64,256]{1,0:T(8,128)S(1)}, u32[]{:S(2)}, u32[]{:S(2)}) collective-permute-start(f32[64,256]{1,0:T(8,128)S(1)} %collective-permute-done.16.refs_12_), channel_id=1, source_target_pairs={{0,1},{1,0},{2,3},{3,2},{4,5},{5,4},{6,7},{7,6},{8,9},{9,8},{10,11... | collective-permute-start | bytes 196616 | tf_op jit(solution)/shard_map/ppermute | solution.py:68

commit v11 on v10

--- a/solution.py
+++ b/solution.py
@@ -371,9 +371,9 @@
 
 
 def send_maps(parts, k, t):
-    for i, block in enumerate(k_blocks(k)):
-        parts[0][i] = block
-    send_blocks(parts[1:], quarters(t))
+    parts[0][0], parts[0][1], parts[-1][0] = k_blocks(k)
+    half = t.shape[0] // 2
+    parts[1][...], parts[2][...] = t[:half], t[half:]
 
 
 def first_merge_kernel(*refs):
@@ -404,11 +404,11 @@
 
 
 def merge_kernel(bit, last, *refs):
-    own, other, mine, pairs, mixed = refs[:5]
-    kept, mixed_n, halves, curve_u, total_u, total_l, *parts = refs[5:]
+    own, other, rest, first_t, second_t, mixed = refs[:6]
+    kept, mixed_n, halves, curve_u, total_u, total_l, *parts = refs[6:]
     upper = bit_of("leaf", bit) == 1
     own_k, own_t = own[0], own[1]
-    other_k, other_t = k_of(other), joined(*came_blocks([mine], [pairs], 4))
+    other_k, other_t = k_of([other[0], other[1], rest[0]]), jnp.concatenate([first_t[...], second_t[...]], axis=0)
     low_s = split(jnp.where(upper, other_t, own_t))
     up_s = split(jnp.where(upper, own_t, other_t))
     k_low = jnp.where(upper, other_k, own_k)
@@ -433,9 +433,9 @@
         mixed_n[0], mixed_n[1] = a_n, e_n
 
 
-def boundary_kernel(own, other, blocks):
+def boundary_kernel(own, other, rest, blocks):
     k, t = own[0], split(own[1])
-    x = dot3(split(k_of(other)), t, NN)
+    x = dot3(split(k_of([other[0], other[1], rest[0]])), t, NN)
     for i, block in enumerate(k_blocks(k + dot3(t, split(x), TN))):
         blocks[i] = block
 
@@ -445,7 +445,7 @@
     half = size // 2
     if last:
         return [((8, 128), F32)] + [both] * 5
-    sends = [((i, half, half), F32) for i in (3, 2)]
+    sends = [((2, half, half), F32)] + [((half, size), F32)] * 2 + [((1, half, half), F32)]
     return [whole, whole, both, both, both, both] + sends
 
 
@@ -468,28 +468,35 @@
     message[rows:] = dot3(split(value), split(own_map[...]), NN)
 
 
-def step_kernel(bit, last, held, *refs):
+def step_kernel(bit, rounds, held, *refs):
     sol, own, other, halves, curve_u, total_u, total_l = refs[:7]
     sol_n, message = refs[7 + held], refs[8 + held :]
+    last = bit == rounds - 2
     upper = bit_of("leaf", bit) == 1
     rows = sol.shape[0]
-    z_own, p_own, z_other, p_other = own[:rows], own[rows:], other[:rows], other[rows:]
+    z_own, p_own = own[:rows], own[rows:]
+    if last:
+        z_other = p_other = other[...]
+    else:
+        z_other, p_other = other[:rows], other[rows:]
     z_low = jnp.where(upper, z_other, z_own)
-    z_up = jnp.where(upper, z_own, z_other)
-    p_low = jnp.where(upper, p_other, p_own)
     p_up = jnp.where(upper, p_own, p_other)
     z_low_s = split(z_low)
     middle = p_up + dot3(z_low_s, pair(curve_u), NN)
     middle_s = split(middle)
+    given = split(jnp.where(upper, z_low, middle))
+    sol_n[...] = sol[...] + dot3(given, pair(halves), NN)
+    z_up = z_own if last else jnp.where(upper, z_own, z_other)
+    p_low = p_own if last else jnp.where(upper, p_other, p_own)
     z_new = z_up + dot3(z_low_s, pair(total_u), NT)
     p_new = p_low + dot3(middle_s, pair(total_l), NN)
-    given = split(jnp.where(upper, z_low, middle))
-    sol_n[...] = sol[...] + dot3(given, pair(halves), NN)
     if last:
         message[0][...] = jnp.where(bit_of("leaf", bit + 1) == 1, p_new, z_new)
         message[1][...] = z_new
-    else:
-        message[0][:rows], message[0][rows:] = z_new, p_new
+        return
+    message[0][:rows], message[0][rows:] = z_new, p_new
+    if bit == rounds - 3:
+        message[1][...] = jnp.where(bit_of("leaf", bit + 1) == 1, p_new, z_new)
 
 
 def turn_kernel(bit, own_z, came, blocks, given):
@@ -582,31 +589,32 @@
     boundary += [(i, i ^ 1) for i in range(leaves) if i not in paired]
     for bit in range(rounds - 1):
         last = bit == rounds - 2
-        received = exchange(message, "leaf", bit)
+        received = exchange(short[0] if last else message, "leaf", bit)
         ahead = []
         if not last:
-            other, mine = [exchange(part, "leaf", bit + 1) for part in parts]
+            other, *came_t, rest = [exchange(part, "leaf", bit + 1) for part in parts]
             ahead = [other]
         if bit == rounds - 3:
             ahead = (blocks,) = call(
-                boundary_kernel, "boundary", [(V, kept), (V, other)], [(other.shape, F32)]
+                boundary_kernel,
+                "boundary",
+                [(V, kept), (V, other), (V, rest)],
+                [((3, size // 2, size // 2), F32)],
             )
             blocks = lax.ppermute(blocks, "leaf", boundary)
         sol, *message = call(
-            lambda *refs, bit=bit, last=last: step_kernel(bit, last, len(ahead), *refs),
+            lambda *refs, bit=bit: step_kernel(bit, rounds, len(ahead), *refs),
             f"step_{bit}",
             [(V, a) for a in (sol, message, received, *tools)] + [(pl.ANY, a) for a in ahead],
-            [share] + ([share, share] if last else [((2 * chunk, size), F32)]),
+            [share] + ([share] if last else [((2 * chunk, size), F32)]) + [share] * (bit >= rounds - 3),
         )
         if not last:
-            (message,) = message
-            mine, _ = lax.optimization_barrier((mine, sol))
-            pairs = exchange(mine, "front", 0)
+            message, *short = message
             last = bit == rounds - 3
             kept, mixed, *tools = call(
                 lambda *refs, bit=bit, last=last: merge_kernel(bit + 1, last, *refs),
                 f"merge_{bit + 1}",
-                [(V, a) for a in (kept, other, mine, pairs, mixed)],
+                [(V, a) for a in (kept, other, rest, *came_t, mixed)],
                 maps(size, last),
             )
             tools, parts = tools[:4], tools[4:]

time: 55.2 us -> 55.9 us (1.013)
  starting transfers between devices: 18.7 us -> 20.2 us
  waiting for transfers between devices: 15.8 us -> 15.1 us
    ppermute x16 -> x17, starting transfers between devices: 15.9 us -> 18.7 us  [swap(): return lax.ppermute(x, axis, [(i, i ^ mask) for i in range(n)])]
    ppermute x16 -> x17, waiting for transfers between devices: 12.9 us -> 11.7 us  [swap(): return lax.ppermute(x, axis, [(i, i ^ mask) for i in range(n)])]
    ppermute x1, starting transfers between devices: 1.39 us -> 0.57 us  [local(): blocks = lax.ppermute(blocks, 'leaf', boundary)]
  transfers between devices with their start and end apart: 18 -> 19, of which waited for: 11 -> 11; matrix products, arithmetic and copies ran while one was open for 0% -> 0% of each run, Pallas kernels for 24% -> 24%
where the time goes in v11:
time: 55.9 us; the launch traced here: 55.7 us
  starting transfers between devices  20.2 us (36%)
  Pallas kernels  19.7 us (35%)
  waiting for transfers between devices  15.1 us (27%)
  between operations  0.76 us (1%)
    ppermute x17, starting transfers between devices, swap(): return lax.ppermute(x, axis, [(i, i ^ mask) for i in range(n)])  18.7 us
    pallas_call x14, Pallas kernels, call(): pl.pallas_call(kernel, name=name, in_specs=specs, out_specs=tuple((pl.Blo...  15.2 us
    ppermute x17, waiting for transfers between devices, swap(): return lax.ppermute(x, axis, [(i, i ^ mask) for i in range(n)])  11.7 us
    pallas_call x1, Pallas kernels, local_backward(): pl.pallas_call(lambda *refs: backward_kernel(nodes, fronts, *refs), name=...  4.55 us
    ppermute x1, waiting for transfers between devices, local(): came = lax.ppermute(message[0], 'leaf', boundary)  3.38 us
  transfers between devices with their start and end apart: 19, of which 11 were waited for; matrix products, arithmetic and copies ran while one was open for 0% of the time, Pallas kernels for 24%

profile of v11, /device:TPU:0, one launch (start us, length us, event | category | flops | bytes accessed | tf_op | source)
XLA Modules:
  0.0 55.7 jit_solution(14663109899368299717)
XLA Ops:
  0.6 0.9 %stack.1.refs_5_.refs_0_ = f32[2,64,256]{2,1,0:T(8,128)S(1)} custom-call(f32[64,256]{1,0:T(8,128)} %first.1, f32[64,256]{1,0:T(8,128)} %second.1), custom_call_target="tpu_custom_call" | custom-call | tf_op jit(solution)/shard_map/stack/pallas_call | solution.py:51
  1.5 3.0 %collective-permute-start.1 = (f32[2,64,256]{2,1,0:T(8,128)S(1)}, f32[2,64,256]{2,1,0:T(8,128)S(1)}, u32[]{:S(2)}, u32[]{:S(2)}) collective-permute-start(f32[2,64,256]{2,1,0:T(8,128)S(1)} %stack.1.refs_5_.refs_0_), channel_id=1, source_target_pairs={{0,2},{1,3},{2,0},{3,1},{4,6},{5,7},{6,4},{7,5},{8,10},{9,11},{10,... | collective-permute-start | bytes 393224 | tf_op jit(solution)/shard_map/ppermute | solution.py:68
  4.5 4.3 %prepare_first.1 = (f32[2,4,128,256]{3,2,1,0:T(8,128)S(1)}, bf16[4,256,256]{2,1,0:T(8,128)(2,1)S(1)}, bf16[4,256,256]{2,1,0:T(8,128)(2,1)S(1)}, bf16[4,256,256]{...) custom-call(s32[8,256]{1,0:T(8,128)} %refs_0_.3, ...), custom_call_target="tpu_custom_call" | custom-call | tf_op jit(solution)/shard_map/prepare_first/pallas_call | solution.py:51
  10.7 1.6 %collective-permute-start.3 = (f32[1,128,256]{2,1,0:T(8,128)S(1)}, f32[1,128,256]{2,1,0:T(8,128)S(1)}, u32[]{:S(2)}, u32[]{:S(2)}) collective-permute-start(f32[1,128,256]{2,1,0:T(8,128)S(1)} %get-tuple-element.70), channel_id=1, source_target_pairs={{0,4},{4,0},{8,12},{12,8},{16,20},{20,16},{24,28},{28,24},{1,5},{5... | collective-permute-start | bytes 393224 | tf_op jit(solution)/shard_map/ppermute | solution.py:68
  12.3 4.1 %local_forward.1 = (f32[8,256,256]{2,1,0:T(8,128)S(1)}, f32[128,256]{1,0:T(8,128)S(1)}, f32[128,256]{1,0:T(8,128)S(1)}) custom-call(s32[8]{0:T(128)} %refs_0_.5, f32[2,4,128,256]{3,2,1,0:T(8,128)S(1)} %get-tuple-element.51.refs_4_.refs_1_, f32[2,4,128,256]{3,2,1,0:T(8,128)S(1)} %get-tuple-element.56.refs_4_.refs_2_, ...), custom_call_target="tpu_custom_call" | custom-call | tf_op jit(solution)/shard_map/local_forward/pallas_call | solution.py:51
  17.0 0.8 %collective-permute-done.4.refs_1_ = f32[128,256]{1,0:T(8,128)S(1)} collective-permute-done((f32[128,256]{1,0:T(8,128)S(1)}, f32[128,256]{1,0:T(8,128)S(1)}, u32[]{:S(2)}, u32[]{:S(2)}) %collective-permute-start.4) | collective-permute-done | bytes 131104 | tf_op jit(solution)/shard_map/ppermute | solution.py:68
  17.9 0.7 %collective-permute-start.5 = (f32[64,256]{1,0:T(8,128)S(1)}, f32[64,256]{1,0:T(8,128)S(1)}, u32[]{:S(2)}, u32[]{:S(2)}) collective-permute-start(f32[64,256]{1,0:T(8,128)S(1)} %get-tuple-element.74.refs_3_), channel_id=1, source_target_pairs={{0,2},{1,3},{2,0},{3,1},{4,6},{5,7},{6,4},{7,5},{8,10},{9,11},{10,... | collective-permute-start | bytes 196616 | tf_op jit(solution)/shard_map/ppermute | solution.py:68
  18.7 1.0 %merge_0.1 = (f32[2,256,256]{2,1,0:T(8,128)S(1)}, f32[2,256,256]{2,1,0:T(8,128)S(1)}, bf16[2,256,256]{2,1,0:T(8,128)(2,1)S(1)}, bf16[2,256,256]{2,1,0:T(8,128)(2...) custom-call(f32[256,256]{1,0:T(8,128)S(1)} %get-tuple-element.67.ref, ...), custom_call_target="tpu_custom_call" | custom-call | tf_op jit(solution)/shard_map/merge_0/pallas_call | solution.py:51
  19.7 1.6 %collective-permute-start.8 = (f32[2,128,128]{2,1,0:T(8,128)S(1)}, f32[2,128,128]{2,1,0:T(8,128)S(1)}, u32[]{:S(2)}, u32[]{:S(2)}) collective-permute-start(f32[2,128,128]{2,1,0:T(8,128)S(1)} %get-tuple-element.84), channel_id=1, source_target_pairs={{0,8},{4,12},{8,0},{12,4},{16,24},{20,28},{24,16},{28,20},{1,9},{5... | collective-permute-start | bytes 393224 | tf_op jit(solution)/shard_map/ppermute | solution.py:68
  21.3 0.9 %collective-permute-done.5.other = f32[64,256]{1,0:T(8,128)S(1)} collective-permute-done((f32[64,256]{1,0:T(8,128)S(1)}, f32[64,256]{1,0:T(8,128)S(1)}, u32[]{:S(2)}, u32[]{:S(2)}) %collective-permute-start.5) | collective-permute-done | bytes 65568 | tf_op jit(solution)/shard_map/ppermute | solution.py:68
  22.7 1.6 %collective-permute-start.6 = (f32[128,256]{1,0:T(8,128)S(1)}, f32[128,256]{1,0:T(8,128)S(1)}, u32[]{:S(2)}, u32[]{:S(2)}) collective-permute-start(f32[128,256]{1,0:T(8,128)S(1)} %get-tuple-element.77.refs_1_), channel_id=1, source_target_pairs={{0,4},{4,0},{8,12},{12,8},{16,20},{20,16},{24,28},{28,24},{1,5},{5... | collective-permute-start | bytes 393224 | tf_op jit(solution)/shard_map/ppermute | solution.py:68
  24.2 1.6 %collective-permute-start.9 = (f32[1,128,128]{2,1,0:T(8,128)S(1)}, f32[1,128,128]{2,1,0:T(8,128)S(1)}, u32[]{:S(2)}, u32[]{:S(2)}) collective-permute-start(f32[1,128,128]{2,1,0:T(8,128)S(1)} %get-tuple-element.85), channel_id=1, source_target_pairs={{0,8},{4,12},{8,0},{12,4},{16,24},{20,28},{24,16},{28,20},{1,9},{5... | collective-permute-start | bytes 196616 | tf_op jit(solution)/shard_map/ppermute | solution.py:68
  26.3 1.6 %collective-permute-start.12 = (f32[128,256]{1,0:T(8,128)S(1)}, f32[128,256]{1,0:T(8,128)S(1)}, u32[]{:S(2)}, u32[]{:S(2)}) collective-permute-start(f32[128,256]{1,0:T(8,128)S(1)} %get-tuple-element.90), channel_id=1, source_target_pairs={{0,8},{4,12},{8,0},{12,4},{16,24},{20,28},{24,16},{28,20},{1,9},{5... | collective-permute-start | bytes 393224 | tf_op jit(solution)/shard_map/ppermute | solution.py:68
  27.9 1.3 %collective-permute-done.9.rest.refs_2_ = f32[1,128,128]{2,1,0:T(8,128)S(1)} collective-permute-done((f32[1,128,128]{2,1,0:T(8,128)S(1)}, f32[1,128,128]{2,1,0:T(8,128)S(1)}, u32[]{:S(2)}, u32[]{:S(2)}) %collective-permute-start.9) | collective-permute-done | bytes 65568 | tf_op jit(solution)/shard_map/ppermute | solution.py:68
  29.2 0.7 %boundary.1.refs_7_ = f32[3,128,128]{2,1,0:T(8,128)S(1)} custom-call(f32[2,256,256]{2,1,0:T(8,128)S(1)} %get-tuple-element.83.own.refs_0_, f32[2,128,128]{2,1,0:T(8,128)S(1)} %collective-permute-done.8.other.refs_1_, f32[1,128,128]{2,1,0:T(8,128)S(1)} %collective-permute-done.9.rest.refs_2_), custom_call_target="tpu_custom_call" | custom-call | tf_op jit(solution)/shard_map/boundary/pallas_call | solution.py:51
  30.9 2.7 %collective-permute-start.10 = (f32[64,256]{1,0:T(8,128)S(1)}, f32[64,256]{1,0:T(8,128)S(1)}, u32[]{:S(2)}, u32[]{:S(2)}) collective-permute-start(f32[64,256]{1,0:T(8,128)S(1)} %get-tuple-element.88), channel_id=1, source_target_pairs={{0,8},{4,12},{8,0},{12,4},{16,24},{20,28},{24,16},{28,20},{1,9},{5... | collective-permute-start | bytes 196616 | tf_op jit(solution)/shard_map/ppermute | solution.py:68
  33.9 1.3 %merge_1.1 = (f32[8,128]{1,0:T(8,128)}, bf16[2,256,256]{2,1,0:T(8,128)(2,1)S(1)}, bf16[2,256,256]{2,1,0:T(8,128)(2,1)S(1)}, bf16[2,256,256]{2,1,0:T(8,128)(2,1)S...) custom-call(f32[2,256,256]{2,1,0:T(8,128)S(1)} %get-tuple-element.83.own.refs_0_, ...), custom_call_target="tpu_custom_call" | custom-call | tf_op jit(solution)/shard_map/merge_1/pallas_call | solution.py:51
  36.3 1.0 %collective-permute-start.13 = (f32[64,256]{1,0:T(8,128)S(1)}, f32[64,256]{1,0:T(8,128)S(1)}, u32[]{:S(2)}, u32[]{:S(2)}) collective-permute-start(f32[64,256]{1,0:T(8,128)S(1)} %get-tuple-element.98), channel_id=1, source_target_pairs={{8,16},{12,20},{16,8},{20,12},{0,4},{4,0},{24,28},{28,24},{9,17},{... | collective-permute-start | bytes 196616 | tf_op jit(solution)/shard_map/ppermute | solution.py:621
  37.3 3.4 %collective-permute-done.13.refs_1_ = f32[64,256]{1,0:T(8,128)S(1)} collective-permute-done((f32[64,256]{1,0:T(8,128)S(1)}, f32[64,256]{1,0:T(8,128)S(1)}, u32[]{:S(2)}, u32[]{:S(2)}) %collective-permute-start.13) | collective-permute-done | bytes 65568 | tf_op jit(solution)/shard_map/ppermute | solution.py:621
  40.9 2.1 %collective-permute-start.15 = (f32[64,256]{1,0:T(8,128)S(1)}, f32[64,256]{1,0:T(8,128)S(1)}, u32[]{:S(2)}, u32[]{:S(2)}) collective-permute-start(f32[64,256]{1,0:T(8,128)S(1)} %turn.1.refs_1_), channel_id=1, source_target_pairs={{0,8},{4,12},{8,0},{12,4},{16,24},{20,28},{24,16},{28,20},{1,9},{5... | collective-permute-start | bytes 196616 | tf_op jit(solution)/shard_map/ppermute | solution.py:68
  43.0 2.2 %collective-permute-done.15.refs_2_ = f32[64,256]{1,0:T(8,128)S(1)} collective-permute-done((f32[64,256]{1,0:T(8,128)S(1)}, f32[64,256]{1,0:T(8,128)S(1)}, u32[]{:S(2)}, u32[]{:S(2)}) %collective-permute-start.15) | collective-permute-done | bytes 65568 | tf_op jit(solution)/shard_map/ppermute | solution.py:68
  46.2 3.7 %collective-permute-done.17.refs_12_ = f32[64,256]{1,0:T(8,128)S(1)} collective-permute-done((f32[64,256]{1,0:T(8,128)S(1)}, f32[64,256]{1,0:T(8,128)S(1)}, u32[]{:S(2)}, u32[]{:S(2)}) %collective-permute-start.17) | collective-permute-done | bytes 65568 | tf_op jit(solution)/shard_map/ppermute | solution.py:68
  49.9 1.2 %collective-permute-done.18.refs_13_ = f32[64,256]{1,0:T(8,128)S(1)} collective-permute-done((f32[64,256]{1,0:T(8,128)S(1)}, f32[64,256]{1,0:T(8,128)S(1)}, u32[]{:S(2)}, u32[]{:S(2)}) %collective-permute-start.18) | collective-permute-done | bytes 65568 | tf_op jit(solution)/shard_map/ppermute | solution.py:68
  51.2 4.5 %local_backward.1 = (f32[8,256,256]{2,1,0:T(8,128)}, f32[64,256]{1,0:T(8,128)}) custom-call(s32[8]{0:T(128)} %refs_0_.5, f32[8,256,256]{2,1,0:T(8,128)S(1)} %get-tuple-element.68.refs_1_, bf16[4,256,256]{2,1,0:T(8,128)(2,1)S(1)} %get-tuple-element.58.refs_4_.refs_2_, bf16[4,256,256]{2,1,0:T(8,128)(2,1)S(1)} %get-tuple-element.59.refs_5_.refs_3_, ...), custom_call_target="tpu_custom_call" | custom-call | tf_op jit(solution)/shard_map/local_backward/pallas_call | solution.py:278
  (29 shorter events, 6.9 us)
Async XLA Ops:
  1.5 7.3 %collective-permute-start.1 = (f32[2,64,256]{2,1,0:T(8,128)S(1)}, f32[2,64,256]{2,1,0:T(8,128)S(1)}, u32[]{:S(2)}, u32[]{:S(2)}) collective-permute-start(f32[2,64,256]{2,1,0:T(8,128)S(1)} %stack.1.refs_5_.refs_0_), channel_id=1, source_target_pairs={{0,2},{1,3},{2,0},{3,1},{4,6},{5,7},{6,4},{7,5},{8,10},{9,11},{10,... | collective-permute-start | bytes 393224 | tf_op jit(solution)/shard_map/ppermute | solution.py:68
  4.5 5.5 %collective-permute-start = (f32[2,64,256]{2,1,0:T(8,128)S(1)}, f32[2,64,256]{2,1,0:T(8,128)S(1)}, u32[]{:S(2)}, u32[]{:S(2)}) collective-permute-start(f32[2,64,256]{2,1,0:T(8,128)S(1)} %stack.1.refs_5_.refs_0_), channel_id=1, source_target_pairs={{0,1},{1,0},{2,3},{3,2},{4,5},{5,4},{6,7},{7,6},{8,9},{9,8},{10,11... | collective-permute-start | bytes 393224 | tf_op jit(solution)/shard_map/ppermute | solution.py:68
  8.8 1.6 %collective-permute-start.2 = (f32[2,64,256]{2,1,0:T(8,128)S(1)}, f32[2,64,256]{2,1,0:T(8,128)S(1)}, u32[]{:S(2)}, u32[]{:S(2)}) collective-permute-start(f32[2,64,256]{2,1,0:T(8,128)S(1)} %collective-permute-done.1.refs_2_), channel_id=1, source_target_pairs={{0,1},{1,0},{2,3},{3,2},{4,5},{5,4},{6,7},{7,6},{8,9},{9,8},{10,11... | collective-permute-start | bytes 393224 | tf_op jit(solution)/shard_map/ppermute | solution.py:68
  10.7 5.8 %collective-permute-start.3 = (f32[1,128,256]{2,1,0:T(8,128)S(1)}, f32[1,128,256]{2,1,0:T(8,128)S(1)}, u32[]{:S(2)}, u32[]{:S(2)}) collective-permute-start(f32[1,128,256]{2,1,0:T(8,128)S(1)} %get-tuple-element.70), channel_id=1, source_target_pairs={{0,4},{4,0},{8,12},{12,8},{16,20},{20,16},{24,28},{28,24},{1,5},{5... | collective-permute-start | bytes 393224 | tf_op jit(solution)/shard_map/ppermute | solution.py:68
  16.5 1.3 %collective-permute-start.4 = (f32[128,256]{1,0:T(8,128)S(1)}, f32[128,256]{1,0:T(8,128)S(1)}, u32[]{:S(2)}, u32[]{:S(2)}) collective-permute-start(f32[128,256]{1,0:T(8,128)S(1)} %get-tuple-element.72), channel_id=1, source_target_pairs={{0,1},{1,0},{2,3},{3,2},{4,5},{5,4},{6,7},{7,6},{8,9},{9,8},{10,11... | collective-permute-start | bytes 393224 | tf_op jit(solution)/shard_map/ppermute | solution.py:68
  16.5 2.1 %collective-permute-start.7 = (f32[1,128,256]{2,1,0:T(8,128)S(1)}, f32[1,128,256]{2,1,0:T(8,128)S(1)}, u32[]{:S(2)}, u32[]{:S(2)}) collective-permute-start(f32[1,128,256]{2,1,0:T(8,128)S(1)} %collective-permute-done.3.refs_1_), channel_id=1, source_target_pairs={{0,1},{1,0},{2,3},{3,2},{4,5},{5,4},{6,7},{7,6},{8,9},{9,8},{10,11... | collective-permute-start | bytes 393224 | tf_op jit(solution)/shard_map/ppermute | solution.py:68
  17.9 4.3 %collective-permute-start.5 = (f32[64,256]{1,0:T(8,128)S(1)}, f32[64,256]{1,0:T(8,128)S(1)}, u32[]{:S(2)}, u32[]{:S(2)}) collective-permute-start(f32[64,256]{1,0:T(8,128)S(1)} %get-tuple-element.74.refs_3_), channel_id=1, source_target_pairs={{0,2},{1,3},{2,0},{3,1},{4,6},{5,7},{6,4},{7,5},{8,10},{9,11},{10,... | collective-permute-start | bytes 196616 | tf_op jit(solution)/shard_map/ppermute | solution.py:68
  19.7 9.5 %collective-permute-start.8 = (f32[2,128,128]{2,1,0:T(8,128)S(1)}, f32[2,128,128]{2,1,0:T(8,128)S(1)}, u32[]{:S(2)}, u32[]{:S(2)}) collective-permute-start(f32[2,128,128]{2,1,0:T(8,128)S(1)} %get-tuple-element.84), channel_id=1, source_target_pairs={{0,8},{4,12},{8,0},{12,4},{16,24},{20,28},{24,16},{28,20},{1,9},{5... | collective-permute-start | bytes 393224 | tf_op jit(solution)/shard_map/ppermute | solution.py:68
  22.7 7.8 %collective-permute-start.6 = (f32[128,256]{1,0:T(8,128)S(1)}, f32[128,256]{1,0:T(8,128)S(1)}, u32[]{:S(2)}, u32[]{:S(2)}) collective-permute-start(f32[128,256]{1,0:T(8,128)S(1)} %get-tuple-element.77.refs_1_), channel_id=1, source_target_pairs={{0,4},{4,0},{8,12},{12,8},{16,20},{20,16},{24,28},{28,24},{1,5},{5... | collective-permute-start | bytes 393224 | tf_op jit(solution)/shard_map/ppermute | solution.py:68
  24.2 5.0 %collective-permute-start.9 = (f32[1,128,128]{2,1,0:T(8,128)S(1)}, f32[1,128,128]{2,1,0:T(8,128)S(1)}, u32[]{:S(2)}, u32[]{:S(2)}) collective-permute-start(f32[1,128,128]{2,1,0:T(8,128)S(1)} %get-tuple-element.85), channel_id=1, source_target_pairs={{0,8},{4,12},{8,0},{12,4},{16,24},{20,28},{24,16},{28,20},{1,9},{5... | collective-permute-start | bytes 196616 | tf_op jit(solution)/shard_map/ppermute | solution.py:68
  25.8 7.8 %collective-permute-start.11 = (f32[128,256]{1,0:T(8,128)S(1)}, f32[128,256]{1,0:T(8,128)S(1)}, u32[]{:S(2)}, u32[]{:S(2)}) collective-permute-start(f32[128,256]{1,0:T(8,128)S(1)} %get-tuple-element.89), channel_id=1, source_target_pairs={{0,8},{4,12},{8,0},{12,4},{16,24},{20,28},{24,16},{28,20},{1,9},{5... | collective-permute-start | bytes 393224 | tf_op jit(solution)/shard_map/ppermute | solution.py:68
  26.3 7.6 %collective-permute-start.12 = (f32[128,256]{1,0:T(8,128)S(1)}, f32[128,256]{1,0:T(8,128)S(1)}, u32[]{:S(2)}, u32[]{:S(2)}) collective-permute-start(f32[128,256]{1,0:T(8,128)S(1)} %get-tuple-element.90), channel_id=1, source_target_pairs={{0,8},{4,12},{8,0},{12,4},{16,24},{20,28},{24,16},{28,20},{1,9},{5... | collective-permute-start | bytes 393224 | tf_op jit(solution)/shard_map/ppermute | solution.py:68
  29.9 10.7 %collective-permute-start.14 = (f32[3,128,128]{2,1,0:T(8,128)S(1)}, f32[3,128,128]{2,1,0:T(8,128)S(1)}, u32[]{:S(2)}, u32[]{:S(2)}) collective-permute-start(f32[3,128,128]{2,1,0:T(8,128)S(1)} %boundary.1.refs_7_), channel_id=1, source_target_pairs={{8,16},{12,20},{16,8},{20,12},{0,4},{4,0},{24,28},{28,24},{9,17},{... | collective-permute-start | bytes 589832 | tf_op jit(solution)/shard_map/ppermute | solution.py:604
  30.9 5.0 %collective-permute-start.10 = (f32[64,256]{1,0:T(8,128)S(1)}, f32[64,256]{1,0:T(8,128)S(1)}, u32[]{:S(2)}, u32[]{:S(2)}) collective-permute-start(f32[64,256]{1,0:T(8,128)S(1)} %get-tuple-element.88), channel_id=1, source_target_pairs={{0,8},{4,12},{8,0},{12,4},{16,24},{20,28},{24,16},{28,20},{1,9},{5... | collective-permute-start | bytes 196616 | tf_op jit(solution)/shard_map/ppermute | solution.py:68
  36.3 4.3 %collective-permute-start.13 = (f32[64,256]{1,0:T(8,128)S(1)}, f32[64,256]{1,0:T(8,128)S(1)}, u32[]{:S(2)}, u32[]{:S(2)}) collective-permute-start(f32[64,256]{1,0:T(8,128)S(1)} %get-tuple-element.98), channel_id=1, source_target_pairs={{8,16},{12,20},{16,8},{20,12},{0,4},{4,0},{24,28},{28,24},{9,17},{... | collective-permute-start | bytes 196616 | tf_op jit(solution)/shard_map/ppermute | solution.py:621
  40.9 4.3 %collective-permute-start.15 = (f32[64,256]{1,0:T(8,128)S(1)}, f32[64,256]{1,0:T(8,128)S(1)}, u32[]{:S(2)}, u32[]{:S(2)}) collective-permute-start(f32[64,256]{1,0:T(8,128)S(1)} %turn.1.refs_1_), channel_id=1, source_target_pairs={{0,8},{4,12},{8,0},{12,4},{16,24},{20,28},{24,16},{28,20},{1,9},{5... | collective-permute-start | bytes 196616 | tf_op jit(solution)/shard_map/ppermute | solution.py:68
  45.6 4.3 %collective-permute-start.17 = (f32[64,256]{1,0:T(8,128)S(1)}, f32[64,256]{1,0:T(8,128)S(1)}, u32[]{:S(2)}, u32[]{:S(2)}) collective-permute-start(f32[64,256]{1,0:T(8,128)S(1)} %leave.1.refs_10_), channel_id=1, source_target_pairs={{0,2},{1,3},{2,0},{3,1},{4,6},{5,7},{6,4},{7,5},{8,10},{9,11},{10,... | collective-permute-start | bytes 196616 | tf_op jit(solution)/shard_map/ppermute | solution.py:68
  46.2 3.7 %collective-permute-start.16 = (f32[64,256]{1,0:T(8,128)S(1)}, f32[64,256]{1,0:T(8,128)S(1)}, u32[]{:S(2)}, u32[]{:S(2)}) collective-permute-start(f32[64,256]{1,0:T(8,128)S(1)} %leave.1.refs_10_), channel_id=1, source_target_pairs={{0,1},{1,0},{2,3},{3,2},{4,5},{5,4},{6,7},{7,6},{8,9},{9,8},{10,11... | collective-permute-start | bytes 196616 | tf_op jit(solution)/shard_map/ppermute | solution.py:68
  49.9 1.3 %collective-permute-start.18 = (f32[64,256]{1,0:T(8,128)S(1)}, f32[64,256]{1,0:T(8,128)S(1)}, u32[]{:S(2)}, u32[]{:S(2)}) collective-permute-start(f32[64,256]{1,0:T(8,128)S(1)} %collective-permute-done.17.refs_12_), channel_id=1, source_target_pairs={{0,1},{1,0},{2,3},{3,2},{4,5},{5,4},{6,7},{7,6},{8,9},{9,8},{10,11... | collective-permute-start | bytes 196616 | tf_op jit(solution)/shard_map/ppermute | solution.py:68

commit v12 on v11

--- a/solution.py
+++ b/solution.py
@@ -371,9 +371,9 @@
 
 
 def send_maps(parts, k, t):
-    parts[0][0], parts[0][1], parts[-1][0] = k_blocks(k)
-    half = t.shape[0] // 2
-    parts[1][...], parts[2][...] = t[:half], t[half:]
+    for i, block in enumerate(k_blocks(k)):
+        parts[0][i] = block
+    send_blocks(parts[1:], quarters(t))
 
 
 def first_merge_kernel(*refs):
@@ -404,11 +404,11 @@
 
 
 def merge_kernel(bit, last, *refs):
-    own, other, rest, first_t, second_t, mixed = refs[:6]
-    kept, mixed_n, halves, curve_u, total_u, total_l, *parts = refs[6:]
+    own, other, mine, pairs, mixed = refs[:5]
+    kept, mixed_n, halves, curve_u, total_u, total_l, *parts = refs[5:]
     upper = bit_of("leaf", bit) == 1
     own_k, own_t = own[0], own[1]
-    other_k, other_t = k_of([other[0], other[1], rest[0]]), jnp.concatenate([first_t[...], second_t[...]], axis=0)
+    other_k, other_t = k_of(other), joined(*came_blocks([mine], [pairs], 4))
     low_s = split(jnp.where(upper, other_t, own_t))
     up_s = split(jnp.where(upper, own_t, other_t))
     k_low = jnp.where(upper, other_k, own_k)
@@ -433,9 +433,9 @@
         mixed_n[0], mixed_n[1] = a_n, e_n
 
 
-def boundary_kernel(own, other, rest, blocks):
+def boundary_kernel(own, other, blocks):
     k, t = own[0], split(own[1])
-    x = dot3(split(k_of([other[0], other[1], rest[0]])), t, NN)
+    x = dot3(split(k_of(other)), t, NN)
     for i, block in enumerate(k_blocks(k + dot3(t, split(x), TN))):
         blocks[i] = block
 
@@ -445,7 +445,7 @@
     half = size // 2
     if last:
         return [((8, 128), F32)] + [both] * 5
-    sends = [((2, half, half), F32)] + [((half, size), F32)] * 2 + [((1, half, half), F32)]
+    sends = [((i, half, half), F32) for i in (3, 2)]
     return [whole, whole, both, both, both, both] + sends
 
 
@@ -592,14 +592,11 @@
         received = exchange(short[0] if last else message, "leaf", bit)
         ahead = []
         if not last:
-            other, *came_t, rest = [exchange(part, "leaf", bit + 1) for part in parts]
+            other, mine = [exchange(part, "leaf", bit + 1) for part in parts]
             ahead = [other]
         if bit == rounds - 3:
             ahead = (blocks,) = call(
-                boundary_kernel,
-                "boundary",
-                [(V, kept), (V, other), (V, rest)],
-                [((3, size // 2, size // 2), F32)],
+                boundary_kernel, "boundary", [(V, kept), (V, other)], [(other.shape, F32)]
             )
             blocks = lax.ppermute(blocks, "leaf", boundary)
         sol, *message = call(
@@ -610,11 +607,13 @@
         )
         if not last:
             message, *short = message
+            mine, _ = lax.optimization_barrier((mine, sol))
+            pairs = exchange(mine, "front", 0)
             last = bit == rounds - 3
             kept, mixed, *tools = call(
                 lambda *refs, bit=bit, last=last: merge_kernel(bit + 1, last, *refs),
                 f"merge_{bit + 1}",
-                [(V, a) for a in (kept, other, rest, *came_t, mixed)],
+                [(V, a) for a in (kept, other, mine, pairs, mixed)],
                 maps(size, last),
             )
             tools, parts = tools[:4], tools[4:]

time: 55.9 us -> 54.9 us (0.982)
  starting transfers between devices: 20.2 us -> 19.2 us
    ppermute x17 -> x16, starting transfers between devices: 18.7 us -> 16.4 us  [swap(): return lax.ppermute(x, axis, [(i, i ^ mask) for i in range(n)])]
    ppermute x1, starting transfers between devices: 0.57 us -> 1.38 us  [local(): blocks = lax.ppermute(blocks, 'leaf', boundary)]
    ppermute x17 -> x16, waiting for transfers between devices: 11.7 us -> 12.2 us  [swap(): return lax.ppermute(x, axis, [(i, i ^ mask) for i in range(n)])]
  transfers between devices with their start and end apart: 19 -> 18, of which waited for: 11 -> 11; matrix products, arithmetic and copies ran while one was open for 0% -> 0% of each run, Pallas kernels for 24% -> 24%
where the time goes in v12:
time: 54.9 us; the launch traced here: 54.7 us
  Pallas kernels  19.7 us (36%)
  starting transfers between devices  19.2 us (35%)
  waiting for transfers between devices  15.1 us (28%)
  between operations  0.76 us (1%)
    ppermute x16, starting transfers between devices, swap(): return lax.ppermute(x, axis, [(i, i ^ mask) for i in range(n)])  16.4 us
    pallas_call x14, Pallas kernels, call(): pl.pallas_call(kernel, name=name, in_specs=specs, out_specs=tuple((pl.Blo...  15.2 us
    ppermute x16, waiting for transfers between devices, swap(): return lax.ppermute(x, axis, [(i, i ^ mask) for i in range(n)])  12.2 us
    pallas_call x1, Pallas kernels, local_backward(): pl.pallas_call(lambda *refs: backward_kernel(nodes, fronts, *refs), name=...  4.55 us
    ppermute x1, waiting for transfers between devices, local(): came = lax.ppermute(message[0], 'leaf', boundary)  2.9 us
    ppermute x1, starting transfers between devices, local(): came = lax.ppermute(message[0], 'leaf', boundary)  1.43 us
    ppermute x1, starting transfers between devices, local(): blocks = lax.ppermute(blocks, 'leaf', boundary)  1.38 us
  transfers between devices with their start and end apart: 18, of which 11 were waited for; matrix products, arithmetic and copies ran while one was open for 0% of the time, Pallas kernels for 24%

profile of v12, /device:TPU:0, one launch (start us, length us, event | category | flops | bytes accessed | tf_op | source)
XLA Modules:
  0.0 54.7 jit_solution(14166641514309365139)
XLA Ops:
  0.6 0.9 %stack.1.refs_5_.refs_0_ = f32[2,64,256]{2,1,0:T(8,128)S(1)} custom-call(f32[64,256]{1,0:T(8,128)} %first.1, f32[64,256]{1,0:T(8,128)} %second.1), custom_call_target="tpu_custom_call" | custom-call | tf_op jit(solution)/shard_map/stack/pallas_call | solution.py:51
  1.5 3.0 %collective-permute-start.1 = (f32[2,64,256]{2,1,0:T(8,128)S(1)}, f32[2,64,256]{2,1,0:T(8,128)S(1)}, u32[]{:S(2)}, u32[]{:S(2)}) collective-permute-start(f32[2,64,256]{2,1,0:T(8,128)S(1)} %stack.1.refs_5_.refs_0_), channel_id=1, source_target_pairs={{0,2},{1,3},{2,0},{3,1},{4,6},{5,7},{6,4},{7,5},{8,10},{9,11},{10,... | collective-permute-start | bytes 393224 | tf_op jit(solution)/shard_map/ppermute | solution.py:68
  4.5 4.3 %prepare_first.1 = (f32[2,4,128,256]{3,2,1,0:T(8,128)S(1)}, bf16[4,256,256]{2,1,0:T(8,128)(2,1)S(1)}, bf16[4,256,256]{2,1,0:T(8,128)(2,1)S(1)}, bf16[4,256,256]{...) custom-call(s32[8,256]{1,0:T(8,128)} %refs_0_.3, ...), custom_call_target="tpu_custom_call" | custom-call | tf_op jit(solution)/shard_map/prepare_first/pallas_call | solution.py:51
  10.7 1.6 %collective-permute-start.3 = (f32[1,128,256]{2,1,0:T(8,128)S(1)}, f32[1,128,256]{2,1,0:T(8,128)S(1)}, u32[]{:S(2)}, u32[]{:S(2)}) collective-permute-start(f32[1,128,256]{2,1,0:T(8,128)S(1)} %get-tuple-element.69), channel_id=1, source_target_pairs={{0,4},{4,0},{8,12},{12,8},{16,20},{20,16},{24,28},{28,24},{1,5},{5... | collective-permute-start | bytes 393224 | tf_op jit(solution)/shard_map/ppermute | solution.py:68
  12.3 4.1 %local_forward.1 = (f32[8,256,256]{2,1,0:T(8,128)S(1)}, f32[128,256]{1,0:T(8,128)S(1)}, f32[128,256]{1,0:T(8,128)S(1)}) custom-call(s32[8]{0:T(128)} %refs_0_.5, f32[2,4,128,256]{3,2,1,0:T(8,128)S(1)} %get-tuple-element.50.refs_4_.refs_1_, f32[2,4,128,256]{3,2,1,0:T(8,128)S(1)} %get-tuple-element.55.refs_4_.refs_2_, ...), custom_call_target="tpu_custom_call" | custom-call | tf_op jit(solution)/shard_map/local_forward/pallas_call | solution.py:51
  18.7 1.0 %merge_0.1 = (f32[2,256,256]{2,1,0:T(8,128)S(1)}, f32[2,256,256]{2,1,0:T(8,128)S(1)}, bf16[2,256,256]{2,1,0:T(8,128)(2,1)S(1)}, bf16[2,256,256]{2,1,0:T(8,128)(2...) custom-call(f32[256,256]{1,0:T(8,128)S(1)} %get-tuple-element.66.ref, ...), custom_call_target="tpu_custom_call" | custom-call | tf_op jit(solution)/shard_map/merge_0/pallas_call | solution.py:51
  19.7 1.6 %collective-permute-start.8 = (f32[3,128,128]{2,1,0:T(8,128)S(1)}, f32[3,128,128]{2,1,0:T(8,128)S(1)}, u32[]{:S(2)}, u32[]{:S(2)}) collective-permute-start(f32[3,128,128]{2,1,0:T(8,128)S(1)} %get-tuple-element.83), channel_id=1, source_target_pairs={{0,8},{4,12},{8,0},{12,4},{16,24},{20,28},{24,16},{28,20},{1,9},{5... | collective-permute-start | bytes 589832 | tf_op jit(solution)/shard_map/ppermute | solution.py:68
  21.3 0.9 %collective-permute-done.5.other = f32[64,256]{1,0:T(8,128)S(1)} collective-permute-done((f32[64,256]{1,0:T(8,128)S(1)}, f32[64,256]{1,0:T(8,128)S(1)}, u32[]{:S(2)}, u32[]{:S(2)}) %collective-permute-start.5) | collective-permute-done | bytes 65568 | tf_op jit(solution)/shard_map/ppermute | solution.py:68
  22.7 1.6 %collective-permute-start.6 = (f32[128,256]{1,0:T(8,128)S(1)}, f32[128,256]{1,0:T(8,128)S(1)}, u32[]{:S(2)}, u32[]{:S(2)}) collective-permute-start(f32[128,256]{1,0:T(8,128)S(1)} %get-tuple-element.76.refs_1_), channel_id=1, source_target_pairs={{0,4},{4,0},{8,12},{12,8},{16,20},{20,16},{24,28},{28,24},{1,5},{5... | collective-permute-start | bytes 393224 | tf_op jit(solution)/shard_map/ppermute | solution.py:68
  24.2 1.6 %collective-permute-start.10 = (f32[2,128,128]{2,1,0:T(8,128)S(1)}, f32[2,128,128]{2,1,0:T(8,128)S(1)}, u32[]{:S(2)}, u32[]{:S(2)}) collective-permute-start(f32[2,128,128]{2,1,0:T(8,128)S(1)} %get-tuple-element.87), channel_id=1, source_target_pairs={{0,8},{4,12},{8,0},{12,4},{16,24},{20,28},{24,16},{28,20},{1,9},{5... | collective-permute-start | bytes 393224 | tf_op jit(solution)/shard_map/ppermute | solution.py:68
  25.8 1.4 %collective-permute-done.8.other.refs_1_ = f32[3,128,128]{2,1,0:T(8,128)S(1)} collective-permute-done((f32[3,128,128]{2,1,0:T(8,128)S(1)}, f32[3,128,128]{2,1,0:T(8,128)S(1)}, u32[]{:S(2)}, u32[]{:S(2)}) %collective-permute-start.8) | collective-permute-done | bytes 196640 | tf_op jit(solution)/shard_map/ppermute | solution.py:68
  28.4 0.9 %collective-permute-done.10.refs_2_ = f32[2,128,128]{2,1,0:T(8,128)S(1)} collective-permute-done((f32[2,128,128]{2,1,0:T(8,128)S(1)}, f32[2,128,128]{2,1,0:T(8,128)S(1)}, u32[]{:S(2)}, u32[]{:S(2)}) %collective-permute-start.10) | collective-permute-done | bytes 131104 | tf_op jit(solution)/shard_map/ppermute | solution.py:68
  29.2 1.4 %collective-permute-start.13 = (f32[3,128,128]{2,1,0:T(8,128)S(1)}, f32[3,128,128]{2,1,0:T(8,128)S(1)}, u32[]{:S(2)}, u32[]{:S(2)}) collective-permute-start(f32[3,128,128]{2,1,0:T(8,128)S(1)} %boundary.1.refs_7_), channel_id=1, source_target_pairs={{8,16},{12,20},{16,8},{20,12},{0,4},{4,0},{24,28},{28,24},{9,17},{... | collective-permute-start | bytes 589832 | tf_op jit(solution)/shard_map/ppermute | solution.py:601
  30.6 1.8 %collective-permute-start.9 = (f32[64,256]{1,0:T(8,128)S(1)}, f32[64,256]{1,0:T(8,128)S(1)}, u32[]{:S(2)}, u32[]{:S(2)}) collective-permute-start(f32[64,256]{1,0:T(8,128)S(1)} %get-tuple-element.86), channel_id=1, source_target_pairs={{0,8},{4,12},{8,0},{12,4},{16,24},{20,28},{24,16},{28,20},{1,9},{5... | collective-permute-start | bytes 196616 | tf_op jit(solution)/shard_map/ppermute | solution.py:68
  32.4 1.3 %merge_1.1 = (f32[8,128]{1,0:T(8,128)}, bf16[2,256,256]{2,1,0:T(8,128)(2,1)S(1)}, bf16[2,256,256]{2,1,0:T(8,128)(2,1)S(1)}, bf16[2,256,256]{2,1,0:T(8,128)(2,1)S...) custom-call(f32[2,256,256]{2,1,0:T(8,128)S(1)} %get-tuple-element.82.own.refs_0_, ...), custom_call_target="tpu_custom_call" | custom-call | tf_op jit(solution)/shard_map/merge_1/pallas_call | solution.py:51
  33.7 1.2 %collective-permute-done.9.refs_2_ = f32[64,256]{1,0:T(8,128)S(1)} collective-permute-done((f32[64,256]{1,0:T(8,128)S(1)}, f32[64,256]{1,0:T(8,128)S(1)}, u32[]{:S(2)}, u32[]{:S(2)}) %collective-permute-start.9) | collective-permute-done | bytes 65568 | tf_op jit(solution)/shard_map/ppermute | solution.py:68
  35.3 1.4 %collective-permute-start.12 = (f32[64,256]{1,0:T(8,128)S(1)}, f32[64,256]{1,0:T(8,128)S(1)}, u32[]{:S(2)}, u32[]{:S(2)}) collective-permute-start(f32[64,256]{1,0:T(8,128)S(1)} %get-tuple-element.96), channel_id=1, source_target_pairs={{8,16},{12,20},{16,8},{20,12},{0,4},{4,0},{24,28},{28,24},{9,17},{... | collective-permute-start | bytes 196616 | tf_op jit(solution)/shard_map/ppermute | solution.py:620
  36.8 2.9 %collective-permute-done.12.refs_1_ = f32[64,256]{1,0:T(8,128)S(1)} collective-permute-done((f32[64,256]{1,0:T(8,128)S(1)}, f32[64,256]{1,0:T(8,128)S(1)}, u32[]{:S(2)}, u32[]{:S(2)}) %collective-permute-start.12) | collective-permute-done | bytes 65568 | tf_op jit(solution)/shard_map/ppermute | solution.py:620
  39.9 1.8 %collective-permute-start.14 = (f32[64,256]{1,0:T(8,128)S(1)}, f32[64,256]{1,0:T(8,128)S(1)}, u32[]{:S(2)}, u32[]{:S(2)}) collective-permute-start(f32[64,256]{1,0:T(8,128)S(1)} %turn.1.refs_1_), channel_id=1, source_target_pairs={{0,8},{4,12},{8,0},{12,4},{16,24},{20,28},{24,16},{28,20},{1,9},{5... | collective-permute-start | bytes 196616 | tf_op jit(solution)/shard_map/ppermute | solution.py:68
  41.8 2.5 %collective-permute-done.14.refs_2_ = f32[64,256]{1,0:T(8,128)S(1)} collective-permute-done((f32[64,256]{1,0:T(8,128)S(1)}, f32[64,256]{1,0:T(8,128)S(1)}, u32[]{:S(2)}, u32[]{:S(2)}) %collective-permute-start.14) | collective-permute-done | bytes 65568 | tf_op jit(solution)/shard_map/ppermute | solution.py:68
  44.6 1.5 %collective-permute-start.16 = (f32[64,256]{1,0:T(8,128)S(1)}, f32[64,256]{1,0:T(8,128)S(1)}, u32[]{:S(2)}, u32[]{:S(2)}) collective-permute-start(f32[64,256]{1,0:T(8,128)S(1)} %leave.1.refs_10_), channel_id=1, source_target_pairs={{0,2},{1,3},{2,0},{3,1},{4,6},{5,7},{6,4},{7,5},{8,10},{9,11},{10,... | collective-permute-start | bytes 196616 | tf_op jit(solution)/shard_map/ppermute | solution.py:68
  46.2 2.8 %collective-permute-done.16.refs_12_ = f32[64,256]{1,0:T(8,128)S(1)} collective-permute-done((f32[64,256]{1,0:T(8,128)S(1)}, f32[64,256]{1,0:T(8,128)S(1)}, u32[]{:S(2)}, u32[]{:S(2)}) %collective-permute-start.16) | collective-permute-done | bytes 65568 | tf_op jit(solution)/shard_map/ppermute | solution.py:68
  49.0 1.2 %collective-permute-done.17.refs_13_ = f32[64,256]{1,0:T(8,128)S(1)} collective-permute-done((f32[64,256]{1,0:T(8,128)S(1)}, f32[64,256]{1,0:T(8,128)S(1)}, u32[]{:S(2)}, u32[]{:S(2)}) %collective-permute-start.17) | collective-permute-done | bytes 65568 | tf_op jit(solution)/shard_map/ppermute | solution.py:68
  50.2 4.5 %local_backward.1 = (f32[8,256,256]{2,1,0:T(8,128)}, f32[64,256]{1,0:T(8,128)}) custom-call(s32[8]{0:T(128)} %refs_0_.5, f32[8,256,256]{2,1,0:T(8,128)S(1)} %get-tuple-element.67.refs_1_, bf16[4,256,256]{2,1,0:T(8,128)(2,1)S(1)} %get-tuple-element.57.refs_4_.refs_2_, bf16[4,256,256]{2,1,0:T(8,128)(2,1)S(1)} %get-tuple-element.58.refs_5_.refs_3_, ...), custom_call_target="tpu_custom_call" | custom-call | tf_op jit(solution)/shard_map/local_backward/pallas_call | solution.py:278
  (27 shorter events, 6.7 us)
Async XLA Ops:
  1.5 7.3 %collective-permute-start.1 = (f32[2,64,256]{2,1,0:T(8,128)S(1)}, f32[2,64,256]{2,1,0:T(8,128)S(1)}, u32[]{:S(2)}, u32[]{:S(2)}) collective-permute-start(f32[2,64,256]{2,1,0:T(8,128)S(1)} %stack.1.refs_5_.refs_0_), channel_id=1, source_target_pairs={{0,2},{1,3},{2,0},{3,1},{4,6},{5,7},{6,4},{7,5},{8,10},{9,11},{10,... | collective-permute-start | bytes 393224 | tf_op jit(solution)/shard_map/ppermute | solution.py:68
  4.5 5.5 %collective-permute-start = (f32[2,64,256]{2,1,0:T(8,128)S(1)}, f32[2,64,256]{2,1,0:T(8,128)S(1)}, u32[]{:S(2)}, u32[]{:S(2)}) collective-permute-start(f32[2,64,256]{2,1,0:T(8,128)S(1)} %stack.1.refs_5_.refs_0_), channel_id=1, source_target_pairs={{0,1},{1,0},{2,3},{3,2},{4,5},{5,4},{6,7},{7,6},{8,9},{9,8},{10,11... | collective-permute-start | bytes 393224 | tf_op jit(solution)/shard_map/ppermute | solution.py:68
  8.8 1.6 %collective-permute-start.2 = (f32[2,64,256]{2,1,0:T(8,128)S(1)}, f32[2,64,256]{2,1,0:T(8,128)S(1)}, u32[]{:S(2)}, u32[]{:S(2)}) collective-permute-start(f32[2,64,256]{2,1,0:T(8,128)S(1)} %collective-permute-done.1.refs_2_), channel_id=1, source_target_pairs={{0,1},{1,0},{2,3},{3,2},{4,5},{5,4},{6,7},{7,6},{8,9},{9,8},{10,11... | collective-permute-start | bytes 393224 | tf_op jit(solution)/shard_map/ppermute | solution.py:68
  10.7 5.8 %collective-permute-start.3 = (f32[1,128,256]{2,1,0:T(8,128)S(1)}, f32[1,128,256]{2,1,0:T(8,128)S(1)}, u32[]{:S(2)}, u32[]{:S(2)}) collective-permute-start(f32[1,128,256]{2,1,0:T(8,128)S(1)} %get-tuple-element.69), channel_id=1, source_target_pairs={{0,4},{4,0},{8,12},{12,8},{16,20},{20,16},{24,28},{28,24},{1,5},{5... | collective-permute-start | bytes 393224 | tf_op jit(solution)/shard_map/ppermute | solution.py:68
  16.5 1.3 %collective-permute-start.4 = (f32[128,256]{1,0:T(8,128)S(1)}, f32[128,256]{1,0:T(8,128)S(1)}, u32[]{:S(2)}, u32[]{:S(2)}) collective-permute-start(f32[128,256]{1,0:T(8,128)S(1)} %get-tuple-element.71), channel_id=1, source_target_pairs={{0,1},{1,0},{2,3},{3,2},{4,5},{5,4},{6,7},{7,6},{8,9},{9,8},{10,11... | collective-permute-start | bytes 393224 | tf_op jit(solution)/shard_map/ppermute | solution.py:68
  16.5 2.1 %collective-permute-start.7 = (f32[1,128,256]{2,1,0:T(8,128)S(1)}, f32[1,128,256]{2,1,0:T(8,128)S(1)}, u32[]{:S(2)}, u32[]{:S(2)}) collective-permute-start(f32[1,128,256]{2,1,0:T(8,128)S(1)} %collective-permute-done.3.refs_1_), channel_id=1, source_target_pairs={{0,1},{1,0},{2,3},{3,2},{4,5},{5,4},{6,7},{7,6},{8,9},{9,8},{10,11... | collective-permute-start | bytes 393224 | tf_op jit(solution)/shard_map/ppermute | solution.py:68
  17.9 4.3 %collective-permute-start.5 = (f32[64,256]{1,0:T(8,128)S(1)}, f32[64,256]{1,0:T(8,128)S(1)}, u32[]{:S(2)}, u32[]{:S(2)}) collective-permute-start(f32[64,256]{1,0:T(8,128)S(1)} %get-tuple-element.73.refs_3_), channel_id=1, source_target_pairs={{0,2},{1,3},{2,0},{3,1},{4,6},{5,7},{6,4},{7,5},{8,10},{9,11},{10,... | collective-permute-start | bytes 196616 | tf_op jit(solution)/shard_map/ppermute | solution.py:68
  19.7 7.5 %collective-permute-start.8 = (f32[3,128,128]{2,1,0:T(8,128)S(1)}, f32[3,128,128]{2,1,0:T(8,128)S(1)}, u32[]{:S(2)}, u32[]{:S(2)}) collective-permute-start(f32[3,128,128]{2,1,0:T(8,128)S(1)} %get-tuple-element.83), channel_id=1, source_target_pairs={{0,8},{4,12},{8,0},{12,4},{16,24},{20,28},{24,16},{28,20},{1,9},{5... | collective-permute-start | bytes 589832 | tf_op jit(solution)/shard_map/ppermute | solution.py:68
  22.7 5.2 %collective-permute-start.6 = (f32[128,256]{1,0:T(8,128)S(1)}, f32[128,256]{1,0:T(8,128)S(1)}, u32[]{:S(2)}, u32[]{:S(2)}) collective-permute-start(f32[128,256]{1,0:T(8,128)S(1)} %get-tuple-element.76.refs_1_), channel_id=1, source_target_pairs={{0,4},{4,0},{8,12},{12,8},{16,20},{20,16},{24,28},{28,24},{1,5},{5... | collective-permute-start | bytes 393224 | tf_op jit(solution)/shard_map/ppermute | solution.py:68
  24.2 5.0 %collective-permute-start.10 = (f32[2,128,128]{2,1,0:T(8,128)S(1)}, f32[2,128,128]{2,1,0:T(8,128)S(1)}, u32[]{:S(2)}, u32[]{:S(2)}) collective-permute-start(f32[2,128,128]{2,1,0:T(8,128)S(1)} %get-tuple-element.87), channel_id=1, source_target_pairs={{0,8},{4,12},{8,0},{12,4},{16,24},{20,28},{24,16},{28,20},{1,9},{5... | collective-permute-start | bytes 393224 | tf_op jit(solution)/shard_map/ppermute | solution.py:68
  29.2 3.2 %collective-permute-start.11 = (f32[2,128,128]{2,1,0:T(8,128)S(1)}, f32[2,128,128]{2,1,0:T(8,128)S(1)}, u32[]{:S(2)}, u32[]{:S(2)}) collective-permute-start(f32[2,128,128]{2,1,0:T(8,128)S(1)} %collective-permute-done.10.refs_2_), channel_id=1, source_target_pairs={{0,1},{1,0},{2,3},{3,2},{4,5},{5,4},{6,7},{7,6},{8,9},{9,8},{10,11... | collective-permute-start | bytes 393224 | tf_op jit(solution)/shard_map/ppermute | solution.py:68
  29.2 10.4 %collective-permute-start.13 = (f32[3,128,128]{2,1,0:T(8,128)S(1)}, f32[3,128,128]{2,1,0:T(8,128)S(1)}, u32[]{:S(2)}, u32[]{:S(2)}) collective-permute-start(f32[3,128,128]{2,1,0:T(8,128)S(1)} %boundary.1.refs_7_), channel_id=1, source_target_pairs={{8,16},{12,20},{16,8},{20,12},{0,4},{4,0},{24,28},{28,24},{9,17},{... | collective-permute-start | bytes 589832 | tf_op jit(solution)/shard_map/ppermute | solution.py:601
  30.6 4.3 %collective-permute-start.9 = (f32[64,256]{1,0:T(8,128)S(1)}, f32[64,256]{1,0:T(8,128)S(1)}, u32[]{:S(2)}, u32[]{:S(2)}) collective-permute-start(f32[64,256]{1,0:T(8,128)S(1)} %get-tuple-element.86), channel_id=1, source_target_pairs={{0,8},{4,12},{8,0},{12,4},{16,24},{20,28},{24,16},{28,20},{1,9},{5... | collective-permute-start | bytes 196616 | tf_op jit(solution)/shard_map/ppermute | solution.py:68
  35.3 4.3 %collective-permute-start.12 = (f32[64,256]{1,0:T(8,128)S(1)}, f32[64,256]{1,0:T(8,128)S(1)}, u32[]{:S(2)}, u32[]{:S(2)}) collective-permute-start(f32[64,256]{1,0:T(8,128)S(1)} %get-tuple-element.96), channel_id=1, source_target_pairs={{8,16},{12,20},{16,8},{20,12},{0,4},{4,0},{24,28},{28,24},{9,17},{... | collective-permute-start | bytes 196616 | tf_op jit(solution)/shard_map/ppermute | solution.py:620
  39.9 4.3 %collective-permute-start.14 = (f32[64,256]{1,0:T(8,128)S(1)}, f32[64,256]{1,0:T(8,128)S(1)}, u32[]{:S(2)}, u32[]{:S(2)}) collective-permute-start(f32[64,256]{1,0:T(8,128)S(1)} %turn.1.refs_1_), channel_id=1, source_target_pairs={{0,8},{4,12},{8,0},{12,4},{16,24},{20,28},{24,16},{28,20},{1,9},{5... | collective-permute-start | bytes 196616 | tf_op jit(solution)/shard_map/ppermute | solution.py:68
  44.6 4.3 %collective-permute-start.16 = (f32[64,256]{1,0:T(8,128)S(1)}, f32[64,256]{1,0:T(8,128)S(1)}, u32[]{:S(2)}, u32[]{:S(2)}) collective-permute-start(f32[64,256]{1,0:T(8,128)S(1)} %leave.1.refs_10_), channel_id=1, source_target_pairs={{0,2},{1,3},{2,0},{3,1},{4,6},{5,7},{6,4},{7,5},{8,10},{9,11},{10,... | collective-permute-start | bytes 196616 | tf_op jit(solution)/shard_map/ppermute | solution.py:68
  46.2 2.8 %collective-permute-start.15 = (f32[64,256]{1,0:T(8,128)S(1)}, f32[64,256]{1,0:T(8,128)S(1)}, u32[]{:S(2)}, u32[]{:S(2)}) collective-permute-start(f32[64,256]{1,0:T(8,128)S(1)} %leave.1.refs_10_), channel_id=1, source_target_pairs={{0,1},{1,0},{2,3},{3,2},{4,5},{5,4},{6,7},{7,6},{8,9},{9,8},{10,11... | collective-permute-start | bytes 196616 | tf_op jit(solution)/shard_map/ppermute | solution.py:68
  48.9 1.3 %collective-permute-start.17 = (f32[64,256]{1,0:T(8,128)S(1)}, f32[64,256]{1,0:T(8,128)S(1)}, u32[]{:S(2)}, u32[]{:S(2)}) collective-permute-start(f32[64,256]{1,0:T(8,128)S(1)} %collective-permute-done.16.refs_12_), channel_id=1, source_target_pairs={{0,1},{1,0},{2,3},{3,2},{4,5},{5,4},{6,7},{7,6},{8,9},{9,8},{10,11... | collective-permute-start | bytes 196616 | tf_op jit(solution)/shard_map/ppermute | solution.py:68

commit v13 on v12

--- a/solution.py
+++ b/solution.py
@@ -72,27 +72,37 @@
     return swap(x, axis, 1 << bit)
 
 
-def prepare_nodes(count, rows_at, row_columns, dinv, upd, rhs, outs, waits):
-    acc, inv_hi, inv_lo, upd_hi, upd_lo = outs
+def node_copies(nodes, sources, targets, sems):
+    copies = []
+    for i, k in enumerate(nodes):
+        group = [
+            pltpu.make_async_copy(src.at[k], dst.at[i], sems.at[j, i])
+            for j, (src, dst) in enumerate(zip(sources, targets))
+        ]
+        for c in group:
+            c.start()
+        copies.append(group)
+    return copies
+
+
+def prepare_node(node, k, waits, row_columns, values, halves):
+    upd, dinv, rhs = values
+    inv_hi, inv_lo, upd_hi, upd_lo = halves
     size = dinv.shape[1]
-    width = acc.shape[2]
+    for c in waits:
+        c.wait()
     lane = lax.broadcasted_iota(jnp.int32, (size, size), 1).astype(F32)
-    for k in range(count):
-        for c in waits[k]:
-            c.wait()
-        inv_hi[k], inv_lo[k] = split(dinv[k])
-        high, low = split(upd[k])
-        chosen = (lane == row_columns[:, rows_at + k : rows_at + k + 1]).astype(BF16)
-        upd_hi[k] = dot1(chosen, high, NN).astype(BF16)
-        upd_lo[k] = dot1(chosen, low, NN).astype(BF16)
-        turned = rhs[k].T
-        for h in range(HALVES):
-            acc[h, k] = turned[h * width : (h + 1) * width]
+    inv_hi[k], inv_lo[k] = split(dinv[k])
+    high, low = split(upd[k])
+    chosen = (lane == row_columns[:, node : node + 1]).astype(BF16)
+    upd_hi[k] = dot1(chosen, high, NN).astype(BF16)
+    upd_lo[k] = dot1(chosen, low, NN).astype(BF16)
+    return rhs[k].T
 
 
 def prepare_first_kernel(nodes, *refs):
     (rows_h, sep_h, rhs_h, dinv_h, upd_h, _), refs = refs[:6], refs[6:]
-    outs, (top, row_columns, rhs_n, dinv_n, upd_n), refs = refs[:5], refs[5:10], refs[10:]
+    outs, (top, row_columns), refs = refs[:5], refs[5:7], refs[7:]
     rhs_v, dinv_v, upd_v, square, rows, sep, sems, small = refs
     cols = rhs_v.shape[2]
     width = cols // HALVES
@@ -103,16 +113,7 @@
     ]
     for c in few:
         c.start()
-    copies = []
-    for k in range(nodes):
-        ins = (upd_v, dinv_v, rhs_v) if k < first else (upd_n, dinv_n, rhs_n)
-        group = [
-            pltpu.make_async_copy(src.at[k], dst.at[k % first], sems.at[i, k])
-            for i, (src, dst) in enumerate(zip((upd_h, dinv_h, rhs_h), ins))
-        ]
-        for c in group:
-            c.start()
-        copies.append(group)
+    copies = node_copies(range(first), (upd_h, dinv_h, rhs_h), (upd_v, dinv_v, rhs_v), sems)
     front = lax.axis_index("front")
     square[...] = jnp.zeros_like(square)
     for c in few:
@@ -123,16 +124,11 @@
     for h in range(HALVES):
         top[h] = turned[h * width : (h + 1) * width]
     row_columns[...] = rows[...].astype(F32).T
-    prepare_nodes(first, 0, row_columns, dinv_v, upd_v, rhs_v, outs, copies[:first])
-    for group in copies[first:]:
-        for c in group:
-            c.wait()
-
-
-def prepare_second_kernel(first, row_columns, rhs, dinv, upd, _, *outs):
-    count = rhs.shape[0]
-    waits = [()] * count
-    prepare_nodes(count, first, row_columns, dinv, upd, rhs, outs, waits)
+    acc, *halves = outs
+    for k in range(first):
+        turned = prepare_node(k, k, copies[k], row_columns, (upd_v, dinv_v, rhs_v), halves)
+        for h in range(HALVES):
+            acc[h, k] = turned[h * width : (h + 1) * width]
 
 
 def prepared(count, size, cols):
@@ -150,38 +146,37 @@
         "prepare_first",
         [(HBM, a) for a in (rows, sep, rhs, dinv, update)] + [(pl.ANY, after)],
         prepared(first, size, cols)
-        + [((HALVES, cols // HALVES, size), F32), ((size, nodes), F32)]
-        + [((nodes - first, *some[1:]), F32)] * 3,
+        + [((HALVES, cols // HALVES, size), F32), ((size, nodes), F32)],
         [big, big, big, pltpu.VMEM((size, cols), F32)]
         + [pltpu.VMEM(rows.shape, jnp.int32), pltpu.VMEM(sep.shape, F32)]
-        + [pltpu.SemaphoreType.DMA((3, nodes)), pltpu.SemaphoreType.DMA((2,))],
-    )
-
-
-def prepare_second(row_columns, rhs, dinv, update, after):
-    count, size, cols = rhs.shape
-    first = row_columns.shape[1] - count
-    return call(
-        lambda *refs: prepare_second_kernel(first, *refs),
-        "prepare_second",
-        [(V, a) for a in (row_columns, rhs, dinv, update)] + [(pl.ANY, after)],
-        prepared(count, size, cols),
+        + [pltpu.SemaphoreType.DMA((3, first)), pltpu.SemaphoreType.DMA((2,))],
     )
 
 
 def forward_kernel(nodes, fronts, *refs):
-    (parent_h, acc_a, acc_b, top), parts, refs = refs[:4], (refs[4:8], refs[8:12]), refs[13:]
-    solved, send, keep, square, parent, sem = refs[:6]
-    accs = refs[6:]
+    (parent_h, rhs_h, dinv_h, upd_h, acc, top, row_columns), refs = refs[:7], refs[7:]
+    first_halves, (solved, send, keep), halves, refs = refs[:4], refs[5:8], refs[8:12], refs[12:]
+    square, parent, rhs_v, dinv_v, upd_v, sem, sems = refs[:7]
+    accs = refs[7:]
+    first, width = acc.shape[1:3]
     copy = pltpu.make_async_copy(parent_h, parent, sem)
     copy.start()
-    first, width = acc_a.shape[1:3]
+    values = (upd_v, dinv_v, rhs_v)
+    copies = node_copies(range(first, nodes), (upd_h, dinv_h, rhs_h), values, sems)
     for h in range(HALVES):
-        for k in range(nodes):
-            accs[h][k] = acc_a[h, k] if k < first else acc_b[h, k - first]
+        for k in range(first):
+            accs[h][k] = acc[h, k]
+        accs[h][first:nodes] = jnp.zeros_like(accs[h][first:nodes])
         accs[h][nodes] = top[h]
+    ready = 0
     for k in range(nodes):
-        inv_hi, inv_lo, upd_hi, upd_lo = parts[k // first]
+        while ready < nodes - first and ready < k:
+            node = first + ready
+            turned = prepare_node(node, ready, copies[ready], row_columns, values, halves)
+            for h in range(HALVES):
+                accs[h][node] = accs[h][node] + turned[h * width : (h + 1) * width]
+            ready += 1
+        inv_hi, inv_lo, upd_hi, upd_lo = first_halves if k < first else halves
         i = k % first
         inverse = (inv_hi[i], inv_lo[i])
         update = (upd_hi[i], upd_lo[i])
@@ -204,19 +199,22 @@
             ref[i * chunk : (i + 1) * chunk] = square[pl.ds(start, chunk), :]
 
 
-def local_forward(parent, acc_a, acc_b, top, first_halves, second_halves, after, fronts):
-    first, (width, size) = acc_a.shape[1], acc_a.shape[2:]
-    nodes = first + acc_b.shape[1]
-    cols = width * HALVES
+def local_forward(parent, rhs, dinv, update, acc, top, row_columns, first_halves, after, fronts):
+    nodes, size, cols = rhs.shape
+    first, width = acc.shape[1:3]
+    count = nodes - first
     part = ((cols // 2, size), F32)
+    half = ((count, size, size), BF16)
+    big = pltpu.VMEM((count, size, cols), F32)
     return call(
         lambda *refs: forward_kernel(nodes, fronts, *refs),
         "local_forward",
-        [(HBM, parent)]
-        + [(V, a) for a in (acc_a, acc_b, top, *first_halves, *second_halves)]
+        [(HBM, a) for a in (parent, rhs, dinv, update)]
+        + [(V, a) for a in (acc, top, row_columns, *first_halves)]
         + [(pl.ANY, after)],
-        [((nodes, cols, size), F32), part, part],
-        [pltpu.VMEM((cols, size), F32), pltpu.SMEM((nodes,), jnp.int32), pltpu.SemaphoreType.DMA]
+        [((nodes, cols, size), F32), part, part, half, half, half, half],
+        [pltpu.VMEM((cols, size), F32), pltpu.SMEM((nodes,), jnp.int32), big, big, big]
+        + [pltpu.SemaphoreType.DMA, pltpu.SemaphoreType.DMA((3, count))]
         + [pltpu.VMEM((nodes + 1, width, size), F32)] * HALVES,
     )
 
@@ -546,15 +544,23 @@
     acc_a, *first_halves = prepare_first(
         rhs_local, dinv_local, update_local, row_blocks, sep_rhs, stacked
     )
-    first_halves, (top, row_columns, *raw) = first_halves[:4], first_halves[4:]
+    first_halves, (top, row_columns) = first_halves[:4], first_halves[4:]
     for i in range(2, fronts, 2):
         held, _ = lax.optimization_barrier((came[i], acc_a))
         came[i + 1] = exchange(held, "front", 0)
-    acc_b, *second_halves = prepare_second(row_columns, *raw, acc_a)
-    own_map, part, inverse = block_map([came[i] for i in range(fronts)], acc_b)
+    own_map, part, inverse = block_map([came[i] for i in range(fronts)], acc_a)
     mine = exchange(part, "leaf", 0)
-    solved, send, keep = local_forward(
-        parent, acc_a, acc_b, top, first_halves, second_halves, own_map, fronts
+    solved, send, keep, *second_halves = local_forward(
+        parent,
+        rhs_local,
+        dinv_local,
+        update_local,
+        acc_a,
+        top,
+        row_columns,
+        first_halves,
+        own_map,
+        fronts,
     )
     mine, send = lax.optimization_barrier((mine, send))
     pairs = exchange(mine, "front", 0)

time: 54.9 us -> 56.6 us (1.031)
  waiting for transfers between devices: 15.1 us -> 18.6 us
  starting transfers between devices: 19.2 us -> 17.4 us
    ppermute x16, waiting for transfers between devices: 12.2 us -> 15 us  [swap(): return lax.ppermute(x, axis, [(i, i ^ mask) for i in range(n)])]
    ppermute x1, starting transfers between devices: 1.38 us -> 0.51 us  [local(): blocks = lax.ppermute(blocks, 'leaf', boundary)]
    ppermute x1, starting transfers between devices: 1.43 us -> 0.71 us  [local(): came = lax.ppermute(message[0], 'leaf', boundary)]
    ppermute x1, waiting for transfers between devices: 2.9 us -> 3.62 us  [local(): came = lax.ppermute(message[0], 'leaf', boundary)]
    pallas_call x14 -> x13, Pallas kernels: 15.2 us -> 15.1 us  [call(): pl.pallas_call(kernel, name=name, in_specs=specs, out_specs=tuple((pl.Blo...]
  transfers between devices with their start and end apart: 18 -> 18, of which waited for: 11 -> 11; matrix products, arithmetic and copies ran while one was open for 0% -> 0% of each run, Pallas kernels for 24% -> 23%
where the time goes in v13:
time: 56.6 us; the launch traced here: 56.4 us
  Pallas kernels  19.6 us (35%)
  waiting for transfers between devices  18.6 us (33%)
  starting transfers between devices  17.4 us (31%)
  between operations  0.76 us (1%)
    ppermute x16, starting transfers between devices, swap(): return lax.ppermute(x, axis, [(i, i ^ mask) for i in range(n)])  16.2 us
    pallas_call x13, Pallas kernels, call(): pl.pallas_call(kernel, name=name, in_specs=specs, out_specs=tuple((pl.Blo...  15.1 us
    ppermute x16, waiting for transfers between devices, swap(): return lax.ppermute(x, axis, [(i, i ^ mask) for i in range(n)])  15 us
    pallas_call x1, Pallas kernels, local_backward(): pl.pallas_call(lambda *refs: backward_kernel(nodes, fronts, *refs), name=...  4.54 us
    ppermute x1, waiting for transfers between devices, local(): came = lax.ppermute(message[0], 'leaf', boundary)  3.62 us
  transfers between devices with their start and end apart: 18, of which 11 were waited for; matrix products, arithmetic and copies ran while one was open for 0% of the time, Pallas kernels for 23%

profile of v13, /device:TPU:0, one launch (start us, length us, event | category | flops | bytes accessed | tf_op | source)
XLA Modules:
  0.0 56.4 jit_solution(1583481110422749041)
XLA Ops:
  0.6 0.9 %stack.1.refs_5_.refs_0_ = f32[2,64,256]{2,1,0:T(8,128)S(1)} custom-call(f32[64,256]{1,0:T(8,128)} %first.1, f32[64,256]{1,0:T(8,128)} %second.1), custom_call_target="tpu_custom_call" | custom-call | tf_op jit(solution)/shard_map/stack/pallas_call | solution.py:51
  1.5 3.0 %collective-permute-start.1 = (f32[2,64,256]{2,1,0:T(8,128)S(1)}, f32[2,64,256]{2,1,0:T(8,128)S(1)}, u32[]{:S(2)}, u32[]{:S(2)}) collective-permute-start(f32[2,64,256]{2,1,0:T(8,128)S(1)} %stack.1.refs_5_.refs_0_), channel_id=1, source_target_pairs={{0,2},{1,3},{2,0},{3,1},{4,6},{5,7},{6,4},{7,5},{8,10},{9,11},{10,... | collective-permute-start | bytes 393224 | tf_op jit(solution)/shard_map/ppermute | solution.py:68
  4.5 3.2 %prepare_first.1 = (f32[2,4,128,256]{3,2,1,0:T(8,128)S(1)}, bf16[4,256,256]{2,1,0:T(8,128)(2,1)S(1)}, bf16[4,256,256]{2,1,0:T(8,128)(2,1)S(1)}, bf16[4,256,256]{...) custom-call(s32[8,256]{1,0:T(8,128)} %refs_0_.3, ...), custom_call_target="tpu_custom_call" | custom-call | tf_op jit(solution)/shard_map/prepare_first/pallas_call | solution.py:51
  8.3 1.0 %collective-permute-done.2.refs_3_ = f32[2,64,256]{2,1,0:T(8,128)S(1)} collective-permute-done((f32[2,64,256]{2,1,0:T(8,128)S(1)}, f32[2,64,256]{2,1,0:T(8,128)S(1)}, u32[]{:S(2)}, u32[]{:S(2)}) %collective-permute-start.2) | collective-permute-done | bytes 131104 | tf_op jit(solution)/shard_map/ppermute | solution.py:68
  9.7 1.8 %collective-permute-start.3 = (f32[1,128,256]{2,1,0:T(8,128)S(1)}, f32[1,128,256]{2,1,0:T(8,128)S(1)}, u32[]{:S(2)}, u32[]{:S(2)}) collective-permute-start(f32[1,128,256]{2,1,0:T(8,128)S(1)} %get-tuple-element.61), channel_id=1, source_target_pairs={{0,4},{4,0},{8,12},{12,8},{16,20},{20,16},{24,28},{28,24},{1,5},{5... | collective-permute-start | bytes 393224 | tf_op jit(solution)/shard_map/ppermute | solution.py:68
  11.5 5.7 %local_forward.1 = (f32[8,256,256]{2,1,0:T(8,128)S(1)}, f32[128,256]{1,0:T(8,128)S(1)}, f32[128,256]{1,0:T(8,128)S(1)}, bf16[4,256,256]{2,1,0:T(8,128)(2,1)S(1)}...) custom-call(s32[8]{0:T(128)} %refs_0_.5, ...), custom_call_target="tpu_custom_call" | custom-call | tf_op jit(solution)/shard_map/local_forward/pallas_call | solution.py:51
  17.9 0.8 %collective-permute-done.4.refs_1_ = f32[128,256]{1,0:T(8,128)S(1)} collective-permute-done((f32[128,256]{1,0:T(8,128)S(1)}, f32[128,256]{1,0:T(8,128)S(1)}, u32[]{:S(2)}, u32[]{:S(2)}) %collective-permute-start.4) | collective-permute-done | bytes 131104 | tf_op jit(solution)/shard_map/ppermute | solution.py:68
  18.7 1.5 %collective-permute-start.5 = (f32[64,256]{1,0:T(8,128)S(1)}, f32[64,256]{1,0:T(8,128)S(1)}, u32[]{:S(2)}, u32[]{:S(2)}) collective-permute-start(f32[64,256]{1,0:T(8,128)S(1)} %get-tuple-element.65.refs_3_), channel_id=1, source_target_pairs={{0,2},{1,3},{2,0},{3,1},{4,6},{5,7},{6,4},{7,5},{8,10},{9,11},{10,... | collective-permute-start | bytes 196616 | tf_op jit(solution)/shard_map/ppermute | solution.py:68
  20.3 1.0 %merge_0.1 = (f32[2,256,256]{2,1,0:T(8,128)S(1)}, f32[2,256,256]{2,1,0:T(8,128)S(1)}, bf16[2,256,256]{2,1,0:T(8,128)(2,1)S(1)}, bf16[2,256,256]{2,1,0:T(8,128)(2...) custom-call(f32[256,256]{1,0:T(8,128)S(1)} %get-tuple-element.54.ref, ...), custom_call_target="tpu_custom_call" | custom-call | tf_op jit(solution)/shard_map/merge_0/pallas_call | solution.py:51
  21.3 1.6 %collective-permute-start.8 = (f32[3,128,128]{2,1,0:T(8,128)S(1)}, f32[3,128,128]{2,1,0:T(8,128)S(1)}, u32[]{:S(2)}, u32[]{:S(2)}) collective-permute-start(f32[3,128,128]{2,1,0:T(8,128)S(1)} %get-tuple-element.75), channel_id=1, source_target_pairs={{0,8},{4,12},{8,0},{12,4},{16,24},{20,28},{24,16},{28,20},{1,9},{5... | collective-permute-start | bytes 589832 | tf_op jit(solution)/shard_map/ppermute | solution.py:68
  23.9 1.7 %collective-permute-start.10 = (f32[2,128,128]{2,1,0:T(8,128)S(1)}, f32[2,128,128]{2,1,0:T(8,128)S(1)}, u32[]{:S(2)}, u32[]{:S(2)}) collective-permute-start(f32[2,128,128]{2,1,0:T(8,128)S(1)} %get-tuple-element.79), channel_id=1, source_target_pairs={{0,8},{4,12},{8,0},{12,4},{16,24},{20,28},{24,16},{28,20},{1,9},{5... | collective-permute-start | bytes 393224 | tf_op jit(solution)/shard_map/ppermute | solution.py:68
  25.6 3.5 %collective-permute-done.8.other.refs_1_ = f32[3,128,128]{2,1,0:T(8,128)S(1)} collective-permute-done((f32[3,128,128]{2,1,0:T(8,128)S(1)}, f32[3,128,128]{2,1,0:T(8,128)S(1)}, u32[]{:S(2)}, u32[]{:S(2)}) %collective-permute-start.8) | collective-permute-done | bytes 196640 | tf_op jit(solution)/shard_map/ppermute | solution.py:68
  29.2 0.7 %boundary.1.refs_7_ = f32[3,128,128]{2,1,0:T(8,128)S(1)} custom-call(f32[2,256,256]{2,1,0:T(8,128)S(1)} %get-tuple-element.74.own.refs_0_, f32[3,128,128]{2,1,0:T(8,128)S(1)} %collective-permute-done.8.other.refs_1_), custom_call_target="tpu_custom_call" | custom-call | tf_op jit(solution)/shard_map/boundary/pallas_call | solution.py:51
  31.4 2.7 %collective-permute-start.9 = (f32[64,256]{1,0:T(8,128)S(1)}, f32[64,256]{1,0:T(8,128)S(1)}, u32[]{:S(2)}, u32[]{:S(2)}) collective-permute-start(f32[64,256]{1,0:T(8,128)S(1)} %get-tuple-element.78), channel_id=1, source_target_pairs={{0,8},{4,12},{8,0},{12,4},{16,24},{20,28},{24,16},{28,20},{1,9},{5... | collective-permute-start | bytes 196616 | tf_op jit(solution)/shard_map/ppermute | solution.py:68
  34.0 1.3 %merge_1.1 = (f32[8,128]{1,0:T(8,128)}, bf16[2,256,256]{2,1,0:T(8,128)(2,1)S(1)}, bf16[2,256,256]{2,1,0:T(8,128)(2,1)S(1)}, bf16[2,256,256]{2,1,0:T(8,128)(2,1)S...) custom-call(f32[2,256,256]{2,1,0:T(8,128)S(1)} %get-tuple-element.74.own.refs_0_, ...), custom_call_target="tpu_custom_call" | custom-call | tf_op jit(solution)/shard_map/merge_1/pallas_call | solution.py:51
  35.4 1.1 %collective-permute-done.9.refs_2_ = f32[64,256]{1,0:T(8,128)S(1)} collective-permute-done((f32[64,256]{1,0:T(8,128)S(1)}, f32[64,256]{1,0:T(8,128)S(1)}, u32[]{:S(2)}, u32[]{:S(2)}) %collective-permute-start.9) | collective-permute-done | bytes 65568 | tf_op jit(solution)/shard_map/ppermute | solution.py:68
  36.9 0.7 %collective-permute-start.12 = (f32[64,256]{1,0:T(8,128)S(1)}, f32[64,256]{1,0:T(8,128)S(1)}, u32[]{:S(2)}, u32[]{:S(2)}) collective-permute-start(f32[64,256]{1,0:T(8,128)S(1)} %get-tuple-element.88), channel_id=1, source_target_pairs={{8,16},{12,20},{16,8},{20,12},{0,4},{4,0},{24,28},{28,24},{9,17},{... | collective-permute-start | bytes 196616 | tf_op jit(solution)/shard_map/ppermute | solution.py:626
  37.7 3.6 %collective-permute-done.12.refs_1_ = f32[64,256]{1,0:T(8,128)S(1)} collective-permute-done((f32[64,256]{1,0:T(8,128)S(1)}, f32[64,256]{1,0:T(8,128)S(1)}, u32[]{:S(2)}, u32[]{:S(2)}) %collective-permute-start.12) | collective-permute-done | bytes 65568 | tf_op jit(solution)/shard_map/ppermute | solution.py:626
  41.5 1.9 %collective-permute-start.14 = (f32[64,256]{1,0:T(8,128)S(1)}, f32[64,256]{1,0:T(8,128)S(1)}, u32[]{:S(2)}, u32[]{:S(2)}) collective-permute-start(f32[64,256]{1,0:T(8,128)S(1)} %turn.1.refs_1_), channel_id=1, source_target_pairs={{0,8},{4,12},{8,0},{12,4},{16,24},{20,28},{24,16},{28,20},{1,9},{5... | collective-permute-start | bytes 196616 | tf_op jit(solution)/shard_map/ppermute | solution.py:68
  43.4 2.5 %collective-permute-done.14.refs_2_ = f32[64,256]{1,0:T(8,128)S(1)} collective-permute-done((f32[64,256]{1,0:T(8,128)S(1)}, f32[64,256]{1,0:T(8,128)S(1)}, u32[]{:S(2)}, u32[]{:S(2)}) %collective-permute-start.14) | collective-permute-done | bytes 65568 | tf_op jit(solution)/shard_map/ppermute | solution.py:68
  46.2 0.6 %collective-permute-start.16 = (f32[64,256]{1,0:T(8,128)S(1)}, f32[64,256]{1,0:T(8,128)S(1)}, u32[]{:S(2)}, u32[]{:S(2)}) collective-permute-start(f32[64,256]{1,0:T(8,128)S(1)} %leave.1.refs_10_), channel_id=1, source_target_pairs={{0,2},{1,3},{2,0},{3,1},{4,6},{5,7},{6,4},{7,5},{8,10},{9,11},{10,... | collective-permute-start | bytes 196616 | tf_op jit(solution)/shard_map/ppermute | solution.py:68
  46.8 3.7 %collective-permute-done.16.refs_12_ = f32[64,256]{1,0:T(8,128)S(1)} collective-permute-done((f32[64,256]{1,0:T(8,128)S(1)}, f32[64,256]{1,0:T(8,128)S(1)}, u32[]{:S(2)}, u32[]{:S(2)}) %collective-permute-start.16) | collective-permute-done | bytes 65568 | tf_op jit(solution)/shard_map/ppermute | solution.py:68
  50.6 1.2 %collective-permute-done.17.refs_13_ = f32[64,256]{1,0:T(8,128)S(1)} collective-permute-done((f32[64,256]{1,0:T(8,128)S(1)}, f32[64,256]{1,0:T(8,128)S(1)}, u32[]{:S(2)}, u32[]{:S(2)}) %collective-permute-start.17) | collective-permute-done | bytes 65568 | tf_op jit(solution)/shard_map/ppermute | solution.py:68
  51.8 4.5 %local_backward.1 = (f32[8,256,256]{2,1,0:T(8,128)}, f32[64,256]{1,0:T(8,128)}) custom-call(s32[8]{0:T(128)} %refs_0_.5, f32[8,256,256]{2,1,0:T(8,128)S(1)} %get-tuple-element.55.refs_1_, bf16[4,256,256]{2,1,0:T(8,128)(2,1)S(1)} %get-tuple-element.49.refs_7_.refs_2_, bf16[4,256,256]{2,1,0:T(8,128)(2,1)S(1)} %get-tuple-element.50.refs_8_.refs_3_, ...), custom_call_target="tpu_custom_call" | custom-call | tf_op jit(solution)/shard_map/local_backward/pallas_call | solution.py:276
  (26 shorter events, 5.1 us)
Async XLA Ops:
  1.5 6.5 %collective-permute-start.1 = (f32[2,64,256]{2,1,0:T(8,128)S(1)}, f32[2,64,256]{2,1,0:T(8,128)S(1)}, u32[]{:S(2)}, u32[]{:S(2)}) collective-permute-start(f32[2,64,256]{2,1,0:T(8,128)S(1)} %stack.1.refs_5_.refs_0_), channel_id=1, source_target_pairs={{0,2},{1,3},{2,0},{3,1},{4,6},{5,7},{6,4},{7,5},{8,10},{9,11},{10,... | collective-permute-start | bytes 393224 | tf_op jit(solution)/shard_map/ppermute | solution.py:68
  4.5 3.8 %collective-permute-start = (f32[2,64,256]{2,1,0:T(8,128)S(1)}, f32[2,64,256]{2,1,0:T(8,128)S(1)}, u32[]{:S(2)}, u32[]{:S(2)}) collective-permute-start(f32[2,64,256]{2,1,0:T(8,128)S(1)} %stack.1.refs_5_.refs_0_), channel_id=1, source_target_pairs={{0,1},{1,0},{2,3},{3,2},{4,5},{5,4},{6,7},{7,6},{8,9},{9,8},{10,11... | collective-permute-start | bytes 393224 | tf_op jit(solution)/shard_map/ppermute | solution.py:68
  8.0 1.3 %collective-permute-start.2 = (f32[2,64,256]{2,1,0:T(8,128)S(1)}, f32[2,64,256]{2,1,0:T(8,128)S(1)}, u32[]{:S(2)}, u32[]{:S(2)}) collective-permute-start(f32[2,64,256]{2,1,0:T(8,128)S(1)} %collective-permute-done.1.refs_2_), channel_id=1, source_target_pairs={{0,1},{1,0},{2,3},{3,2},{4,5},{5,4},{6,7},{7,6},{8,9},{9,8},{10,11... | collective-permute-start | bytes 393224 | tf_op jit(solution)/shard_map/ppermute | solution.py:68
  9.7 7.6 %collective-permute-start.3 = (f32[1,128,256]{2,1,0:T(8,128)S(1)}, f32[1,128,256]{2,1,0:T(8,128)S(1)}, u32[]{:S(2)}, u32[]{:S(2)}) collective-permute-start(f32[1,128,256]{2,1,0:T(8,128)S(1)} %get-tuple-element.61), channel_id=1, source_target_pairs={{0,4},{4,0},{8,12},{12,8},{16,20},{20,16},{24,28},{28,24},{1,5},{5... | collective-permute-start | bytes 393224 | tf_op jit(solution)/shard_map/ppermute | solution.py:68
  17.3 1.4 %collective-permute-start.4 = (f32[128,256]{1,0:T(8,128)S(1)}, f32[128,256]{1,0:T(8,128)S(1)}, u32[]{:S(2)}, u32[]{:S(2)}) collective-permute-start(f32[128,256]{1,0:T(8,128)S(1)} %get-tuple-element.63), channel_id=1, source_target_pairs={{0,1},{1,0},{2,3},{3,2},{4,5},{5,4},{6,7},{7,6},{8,9},{9,8},{10,11... | collective-permute-start | bytes 393224 | tf_op jit(solution)/shard_map/ppermute | solution.py:68
  17.4 2.9 %collective-permute-start.7 = (f32[1,128,256]{2,1,0:T(8,128)S(1)}, f32[1,128,256]{2,1,0:T(8,128)S(1)}, u32[]{:S(2)}, u32[]{:S(2)}) collective-permute-start(f32[1,128,256]{2,1,0:T(8,128)S(1)} %collective-permute-done.3.refs_1_), channel_id=1, source_target_pairs={{0,1},{1,0},{2,3},{3,2},{4,5},{5,4},{6,7},{7,6},{8,9},{9,8},{10,11... | collective-permute-start | bytes 393224 | tf_op jit(solution)/shard_map/ppermute | solution.py:68
  18.7 4.3 %collective-permute-start.5 = (f32[64,256]{1,0:T(8,128)S(1)}, f32[64,256]{1,0:T(8,128)S(1)}, u32[]{:S(2)}, u32[]{:S(2)}) collective-permute-start(f32[64,256]{1,0:T(8,128)S(1)} %get-tuple-element.65.refs_3_), channel_id=1, source_target_pairs={{0,2},{1,3},{2,0},{3,1},{4,6},{5,7},{6,4},{7,5},{8,10},{9,11},{10,... | collective-permute-start | bytes 196616 | tf_op jit(solution)/shard_map/ppermute | solution.py:68
  21.3 7.8 %collective-permute-start.8 = (f32[3,128,128]{2,1,0:T(8,128)S(1)}, f32[3,128,128]{2,1,0:T(8,128)S(1)}, u32[]{:S(2)}, u32[]{:S(2)}) collective-permute-start(f32[3,128,128]{2,1,0:T(8,128)S(1)} %get-tuple-element.75), channel_id=1, source_target_pairs={{0,8},{4,12},{8,0},{12,4},{16,24},{20,28},{24,16},{28,20},{1,9},{5... | collective-permute-start | bytes 589832 | tf_op jit(solution)/shard_map/ppermute | solution.py:68
  23.5 6.4 %collective-permute-start.6 = (f32[128,256]{1,0:T(8,128)S(1)}, f32[128,256]{1,0:T(8,128)S(1)}, u32[]{:S(2)}, u32[]{:S(2)}) collective-permute-start(f32[128,256]{1,0:T(8,128)S(1)} %get-tuple-element.68.refs_1_), channel_id=1, source_target_pairs={{0,4},{4,0},{8,12},{12,8},{16,20},{20,16},{24,28},{28,24},{1,5},{5... | collective-permute-start | bytes 393224 | tf_op jit(solution)/shard_map/ppermute | solution.py:68
  23.9 6.9 %collective-permute-start.10 = (f32[2,128,128]{2,1,0:T(8,128)S(1)}, f32[2,128,128]{2,1,0:T(8,128)S(1)}, u32[]{:S(2)}, u32[]{:S(2)}) collective-permute-start(f32[2,128,128]{2,1,0:T(8,128)S(1)} %get-tuple-element.79), channel_id=1, source_target_pairs={{0,8},{4,12},{8,0},{12,4},{16,24},{20,28},{24,16},{28,20},{1,9},{5... | collective-permute-start | bytes 393224 | tf_op jit(solution)/shard_map/ppermute | solution.py:68
  30.9 3.2 %collective-permute-start.11 = (f32[2,128,128]{2,1,0:T(8,128)S(1)}, f32[2,128,128]{2,1,0:T(8,128)S(1)}, u32[]{:S(2)}, u32[]{:S(2)}) collective-permute-start(f32[2,128,128]{2,1,0:T(8,128)S(1)} %collective-permute-done.10.refs_2_), channel_id=1, source_target_pairs={{0,1},{1,0},{2,3},{3,2},{4,5},{5,4},{6,7},{7,6},{8,9},{9,8},{10,11... | collective-permute-start | bytes 393224 | tf_op jit(solution)/shard_map/ppermute | solution.py:68
  30.9 10.4 %collective-permute-start.13 = (f32[3,128,128]{2,1,0:T(8,128)S(1)}, f32[3,128,128]{2,1,0:T(8,128)S(1)}, u32[]{:S(2)}, u32[]{:S(2)}) collective-permute-start(f32[3,128,128]{2,1,0:T(8,128)S(1)} %boundary.1.refs_7_), channel_id=1, source_target_pairs={{8,16},{12,20},{16,8},{20,12},{0,4},{4,0},{24,28},{28,24},{9,17},{... | collective-permute-start | bytes 589832 | tf_op jit(solution)/shard_map/ppermute | solution.py:607
  31.4 5.1 %collective-permute-start.9 = (f32[64,256]{1,0:T(8,128)S(1)}, f32[64,256]{1,0:T(8,128)S(1)}, u32[]{:S(2)}, u32[]{:S(2)}) collective-permute-start(f32[64,256]{1,0:T(8,128)S(1)} %get-tuple-element.78), channel_id=1, source_target_pairs={{0,8},{4,12},{8,0},{12,4},{16,24},{20,28},{24,16},{28,20},{1,9},{5... | collective-permute-start | bytes 196616 | tf_op jit(solution)/shard_map/ppermute | solution.py:68
  36.9 4.3 %collective-permute-start.12 = (f32[64,256]{1,0:T(8,128)S(1)}, f32[64,256]{1,0:T(8,128)S(1)}, u32[]{:S(2)}, u32[]{:S(2)}) collective-permute-start(f32[64,256]{1,0:T(8,128)S(1)} %get-tuple-element.88), channel_id=1, source_target_pairs={{8,16},{12,20},{16,8},{20,12},{0,4},{4,0},{24,28},{28,24},{9,17},{... | collective-permute-start | bytes 196616 | tf_op jit(solution)/shard_map/ppermute | solution.py:626
  41.5 4.3 %collective-permute-start.14 = (f32[64,256]{1,0:T(8,128)S(1)}, f32[64,256]{1,0:T(8,128)S(1)}, u32[]{:S(2)}, u32[]{:S(2)}) collective-permute-start(f32[64,256]{1,0:T(8,128)S(1)} %turn.1.refs_1_), channel_id=1, source_target_pairs={{0,8},{4,12},{8,0},{12,4},{16,24},{20,28},{24,16},{28,20},{1,9},{5... | collective-permute-start | bytes 196616 | tf_op jit(solution)/shard_map/ppermute | solution.py:68
  46.2 4.3 %collective-permute-start.16 = (f32[64,256]{1,0:T(8,128)S(1)}, f32[64,256]{1,0:T(8,128)S(1)}, u32[]{:S(2)}, u32[]{:S(2)}) collective-permute-start(f32[64,256]{1,0:T(8,128)S(1)} %leave.1.refs_10_), channel_id=1, source_target_pairs={{0,2},{1,3},{2,0},{3,1},{4,6},{5,7},{6,4},{7,5},{8,10},{9,11},{10,... | collective-permute-start | bytes 196616 | tf_op jit(solution)/shard_map/ppermute | solution.py:68
  46.8 3.7 %collective-permute-start.15 = (f32[64,256]{1,0:T(8,128)S(1)}, f32[64,256]{1,0:T(8,128)S(1)}, u32[]{:S(2)}, u32[]{:S(2)}) collective-permute-start(f32[64,256]{1,0:T(8,128)S(1)} %leave.1.refs_10_), channel_id=1, source_target_pairs={{0,1},{1,0},{2,3},{3,2},{4,5},{5,4},{6,7},{7,6},{8,9},{9,8},{10,11... | collective-permute-start | bytes 196616 | tf_op jit(solution)/shard_map/ppermute | solution.py:68
  50.6 1.3 %collective-permute-start.17 = (f32[64,256]{1,0:T(8,128)S(1)}, f32[64,256]{1,0:T(8,128)S(1)}, u32[]{:S(2)}, u32[]{:S(2)}) collective-permute-start(f32[64,256]{1,0:T(8,128)S(1)} %collective-permute-done.16.refs_12_), channel_id=1, source_target_pairs={{0,1},{1,0},{2,3},{3,2},{4,5},{5,4},{6,7},{7,6},{8,9},{9,8},{10,11... | collective-permute-start | bytes 196616 | tf_op jit(solution)/shard_map/ppermute | solution.py:68

commit v14 on v12

--- a/solution.py
+++ b/solution.py
@@ -433,11 +433,10 @@
         mixed_n[0], mixed_n[1] = a_n, e_n
 
 
-def boundary_kernel(own, other, blocks):
+def boundary_kernel(own, other, two, one):
     k, t = own[0], split(own[1])
     x = dot3(split(k_of(other)), t, NN)
-    for i, block in enumerate(k_blocks(k + dot3(t, split(x), TN))):
-        blocks[i] = block
+    two[0], two[1], one[0] = k_blocks(k + dot3(t, split(x), TN))
 
 
 def maps(size, last):
@@ -499,9 +498,9 @@
         message[1][...] = jnp.where(bit_of("leaf", bit + 1) == 1, p_new, z_new)
 
 
-def turn_kernel(bit, own_z, came, blocks, given):
+def turn_kernel(bit, own_z, came, two, one, given):
     value = came[...]
-    middle = value + dot3(split(own_z[...]), split(k_of(blocks)), NN)
+    middle = value + dot3(split(own_z[...]), split(k_of([two[0], two[1], one[0]])), NN)
     given[...] = jnp.where(bit_of("leaf", bit) == 1, value, middle)
 
 
@@ -595,10 +594,14 @@
             other, mine = [exchange(part, "leaf", bit + 1) for part in parts]
             ahead = [other]
         if bit == rounds - 3:
-            ahead = (blocks,) = call(
-                boundary_kernel, "boundary", [(V, kept), (V, other)], [(other.shape, F32)]
+            half = size // 2
+            ahead = call(
+                boundary_kernel,
+                "boundary",
+                [(V, kept), (V, other)],
+                [((2, half, half), F32), ((1, half, half), F32)],
             )
-            blocks = lax.ppermute(blocks, "leaf", boundary)
+            blocks = [lax.ppermute(b, "leaf", boundary) for b in ahead]
         sol, *message = call(
             lambda *refs, bit=bit: step_kernel(bit, rounds, len(ahead), *refs),
             f"step_{bit}",
@@ -621,7 +624,7 @@
     (given,) = call(
         lambda *refs: turn_kernel(rounds - 1, *refs),
         "turn",
-        [(V, a) for a in (message[1], came, blocks)],
+        [(V, a) for a in (message[1], came, *blocks)],
         [share],
     )
     for bit in reversed(range(2, rounds - 1)):

time: 54.9 us -> 54.5 us (level)
    ppermute x1 -> x2, waiting for transfers between devices: 0.01 us -> 2.48 us  [local(): blocks = [lax.ppermute(b, 'leaf', boundary) for b in ahead]]
    ppermute x1, waiting for transfers between devices: 2.9 us -> 0.7 us  [local(): came = lax.ppermute(message[0], 'leaf', boundary)]
    ppermute x16, starting transfers between devices: 16.4 us -> 15.7 us  [swap(): return lax.ppermute(x, axis, [(i, i ^ mask) for i in range(n)])]
    ppermute x16, waiting for transfers between devices: 12.2 us -> 11.5 us  [swap(): return lax.ppermute(x, axis, [(i, i ^ mask) for i in range(n)])]
    ppermute x1 -> x2, starting transfers between devices: 1.38 us -> 2.03 us  [local(): blocks = [lax.ppermute(b, 'leaf', boundary) for b in ahead]]
  transfers between devices with their start and end apart: 18 -> 19, of which waited for: 11 -> 11; matrix products, arithmetic and copies ran while one was open for 0% -> 0% of each run, Pallas kernels for 24% -> 25%
where the time goes in v14:
time: 54.5 us; the launch traced here: 54.3 us
  Pallas kernels  19.7 us (36%)
  starting transfers between devices  19.2 us (35%)
  waiting for transfers between devices  14.7 us (27%)
  between operations  0.76 us (1%)
    ppermute x16, starting transfers between devices, swap(): return lax.ppermute(x, axis, [(i, i ^ mask) for i in range(n)])  15.7 us
    pallas_call x14, Pallas kernels, call(): pl.pallas_call(kernel, name=name, in_specs=specs, out_specs=tuple((pl.Blo...  15.2 us
    ppermute x16, waiting for transfers between devices, swap(): return lax.ppermute(x, axis, [(i, i ^ mask) for i in range(n)])  11.5 us
    pallas_call x1, Pallas kernels, local_backward(): pl.pallas_call(lambda *refs: backward_kernel(nodes, fronts, *refs), name=...  4.54 us
    ppermute x2, waiting for transfers between devices, local(): blocks = [lax.ppermute(b, 'leaf', boundary) for b in ahead]  2.48 us
    ppermute x2, starting transfers between devices, local(): blocks = [lax.ppermute(b, 'leaf', boundary) for b in ahead]  2.03 us
    ppermute x1, starting transfers between devices, local(): came = lax.ppermute(message[0], 'leaf', boundary)  1.46 us
  transfers between devices with their start and end apart: 19, of which 11 were waited for; matrix products, arithmetic and copies ran while one was open for 0% of the time, Pallas kernels for 25%

profile of v14, /device:TPU:0, one launch (start us, length us, event | category | flops | bytes accessed | tf_op | source)
XLA Modules:
  0.0 54.3 jit_solution(8553545753451441108)
XLA Ops:
  0.6 0.9 %stack.1.refs_5_.refs_0_ = f32[2,64,256]{2,1,0:T(8,128)S(1)} custom-call(f32[64,256]{1,0:T(8,128)} %first.1, f32[64,256]{1,0:T(8,128)} %second.1), custom_call_target="tpu_custom_call" | custom-call | tf_op jit(solution)/shard_map/stack/pallas_call | solution.py:51
  1.5 3.0 %collective-permute-start.1 = (f32[2,64,256]{2,1,0:T(8,128)S(1)}, f32[2,64,256]{2,1,0:T(8,128)S(1)}, u32[]{:S(2)}, u32[]{:S(2)}) collective-permute-start(f32[2,64,256]{2,1,0:T(8,128)S(1)} %stack.1.refs_5_.refs_0_), channel_id=1, source_target_pairs={{0,2},{1,3},{2,0},{3,1},{4,6},{5,7},{6,4},{7,5},{8,10},{9,11},{10,... | collective-permute-start | bytes 393224 | tf_op jit(solution)/shard_map/ppermute | solution.py:68
  4.5 4.3 %prepare_first.1 = (f32[2,4,128,256]{3,2,1,0:T(8,128)S(1)}, bf16[4,256,256]{2,1,0:T(8,128)(2,1)S(1)}, bf16[4,256,256]{2,1,0:T(8,128)(2,1)S(1)}, bf16[4,256,256]{...) custom-call(s32[8,256]{1,0:T(8,128)} %refs_0_.3, ...), custom_call_target="tpu_custom_call" | custom-call | tf_op jit(solution)/shard_map/prepare_first/pallas_call | solution.py:51
  10.7 1.6 %collective-permute-start.3 = (f32[1,128,256]{2,1,0:T(8,128)S(1)}, f32[1,128,256]{2,1,0:T(8,128)S(1)}, u32[]{:S(2)}, u32[]{:S(2)}) collective-permute-start(f32[1,128,256]{2,1,0:T(8,128)S(1)} %get-tuple-element.71), channel_id=1, source_target_pairs={{0,4},{4,0},{8,12},{12,8},{16,20},{20,16},{24,28},{28,24},{1,5},{5... | collective-permute-start | bytes 393224 | tf_op jit(solution)/shard_map/ppermute | solution.py:68
  12.3 4.1 %local_forward.1 = (f32[8,256,256]{2,1,0:T(8,128)S(1)}, f32[128,256]{1,0:T(8,128)S(1)}, f32[128,256]{1,0:T(8,128)S(1)}) custom-call(s32[8]{0:T(128)} %refs_0_.5, f32[2,4,128,256]{3,2,1,0:T(8,128)S(1)} %get-tuple-element.52.refs_4_.refs_1_, f32[2,4,128,256]{3,2,1,0:T(8,128)S(1)} %get-tuple-element.57.refs_4_.refs_2_, ...), custom_call_target="tpu_custom_call" | custom-call | tf_op jit(solution)/shard_map/local_forward/pallas_call | solution.py:51
  17.0 0.8 %collective-permute-done.4.refs_1_ = f32[128,256]{1,0:T(8,128)S(1)} collective-permute-done((f32[128,256]{1,0:T(8,128)S(1)}, f32[128,256]{1,0:T(8,128)S(1)}, u32[]{:S(2)}, u32[]{:S(2)}) %collective-permute-start.4) | collective-permute-done | bytes 131104 | tf_op jit(solution)/shard_map/ppermute | solution.py:68
  18.7 1.0 %merge_0.1 = (f32[2,256,256]{2,1,0:T(8,128)S(1)}, f32[2,256,256]{2,1,0:T(8,128)S(1)}, bf16[2,256,256]{2,1,0:T(8,128)(2,1)S(1)}, bf16[2,256,256]{2,1,0:T(8,128)(2...) custom-call(f32[256,256]{1,0:T(8,128)S(1)} %get-tuple-element.68.ref, ...), custom_call_target="tpu_custom_call" | custom-call | tf_op jit(solution)/shard_map/merge_0/pallas_call | solution.py:51
  19.7 1.6 %collective-permute-start.8 = (f32[3,128,128]{2,1,0:T(8,128)S(1)}, f32[3,128,128]{2,1,0:T(8,128)S(1)}, u32[]{:S(2)}, u32[]{:S(2)}) collective-permute-start(f32[3,128,128]{2,1,0:T(8,128)S(1)} %get-tuple-element.85), channel_id=1, source_target_pairs={{0,8},{4,12},{8,0},{12,4},{16,24},{20,28},{24,16},{28,20},{1,9},{5... | collective-permute-start | bytes 589832 | tf_op jit(solution)/shard_map/ppermute | solution.py:68
  21.3 0.9 %collective-permute-done.5.other = f32[64,256]{1,0:T(8,128)S(1)} collective-permute-done((f32[64,256]{1,0:T(8,128)S(1)}, f32[64,256]{1,0:T(8,128)S(1)}, u32[]{:S(2)}, u32[]{:S(2)}) %collective-permute-start.5) | collective-permute-done | bytes 65568 | tf_op jit(solution)/shard_map/ppermute | solution.py:68
  22.7 1.6 %collective-permute-start.6 = (f32[128,256]{1,0:T(8,128)S(1)}, f32[128,256]{1,0:T(8,128)S(1)}, u32[]{:S(2)}, u32[]{:S(2)}) collective-permute-start(f32[128,256]{1,0:T(8,128)S(1)} %get-tuple-element.78.refs_1_), channel_id=1, source_target_pairs={{0,4},{4,0},{8,12},{12,8},{16,20},{20,16},{24,28},{28,24},{1,5},{5... | collective-permute-start | bytes 393224 | tf_op jit(solution)/shard_map/ppermute | solution.py:68
  24.2 1.6 %collective-permute-start.10 = (f32[2,128,128]{2,1,0:T(8,128)S(1)}, f32[2,128,128]{2,1,0:T(8,128)S(1)}, u32[]{:S(2)}, u32[]{:S(2)}) collective-permute-start(f32[2,128,128]{2,1,0:T(8,128)S(1)} %get-tuple-element.91), channel_id=1, source_target_pairs={{0,8},{4,12},{8,0},{12,4},{16,24},{20,28},{24,16},{28,20},{1,9},{5... | collective-permute-start | bytes 393224 | tf_op jit(solution)/shard_map/ppermute | solution.py:68
  25.8 1.4 %collective-permute-done.8.other.refs_1_ = f32[3,128,128]{2,1,0:T(8,128)S(1)} collective-permute-done((f32[3,128,128]{2,1,0:T(8,128)S(1)}, f32[3,128,128]{2,1,0:T(8,128)S(1)}, u32[]{:S(2)}, u32[]{:S(2)}) %collective-permute-start.8) | collective-permute-done | bytes 196640 | tf_op jit(solution)/shard_map/ppermute | solution.py:68
  28.4 0.9 %collective-permute-done.10.refs_2_ = f32[2,128,128]{2,1,0:T(8,128)S(1)} collective-permute-done((f32[2,128,128]{2,1,0:T(8,128)S(1)}, f32[2,128,128]{2,1,0:T(8,128)S(1)}, u32[]{:S(2)}, u32[]{:S(2)}) %collective-permute-start.10) | collective-permute-done | bytes 131104 | tf_op jit(solution)/shard_map/ppermute | solution.py:68
  29.2 1.6 %collective-permute-start.9 = (f32[64,256]{1,0:T(8,128)S(1)}, f32[64,256]{1,0:T(8,128)S(1)}, u32[]{:S(2)}, u32[]{:S(2)}) collective-permute-start(f32[64,256]{1,0:T(8,128)S(1)} %get-tuple-element.90), channel_id=1, source_target_pairs={{0,8},{4,12},{8,0},{12,4},{16,24},{20,28},{24,16},{28,20},{1,9},{5... | collective-permute-start | bytes 196616 | tf_op jit(solution)/shard_map/ppermute | solution.py:68
  30.8 1.4 %collective-permute-start.13 = (f32[2,128,128]{2,1,0:T(8,128)S(1)}, f32[2,128,128]{2,1,0:T(8,128)S(1)}, u32[]{:S(2)}, u32[]{:S(2)}) collective-permute-start(f32[2,128,128]{2,1,0:T(8,128)S(1)} %get-tuple-element.86.refs_7_), channel_id=1, source_target_pairs={{8,16},{12,20},{16,8},{20,12},{0,4},{4,0},{24,28},{28,24},{9,17},{... | collective-permute-start | bytes 393224 | tf_op jit(solution)/shard_map/ppermute | solution.py:604
  32.8 1.3 %merge_1.1 = (f32[8,128]{1,0:T(8,128)}, bf16[2,256,256]{2,1,0:T(8,128)(2,1)S(1)}, bf16[2,256,256]{2,1,0:T(8,128)(2,1)S(1)}, bf16[2,256,256]{2,1,0:T(8,128)(2,1)S...) custom-call(f32[2,256,256]{2,1,0:T(8,128)S(1)} %get-tuple-element.84.own.refs_0_, ...), custom_call_target="tpu_custom_call" | custom-call | tf_op jit(solution)/shard_map/merge_1/pallas_call | solution.py:51
  34.6 1.5 %collective-permute-start.12 = (f32[64,256]{1,0:T(8,128)S(1)}, f32[64,256]{1,0:T(8,128)S(1)}, u32[]{:S(2)}, u32[]{:S(2)}) collective-permute-start(f32[64,256]{1,0:T(8,128)S(1)} %get-tuple-element.100), channel_id=1, source_target_pairs={{8,16},{12,20},{16,8},{20,12},{0,4},{4,0},{24,28},{28,24},{9,17},{... | collective-permute-start | bytes 196616 | tf_op jit(solution)/shard_map/ppermute | solution.py:623
  36.1 2.5 %collective-permute-done.14.refs_3_ = f32[1,128,128]{2,1,0:T(8,128)S(1)} collective-permute-done((f32[1,128,128]{2,1,0:T(8,128)S(1)}, f32[1,128,128]{2,1,0:T(8,128)S(1)}, u32[]{:S(2)}, u32[]{:S(2)}) %collective-permute-start.14) | collective-permute-done | bytes 65568 | tf_op jit(solution)/shard_map/ppermute | solution.py:604
  39.5 1.5 %collective-permute-start.15 = (f32[64,256]{1,0:T(8,128)S(1)}, f32[64,256]{1,0:T(8,128)S(1)}, u32[]{:S(2)}, u32[]{:S(2)}) collective-permute-start(f32[64,256]{1,0:T(8,128)S(1)} %turn.1.refs_1_), channel_id=1, source_target_pairs={{0,8},{4,12},{8,0},{12,4},{16,24},{20,28},{24,16},{28,20},{1,9},{5... | collective-permute-start | bytes 196616 | tf_op jit(solution)/shard_map/ppermute | solution.py:68
  41.0 2.9 %collective-permute-done.15.refs_2_ = f32[64,256]{1,0:T(8,128)S(1)} collective-permute-done((f32[64,256]{1,0:T(8,128)S(1)}, f32[64,256]{1,0:T(8,128)S(1)}, u32[]{:S(2)}, u32[]{:S(2)}) %collective-permute-start.15) | collective-permute-done | bytes 65568 | tf_op jit(solution)/shard_map/ppermute | solution.py:68
  44.2 1.4 %collective-permute-start.17 = (f32[64,256]{1,0:T(8,128)S(1)}, f32[64,256]{1,0:T(8,128)S(1)}, u32[]{:S(2)}, u32[]{:S(2)}) collective-permute-start(f32[64,256]{1,0:T(8,128)S(1)} %leave.1.refs_10_), channel_id=1, source_target_pairs={{0,2},{1,3},{2,0},{3,1},{4,6},{5,7},{6,4},{7,5},{8,10},{9,11},{10,... | collective-permute-start | bytes 196616 | tf_op jit(solution)/shard_map/ppermute | solution.py:68
  45.6 2.9 %collective-permute-done.17.refs_12_ = f32[64,256]{1,0:T(8,128)S(1)} collective-permute-done((f32[64,256]{1,0:T(8,128)S(1)}, f32[64,256]{1,0:T(8,128)S(1)}, u32[]{:S(2)}, u32[]{:S(2)}) %collective-permute-start.17) | collective-permute-done | bytes 65568 | tf_op jit(solution)/shard_map/ppermute | solution.py:68
  48.5 1.2 %collective-permute-done.18.refs_13_ = f32[64,256]{1,0:T(8,128)S(1)} collective-permute-done((f32[64,256]{1,0:T(8,128)S(1)}, f32[64,256]{1,0:T(8,128)S(1)}, u32[]{:S(2)}, u32[]{:S(2)}) %collective-permute-start.18) | collective-permute-done | bytes 65568 | tf_op jit(solution)/shard_map/ppermute | solution.py:68
  49.8 4.5 %local_backward.1 = (f32[8,256,256]{2,1,0:T(8,128)}, f32[64,256]{1,0:T(8,128)}) custom-call(s32[8]{0:T(128)} %refs_0_.5, f32[8,256,256]{2,1,0:T(8,128)S(1)} %get-tuple-element.69.refs_1_, bf16[4,256,256]{2,1,0:T(8,128)(2,1)S(1)} %get-tuple-element.59.refs_4_.refs_2_, bf16[4,256,256]{2,1,0:T(8,128)(2,1)S(1)} %get-tuple-element.60.refs_5_.refs_3_, ...), custom_call_target="tpu_custom_call" | custom-call | tf_op jit(solution)/shard_map/local_backward/pallas_call | solution.py:278
  (29 shorter events, 7.2 us)
Async XLA Ops:
  1.5 7.3 %collective-permute-start.1 = (f32[2,64,256]{2,1,0:T(8,128)S(1)}, f32[2,64,256]{2,1,0:T(8,128)S(1)}, u32[]{:S(2)}, u32[]{:S(2)}) collective-permute-start(f32[2,64,256]{2,1,0:T(8,128)S(1)} %stack.1.refs_5_.refs_0_), channel_id=1, source_target_pairs={{0,2},{1,3},{2,0},{3,1},{4,6},{5,7},{6,4},{7,5},{8,10},{9,11},{10,... | collective-permute-start | bytes 393224 | tf_op jit(solution)/shard_map/ppermute | solution.py:68
  4.5 5.5 %collective-permute-start = (f32[2,64,256]{2,1,0:T(8,128)S(1)}, f32[2,64,256]{2,1,0:T(8,128)S(1)}, u32[]{:S(2)}, u32[]{:S(2)}) collective-permute-start(f32[2,64,256]{2,1,0:T(8,128)S(1)} %stack.1.refs_5_.refs_0_), channel_id=1, source_target_pairs={{0,1},{1,0},{2,3},{3,2},{4,5},{5,4},{6,7},{7,6},{8,9},{9,8},{10,11... | collective-permute-start | bytes 393224 | tf_op jit(solution)/shard_map/ppermute | solution.py:68
  8.8 1.6 %collective-permute-start.2 = (f32[2,64,256]{2,1,0:T(8,128)S(1)}, f32[2,64,256]{2,1,0:T(8,128)S(1)}, u32[]{:S(2)}, u32[]{:S(2)}) collective-permute-start(f32[2,64,256]{2,1,0:T(8,128)S(1)} %collective-permute-done.1.refs_2_), channel_id=1, source_target_pairs={{0,1},{1,0},{2,3},{3,2},{4,5},{5,4},{6,7},{7,6},{8,9},{9,8},{10,11... | collective-permute-start | bytes 393224 | tf_op jit(solution)/shard_map/ppermute | solution.py:68
  10.7 5.8 %collective-permute-start.3 = (f32[1,128,256]{2,1,0:T(8,128)S(1)}, f32[1,128,256]{2,1,0:T(8,128)S(1)}, u32[]{:S(2)}, u32[]{:S(2)}) collective-permute-start(f32[1,128,256]{2,1,0:T(8,128)S(1)} %get-tuple-element.71), channel_id=1, source_target_pairs={{0,4},{4,0},{8,12},{12,8},{16,20},{20,16},{24,28},{28,24},{1,5},{5... | collective-permute-start | bytes 393224 | tf_op jit(solution)/shard_map/ppermute | solution.py:68
  16.5 1.3 %collective-permute-start.4 = (f32[128,256]{1,0:T(8,128)S(1)}, f32[128,256]{1,0:T(8,128)S(1)}, u32[]{:S(2)}, u32[]{:S(2)}) collective-permute-start(f32[128,256]{1,0:T(8,128)S(1)} %get-tuple-element.73), channel_id=1, source_target_pairs={{0,1},{1,0},{2,3},{3,2},{4,5},{5,4},{6,7},{7,6},{8,9},{9,8},{10,11... | collective-permute-start | bytes 393224 | tf_op jit(solution)/shard_map/ppermute | solution.py:68
  16.5 2.1 %collective-permute-start.7 = (f32[1,128,256]{2,1,0:T(8,128)S(1)}, f32[1,128,256]{2,1,0:T(8,128)S(1)}, u32[]{:S(2)}, u32[]{:S(2)}) collective-permute-start(f32[1,128,256]{2,1,0:T(8,128)S(1)} %collective-permute-done.3.refs_1_), channel_id=1, source_target_pairs={{0,1},{1,0},{2,3},{3,2},{4,5},{5,4},{6,7},{7,6},{8,9},{9,8},{10,11... | collective-permute-start | bytes 393224 | tf_op jit(solution)/shard_map/ppermute | solution.py:68
  17.9 4.3 %collective-permute-start.5 = (f32[64,256]{1,0:T(8,128)S(1)}, f32[64,256]{1,0:T(8,128)S(1)}, u32[]{:S(2)}, u32[]{:S(2)}) collective-permute-start(f32[64,256]{1,0:T(8,128)S(1)} %get-tuple-element.75.refs_3_), channel_id=1, source_target_pairs={{0,2},{1,3},{2,0},{3,1},{4,6},{5,7},{6,4},{7,5},{8,10},{9,11},{10,... | collective-permute-start | bytes 196616 | tf_op jit(solution)/shard_map/ppermute | solution.py:68
  19.7 7.5 %collective-permute-start.8 = (f32[3,128,128]{2,1,0:T(8,128)S(1)}, f32[3,128,128]{2,1,0:T(8,128)S(1)}, u32[]{:S(2)}, u32[]{:S(2)}) collective-permute-start(f32[3,128,128]{2,1,0:T(8,128)S(1)} %get-tuple-element.85), channel_id=1, source_target_pairs={{0,8},{4,12},{8,0},{12,4},{16,24},{20,28},{24,16},{28,20},{1,9},{5... | collective-permute-start | bytes 589832 | tf_op jit(solution)/shard_map/ppermute | solution.py:68
  22.7 5.2 %collective-permute-start.6 = (f32[128,256]{1,0:T(8,128)S(1)}, f32[128,256]{1,0:T(8,128)S(1)}, u32[]{:S(2)}, u32[]{:S(2)}) collective-permute-start(f32[128,256]{1,0:T(8,128)S(1)} %get-tuple-element.78.refs_1_), channel_id=1, source_target_pairs={{0,4},{4,0},{8,12},{12,8},{16,20},{20,16},{24,28},{28,24},{1,5},{5... | collective-permute-start | bytes 393224 | tf_op jit(solution)/shard_map/ppermute | solution.py:68
  24.2 5.0 %collective-permute-start.10 = (f32[2,128,128]{2,1,0:T(8,128)S(1)}, f32[2,128,128]{2,1,0:T(8,128)S(1)}, u32[]{:S(2)}, u32[]{:S(2)}) collective-permute-start(f32[2,128,128]{2,1,0:T(8,128)S(1)} %get-tuple-element.91), channel_id=1, source_target_pairs={{0,8},{4,12},{8,0},{12,4},{16,24},{20,28},{24,16},{28,20},{1,9},{5... | collective-permute-start | bytes 393224 | tf_op jit(solution)/shard_map/ppermute | solution.py:68
  29.2 3.6 %collective-permute-start.11 = (f32[2,128,128]{2,1,0:T(8,128)S(1)}, f32[2,128,128]{2,1,0:T(8,128)S(1)}, u32[]{:S(2)}, u32[]{:S(2)}) collective-permute-start(f32[2,128,128]{2,1,0:T(8,128)S(1)} %collective-permute-done.10.refs_2_), channel_id=1, source_target_pairs={{0,1},{1,0},{2,3},{3,2},{4,5},{5,4},{6,7},{7,6},{8,9},{9,8},{10,11... | collective-permute-start | bytes 393224 | tf_op jit(solution)/shard_map/ppermute | solution.py:68
  29.2 4.9 %collective-permute-start.9 = (f32[64,256]{1,0:T(8,128)S(1)}, f32[64,256]{1,0:T(8,128)S(1)}, u32[]{:S(2)}, u32[]{:S(2)}) collective-permute-start(f32[64,256]{1,0:T(8,128)S(1)} %get-tuple-element.90), channel_id=1, source_target_pairs={{0,8},{4,12},{8,0},{12,4},{16,24},{20,28},{24,16},{28,20},{1,9},{5... | collective-permute-start | bytes 196616 | tf_op jit(solution)/shard_map/ppermute | solution.py:68
  30.8 7.7 %collective-permute-start.13 = (f32[2,128,128]{2,1,0:T(8,128)S(1)}, f32[2,128,128]{2,1,0:T(8,128)S(1)}, u32[]{:S(2)}, u32[]{:S(2)}) collective-permute-start(f32[2,128,128]{2,1,0:T(8,128)S(1)} %get-tuple-element.86.refs_7_), channel_id=1, source_target_pairs={{8,16},{12,20},{16,8},{20,12},{0,4},{4,0},{24,28},{28,24},{9,17},{... | collective-permute-start | bytes 393224 | tf_op jit(solution)/shard_map/ppermute | solution.py:604
  32.2 6.3 %collective-permute-start.14 = (f32[1,128,128]{2,1,0:T(8,128)S(1)}, f32[1,128,128]{2,1,0:T(8,128)S(1)}, u32[]{:S(2)}, u32[]{:S(2)}) collective-permute-start(f32[1,128,128]{2,1,0:T(8,128)S(1)} %get-tuple-element.87.refs_8_), channel_id=1, source_target_pairs={{8,16},{12,20},{16,8},{20,12},{0,4},{4,0},{24,28},{28,24},{9,17},{... | collective-permute-start | bytes 196616 | tf_op jit(solution)/shard_map/ppermute | solution.py:604
  34.6 4.6 %collective-permute-start.12 = (f32[64,256]{1,0:T(8,128)S(1)}, f32[64,256]{1,0:T(8,128)S(1)}, u32[]{:S(2)}, u32[]{:S(2)}) collective-permute-start(f32[64,256]{1,0:T(8,128)S(1)} %get-tuple-element.100), channel_id=1, source_target_pairs={{8,16},{12,20},{16,8},{20,12},{0,4},{4,0},{24,28},{28,24},{9,17},{... | collective-permute-start | bytes 196616 | tf_op jit(solution)/shard_map/ppermute | solution.py:623
  39.5 4.3 %collective-permute-start.15 = (f32[64,256]{1,0:T(8,128)S(1)}, f32[64,256]{1,0:T(8,128)S(1)}, u32[]{:S(2)}, u32[]{:S(2)}) collective-permute-start(f32[64,256]{1,0:T(8,128)S(1)} %turn.1.refs_1_), channel_id=1, source_target_pairs={{0,8},{4,12},{8,0},{12,4},{16,24},{20,28},{24,16},{28,20},{1,9},{5... | collective-permute-start | bytes 196616 | tf_op jit(solution)/shard_map/ppermute | solution.py:68
  44.2 4.3 %collective-permute-start.17 = (f32[64,256]{1,0:T(8,128)S(1)}, f32[64,256]{1,0:T(8,128)S(1)}, u32[]{:S(2)}, u32[]{:S(2)}) collective-permute-start(f32[64,256]{1,0:T(8,128)S(1)} %leave.1.refs_10_), channel_id=1, source_target_pairs={{0,2},{1,3},{2,0},{3,1},{4,6},{5,7},{6,4},{7,5},{8,10},{9,11},{10,... | collective-permute-start | bytes 196616 | tf_op jit(solution)/shard_map/ppermute | solution.py:68
  45.6 2.9 %collective-permute-start.16 = (f32[64,256]{1,0:T(8,128)S(1)}, f32[64,256]{1,0:T(8,128)S(1)}, u32[]{:S(2)}, u32[]{:S(2)}) collective-permute-start(f32[64,256]{1,0:T(8,128)S(1)} %leave.1.refs_10_), channel_id=1, source_target_pairs={{0,1},{1,0},{2,3},{3,2},{4,5},{5,4},{6,7},{7,6},{8,9},{9,8},{10,11... | collective-permute-start | bytes 196616 | tf_op jit(solution)/shard_map/ppermute | solution.py:68
  48.5 1.3 %collective-permute-start.18 = (f32[64,256]{1,0:T(8,128)S(1)}, f32[64,256]{1,0:T(8,128)S(1)}, u32[]{:S(2)}, u32[]{:S(2)}) collective-permute-start(f32[64,256]{1,0:T(8,128)S(1)} %collective-permute-done.17.refs_12_), channel_id=1, source_target_pairs={{0,1},{1,0},{2,3},{3,2},{4,5},{5,4},{6,7},{7,6},{8,9},{9,8},{10,11... | collective-permute-start | bytes 196616 | tf_op jit(solution)/shard_map/ppermute | solution.py:68

commit v15 on v14

--- a/solution.py
+++ b/solution.py
@@ -403,7 +403,7 @@
     mixed[1] = jnp.where(upper, unit, up)
 
 
-def merge_kernel(bit, last, *refs):
+def merge_kernel(bit, *refs):
     own, other, mine, pairs, mixed = refs[:5]
     kept, mixed_n, halves, curve_u, total_u, total_l, *parts = refs[5:]
     upper = bit_of("leaf", bit) == 1
@@ -422,28 +422,36 @@
     a_s, e_s = split(a), split(e)
     a_n = jnp.where(upper, dot3(a_s, low_s, NN), a + dot3(e_s, x_s, TN))
     e_n = jnp.where(upper, e, dot3(up_s, e_s, NN))
-    if last:
-        kept[...] = jnp.zeros_like(kept)
-        keep_split(mixed_n, jnp.where(bit_of("leaf", bit + 1) == 1, a_n.T, e_n))
-    else:
-        k = k_low + dot3(low_s, x_s, TN)
-        t = dot3(up_s, low_s, NN)
-        kept[0], kept[1] = k, t
-        send_maps(parts, k, t)
-        mixed_n[0], mixed_n[1] = a_n, e_n
-
-
-def boundary_kernel(own, other, two, one):
-    k, t = own[0], split(own[1])
-    x = dot3(split(k_of(other)), t, NN)
+    k = k_low + dot3(low_s, x_s, TN)
+    t = dot3(up_s, low_s, NN)
+    kept[0], kept[1] = k, t
+    send_maps(parts, k, t)
+    mixed_n[0], mixed_n[1] = a_n, e_n
+
+
+def boundary_kernel(bit, own, other, mixed, two, one, halves, curve, total):
+    k, t, k_up = own[0], split(own[1]), split(k_of(other))
+    total[0], total[1] = t
+    curve[0], curve[1] = k_up
+    keep_split(halves, jnp.where(bit_of("leaf", bit) == 1, mixed[0].T, mixed[1]))
+    x = dot3(k_up, t, NN)
     two[0], two[1], one[0] = k_blocks(k + dot3(t, split(x), TN))
 
 
-def maps(size, last):
+def last_merge_kernel(bit, mixed, mine, pairs, curve, total, added):
+    upper = bit_of("leaf", bit) == 1
+    came = split(joined(*came_blocks([mine], [pairs], 4)))
+    a, e = mixed[0], mixed[1]
+    a_s, e_s = split(a), split(e)
+    x = split(dot3(pair(curve), pair(total), NN))
+    a_n = jnp.where(upper, dot3(a_s, came, NN), a + dot3(e_s, x, TN))
+    e_n = jnp.where(upper, e, dot3(came, e_s, NN))
+    keep_split(added, jnp.where(bit_of("leaf", bit + 1) == 1, a_n.T, e_n))
+
+
+def maps(size):
     both, whole = ((2, size, size), BF16), ((2, size, size), F32)
     half = size // 2
-    if last:
-        return [((8, 128), F32)] + [both] * 5
     sends = [((i, half, half), F32) for i in (3, 2)]
     return [whole, whole, both, both, both, both] + sends
 
@@ -571,7 +579,7 @@
         first_merge_kernel,
         "merge_0",
         [(V, own_map), (V, mine), (V, pairs), (pl.ANY, send)],
-        maps(size, False),
+        maps(size),
     )
     tools, parts = tools[:4], tools[4:]
     sol, message = call(
@@ -595,11 +603,11 @@
             ahead = [other]
         if bit == rounds - 3:
             half = size // 2
-            ahead = call(
-                boundary_kernel,
+            *ahead, halves, curve, own_t = call(
+                lambda *refs: boundary_kernel(rounds - 2, *refs),
                 "boundary",
-                [(V, kept), (V, other)],
-                [((2, half, half), F32), ((1, half, half), F32)],
+                [(V, kept), (V, other), (V, mixed)],
+                [((2, half, half), F32), ((1, half, half), F32)] + [((2, size, size), BF16)] * 3,
             )
             blocks = [lax.ppermute(b, "leaf", boundary) for b in ahead]
         sol, *message = call(
@@ -610,16 +618,26 @@
         )
         if not last:
             message, *short = message
+        if bit == rounds - 3:
+            tools = [halves, curve, own_t, own_t]
+        elif not last:
             mine, _ = lax.optimization_barrier((mine, sol))
             pairs = exchange(mine, "front", 0)
-            last = bit == rounds - 3
             kept, mixed, *tools = call(
-                lambda *refs, bit=bit, last=last: merge_kernel(bit + 1, last, *refs),
+                lambda *refs, bit=bit: merge_kernel(bit + 1, *refs),
                 f"merge_{bit + 1}",
                 [(V, a) for a in (kept, other, mine, pairs, mixed)],
-                maps(size, last),
+                maps(size),
             )
             tools, parts = tools[:4], tools[4:]
+    mine, _ = lax.optimization_barrier((mine, sol))
+    pairs = exchange(mine, "front", 0)
+    (added,) = call(
+        lambda *refs: last_merge_kernel(rounds - 2, *refs),
+        "last_merge",
+        [(V, a) for a in (mixed, mine, pairs, curve, own_t)],
+        [((2, size, size), BF16)],
+    )
     came = lax.ppermute(message[0], "leaf", boundary)
     (given,) = call(
         lambda *refs: turn_kernel(rounds - 1, *refs),
@@ -633,7 +651,7 @@
     (top,) = call(
         lambda *refs: leave_kernel(rounds - 1, *refs),
         "leave",
-        [(V, a) for a in (sol, given, received, mixed, inverse)],
+        [(V, a) for a in (sol, given, received, added, inverse)],
         [share],
     )
     pieces = gather_front(top, front_bits)

time: 54.5 us -> 52.7 us (0.967)
  waiting for transfers between devices: 14.7 us -> 12.6 us
  starting transfers between devices: 19.2 us -> 20 us
  Pallas kernels: 19.7 us -> 19.1 us
    ppermute x16, waiting for transfers between devices: 11.5 us -> 10 us  [swap(): return lax.ppermute(x, axis, [(i, i ^ mask) for i in range(n)])]
    ppermute x2, waiting for transfers between devices: 2.48 us -> 1.07 us  [local(): blocks = [lax.ppermute(b, 'leaf', boundary) for b in ahead]]
    ppermute x1, waiting for transfers between devices: 0.7 us -> 1.5 us  [local(): came = lax.ppermute(message[0], 'leaf', boundary)]
    pallas_call x14, Pallas kernels: 15.2 us -> 14.6 us  [call(): pl.pallas_call(kernel, name=name, in_specs=specs, out_specs=tuple((pl.Blo...]
where the time goes in v15:
time: 52.7 us; the launch traced here: 52.6 us
  starting transfers between devices  20 us (38%)
  Pallas kernels  19.1 us (36%)
  waiting for transfers between devices  12.6 us (24%)
  between operations  0.78 us (1%)
    ppermute x16, starting transfers between devices, swap(): return lax.ppermute(x, axis, [(i, i ^ mask) for i in range(n)])  16.2 us
    pallas_call x14, Pallas kernels, call(): pl.pallas_call(kernel, name=name, in_specs=specs, out_specs=tuple((pl.Blo...  14.6 us
    ppermute x16, waiting for transfers between devices, swap(): return lax.ppermute(x, axis, [(i, i ^ mask) for i in range(n)])  10 us
    pallas_call x1, Pallas kernels, local_backward(): pl.pallas_call(lambda *refs: backward_kernel(nodes, fronts, *refs), name=...  4.54 us
    ppermute x2, starting transfers between devices, local(): blocks = [lax.ppermute(b, 'leaf', boundary) for b in ahead]  2.03 us
    ppermute x1, starting transfers between devices, local(): came = lax.ppermute(message[0], 'leaf', boundary)  1.76 us
    ppermute x1, waiting for transfers between devices, local(): came = lax.ppermute(message[0], 'leaf', boundary)  1.5 us
    ppermute x2, waiting for transfers between devices, local(): blocks = [lax.ppermute(b, 'leaf', boundary) for b in ahead]  1.07 us
  transfers between devices with their start and end apart: 19, of which 11 were waited for; matrix products, arithmetic and copies ran while one was open for 0% of the time, Pallas kernels for 25%

profile of v15, /device:TPU:0, one launch (start us, length us, event | category | flops | bytes accessed | tf_op | source)
XLA Modules:
  0.0 52.6 jit_solution(796699213106316071)
XLA Ops:
  0.6 0.9 %stack.1.refs_5_.refs_0_ = f32[2,64,256]{2,1,0:T(8,128)S(1)} custom-call(f32[64,256]{1,0:T(8,128)} %first.1, f32[64,256]{1,0:T(8,128)} %second.1), custom_call_target="tpu_custom_call" | custom-call | tf_op jit(solution)/shard_map/stack/pallas_call | solution.py:51
  1.5 3.0 %collective-permute-start.1 = (f32[2,64,256]{2,1,0:T(8,128)S(1)}, f32[2,64,256]{2,1,0:T(8,128)S(1)}, u32[]{:S(2)}, u32[]{:S(2)}) collective-permute-start(f32[2,64,256]{2,1,0:T(8,128)S(1)} %stack.1.refs_5_.refs_0_), channel_id=1, source_target_pairs={{0,2},{1,3},{2,0},{3,1},{4,6},{5,7},{6,4},{7,5},{8,10},{9,11},{10,... | collective-permute-start | bytes 393224 | tf_op jit(solution)/shard_map/ppermute | solution.py:68
  4.5 4.3 %prepare_first.1 = (f32[2,4,128,256]{3,2,1,0:T(8,128)S(1)}, bf16[4,256,256]{2,1,0:T(8,128)(2,1)S(1)}, bf16[4,256,256]{2,1,0:T(8,128)(2,1)S(1)}, bf16[4,256,256]{...) custom-call(s32[8,256]{1,0:T(8,128)} %refs_0_.3, ...), custom_call_target="tpu_custom_call" | custom-call | tf_op jit(solution)/shard_map/prepare_first/pallas_call | solution.py:51
  10.7 1.6 %collective-permute-start.3 = (f32[1,128,256]{2,1,0:T(8,128)S(1)}, f32[1,128,256]{2,1,0:T(8,128)S(1)}, u32[]{:S(2)}, u32[]{:S(2)}) collective-permute-start(f32[1,128,256]{2,1,0:T(8,128)S(1)} %get-tuple-element.69), channel_id=1, source_target_pairs={{0,4},{4,0},{8,12},{12,8},{16,20},{20,16},{24,28},{28,24},{1,5},{5... | collective-permute-start | bytes 393224 | tf_op jit(solution)/shard_map/ppermute | solution.py:68
  12.3 4.1 %local_forward.1 = (f32[8,256,256]{2,1,0:T(8,128)S(1)}, f32[128,256]{1,0:T(8,128)S(1)}, f32[128,256]{1,0:T(8,128)S(1)}) custom-call(s32[8]{0:T(128)} %refs_0_.5, f32[2,4,128,256]{3,2,1,0:T(8,128)S(1)} %get-tuple-element.50.refs_4_.refs_1_, f32[2,4,128,256]{3,2,1,0:T(8,128)S(1)} %get-tuple-element.55.refs_4_.refs_2_, ...), custom_call_target="tpu_custom_call" | custom-call | tf_op jit(solution)/shard_map/local_forward/pallas_call | solution.py:51
  17.0 0.8 %collective-permute-done.4.refs_1_ = f32[128,256]{1,0:T(8,128)S(1)} collective-permute-done((f32[128,256]{1,0:T(8,128)S(1)}, f32[128,256]{1,0:T(8,128)S(1)}, u32[]{:S(2)}, u32[]{:S(2)}) %collective-permute-start.4) | collective-permute-done | bytes 131104 | tf_op jit(solution)/shard_map/ppermute | solution.py:68
  18.7 1.0 %merge_0.1 = (f32[2,256,256]{2,1,0:T(8,128)S(1)}, f32[2,256,256]{2,1,0:T(8,128)S(1)}, bf16[2,256,256]{2,1,0:T(8,128)(2,1)S(1)}, bf16[2,256,256]{2,1,0:T(8,128)(2...) custom-call(f32[256,256]{1,0:T(8,128)S(1)} %get-tuple-element.66.ref, ...), custom_call_target="tpu_custom_call" | custom-call | tf_op jit(solution)/shard_map/merge_0/pallas_call | solution.py:51
  19.7 1.6 %collective-permute-start.8 = (f32[3,128,128]{2,1,0:T(8,128)S(1)}, f32[3,128,128]{2,1,0:T(8,128)S(1)}, u32[]{:S(2)}, u32[]{:S(2)}) collective-permute-start(f32[3,128,128]{2,1,0:T(8,128)S(1)} %get-tuple-element.83), channel_id=1, source_target_pairs={{0,8},{4,12},{8,0},{12,4},{16,24},{20,28},{24,16},{28,20},{1,9},{5... | collective-permute-start | bytes 589832 | tf_op jit(solution)/shard_map/ppermute | solution.py:68
  21.3 0.9 %collective-permute-done.5.other = f32[64,256]{1,0:T(8,128)S(1)} collective-permute-done((f32[64,256]{1,0:T(8,128)S(1)}, f32[64,256]{1,0:T(8,128)S(1)}, u32[]{:S(2)}, u32[]{:S(2)}) %collective-permute-start.5) | collective-permute-done | bytes 65568 | tf_op jit(solution)/shard_map/ppermute | solution.py:68
  22.7 1.6 %collective-permute-start.6 = (f32[128,256]{1,0:T(8,128)S(1)}, f32[128,256]{1,0:T(8,128)S(1)}, u32[]{:S(2)}, u32[]{:S(2)}) collective-permute-start(f32[128,256]{1,0:T(8,128)S(1)} %get-tuple-element.76.refs_1_), channel_id=1, source_target_pairs={{0,4},{4,0},{8,12},{12,8},{16,20},{20,16},{24,28},{28,24},{1,5},{5... | collective-permute-start | bytes 393224 | tf_op jit(solution)/shard_map/ppermute | solution.py:68
  24.2 1.6 %collective-permute-start.14 = (f32[2,128,128]{2,1,0:T(8,128)S(1)}, f32[2,128,128]{2,1,0:T(8,128)S(1)}, u32[]{:S(2)}, u32[]{:S(2)}) collective-permute-start(f32[2,128,128]{2,1,0:T(8,128)S(1)} %get-tuple-element.96), channel_id=1, source_target_pairs={{0,8},{4,12},{8,0},{12,4},{16,24},{20,28},{24,16},{28,20},{1,9},{5... | collective-permute-start | bytes 393224 | tf_op jit(solution)/shard_map/ppermute | solution.py:68
  25.8 1.4 %collective-permute-done.8.refs_1_ = f32[3,128,128]{2,1,0:T(8,128)S(1)} collective-permute-done((f32[3,128,128]{2,1,0:T(8,128)S(1)}, f32[3,128,128]{2,1,0:T(8,128)S(1)}, u32[]{:S(2)}, u32[]{:S(2)}) %collective-permute-start.8) | collective-permute-done | bytes 196640 | tf_op jit(solution)/shard_map/ppermute | solution.py:68
  28.4 1.6 %collective-permute-start.9 = (f32[64,256]{1,0:T(8,128)S(1)}, f32[64,256]{1,0:T(8,128)S(1)}, u32[]{:S(2)}, u32[]{:S(2)}) collective-permute-start(f32[64,256]{1,0:T(8,128)S(1)} %get-tuple-element.89), channel_id=1, source_target_pairs={{0,8},{4,12},{8,0},{12,4},{16,24},{20,28},{24,16},{28,20},{1,9},{5... | collective-permute-start | bytes 196616 | tf_op jit(solution)/shard_map/ppermute | solution.py:68
  30.0 1.7 %collective-permute-start.11 = (f32[2,128,128]{2,1,0:T(8,128)S(1)}, f32[2,128,128]{2,1,0:T(8,128)S(1)}, u32[]{:S(2)}, u32[]{:S(2)}) collective-permute-start(f32[2,128,128]{2,1,0:T(8,128)S(1)} %get-tuple-element.85.refs_7_), channel_id=1, source_target_pairs={{8,16},{12,20},{16,8},{20,12},{0,4},{4,0},{24,28},{28,24},{9,17},{... | collective-permute-start | bytes 393224 | tf_op jit(solution)/shard_map/ppermute | solution.py:612
  33.1 1.8 %collective-permute-start.10 = (f32[64,256]{1,0:T(8,128)S(1)}, f32[64,256]{1,0:T(8,128)S(1)}, u32[]{:S(2)}, u32[]{:S(2)}) collective-permute-start(f32[64,256]{1,0:T(8,128)S(1)} %get-tuple-element.95), channel_id=1, source_target_pairs={{8,16},{12,20},{16,8},{20,12},{0,4},{4,0},{24,28},{28,24},{9,17},{... | collective-permute-start | bytes 196616 | tf_op jit(solution)/shard_map/ppermute | solution.py:641
  34.9 1.1 %collective-permute-done.12.refs_3_ = f32[1,128,128]{2,1,0:T(8,128)S(1)} collective-permute-done((f32[1,128,128]{2,1,0:T(8,128)S(1)}, f32[1,128,128]{2,1,0:T(8,128)S(1)}, u32[]{:S(2)}, u32[]{:S(2)}) %collective-permute-start.12) | collective-permute-done | bytes 65568 | tf_op jit(solution)/shard_map/ppermute | solution.py:612
  36.0 1.5 %collective-permute-done.10.refs_1_ = f32[64,256]{1,0:T(8,128)S(1)} collective-permute-done((f32[64,256]{1,0:T(8,128)S(1)}, f32[64,256]{1,0:T(8,128)S(1)}, u32[]{:S(2)}, u32[]{:S(2)}) %collective-permute-start.10) | collective-permute-done | bytes 65568 | tf_op jit(solution)/shard_map/ppermute | solution.py:641
  37.7 1.6 %collective-permute-start.13 = (f32[64,256]{1,0:T(8,128)S(1)}, f32[64,256]{1,0:T(8,128)S(1)}, u32[]{:S(2)}, u32[]{:S(2)}) collective-permute-start(f32[64,256]{1,0:T(8,128)S(1)} %turn.1.refs_1_), channel_id=1, source_target_pairs={{0,8},{4,12},{8,0},{12,4},{16,24},{20,28},{24,16},{28,20},{1,9},{5... | collective-permute-start | bytes 196616 | tf_op jit(solution)/shard_map/ppermute | solution.py:68
  39.4 0.8 %last_merge.1.refs_3_ = bf16[2,256,256]{2,1,0:T(8,128)(2,1)S(1)} custom-call(f32[2,256,256]{2,1,0:T(8,128)S(1)} %get-tuple-element.84.refs_2_.refs_0_, f32[2,128,128]{2,1,0:T(8,128)S(1)} %collective-permute-done.14.refs_1_, f32[2,128,128]{2,1,0:T(8,128)S(1)} %collective-permute-done.15.refs_2_, bf16[2,256,256]{2,1,0:T(8,128)(2,1)S(1)} %get-tuple-element.91.refs_4_.refs_3_, ...), custom_call_target="tpu_custom_call" | custom-call | tf_op jit(solution)/shard_map/last_merge/pallas_call | solution.py:51
  40.1 1.9 %collective-permute-done.13.refs_2_ = f32[64,256]{1,0:T(8,128)S(1)} collective-permute-done((f32[64,256]{1,0:T(8,128)S(1)}, f32[64,256]{1,0:T(8,128)S(1)}, u32[]{:S(2)}, u32[]{:S(2)}) %collective-permute-start.13) | collective-permute-done | bytes 65568 | tf_op jit(solution)/shard_map/ppermute | solution.py:68
  42.4 1.7 %collective-permute-start.17 = (f32[64,256]{1,0:T(8,128)S(1)}, f32[64,256]{1,0:T(8,128)S(1)}, u32[]{:S(2)}, u32[]{:S(2)}) collective-permute-start(f32[64,256]{1,0:T(8,128)S(1)} %leave.1.refs_10_), channel_id=1, source_target_pairs={{0,2},{1,3},{2,0},{3,1},{4,6},{5,7},{6,4},{7,5},{8,10},{9,11},{10,... | collective-permute-start | bytes 196616 | tf_op jit(solution)/shard_map/ppermute | solution.py:68
  44.2 2.6 %collective-permute-done.17.refs_12_ = f32[64,256]{1,0:T(8,128)S(1)} collective-permute-done((f32[64,256]{1,0:T(8,128)S(1)}, f32[64,256]{1,0:T(8,128)S(1)}, u32[]{:S(2)}, u32[]{:S(2)}) %collective-permute-start.17) | collective-permute-done | bytes 65568 | tf_op jit(solution)/shard_map/ppermute | solution.py:68
  46.8 1.2 %collective-permute-done.18.refs_13_ = f32[64,256]{1,0:T(8,128)S(1)} collective-permute-done((f32[64,256]{1,0:T(8,128)S(1)}, f32[64,256]{1,0:T(8,128)S(1)}, u32[]{:S(2)}, u32[]{:S(2)}) %collective-permute-start.18) | collective-permute-done | bytes 65568 | tf_op jit(solution)/shard_map/ppermute | solution.py:68
  48.0 4.5 %local_backward.1 = (f32[8,256,256]{2,1,0:T(8,128)}, f32[64,256]{1,0:T(8,128)}) custom-call(s32[8]{0:T(128)} %refs_0_.5, f32[8,256,256]{2,1,0:T(8,128)S(1)} %get-tuple-element.67.refs_1_, bf16[4,256,256]{2,1,0:T(8,128)(2,1)S(1)} %get-tuple-element.57.refs_4_.refs_2_, bf16[4,256,256]{2,1,0:T(8,128)(2,1)S(1)} %get-tuple-element.58.refs_5_.refs_3_, ...), custom_call_target="tpu_custom_call" | custom-call | tf_op jit(solution)/shard_map/local_backward/pallas_call | solution.py:278
  (29 shorter events, 6.9 us)
Async XLA Ops:
  1.5 7.3 %collective-permute-start.1 = (f32[2,64,256]{2,1,0:T(8,128)S(1)}, f32[2,64,256]{2,1,0:T(8,128)S(1)}, u32[]{:S(2)}, u32[]{:S(2)}) collective-permute-start(f32[2,64,256]{2,1,0:T(8,128)S(1)} %stack.1.refs_5_.refs_0_), channel_id=1, source_target_pairs={{0,2},{1,3},{2,0},{3,1},{4,6},{5,7},{6,4},{7,5},{8,10},{9,11},{10,... | collective-permute-start | bytes 393224 | tf_op jit(solution)/shard_map/ppermute | solution.py:68
  4.5 5.5 %collective-permute-start = (f32[2,64,256]{2,1,0:T(8,128)S(1)}, f32[2,64,256]{2,1,0:T(8,128)S(1)}, u32[]{:S(2)}, u32[]{:S(2)}) collective-permute-start(f32[2,64,256]{2,1,0:T(8,128)S(1)} %stack.1.refs_5_.refs_0_), channel_id=1, source_target_pairs={{0,1},{1,0},{2,3},{3,2},{4,5},{5,4},{6,7},{7,6},{8,9},{9,8},{10,11... | collective-permute-start | bytes 393224 | tf_op jit(solution)/shard_map/ppermute | solution.py:68
  8.8 1.6 %collective-permute-start.2 = (f32[2,64,256]{2,1,0:T(8,128)S(1)}, f32[2,64,256]{2,1,0:T(8,128)S(1)}, u32[]{:S(2)}, u32[]{:S(2)}) collective-permute-start(f32[2,64,256]{2,1,0:T(8,128)S(1)} %collective-permute-done.1.refs_2_), channel_id=1, source_target_pairs={{0,1},{1,0},{2,3},{3,2},{4,5},{5,4},{6,7},{7,6},{8,9},{9,8},{10,11... | collective-permute-start | bytes 393224 | tf_op jit(solution)/shard_map/ppermute | solution.py:68
  10.7 5.8 %collective-permute-start.3 = (f32[1,128,256]{2,1,0:T(8,128)S(1)}, f32[1,128,256]{2,1,0:T(8,128)S(1)}, u32[]{:S(2)}, u32[]{:S(2)}) collective-permute-start(f32[1,128,256]{2,1,0:T(8,128)S(1)} %get-tuple-element.69), channel_id=1, source_target_pairs={{0,4},{4,0},{8,12},{12,8},{16,20},{20,16},{24,28},{28,24},{1,5},{5... | collective-permute-start | bytes 393224 | tf_op jit(solution)/shard_map/ppermute | solution.py:68
  16.5 1.3 %collective-permute-start.4 = (f32[128,256]{1,0:T(8,128)S(1)}, f32[128,256]{1,0:T(8,128)S(1)}, u32[]{:S(2)}, u32[]{:S(2)}) collective-permute-start(f32[128,256]{1,0:T(8,128)S(1)} %get-tuple-element.71), channel_id=1, source_target_pairs={{0,1},{1,0},{2,3},{3,2},{4,5},{5,4},{6,7},{7,6},{8,9},{9,8},{10,11... | collective-permute-start | bytes 393224 | tf_op jit(solution)/shard_map/ppermute | solution.py:68
  16.5 2.1 %collective-permute-start.7 = (f32[1,128,256]{2,1,0:T(8,128)S(1)}, f32[1,128,256]{2,1,0:T(8,128)S(1)}, u32[]{:S(2)}, u32[]{:S(2)}) collective-permute-start(f32[1,128,256]{2,1,0:T(8,128)S(1)} %collective-permute-done.3.refs_1_), channel_id=1, source_target_pairs={{0,1},{1,0},{2,3},{3,2},{4,5},{5,4},{6,7},{7,6},{8,9},{9,8},{10,11... | collective-permute-start | bytes 393224 | tf_op jit(solution)/shard_map/ppermute | solution.py:68
  17.9 4.3 %collective-permute-start.5 = (f32[64,256]{1,0:T(8,128)S(1)}, f32[64,256]{1,0:T(8,128)S(1)}, u32[]{:S(2)}, u32[]{:S(2)}) collective-permute-start(f32[64,256]{1,0:T(8,128)S(1)} %get-tuple-element.73.refs_3_), channel_id=1, source_target_pairs={{0,2},{1,3},{2,0},{3,1},{4,6},{5,7},{6,4},{7,5},{8,10},{9,11},{10,... | collective-permute-start | bytes 196616 | tf_op jit(solution)/shard_map/ppermute | solution.py:68
  19.7 7.5 %collective-permute-start.8 = (f32[3,128,128]{2,1,0:T(8,128)S(1)}, f32[3,128,128]{2,1,0:T(8,128)S(1)}, u32[]{:S(2)}, u32[]{:S(2)}) collective-permute-start(f32[3,128,128]{2,1,0:T(8,128)S(1)} %get-tuple-element.83), channel_id=1, source_target_pairs={{0,8},{4,12},{8,0},{12,4},{16,24},{20,28},{24,16},{28,20},{1,9},{5... | collective-permute-start | bytes 589832 | tf_op jit(solution)/shard_map/ppermute | solution.py:68
  22.7 5.3 %collective-permute-start.6 = (f32[128,256]{1,0:T(8,128)S(1)}, f32[128,256]{1,0:T(8,128)S(1)}, u32[]{:S(2)}, u32[]{:S(2)}) collective-permute-start(f32[128,256]{1,0:T(8,128)S(1)} %get-tuple-element.76.refs_1_), channel_id=1, source_target_pairs={{0,4},{4,0},{8,12},{12,8},{16,20},{20,16},{24,28},{28,24},{1,5},{5... | collective-permute-start | bytes 393224 | tf_op jit(solution)/shard_map/ppermute | solution.py:68
  24.2 8.9 %collective-permute-start.14 = (f32[2,128,128]{2,1,0:T(8,128)S(1)}, f32[2,128,128]{2,1,0:T(8,128)S(1)}, u32[]{:S(2)}, u32[]{:S(2)}) collective-permute-start(f32[2,128,128]{2,1,0:T(8,128)S(1)} %get-tuple-element.96), channel_id=1, source_target_pairs={{0,8},{4,12},{8,0},{12,4},{16,24},{20,28},{24,16},{28,20},{1,9},{5... | collective-permute-start | bytes 393224 | tf_op jit(solution)/shard_map/ppermute | solution.py:68
  28.4 4.3 %collective-permute-start.9 = (f32[64,256]{1,0:T(8,128)S(1)}, f32[64,256]{1,0:T(8,128)S(1)}, u32[]{:S(2)}, u32[]{:S(2)}) collective-permute-start(f32[64,256]{1,0:T(8,128)S(1)} %get-tuple-element.89), channel_id=1, source_target_pairs={{0,8},{4,12},{8,0},{12,4},{16,24},{20,28},{24,16},{28,20},{1,9},{5... | collective-permute-start | bytes 196616 | tf_op jit(solution)/shard_map/ppermute | solution.py:68
  30.0 7.5 %collective-permute-start.11 = (f32[2,128,128]{2,1,0:T(8,128)S(1)}, f32[2,128,128]{2,1,0:T(8,128)S(1)}, u32[]{:S(2)}, u32[]{:S(2)}) collective-permute-start(f32[2,128,128]{2,1,0:T(8,128)S(1)} %get-tuple-element.85.refs_7_), channel_id=1, source_target_pairs={{8,16},{12,20},{16,8},{20,12},{0,4},{4,0},{24,28},{28,24},{9,17},{... | collective-permute-start | bytes 393224 | tf_op jit(solution)/shard_map/ppermute | solution.py:612
  31.7 4.3 %collective-permute-start.12 = (f32[1,128,128]{2,1,0:T(8,128)S(1)}, f32[1,128,128]{2,1,0:T(8,128)S(1)}, u32[]{:S(2)}, u32[]{:S(2)}) collective-permute-start(f32[1,128,128]{2,1,0:T(8,128)S(1)} %get-tuple-element.86.refs_8_), channel_id=1, source_target_pairs={{8,16},{12,20},{16,8},{20,12},{0,4},{4,0},{24,28},{28,24},{9,17},{... | collective-permute-start | bytes 196616 | tf_op jit(solution)/shard_map/ppermute | solution.py:612
  33.1 4.3 %collective-permute-start.10 = (f32[64,256]{1,0:T(8,128)S(1)}, f32[64,256]{1,0:T(8,128)S(1)}, u32[]{:S(2)}, u32[]{:S(2)}) collective-permute-start(f32[64,256]{1,0:T(8,128)S(1)} %get-tuple-element.95), channel_id=1, source_target_pairs={{8,16},{12,20},{16,8},{20,12},{0,4},{4,0},{24,28},{28,24},{9,17},{... | collective-permute-start | bytes 196616 | tf_op jit(solution)/shard_map/ppermute | solution.py:641
  34.9 4.5 %collective-permute-start.15 = (f32[2,128,128]{2,1,0:T(8,128)S(1)}, f32[2,128,128]{2,1,0:T(8,128)S(1)}, u32[]{:S(2)}, u32[]{:S(2)}) collective-permute-start(f32[2,128,128]{2,1,0:T(8,128)S(1)} %collective-permute-done.14.refs_1_), channel_id=1, source_target_pairs={{0,1},{1,0},{2,3},{3,2},{4,5},{5,4},{6,7},{7,6},{8,9},{9,8},{10,11... | collective-permute-start | bytes 393224 | tf_op jit(solution)/shard_map/ppermute | solution.py:68
  37.7 4.3 %collective-permute-start.13 = (f32[64,256]{1,0:T(8,128)S(1)}, f32[64,256]{1,0:T(8,128)S(1)}, u32[]{:S(2)}, u32[]{:S(2)}) collective-permute-start(f32[64,256]{1,0:T(8,128)S(1)} %turn.1.refs_1_), channel_id=1, source_target_pairs={{0,8},{4,12},{8,0},{12,4},{16,24},{20,28},{24,16},{28,20},{1,9},{5... | collective-permute-start | bytes 196616 | tf_op jit(solution)/shard_map/ppermute | solution.py:68
  42.4 4.3 %collective-permute-start.17 = (f32[64,256]{1,0:T(8,128)S(1)}, f32[64,256]{1,0:T(8,128)S(1)}, u32[]{:S(2)}, u32[]{:S(2)}) collective-permute-start(f32[64,256]{1,0:T(8,128)S(1)} %leave.1.refs_10_), channel_id=1, source_target_pairs={{0,2},{1,3},{2,0},{3,1},{4,6},{5,7},{6,4},{7,5},{8,10},{9,11},{10,... | collective-permute-start | bytes 196616 | tf_op jit(solution)/shard_map/ppermute | solution.py:68
  44.2 2.6 %collective-permute-start.16 = (f32[64,256]{1,0:T(8,128)S(1)}, f32[64,256]{1,0:T(8,128)S(1)}, u32[]{:S(2)}, u32[]{:S(2)}) collective-permute-start(f32[64,256]{1,0:T(8,128)S(1)} %leave.1.refs_10_), channel_id=1, source_target_pairs={{0,1},{1,0},{2,3},{3,2},{4,5},{5,4},{6,7},{7,6},{8,9},{9,8},{10,11... | collective-permute-start | bytes 196616 | tf_op jit(solution)/shard_map/ppermute | solution.py:68
  46.8 1.3 %collective-permute-start.18 = (f32[64,256]{1,0:T(8,128)S(1)}, f32[64,256]{1,0:T(8,128)S(1)}, u32[]{:S(2)}, u32[]{:S(2)}) collective-permute-start(f32[64,256]{1,0:T(8,128)S(1)} %collective-permute-done.17.refs_12_), channel_id=1, source_target_pairs={{0,1},{1,0},{2,3},{3,2},{4,5},{5,4},{6,7},{7,6},{8,9},{9,8},{10,11... | collective-permute-start | bytes 196616 | tf_op jit(solution)/shard_map/ppermute | solution.py:68

commit v16 on v15

--- a/solution.py
+++ b/solution.py
@@ -597,7 +597,7 @@
     for bit in range(rounds - 1):
         last = bit == rounds - 2
         received = exchange(short[0] if last else message, "leaf", bit)
-        ahead = []
+        ahead, held = [], []
         if not last:
             other, mine = [exchange(part, "leaf", bit + 1) for part in parts]
             ahead = [other]
@@ -610,10 +610,11 @@
                 [((2, half, half), F32), ((1, half, half), F32)] + [((2, size, size), BF16)] * 3,
             )
             blocks = [lax.ppermute(b, "leaf", boundary) for b in ahead]
+            held = [other]
         sol, *message = call(
-            lambda *refs, bit=bit: step_kernel(bit, rounds, len(ahead), *refs),
+            lambda *refs, bit=bit: step_kernel(bit, rounds, len(held), *refs),
             f"step_{bit}",
-            [(V, a) for a in (sol, message, received, *tools)] + [(pl.ANY, a) for a in ahead],
+            [(V, a) for a in (sol, message, received, *tools)] + [(pl.ANY, a) for a in held],
             [share] + ([share] if last else [((2 * chunk, size), F32)]) + [share] * (bit >= rounds - 3),
         )
         if not last:

time: 52.7 us -> 52.6 us (level)
  starting transfers between devices: 20 us -> 19.3 us
  waiting for transfers between devices: 12.6 us -> 13.2 us
    ppermute x2, waiting for transfers between devices: 1.07 us -> 1.73 us  [local(): blocks = [lax.ppermute(b, 'leaf', boundary) for b in ahead]]
    ppermute x16, starting transfers between devices: 16.2 us -> 15.7 us  [swap(): return lax.ppermute(x, axis, [(i, i ^ mask) for i in range(n)])]
  transfers between devices with their start and end apart: 19 -> 19, of which waited for: 11 -> 10; matrix products, arithmetic and copies ran while one was open for 0% -> 0% of each run, Pallas kernels for 25% -> 25%
where the time goes in v16:
time: 52.6 us; the launch traced here: 52.4 us
  starting transfers between devices  19.3 us (37%)
  Pallas kernels  19.1 us (36%)
  waiting for transfers between devices  13.2 us (25%)
  between operations  0.76 us (1%)
    ppermute x16, starting transfers between devices, swap(): return lax.ppermute(x, axis, [(i, i ^ mask) for i in range(n)])  15.7 us
    pallas_call x14, Pallas kernels, call(): pl.pallas_call(kernel, name=name, in_specs=specs, out_specs=tuple((pl.Blo...  14.6 us
    ppermute x16, waiting for transfers between devices, swap(): return lax.ppermute(x, axis, [(i, i ^ mask) for i in range(n)])  10.4 us
    pallas_call x1, Pallas kernels, local_backward(): pl.pallas_call(lambda *refs: backward_kernel(nodes, fronts, *refs), name=...  4.54 us
    ppermute x2, starting transfers between devices, local(): blocks = [lax.ppermute(b, 'leaf', boundary) for b in ahead]  2.09 us
    ppermute x2, waiting for transfers between devices, local(): blocks = [lax.ppermute(b, 'leaf', boundary) for b in ahead]  1.73 us
    ppermute x1, starting transfers between devices, local(): came = lax.ppermute(message[0], 'leaf', boundary)  1.58 us
  transfers between devices with their start and end apart: 19, of which 10 were waited for; matrix products, arithmetic and copies ran while one was open for 0% of the time, Pallas kernels for 25%

profile of v16, /device:TPU:0, one launch (start us, length us, event | category | flops | bytes accessed | tf_op | source)
XLA Modules:
  0.0 52.4 jit_solution(6742034460646070305)
XLA Ops:
  0.6 0.9 %stack.1.refs_5_.refs_0_ = f32[2,64,256]{2,1,0:T(8,128)S(1)} custom-call(f32[64,256]{1,0:T(8,128)} %first.1, f32[64,256]{1,0:T(8,128)} %second.1), custom_call_target="tpu_custom_call" | custom-call | tf_op jit(solution)/shard_map/stack/pallas_call | solution.py:51
  1.5 3.0 %collective-permute-start.1 = (f32[2,64,256]{2,1,0:T(8,128)S(1)}, f32[2,64,256]{2,1,0:T(8,128)S(1)}, u32[]{:S(2)}, u32[]{:S(2)}) collective-permute-start(f32[2,64,256]{2,1,0:T(8,128)S(1)} %stack.1.refs_5_.refs_0_), channel_id=1, source_target_pairs={{0,2},{1,3},{2,0},{3,1},{4,6},{5,7},{6,4},{7,5},{8,10},{9,11},{10,... | collective-permute-start | bytes 393224 | tf_op jit(solution)/shard_map/ppermute | solution.py:68
  4.5 4.3 %prepare_first.1 = (f32[2,4,128,256]{3,2,1,0:T(8,128)S(1)}, bf16[4,256,256]{2,1,0:T(8,128)(2,1)S(1)}, bf16[4,256,256]{2,1,0:T(8,128)(2,1)S(1)}, bf16[4,256,256]{...) custom-call(s32[8,256]{1,0:T(8,128)} %refs_0_.3, ...), custom_call_target="tpu_custom_call" | custom-call | tf_op jit(solution)/shard_map/prepare_first/pallas_call | solution.py:51
  10.7 1.6 %collective-permute-start.3 = (f32[1,128,256]{2,1,0:T(8,128)S(1)}, f32[1,128,256]{2,1,0:T(8,128)S(1)}, u32[]{:S(2)}, u32[]{:S(2)}) collective-permute-start(f32[1,128,256]{2,1,0:T(8,128)S(1)} %get-tuple-element.69), channel_id=1, source_target_pairs={{0,4},{4,0},{8,12},{12,8},{16,20},{20,16},{24,28},{28,24},{1,5},{5... | collective-permute-start | bytes 393224 | tf_op jit(solution)/shard_map/ppermute | solution.py:68
  12.3 4.1 %local_forward.1 = (f32[8,256,256]{2,1,0:T(8,128)S(1)}, f32[128,256]{1,0:T(8,128)S(1)}, f32[128,256]{1,0:T(8,128)S(1)}) custom-call(s32[8]{0:T(128)} %refs_0_.5, f32[2,4,128,256]{3,2,1,0:T(8,128)S(1)} %get-tuple-element.50.refs_4_.refs_1_, f32[2,4,128,256]{3,2,1,0:T(8,128)S(1)} %get-tuple-element.55.refs_4_.refs_2_, ...), custom_call_target="tpu_custom_call" | custom-call | tf_op jit(solution)/shard_map/local_forward/pallas_call | solution.py:51
  17.0 0.8 %collective-permute-done.4.refs_1_ = f32[128,256]{1,0:T(8,128)S(1)} collective-permute-done((f32[128,256]{1,0:T(8,128)S(1)}, f32[128,256]{1,0:T(8,128)S(1)}, u32[]{:S(2)}, u32[]{:S(2)}) %collective-permute-start.4) | collective-permute-done | bytes 131104 | tf_op jit(solution)/shard_map/ppermute | solution.py:68
  18.7 1.0 %merge_0.1 = (f32[2,256,256]{2,1,0:T(8,128)S(1)}, f32[2,256,256]{2,1,0:T(8,128)S(1)}, bf16[2,256,256]{2,1,0:T(8,128)(2,1)S(1)}, bf16[2,256,256]{2,1,0:T(8,128)(2...) custom-call(f32[256,256]{1,0:T(8,128)S(1)} %get-tuple-element.66.ref, ...), custom_call_target="tpu_custom_call" | custom-call | tf_op jit(solution)/shard_map/merge_0/pallas_call | solution.py:51
  19.7 1.6 %collective-permute-start.8 = (f32[3,128,128]{2,1,0:T(8,128)S(1)}, f32[3,128,128]{2,1,0:T(8,128)S(1)}, u32[]{:S(2)}, u32[]{:S(2)}) collective-permute-start(f32[3,128,128]{2,1,0:T(8,128)S(1)} %get-tuple-element.82), channel_id=1, source_target_pairs={{0,8},{4,12},{8,0},{12,4},{16,24},{20,28},{24,16},{28,20},{1,9},{5... | collective-permute-start | bytes 589832 | tf_op jit(solution)/shard_map/ppermute | solution.py:68
  21.3 0.9 %collective-permute-done.5.other = f32[64,256]{1,0:T(8,128)S(1)} collective-permute-done((f32[64,256]{1,0:T(8,128)S(1)}, f32[64,256]{1,0:T(8,128)S(1)}, u32[]{:S(2)}, u32[]{:S(2)}) %collective-permute-start.5) | collective-permute-done | bytes 65568 | tf_op jit(solution)/shard_map/ppermute | solution.py:68
  22.7 1.6 %collective-permute-start.6 = (f32[128,256]{1,0:T(8,128)S(1)}, f32[128,256]{1,0:T(8,128)S(1)}, u32[]{:S(2)}, u32[]{:S(2)}) collective-permute-start(f32[128,256]{1,0:T(8,128)S(1)} %get-tuple-element.76.refs_1_), channel_id=1, source_target_pairs={{0,4},{4,0},{8,12},{12,8},{16,20},{20,16},{24,28},{28,24},{1,5},{5... | collective-permute-start | bytes 393224 | tf_op jit(solution)/shard_map/ppermute | solution.py:68
  24.2 1.6 %collective-permute-start.14 = (f32[2,128,128]{2,1,0:T(8,128)S(1)}, f32[2,128,128]{2,1,0:T(8,128)S(1)}, u32[]{:S(2)}, u32[]{:S(2)}) collective-permute-start(f32[2,128,128]{2,1,0:T(8,128)S(1)} %get-tuple-element.96), channel_id=1, source_target_pairs={{0,8},{4,12},{8,0},{12,4},{16,24},{20,28},{24,16},{28,20},{1,9},{5... | collective-permute-start | bytes 393224 | tf_op jit(solution)/shard_map/ppermute | solution.py:68
  25.8 1.9 %collective-permute-done.6.refs_2_ = f32[128,256]{1,0:T(8,128)S(1)} collective-permute-done((f32[128,256]{1,0:T(8,128)S(1)}, f32[128,256]{1,0:T(8,128)S(1)}, u32[]{:S(2)}, u32[]{:S(2)}) %collective-permute-start.6) | collective-permute-done | bytes 131104 | tf_op jit(solution)/shard_map/ppermute | solution.py:68
  28.1 1.6 %collective-permute-start.9 = (f32[64,256]{1,0:T(8,128)S(1)}, f32[64,256]{1,0:T(8,128)S(1)}, u32[]{:S(2)}, u32[]{:S(2)}) collective-permute-start(f32[64,256]{1,0:T(8,128)S(1)} %get-tuple-element.85), channel_id=1, source_target_pairs={{0,8},{4,12},{8,0},{12,4},{16,24},{20,28},{24,16},{28,20},{1,9},{5... | collective-permute-start | bytes 196616 | tf_op jit(solution)/shard_map/ppermute | solution.py:68
  30.5 1.6 %collective-permute-start.11 = (f32[2,128,128]{2,1,0:T(8,128)S(1)}, f32[2,128,128]{2,1,0:T(8,128)S(1)}, u32[]{:S(2)}, u32[]{:S(2)}) collective-permute-start(f32[2,128,128]{2,1,0:T(8,128)S(1)} %get-tuple-element.94), channel_id=1, source_target_pairs={{8,16},{12,20},{16,8},{20,12},{0,4},{4,0},{24,28},{28,24},{9,17},{... | collective-permute-start | bytes 393224 | tf_op jit(solution)/shard_map/ppermute | solution.py:612
  33.0 1.6 %collective-permute-start.10 = (f32[64,256]{1,0:T(8,128)S(1)}, f32[64,256]{1,0:T(8,128)S(1)}, u32[]{:S(2)}, u32[]{:S(2)}) collective-permute-start(f32[64,256]{1,0:T(8,128)S(1)} %get-tuple-element.93), channel_id=1, source_target_pairs={{8,16},{12,20},{16,8},{20,12},{0,4},{4,0},{24,28},{28,24},{9,17},{... | collective-permute-start | bytes 196616 | tf_op jit(solution)/shard_map/ppermute | solution.py:642
  34.6 1.7 %collective-permute-done.12.refs_3_ = f32[1,128,128]{2,1,0:T(8,128)S(1)} collective-permute-done((f32[1,128,128]{2,1,0:T(8,128)S(1)}, f32[1,128,128]{2,1,0:T(8,128)S(1)}, u32[]{:S(2)}, u32[]{:S(2)}) %collective-permute-start.12) | collective-permute-done | bytes 65568 | tf_op jit(solution)/shard_map/ppermute | solution.py:612
  36.3 1.0 %collective-permute-done.10.refs_1_ = f32[64,256]{1,0:T(8,128)S(1)} collective-permute-done((f32[64,256]{1,0:T(8,128)S(1)}, f32[64,256]{1,0:T(8,128)S(1)}, u32[]{:S(2)}, u32[]{:S(2)}) %collective-permute-start.10) | collective-permute-done | bytes 65568 | tf_op jit(solution)/shard_map/ppermute | solution.py:642
  37.6 1.5 %collective-permute-start.13 = (f32[64,256]{1,0:T(8,128)S(1)}, f32[64,256]{1,0:T(8,128)S(1)}, u32[]{:S(2)}, u32[]{:S(2)}) collective-permute-start(f32[64,256]{1,0:T(8,128)S(1)} %turn.1.refs_1_), channel_id=1, source_target_pairs={{0,8},{4,12},{8,0},{12,4},{16,24},{20,28},{24,16},{28,20},{1,9},{5... | collective-permute-start | bytes 196616 | tf_op jit(solution)/shard_map/ppermute | solution.py:68
  39.2 0.7 %last_merge.1.refs_3_ = bf16[2,256,256]{2,1,0:T(8,128)(2,1)S(1)} custom-call(f32[2,256,256]{2,1,0:T(8,128)S(1)} %get-tuple-element.87.refs_2_.refs_0_, f32[2,128,128]{2,1,0:T(8,128)S(1)} %collective-permute-done.14.refs_1_, f32[2,128,128]{2,1,0:T(8,128)S(1)} %collective-permute-done.15.refs_2_, bf16[2,256,256]{2,1,0:T(8,128)(2,1)S(1)} %get-tuple-element.89.refs_4_.refs_3_, ...), custom_call_target="tpu_custom_call" | custom-call | tf_op jit(solution)/shard_map/last_merge/pallas_call | solution.py:51
  39.9 2.0 %collective-permute-done.13.refs_2_ = f32[64,256]{1,0:T(8,128)S(1)} collective-permute-done((f32[64,256]{1,0:T(8,128)S(1)}, f32[64,256]{1,0:T(8,128)S(1)}, u32[]{:S(2)}, u32[]{:S(2)}) %collective-permute-start.13) | collective-permute-done | bytes 65568 | tf_op jit(solution)/shard_map/ppermute | solution.py:68
  42.3 1.2 %collective-permute-start.17 = (f32[64,256]{1,0:T(8,128)S(1)}, f32[64,256]{1,0:T(8,128)S(1)}, u32[]{:S(2)}, u32[]{:S(2)}) collective-permute-start(f32[64,256]{1,0:T(8,128)S(1)} %leave.1.refs_10_), channel_id=1, source_target_pairs={{0,2},{1,3},{2,0},{3,1},{4,6},{5,7},{6,4},{7,5},{8,10},{9,11},{10,... | collective-permute-start | bytes 196616 | tf_op jit(solution)/shard_map/ppermute | solution.py:68
  43.5 3.1 %collective-permute-done.17.refs_12_ = f32[64,256]{1,0:T(8,128)S(1)} collective-permute-done((f32[64,256]{1,0:T(8,128)S(1)}, f32[64,256]{1,0:T(8,128)S(1)}, u32[]{:S(2)}, u32[]{:S(2)}) %collective-permute-start.17) | collective-permute-done | bytes 65568 | tf_op jit(solution)/shard_map/ppermute | solution.py:68
  46.6 1.2 %collective-permute-done.18.refs_13_ = f32[64,256]{1,0:T(8,128)S(1)} collective-permute-done((f32[64,256]{1,0:T(8,128)S(1)}, f32[64,256]{1,0:T(8,128)S(1)}, u32[]{:S(2)}, u32[]{:S(2)}) %collective-permute-start.18) | collective-permute-done | bytes 65568 | tf_op jit(solution)/shard_map/ppermute | solution.py:68
  47.9 4.5 %local_backward.1 = (f32[8,256,256]{2,1,0:T(8,128)}, f32[64,256]{1,0:T(8,128)}) custom-call(s32[8]{0:T(128)} %refs_0_.5, f32[8,256,256]{2,1,0:T(8,128)S(1)} %get-tuple-element.67.refs_1_, bf16[4,256,256]{2,1,0:T(8,128)(2,1)S(1)} %get-tuple-element.57.refs_4_.refs_2_, bf16[4,256,256]{2,1,0:T(8,128)(2,1)S(1)} %get-tuple-element.58.refs_5_.refs_3_, ...), custom_call_target="tpu_custom_call" | custom-call | tf_op jit(solution)/shard_map/local_backward/pallas_call | solution.py:278
  (29 shorter events, 6.4 us)
Async XLA Ops:
  1.5 7.3 %collective-permute-start.1 = (f32[2,64,256]{2,1,0:T(8,128)S(1)}, f32[2,64,256]{2,1,0:T(8,128)S(1)}, u32[]{:S(2)}, u32[]{:S(2)}) collective-permute-start(f32[2,64,256]{2,1,0:T(8,128)S(1)} %stack.1.refs_5_.refs_0_), channel_id=1, source_target_pairs={{0,2},{1,3},{2,0},{3,1},{4,6},{5,7},{6,4},{7,5},{8,10},{9,11},{10,... | collective-permute-start | bytes 393224 | tf_op jit(solution)/shard_map/ppermute | solution.py:68
  4.5 5.5 %collective-permute-start = (f32[2,64,256]{2,1,0:T(8,128)S(1)}, f32[2,64,256]{2,1,0:T(8,128)S(1)}, u32[]{:S(2)}, u32[]{:S(2)}) collective-permute-start(f32[2,64,256]{2,1,0:T(8,128)S(1)} %stack.1.refs_5_.refs_0_), channel_id=1, source_target_pairs={{0,1},{1,0},{2,3},{3,2},{4,5},{5,4},{6,7},{7,6},{8,9},{9,8},{10,11... | collective-permute-start | bytes 393224 | tf_op jit(solution)/shard_map/ppermute | solution.py:68
  8.8 1.6 %collective-permute-start.2 = (f32[2,64,256]{2,1,0:T(8,128)S(1)}, f32[2,64,256]{2,1,0:T(8,128)S(1)}, u32[]{:S(2)}, u32[]{:S(2)}) collective-permute-start(f32[2,64,256]{2,1,0:T(8,128)S(1)} %collective-permute-done.1.refs_2_), channel_id=1, source_target_pairs={{0,1},{1,0},{2,3},{3,2},{4,5},{5,4},{6,7},{7,6},{8,9},{9,8},{10,11... | collective-permute-start | bytes 393224 | tf_op jit(solution)/shard_map/ppermute | solution.py:68
  10.7 5.8 %collective-permute-start.3 = (f32[1,128,256]{2,1,0:T(8,128)S(1)}, f32[1,128,256]{2,1,0:T(8,128)S(1)}, u32[]{:S(2)}, u32[]{:S(2)}) collective-permute-start(f32[1,128,256]{2,1,0:T(8,128)S(1)} %get-tuple-element.69), channel_id=1, source_target_pairs={{0,4},{4,0},{8,12},{12,8},{16,20},{20,16},{24,28},{28,24},{1,5},{5... | collective-permute-start | bytes 393224 | tf_op jit(solution)/shard_map/ppermute | solution.py:68
  16.5 1.3 %collective-permute-start.4 = (f32[128,256]{1,0:T(8,128)S(1)}, f32[128,256]{1,0:T(8,128)S(1)}, u32[]{:S(2)}, u32[]{:S(2)}) collective-permute-start(f32[128,256]{1,0:T(8,128)S(1)} %get-tuple-element.71), channel_id=1, source_target_pairs={{0,1},{1,0},{2,3},{3,2},{4,5},{5,4},{6,7},{7,6},{8,9},{9,8},{10,11... | collective-permute-start | bytes 393224 | tf_op jit(solution)/shard_map/ppermute | solution.py:68
  16.5 2.1 %collective-permute-start.7 = (f32[1,128,256]{2,1,0:T(8,128)S(1)}, f32[1,128,256]{2,1,0:T(8,128)S(1)}, u32[]{:S(2)}, u32[]{:S(2)}) collective-permute-start(f32[1,128,256]{2,1,0:T(8,128)S(1)} %collective-permute-done.3.refs_1_), channel_id=1, source_target_pairs={{0,1},{1,0},{2,3},{3,2},{4,5},{5,4},{6,7},{7,6},{8,9},{9,8},{10,11... | collective-permute-start | bytes 393224 | tf_op jit(solution)/shard_map/ppermute | solution.py:68
  17.9 4.3 %collective-permute-start.5 = (f32[64,256]{1,0:T(8,128)S(1)}, f32[64,256]{1,0:T(8,128)S(1)}, u32[]{:S(2)}, u32[]{:S(2)}) collective-permute-start(f32[64,256]{1,0:T(8,128)S(1)} %get-tuple-element.73.refs_3_), channel_id=1, source_target_pairs={{0,2},{1,3},{2,0},{3,1},{4,6},{5,7},{6,4},{7,5},{8,10},{9,11},{10,... | collective-permute-start | bytes 196616 | tf_op jit(solution)/shard_map/ppermute | solution.py:68
  19.7 8.0 %collective-permute-start.8 = (f32[3,128,128]{2,1,0:T(8,128)S(1)}, f32[3,128,128]{2,1,0:T(8,128)S(1)}, u32[]{:S(2)}, u32[]{:S(2)}) collective-permute-start(f32[3,128,128]{2,1,0:T(8,128)S(1)} %get-tuple-element.82), channel_id=1, source_target_pairs={{0,8},{4,12},{8,0},{12,4},{16,24},{20,28},{24,16},{28,20},{1,9},{5... | collective-permute-start | bytes 589832 | tf_op jit(solution)/shard_map/ppermute | solution.py:68
  22.7 5.0 %collective-permute-start.6 = (f32[128,256]{1,0:T(8,128)S(1)}, f32[128,256]{1,0:T(8,128)S(1)}, u32[]{:S(2)}, u32[]{:S(2)}) collective-permute-start(f32[128,256]{1,0:T(8,128)S(1)} %get-tuple-element.76.refs_1_), channel_id=1, source_target_pairs={{0,4},{4,0},{8,12},{12,8},{16,20},{20,16},{24,28},{28,24},{1,5},{5... | collective-permute-start | bytes 393224 | tf_op jit(solution)/shard_map/ppermute | solution.py:68
  24.2 10.3 %collective-permute-start.14 = (f32[2,128,128]{2,1,0:T(8,128)S(1)}, f32[2,128,128]{2,1,0:T(8,128)S(1)}, u32[]{:S(2)}, u32[]{:S(2)}) collective-permute-start(f32[2,128,128]{2,1,0:T(8,128)S(1)} %get-tuple-element.96), channel_id=1, source_target_pairs={{0,8},{4,12},{8,0},{12,4},{16,24},{20,28},{24,16},{28,20},{1,9},{5... | collective-permute-start | bytes 393224 | tf_op jit(solution)/shard_map/ppermute | solution.py:68
  28.1 4.4 %collective-permute-start.9 = (f32[64,256]{1,0:T(8,128)S(1)}, f32[64,256]{1,0:T(8,128)S(1)}, u32[]{:S(2)}, u32[]{:S(2)}) collective-permute-start(f32[64,256]{1,0:T(8,128)S(1)} %get-tuple-element.85), channel_id=1, source_target_pairs={{0,8},{4,12},{8,0},{12,4},{16,24},{20,28},{24,16},{28,20},{1,9},{5... | collective-permute-start | bytes 196616 | tf_op jit(solution)/shard_map/ppermute | solution.py:68
  30.5 6.9 %collective-permute-start.11 = (f32[2,128,128]{2,1,0:T(8,128)S(1)}, f32[2,128,128]{2,1,0:T(8,128)S(1)}, u32[]{:S(2)}, u32[]{:S(2)}) collective-permute-start(f32[2,128,128]{2,1,0:T(8,128)S(1)} %get-tuple-element.94), channel_id=1, source_target_pairs={{8,16},{12,20},{16,8},{20,12},{0,4},{4,0},{24,28},{28,24},{9,17},{... | collective-permute-start | bytes 393224 | tf_op jit(solution)/shard_map/ppermute | solution.py:612
  32.1 4.3 %collective-permute-start.12 = (f32[1,128,128]{2,1,0:T(8,128)S(1)}, f32[1,128,128]{2,1,0:T(8,128)S(1)}, u32[]{:S(2)}, u32[]{:S(2)}) collective-permute-start(f32[1,128,128]{2,1,0:T(8,128)S(1)} %get-tuple-element.95), channel_id=1, source_target_pairs={{8,16},{12,20},{16,8},{20,12},{0,4},{4,0},{24,28},{28,24},{9,17},{... | collective-permute-start | bytes 196616 | tf_op jit(solution)/shard_map/ppermute | solution.py:612
  33.0 4.3 %collective-permute-start.10 = (f32[64,256]{1,0:T(8,128)S(1)}, f32[64,256]{1,0:T(8,128)S(1)}, u32[]{:S(2)}, u32[]{:S(2)}) collective-permute-start(f32[64,256]{1,0:T(8,128)S(1)} %get-tuple-element.93), channel_id=1, source_target_pairs={{8,16},{12,20},{16,8},{20,12},{0,4},{4,0},{24,28},{28,24},{9,17},{... | collective-permute-start | bytes 196616 | tf_op jit(solution)/shard_map/ppermute | solution.py:642
  34.6 4.6 %collective-permute-start.15 = (f32[2,128,128]{2,1,0:T(8,128)S(1)}, f32[2,128,128]{2,1,0:T(8,128)S(1)}, u32[]{:S(2)}, u32[]{:S(2)}) collective-permute-start(f32[2,128,128]{2,1,0:T(8,128)S(1)} %collective-permute-done.14.refs_1_), channel_id=1, source_target_pairs={{0,1},{1,0},{2,3},{3,2},{4,5},{5,4},{6,7},{7,6},{8,9},{9,8},{10,11... | collective-permute-start | bytes 393224 | tf_op jit(solution)/shard_map/ppermute | solution.py:68
  37.6 4.3 %collective-permute-start.13 = (f32[64,256]{1,0:T(8,128)S(1)}, f32[64,256]{1,0:T(8,128)S(1)}, u32[]{:S(2)}, u32[]{:S(2)}) collective-permute-start(f32[64,256]{1,0:T(8,128)S(1)} %turn.1.refs_1_), channel_id=1, source_target_pairs={{0,8},{4,12},{8,0},{12,4},{16,24},{20,28},{24,16},{28,20},{1,9},{5... | collective-permute-start | bytes 196616 | tf_op jit(solution)/shard_map/ppermute | solution.py:68
  42.3 4.3 %collective-permute-start.17 = (f32[64,256]{1,0:T(8,128)S(1)}, f32[64,256]{1,0:T(8,128)S(1)}, u32[]{:S(2)}, u32[]{:S(2)}) collective-permute-start(f32[64,256]{1,0:T(8,128)S(1)} %leave.1.refs_10_), channel_id=1, source_target_pairs={{0,2},{1,3},{2,0},{3,1},{4,6},{5,7},{6,4},{7,5},{8,10},{9,11},{10,... | collective-permute-start | bytes 196616 | tf_op jit(solution)/shard_map/ppermute | solution.py:68
  43.5 3.1 %collective-permute-start.16 = (f32[64,256]{1,0:T(8,128)S(1)}, f32[64,256]{1,0:T(8,128)S(1)}, u32[]{:S(2)}, u32[]{:S(2)}) collective-permute-start(f32[64,256]{1,0:T(8,128)S(1)} %leave.1.refs_10_), channel_id=1, source_target_pairs={{0,1},{1,0},{2,3},{3,2},{4,5},{5,4},{6,7},{7,6},{8,9},{9,8},{10,11... | collective-permute-start | bytes 196616 | tf_op jit(solution)/shard_map/ppermute | solution.py:68
  46.6 1.3 %collective-permute-start.18 = (f32[64,256]{1,0:T(8,128)S(1)}, f32[64,256]{1,0:T(8,128)S(1)}, u32[]{:S(2)}, u32[]{:S(2)}) collective-permute-start(f32[64,256]{1,0:T(8,128)S(1)} %collective-permute-done.17.refs_12_), channel_id=1, source_target_pairs={{0,1},{1,0},{2,3},{3,2},{4,5},{5,4},{6,7},{7,6},{8,9},{9,8},{10,11... | collective-permute-start | bytes 196616 | tf_op jit(solution)/shard_map/ppermute | solution.py:68

commit v17 on v16

--- a/solution.py
+++ b/solution.py
@@ -257,7 +257,7 @@
         out = pltpu.make_async_copy(staged.at[k], sol.at[k], sems.at[k])
         out.start()
         outs.append(out)
-        if k == nodes - 1:
+        if k == 0:
             for h in range(HALVES):
                 square[:, h * width : (h + 1) * width] = known[h][nodes].T
             share = sep_v.shape[0]

time: 52.6 us -> 52.6 us (level)
  no operation moved by 1% of the time
where the time goes in v17:
time: 52.6 us; the launch traced here: 52.4 us
  starting transfers between devices  19.3 us (37%)
  Pallas kernels  19.1 us (36%)
  waiting for transfers between devices  13.2 us (25%)
  between operations  0.76 us (1%)
    ppermute x16, starting transfers between devices, swap(): return lax.ppermute(x, axis, [(i, i ^ mask) for i in range(n)])  15.7 us
    pallas_call x14, Pallas kernels, call(): pl.pallas_call(kernel, name=name, in_specs=specs, out_specs=tuple((pl.Blo...  14.6 us
    ppermute x16, waiting for transfers between devices, swap(): return lax.ppermute(x, axis, [(i, i ^ mask) for i in range(n)])  10.4 us
    pallas_call x1, Pallas kernels, local_backward(): pl.pallas_call(lambda *refs: backward_kernel(nodes, fronts, *refs), name=...  4.55 us
    ppermute x2, starting transfers between devices, local(): blocks = [lax.ppermute(b, 'leaf', boundary) for b in ahead]  2.09 us
    ppermute x2, waiting for transfers between devices, local(): blocks = [lax.ppermute(b, 'leaf', boundary) for b in ahead]  1.73 us
    ppermute x1, starting transfers between devices, local(): came = lax.ppermute(message[0], 'leaf', boundary)  1.58 us
  transfers between devices with their start and end apart: 19, of which 10 were waited for; matrix products, arithmetic and copies ran while one was open for 0% of the time, Pallas kernels for 25%

profile of v17, /device:TPU:0, one launch (start us, length us, event | category | flops | bytes accessed | tf_op | source)
XLA Modules:
  0.0 52.4 jit_solution(362177437123793265)
XLA Ops:
  0.6 0.9 %stack.1.refs_5_.refs_0_ = f32[2,64,256]{2,1,0:T(8,128)S(1)} custom-call(f32[64,256]{1,0:T(8,128)} %first.1, f32[64,256]{1,0:T(8,128)} %second.1), custom_call_target="tpu_custom_call" | custom-call | tf_op jit(solution)/shard_map/stack/pallas_call | solution.py:51
  1.5 3.0 %collective-permute-start.1 = (f32[2,64,256]{2,1,0:T(8,128)S(1)}, f32[2,64,256]{2,1,0:T(8,128)S(1)}, u32[]{:S(2)}, u32[]{:S(2)}) collective-permute-start(f32[2,64,256]{2,1,0:T(8,128)S(1)} %stack.1.refs_5_.refs_0_), channel_id=1, source_target_pairs={{0,2},{1,3},{2,0},{3,1},{4,6},{5,7},{6,4},{7,5},{8,10},{9,11},{10,... | collective-permute-start | bytes 393224 | tf_op jit(solution)/shard_map/ppermute | solution.py:68
  4.5 4.3 %prepare_first.1 = (f32[2,4,128,256]{3,2,1,0:T(8,128)S(1)}, bf16[4,256,256]{2,1,0:T(8,128)(2,1)S(1)}, bf16[4,256,256]{2,1,0:T(8,128)(2,1)S(1)}, bf16[4,256,256]{...) custom-call(s32[8,256]{1,0:T(8,128)} %refs_0_.3, ...), custom_call_target="tpu_custom_call" | custom-call | tf_op jit(solution)/shard_map/prepare_first/pallas_call | solution.py:51
  10.7 1.6 %collective-permute-start.3 = (f32[1,128,256]{2,1,0:T(8,128)S(1)}, f32[1,128,256]{2,1,0:T(8,128)S(1)}, u32[]{:S(2)}, u32[]{:S(2)}) collective-permute-start(f32[1,128,256]{2,1,0:T(8,128)S(1)} %get-tuple-element.69), channel_id=1, source_target_pairs={{0,4},{4,0},{8,12},{12,8},{16,20},{20,16},{24,28},{28,24},{1,5},{5... | collective-permute-start | bytes 393224 | tf_op jit(solution)/shard_map/ppermute | solution.py:68
  12.3 4.1 %local_forward.1 = (f32[8,256,256]{2,1,0:T(8,128)S(1)}, f32[128,256]{1,0:T(8,128)S(1)}, f32[128,256]{1,0:T(8,128)S(1)}) custom-call(s32[8]{0:T(128)} %refs_0_.5, f32[2,4,128,256]{3,2,1,0:T(8,128)S(1)} %get-tuple-element.50.refs_4_.refs_1_, f32[2,4,128,256]{3,2,1,0:T(8,128)S(1)} %get-tuple-element.55.refs_4_.refs_2_, ...), custom_call_target="tpu_custom_call" | custom-call | tf_op jit(solution)/shard_map/local_forward/pallas_call | solution.py:51
  17.0 0.8 %collective-permute-done.4.refs_1_ = f32[128,256]{1,0:T(8,128)S(1)} collective-permute-done((f32[128,256]{1,0:T(8,128)S(1)}, f32[128,256]{1,0:T(8,128)S(1)}, u32[]{:S(2)}, u32[]{:S(2)}) %collective-permute-start.4) | collective-permute-done | bytes 131104 | tf_op jit(solution)/shard_map/ppermute | solution.py:68
  18.7 1.0 %merge_0.1 = (f32[2,256,256]{2,1,0:T(8,128)S(1)}, f32[2,256,256]{2,1,0:T(8,128)S(1)}, bf16[2,256,256]{2,1,0:T(8,128)(2,1)S(1)}, bf16[2,256,256]{2,1,0:T(8,128)(2...) custom-call(f32[256,256]{1,0:T(8,128)S(1)} %get-tuple-element.66.ref, ...), custom_call_target="tpu_custom_call" | custom-call | tf_op jit(solution)/shard_map/merge_0/pallas_call | solution.py:51
  19.7 1.6 %collective-permute-start.8 = (f32[3,128,128]{2,1,0:T(8,128)S(1)}, f32[3,128,128]{2,1,0:T(8,128)S(1)}, u32[]{:S(2)}, u32[]{:S(2)}) collective-permute-start(f32[3,128,128]{2,1,0:T(8,128)S(1)} %get-tuple-element.82), channel_id=1, source_target_pairs={{0,8},{4,12},{8,0},{12,4},{16,24},{20,28},{24,16},{28,20},{1,9},{5... | collective-permute-start | bytes 589832 | tf_op jit(solution)/shard_map/ppermute | solution.py:68
  21.3 0.9 %collective-permute-done.5.other = f32[64,256]{1,0:T(8,128)S(1)} collective-permute-done((f32[64,256]{1,0:T(8,128)S(1)}, f32[64,256]{1,0:T(8,128)S(1)}, u32[]{:S(2)}, u32[]{:S(2)}) %collective-permute-start.5) | collective-permute-done | bytes 65568 | tf_op jit(solution)/shard_map/ppermute | solution.py:68
  22.7 1.6 %collective-permute-start.6 = (f32[128,256]{1,0:T(8,128)S(1)}, f32[128,256]{1,0:T(8,128)S(1)}, u32[]{:S(2)}, u32[]{:S(2)}) collective-permute-start(f32[128,256]{1,0:T(8,128)S(1)} %get-tuple-element.76.refs_1_), channel_id=1, source_target_pairs={{0,4},{4,0},{8,12},{12,8},{16,20},{20,16},{24,28},{28,24},{1,5},{5... | collective-permute-start | bytes 393224 | tf_op jit(solution)/shard_map/ppermute | solution.py:68
  24.2 1.6 %collective-permute-start.14 = (f32[2,128,128]{2,1,0:T(8,128)S(1)}, f32[2,128,128]{2,1,0:T(8,128)S(1)}, u32[]{:S(2)}, u32[]{:S(2)}) collective-permute-start(f32[2,128,128]{2,1,0:T(8,128)S(1)} %get-tuple-element.96), channel_id=1, source_target_pairs={{0,8},{4,12},{8,0},{12,4},{16,24},{20,28},{24,16},{28,20},{1,9},{5... | collective-permute-start | bytes 393224 | tf_op jit(solution)/shard_map/ppermute | solution.py:68
  25.8 1.9 %collective-permute-done.6.refs_2_ = f32[128,256]{1,0:T(8,128)S(1)} collective-permute-done((f32[128,256]{1,0:T(8,128)S(1)}, f32[128,256]{1,0:T(8,128)S(1)}, u32[]{:S(2)}, u32[]{:S(2)}) %collective-permute-start.6) | collective-permute-done | bytes 131104 | tf_op jit(solution)/shard_map/ppermute | solution.py:68
  28.1 1.6 %collective-permute-start.9 = (f32[64,256]{1,0:T(8,128)S(1)}, f32[64,256]{1,0:T(8,128)S(1)}, u32[]{:S(2)}, u32[]{:S(2)}) collective-permute-start(f32[64,256]{1,0:T(8,128)S(1)} %get-tuple-element.85), channel_id=1, source_target_pairs={{0,8},{4,12},{8,0},{12,4},{16,24},{20,28},{24,16},{28,20},{1,9},{5... | collective-permute-start | bytes 196616 | tf_op jit(solution)/shard_map/ppermute | solution.py:68
  30.5 1.6 %collective-permute-start.11 = (f32[2,128,128]{2,1,0:T(8,128)S(1)}, f32[2,128,128]{2,1,0:T(8,128)S(1)}, u32[]{:S(2)}, u32[]{:S(2)}) collective-permute-start(f32[2,128,128]{2,1,0:T(8,128)S(1)} %get-tuple-element.94), channel_id=1, source_target_pairs={{8,16},{12,20},{16,8},{20,12},{0,4},{4,0},{24,28},{28,24},{9,17},{... | collective-permute-start | bytes 393224 | tf_op jit(solution)/shard_map/ppermute | solution.py:612
  33.0 1.6 %collective-permute-start.10 = (f32[64,256]{1,0:T(8,128)S(1)}, f32[64,256]{1,0:T(8,128)S(1)}, u32[]{:S(2)}, u32[]{:S(2)}) collective-permute-start(f32[64,256]{1,0:T(8,128)S(1)} %get-tuple-element.93), channel_id=1, source_target_pairs={{8,16},{12,20},{16,8},{20,12},{0,4},{4,0},{24,28},{28,24},{9,17},{... | collective-permute-start | bytes 196616 | tf_op jit(solution)/shard_map/ppermute | solution.py:642
  34.6 1.7 %collective-permute-done.12.refs_3_ = f32[1,128,128]{2,1,0:T(8,128)S(1)} collective-permute-done((f32[1,128,128]{2,1,0:T(8,128)S(1)}, f32[1,128,128]{2,1,0:T(8,128)S(1)}, u32[]{:S(2)}, u32[]{:S(2)}) %collective-permute-start.12) | collective-permute-done | bytes 65568 | tf_op jit(solution)/shard_map/ppermute | solution.py:612
  36.3 1.0 %collective-permute-done.10.refs_1_ = f32[64,256]{1,0:T(8,128)S(1)} collective-permute-done((f32[64,256]{1,0:T(8,128)S(1)}, f32[64,256]{1,0:T(8,128)S(1)}, u32[]{:S(2)}, u32[]{:S(2)}) %collective-permute-start.10) | collective-permute-done | bytes 65568 | tf_op jit(solution)/shard_map/ppermute | solution.py:642
  37.6 1.5 %collective-permute-start.13 = (f32[64,256]{1,0:T(8,128)S(1)}, f32[64,256]{1,0:T(8,128)S(1)}, u32[]{:S(2)}, u32[]{:S(2)}) collective-permute-start(f32[64,256]{1,0:T(8,128)S(1)} %turn.1.refs_1_), channel_id=1, source_target_pairs={{0,8},{4,12},{8,0},{12,4},{16,24},{20,28},{24,16},{28,20},{1,9},{5... | collective-permute-start | bytes 196616 | tf_op jit(solution)/shard_map/ppermute | solution.py:68
  39.2 0.7 %last_merge.1.refs_3_ = bf16[2,256,256]{2,1,0:T(8,128)(2,1)S(1)} custom-call(f32[2,256,256]{2,1,0:T(8,128)S(1)} %get-tuple-element.87.refs_2_.refs_0_, f32[2,128,128]{2,1,0:T(8,128)S(1)} %collective-permute-done.14.refs_1_, f32[2,128,128]{2,1,0:T(8,128)S(1)} %collective-permute-done.15.refs_2_, bf16[2,256,256]{2,1,0:T(8,128)(2,1)S(1)} %get-tuple-element.89.refs_4_.refs_3_, ...), custom_call_target="tpu_custom_call" | custom-call | tf_op jit(solution)/shard_map/last_merge/pallas_call | solution.py:51
  39.9 2.0 %collective-permute-done.13.refs_2_ = f32[64,256]{1,0:T(8,128)S(1)} collective-permute-done((f32[64,256]{1,0:T(8,128)S(1)}, f32[64,256]{1,0:T(8,128)S(1)}, u32[]{:S(2)}, u32[]{:S(2)}) %collective-permute-start.13) | collective-permute-done | bytes 65568 | tf_op jit(solution)/shard_map/ppermute | solution.py:68
  42.3 1.2 %collective-permute-start.17 = (f32[64,256]{1,0:T(8,128)S(1)}, f32[64,256]{1,0:T(8,128)S(1)}, u32[]{:S(2)}, u32[]{:S(2)}) collective-permute-start(f32[64,256]{1,0:T(8,128)S(1)} %leave.1.refs_10_), channel_id=1, source_target_pairs={{0,2},{1,3},{2,0},{3,1},{4,6},{5,7},{6,4},{7,5},{8,10},{9,11},{10,... | collective-permute-start | bytes 196616 | tf_op jit(solution)/shard_map/ppermute | solution.py:68
  43.5 3.1 %collective-permute-done.17.refs_12_ = f32[64,256]{1,0:T(8,128)S(1)} collective-permute-done((f32[64,256]{1,0:T(8,128)S(1)}, f32[64,256]{1,0:T(8,128)S(1)}, u32[]{:S(2)}, u32[]{:S(2)}) %collective-permute-start.17) | collective-permute-done | bytes 65568 | tf_op jit(solution)/shard_map/ppermute | solution.py:68
  46.6 1.2 %collective-permute-done.18.refs_13_ = f32[64,256]{1,0:T(8,128)S(1)} collective-permute-done((f32[64,256]{1,0:T(8,128)S(1)}, f32[64,256]{1,0:T(8,128)S(1)}, u32[]{:S(2)}, u32[]{:S(2)}) %collective-permute-start.18) | collective-permute-done | bytes 65568 | tf_op jit(solution)/shard_map/ppermute | solution.py:68
  47.9 4.6 %local_backward.1 = (f32[8,256,256]{2,1,0:T(8,128)}, f32[64,256]{1,0:T(8,128)}) custom-call(s32[8]{0:T(128)} %refs_0_.5, f32[8,256,256]{2,1,0:T(8,128)S(1)} %get-tuple-element.67.refs_1_, bf16[4,256,256]{2,1,0:T(8,128)(2,1)S(1)} %get-tuple-element.57.refs_4_.refs_2_, bf16[4,256,256]{2,1,0:T(8,128)(2,1)S(1)} %get-tuple-element.58.refs_5_.refs_3_, ...), custom_call_target="tpu_custom_call" | custom-call | tf_op jit(solution)/shard_map/local_backward/pallas_call | solution.py:278
  (29 shorter events, 6.4 us)
Async XLA Ops:
  1.5 7.3 %collective-permute-start.1 = (f32[2,64,256]{2,1,0:T(8,128)S(1)}, f32[2,64,256]{2,1,0:T(8,128)S(1)}, u32[]{:S(2)}, u32[]{:S(2)}) collective-permute-start(f32[2,64,256]{2,1,0:T(8,128)S(1)} %stack.1.refs_5_.refs_0_), channel_id=1, source_target_pairs={{0,2},{1,3},{2,0},{3,1},{4,6},{5,7},{6,4},{7,5},{8,10},{9,11},{10,... | collective-permute-start | bytes 393224 | tf_op jit(solution)/shard_map/ppermute | solution.py:68
  4.5 5.5 %collective-permute-start = (f32[2,64,256]{2,1,0:T(8,128)S(1)}, f32[2,64,256]{2,1,0:T(8,128)S(1)}, u32[]{:S(2)}, u32[]{:S(2)}) collective-permute-start(f32[2,64,256]{2,1,0:T(8,128)S(1)} %stack.1.refs_5_.refs_0_), channel_id=1, source_target_pairs={{0,1},{1,0},{2,3},{3,2},{4,5},{5,4},{6,7},{7,6},{8,9},{9,8},{10,11... | collective-permute-start | bytes 393224 | tf_op jit(solution)/shard_map/ppermute | solution.py:68
  8.8 1.6 %collective-permute-start.2 = (f32[2,64,256]{2,1,0:T(8,128)S(1)}, f32[2,64,256]{2,1,0:T(8,128)S(1)}, u32[]{:S(2)}, u32[]{:S(2)}) collective-permute-start(f32[2,64,256]{2,1,0:T(8,128)S(1)} %collective-permute-done.1.refs_2_), channel_id=1, source_target_pairs={{0,1},{1,0},{2,3},{3,2},{4,5},{5,4},{6,7},{7,6},{8,9},{9,8},{10,11... | collective-permute-start | bytes 393224 | tf_op jit(solution)/shard_map/ppermute | solution.py:68
  10.7 5.8 %collective-permute-start.3 = (f32[1,128,256]{2,1,0:T(8,128)S(1)}, f32[1,128,256]{2,1,0:T(8,128)S(1)}, u32[]{:S(2)}, u32[]{:S(2)}) collective-permute-start(f32[1,128,256]{2,1,0:T(8,128)S(1)} %get-tuple-element.69), channel_id=1, source_target_pairs={{0,4},{4,0},{8,12},{12,8},{16,20},{20,16},{24,28},{28,24},{1,5},{5... | collective-permute-start | bytes 393224 | tf_op jit(solution)/shard_map/ppermute | solution.py:68
  16.5 1.3 %collective-permute-start.4 = (f32[128,256]{1,0:T(8,128)S(1)}, f32[128,256]{1,0:T(8,128)S(1)}, u32[]{:S(2)}, u32[]{:S(2)}) collective-permute-start(f32[128,256]{1,0:T(8,128)S(1)} %get-tuple-element.71), channel_id=1, source_target_pairs={{0,1},{1,0},{2,3},{3,2},{4,5},{5,4},{6,7},{7,6},{8,9},{9,8},{10,11... | collective-permute-start | bytes 393224 | tf_op jit(solution)/shard_map/ppermute | solution.py:68
  16.5 2.1 %collective-permute-start.7 = (f32[1,128,256]{2,1,0:T(8,128)S(1)}, f32[1,128,256]{2,1,0:T(8,128)S(1)}, u32[]{:S(2)}, u32[]{:S(2)}) collective-permute-start(f32[1,128,256]{2,1,0:T(8,128)S(1)} %collective-permute-done.3.refs_1_), channel_id=1, source_target_pairs={{0,1},{1,0},{2,3},{3,2},{4,5},{5,4},{6,7},{7,6},{8,9},{9,8},{10,11... | collective-permute-start | bytes 393224 | tf_op jit(solution)/shard_map/ppermute | solution.py:68
  17.9 4.3 %collective-permute-start.5 = (f32[64,256]{1,0:T(8,128)S(1)}, f32[64,256]{1,0:T(8,128)S(1)}, u32[]{:S(2)}, u32[]{:S(2)}) collective-permute-start(f32[64,256]{1,0:T(8,128)S(1)} %get-tuple-element.73.refs_3_), channel_id=1, source_target_pairs={{0,2},{1,3},{2,0},{3,1},{4,6},{5,7},{6,4},{7,5},{8,10},{9,11},{10,... | collective-permute-start | bytes 196616 | tf_op jit(solution)/shard_map/ppermute | solution.py:68
  19.7 8.0 %collective-permute-start.8 = (f32[3,128,128]{2,1,0:T(8,128)S(1)}, f32[3,128,128]{2,1,0:T(8,128)S(1)}, u32[]{:S(2)}, u32[]{:S(2)}) collective-permute-start(f32[3,128,128]{2,1,0:T(8,128)S(1)} %get-tuple-element.82), channel_id=1, source_target_pairs={{0,8},{4,12},{8,0},{12,4},{16,24},{20,28},{24,16},{28,20},{1,9},{5... | collective-permute-start | bytes 589832 | tf_op jit(solution)/shard_map/ppermute | solution.py:68
  22.7 5.0 %collective-permute-start.6 = (f32[128,256]{1,0:T(8,128)S(1)}, f32[128,256]{1,0:T(8,128)S(1)}, u32[]{:S(2)}, u32[]{:S(2)}) collective-permute-start(f32[128,256]{1,0:T(8,128)S(1)} %get-tuple-element.76.refs_1_), channel_id=1, source_target_pairs={{0,4},{4,0},{8,12},{12,8},{16,20},{20,16},{24,28},{28,24},{1,5},{5... | collective-permute-start | bytes 393224 | tf_op jit(solution)/shard_map/ppermute | solution.py:68
  24.2 10.3 %collective-permute-start.14 = (f32[2,128,128]{2,1,0:T(8,128)S(1)}, f32[2,128,128]{2,1,0:T(8,128)S(1)}, u32[]{:S(2)}, u32[]{:S(2)}) collective-permute-start(f32[2,128,128]{2,1,0:T(8,128)S(1)} %get-tuple-element.96), channel_id=1, source_target_pairs={{0,8},{4,12},{8,0},{12,4},{16,24},{20,28},{24,16},{28,20},{1,9},{5... | collective-permute-start | bytes 393224 | tf_op jit(solution)/shard_map/ppermute | solution.py:68
  28.1 4.4 %collective-permute-start.9 = (f32[64,256]{1,0:T(8,128)S(1)}, f32[64,256]{1,0:T(8,128)S(1)}, u32[]{:S(2)}, u32[]{:S(2)}) collective-permute-start(f32[64,256]{1,0:T(8,128)S(1)} %get-tuple-element.85), channel_id=1, source_target_pairs={{0,8},{4,12},{8,0},{12,4},{16,24},{20,28},{24,16},{28,20},{1,9},{5... | collective-permute-start | bytes 196616 | tf_op jit(solution)/shard_map/ppermute | solution.py:68
  30.5 6.9 %collective-permute-start.11 = (f32[2,128,128]{2,1,0:T(8,128)S(1)}, f32[2,128,128]{2,1,0:T(8,128)S(1)}, u32[]{:S(2)}, u32[]{:S(2)}) collective-permute-start(f32[2,128,128]{2,1,0:T(8,128)S(1)} %get-tuple-element.94), channel_id=1, source_target_pairs={{8,16},{12,20},{16,8},{20,12},{0,4},{4,0},{24,28},{28,24},{9,17},{... | collective-permute-start | bytes 393224 | tf_op jit(solution)/shard_map/ppermute | solution.py:612
  32.1 4.3 %collective-permute-start.12 = (f32[1,128,128]{2,1,0:T(8,128)S(1)}, f32[1,128,128]{2,1,0:T(8,128)S(1)}, u32[]{:S(2)}, u32[]{:S(2)}) collective-permute-start(f32[1,128,128]{2,1,0:T(8,128)S(1)} %get-tuple-element.95), channel_id=1, source_target_pairs={{8,16},{12,20},{16,8},{20,12},{0,4},{4,0},{24,28},{28,24},{9,17},{... | collective-permute-start | bytes 196616 | tf_op jit(solution)/shard_map/ppermute | solution.py:612
  33.0 4.3 %collective-permute-start.10 = (f32[64,256]{1,0:T(8,128)S(1)}, f32[64,256]{1,0:T(8,128)S(1)}, u32[]{:S(2)}, u32[]{:S(2)}) collective-permute-start(f32[64,256]{1,0:T(8,128)S(1)} %get-tuple-element.93), channel_id=1, source_target_pairs={{8,16},{12,20},{16,8},{20,12},{0,4},{4,0},{24,28},{28,24},{9,17},{... | collective-permute-start | bytes 196616 | tf_op jit(solution)/shard_map/ppermute | solution.py:642
  34.6 4.6 %collective-permute-start.15 = (f32[2,128,128]{2,1,0:T(8,128)S(1)}, f32[2,128,128]{2,1,0:T(8,128)S(1)}, u32[]{:S(2)}, u32[]{:S(2)}) collective-permute-start(f32[2,128,128]{2,1,0:T(8,128)S(1)} %collective-permute-done.14.refs_1_), channel_id=1, source_target_pairs={{0,1},{1,0},{2,3},{3,2},{4,5},{5,4},{6,7},{7,6},{8,9},{9,8},{10,11... | collective-permute-start | bytes 393224 | tf_op jit(solution)/shard_map/ppermute | solution.py:68
  37.6 4.3 %collective-permute-start.13 = (f32[64,256]{1,0:T(8,128)S(1)}, f32[64,256]{1,0:T(8,128)S(1)}, u32[]{:S(2)}, u32[]{:S(2)}) collective-permute-start(f32[64,256]{1,0:T(8,128)S(1)} %turn.1.refs_1_), channel_id=1, source_target_pairs={{0,8},{4,12},{8,0},{12,4},{16,24},{20,28},{24,16},{28,20},{1,9},{5... | collective-permute-start | bytes 196616 | tf_op jit(solution)/shard_map/ppermute | solution.py:68
  42.3 4.3 %collective-permute-start.17 = (f32[64,256]{1,0:T(8,128)S(1)}, f32[64,256]{1,0:T(8,128)S(1)}, u32[]{:S(2)}, u32[]{:S(2)}) collective-permute-start(f32[64,256]{1,0:T(8,128)S(1)} %leave.1.refs_10_), channel_id=1, source_target_pairs={{0,2},{1,3},{2,0},{3,1},{4,6},{5,7},{6,4},{7,5},{8,10},{9,11},{10,... | collective-permute-start | bytes 196616 | tf_op jit(solution)/shard_map/ppermute | solution.py:68
  43.5 3.1 %collective-permute-start.16 = (f32[64,256]{1,0:T(8,128)S(1)}, f32[64,256]{1,0:T(8,128)S(1)}, u32[]{:S(2)}, u32[]{:S(2)}) collective-permute-start(f32[64,256]{1,0:T(8,128)S(1)} %leave.1.refs_10_), channel_id=1, source_target_pairs={{0,1},{1,0},{2,3},{3,2},{4,5},{5,4},{6,7},{7,6},{8,9},{9,8},{10,11... | collective-permute-start | bytes 196616 | tf_op jit(solution)/shard_map/ppermute | solution.py:68
  46.6 1.3 %collective-permute-start.18 = (f32[64,256]{1,0:T(8,128)S(1)}, f32[64,256]{1,0:T(8,128)S(1)}, u32[]{:S(2)}, u32[]{:S(2)}) collective-permute-start(f32[64,256]{1,0:T(8,128)S(1)} %collective-permute-done.17.refs_12_), channel_id=1, source_target_pairs={{0,1},{1,0},{2,3},{3,2},{4,5},{5,4},{6,7},{7,6},{8,9},{9,8},{10,11... | collective-permute-start | bytes 196616 | tf_op jit(solution)/shard_map/ppermute | solution.py:68

commit v18 on v16

--- a/solution.py
+++ b/solution.py
@@ -108,7 +108,7 @@
         ins = (upd_v, dinv_v, rhs_v) if k < first else (upd_n, dinv_n, rhs_n)
         group = [
             pltpu.make_async_copy(src.at[k], dst.at[k % first], sems.at[i, k])
-            for i, (src, dst) in enumerate(zip((upd_h, dinv_h, rhs_h), ins))
+            for i, (src, dst) in enumerate(zip((upd_h, rhs_h, dinv_h), (ins[0], ins[2], ins[1])))
         ]
         for c in group:
             c.start()

time: 52.6 us -> 52.6 us (level)
  no operation moved by 1% of the time
where the time goes in v18:
time: 52.6 us; the launch traced here: 52.4 us
  starting transfers between devices  19.3 us (37%)
  Pallas kernels  19.1 us (36%)
  waiting for transfers between devices  13.2 us (25%)
  between operations  0.76 us (1%)
    ppermute x16, starting transfers between devices, swap(): return lax.ppermute(x, axis, [(i, i ^ mask) for i in range(n)])  15.7 us
    pallas_call x14, Pallas kernels, call(): pl.pallas_call(kernel, name=name, in_specs=specs, out_specs=tuple((pl.Blo...  14.6 us
    ppermute x16, waiting for transfers between devices, swap(): return lax.ppermute(x, axis, [(i, i ^ mask) for i in range(n)])  10.4 us
    pallas_call x1, Pallas kernels, local_backward(): pl.pallas_call(lambda *refs: backward_kernel(nodes, fronts, *refs), name=...  4.54 us
    ppermute x2, starting transfers between devices, local(): blocks = [lax.ppermute(b, 'leaf', boundary) for b in ahead]  2.09 us
    ppermute x2, waiting for transfers between devices, local(): blocks = [lax.ppermute(b, 'leaf', boundary) for b in ahead]  1.73 us
    ppermute x1, starting transfers between devices, local(): came = lax.ppermute(message[0], 'leaf', boundary)  1.58 us
  transfers between devices with their start and end apart: 19, of which 10 were waited for; matrix products, arithmetic and copies ran while one was open for 0% of the time, Pallas kernels for 25%

profile of v18, /device:TPU:0, one launch (start us, length us, event | category | flops | bytes accessed | tf_op | source)
XLA Modules:
  0.0 52.4 jit_solution(10663348812358504876)
XLA Ops:
  0.6 0.9 %stack.1.refs_5_.refs_0_ = f32[2,64,256]{2,1,0:T(8,128)S(1)} custom-call(f32[64,256]{1,0:T(8,128)} %first.1, f32[64,256]{1,0:T(8,128)} %second.1), custom_call_target="tpu_custom_call" | custom-call | tf_op jit(solution)/shard_map/stack/pallas_call | solution.py:51
  1.5 3.0 %collective-permute-start.1 = (f32[2,64,256]{2,1,0:T(8,128)S(1)}, f32[2,64,256]{2,1,0:T(8,128)S(1)}, u32[]{:S(2)}, u32[]{:S(2)}) collective-permute-start(f32[2,64,256]{2,1,0:T(8,128)S(1)} %stack.1.refs_5_.refs_0_), channel_id=1, source_target_pairs={{0,2},{1,3},{2,0},{3,1},{4,6},{5,7},{6,4},{7,5},{8,10},{9,11},{10,... | collective-permute-start | bytes 393224 | tf_op jit(solution)/shard_map/ppermute | solution.py:68
  4.5 4.3 %prepare_first.1 = (f32[2,4,128,256]{3,2,1,0:T(8,128)S(1)}, bf16[4,256,256]{2,1,0:T(8,128)(2,1)S(1)}, bf16[4,256,256]{2,1,0:T(8,128)(2,1)S(1)}, bf16[4,256,256]{...) custom-call(s32[8,256]{1,0:T(8,128)} %refs_0_.3, ...), custom_call_target="tpu_custom_call" | custom-call | tf_op jit(solution)/shard_map/prepare_first/pallas_call | solution.py:51
  10.7 1.6 %collective-permute-start.3 = (f32[1,128,256]{2,1,0:T(8,128)S(1)}, f32[1,128,256]{2,1,0:T(8,128)S(1)}, u32[]{:S(2)}, u32[]{:S(2)}) collective-permute-start(f32[1,128,256]{2,1,0:T(8,128)S(1)} %get-tuple-element.69), channel_id=1, source_target_pairs={{0,4},{4,0},{8,12},{12,8},{16,20},{20,16},{24,28},{28,24},{1,5},{5... | collective-permute-start | bytes 393224 | tf_op jit(solution)/shard_map/ppermute | solution.py:68
  12.3 4.1 %local_forward.1 = (f32[8,256,256]{2,1,0:T(8,128)S(1)}, f32[128,256]{1,0:T(8,128)S(1)}, f32[128,256]{1,0:T(8,128)S(1)}) custom-call(s32[8]{0:T(128)} %refs_0_.5, f32[2,4,128,256]{3,2,1,0:T(8,128)S(1)} %get-tuple-element.50.refs_4_.refs_1_, f32[2,4,128,256]{3,2,1,0:T(8,128)S(1)} %get-tuple-element.55.refs_4_.refs_2_, ...), custom_call_target="tpu_custom_call" | custom-call | tf_op jit(solution)/shard_map/local_forward/pallas_call | solution.py:51
  17.0 0.8 %collective-permute-done.4.refs_1_ = f32[128,256]{1,0:T(8,128)S(1)} collective-permute-done((f32[128,256]{1,0:T(8,128)S(1)}, f32[128,256]{1,0:T(8,128)S(1)}, u32[]{:S(2)}, u32[]{:S(2)}) %collective-permute-start.4) | collective-permute-done | bytes 131104 | tf_op jit(solution)/shard_map/ppermute | solution.py:68
  18.7 1.0 %merge_0.1 = (f32[2,256,256]{2,1,0:T(8,128)S(1)}, f32[2,256,256]{2,1,0:T(8,128)S(1)}, bf16[2,256,256]{2,1,0:T(8,128)(2,1)S(1)}, bf16[2,256,256]{2,1,0:T(8,128)(2...) custom-call(f32[256,256]{1,0:T(8,128)S(1)} %get-tuple-element.66.ref, ...), custom_call_target="tpu_custom_call" | custom-call | tf_op jit(solution)/shard_map/merge_0/pallas_call | solution.py:51
  19.7 1.6 %collective-permute-start.8 = (f32[3,128,128]{2,1,0:T(8,128)S(1)}, f32[3,128,128]{2,1,0:T(8,128)S(1)}, u32[]{:S(2)}, u32[]{:S(2)}) collective-permute-start(f32[3,128,128]{2,1,0:T(8,128)S(1)} %get-tuple-element.82), channel_id=1, source_target_pairs={{0,8},{4,12},{8,0},{12,4},{16,24},{20,28},{24,16},{28,20},{1,9},{5... | collective-permute-start | bytes 589832 | tf_op jit(solution)/shard_map/ppermute | solution.py:68
  21.3 0.9 %collective-permute-done.5.other = f32[64,256]{1,0:T(8,128)S(1)} collective-permute-done((f32[64,256]{1,0:T(8,128)S(1)}, f32[64,256]{1,0:T(8,128)S(1)}, u32[]{:S(2)}, u32[]{:S(2)}) %collective-permute-start.5) | collective-permute-done | bytes 65568 | tf_op jit(solution)/shard_map/ppermute | solution.py:68
  22.7 1.6 %collective-permute-start.6 = (f32[128,256]{1,0:T(8,128)S(1)}, f32[128,256]{1,0:T(8,128)S(1)}, u32[]{:S(2)}, u32[]{:S(2)}) collective-permute-start(f32[128,256]{1,0:T(8,128)S(1)} %get-tuple-element.76.refs_1_), channel_id=1, source_target_pairs={{0,4},{4,0},{8,12},{12,8},{16,20},{20,16},{24,28},{28,24},{1,5},{5... | collective-permute-start | bytes 393224 | tf_op jit(solution)/shard_map/ppermute | solution.py:68
  24.2 1.6 %collective-permute-start.14 = (f32[2,128,128]{2,1,0:T(8,128)S(1)}, f32[2,128,128]{2,1,0:T(8,128)S(1)}, u32[]{:S(2)}, u32[]{:S(2)}) collective-permute-start(f32[2,128,128]{2,1,0:T(8,128)S(1)} %get-tuple-element.96), channel_id=1, source_target_pairs={{0,8},{4,12},{8,0},{12,4},{16,24},{20,28},{24,16},{28,20},{1,9},{5... | collective-permute-start | bytes 393224 | tf_op jit(solution)/shard_map/ppermute | solution.py:68
  25.8 1.9 %collective-permute-done.6.refs_2_ = f32[128,256]{1,0:T(8,128)S(1)} collective-permute-done((f32[128,256]{1,0:T(8,128)S(1)}, f32[128,256]{1,0:T(8,128)S(1)}, u32[]{:S(2)}, u32[]{:S(2)}) %collective-permute-start.6) | collective-permute-done | bytes 131104 | tf_op jit(solution)/shard_map/ppermute | solution.py:68
  28.1 1.6 %collective-permute-start.9 = (f32[64,256]{1,0:T(8,128)S(1)}, f32[64,256]{1,0:T(8,128)S(1)}, u32[]{:S(2)}, u32[]{:S(2)}) collective-permute-start(f32[64,256]{1,0:T(8,128)S(1)} %get-tuple-element.85), channel_id=1, source_target_pairs={{0,8},{4,12},{8,0},{12,4},{16,24},{20,28},{24,16},{28,20},{1,9},{5... | collective-permute-start | bytes 196616 | tf_op jit(solution)/shard_map/ppermute | solution.py:68
  30.5 1.6 %collective-permute-start.11 = (f32[2,128,128]{2,1,0:T(8,128)S(1)}, f32[2,128,128]{2,1,0:T(8,128)S(1)}, u32[]{:S(2)}, u32[]{:S(2)}) collective-permute-start(f32[2,128,128]{2,1,0:T(8,128)S(1)} %get-tuple-element.94), channel_id=1, source_target_pairs={{8,16},{12,20},{16,8},{20,12},{0,4},{4,0},{24,28},{28,24},{9,17},{... | collective-permute-start | bytes 393224 | tf_op jit(solution)/shard_map/ppermute | solution.py:612
  33.0 1.6 %collective-permute-start.10 = (f32[64,256]{1,0:T(8,128)S(1)}, f32[64,256]{1,0:T(8,128)S(1)}, u32[]{:S(2)}, u32[]{:S(2)}) collective-permute-start(f32[64,256]{1,0:T(8,128)S(1)} %get-tuple-element.93), channel_id=1, source_target_pairs={{8,16},{12,20},{16,8},{20,12},{0,4},{4,0},{24,28},{28,24},{9,17},{... | collective-permute-start | bytes 196616 | tf_op jit(solution)/shard_map/ppermute | solution.py:642
  34.6 1.7 %collective-permute-done.12.refs_3_ = f32[1,128,128]{2,1,0:T(8,128)S(1)} collective-permute-done((f32[1,128,128]{2,1,0:T(8,128)S(1)}, f32[1,128,128]{2,1,0:T(8,128)S(1)}, u32[]{:S(2)}, u32[]{:S(2)}) %collective-permute-start.12) | collective-permute-done | bytes 65568 | tf_op jit(solution)/shard_map/ppermute | solution.py:612
  36.3 1.0 %collective-permute-done.10.refs_1_ = f32[64,256]{1,0:T(8,128)S(1)} collective-permute-done((f32[64,256]{1,0:T(8,128)S(1)}, f32[64,256]{1,0:T(8,128)S(1)}, u32[]{:S(2)}, u32[]{:S(2)}) %collective-permute-start.10) | collective-permute-done | bytes 65568 | tf_op jit(solution)/shard_map/ppermute | solution.py:642
  37.6 1.5 %collective-permute-start.13 = (f32[64,256]{1,0:T(8,128)S(1)}, f32[64,256]{1,0:T(8,128)S(1)}, u32[]{:S(2)}, u32[]{:S(2)}) collective-permute-start(f32[64,256]{1,0:T(8,128)S(1)} %turn.1.refs_1_), channel_id=1, source_target_pairs={{0,8},{4,12},{8,0},{12,4},{16,24},{20,28},{24,16},{28,20},{1,9},{5... | collective-permute-start | bytes 196616 | tf_op jit(solution)/shard_map/ppermute | solution.py:68
  39.2 0.7 %last_merge.1.refs_3_ = bf16[2,256,256]{2,1,0:T(8,128)(2,1)S(1)} custom-call(f32[2,256,256]{2,1,0:T(8,128)S(1)} %get-tuple-element.87.refs_2_.refs_0_, f32[2,128,128]{2,1,0:T(8,128)S(1)} %collective-permute-done.14.refs_1_, f32[2,128,128]{2,1,0:T(8,128)S(1)} %collective-permute-done.15.refs_2_, bf16[2,256,256]{2,1,0:T(8,128)(2,1)S(1)} %get-tuple-element.89.refs_4_.refs_3_, ...), custom_call_target="tpu_custom_call" | custom-call | tf_op jit(solution)/shard_map/last_merge/pallas_call | solution.py:51
  39.9 2.0 %collective-permute-done.13.refs_2_ = f32[64,256]{1,0:T(8,128)S(1)} collective-permute-done((f32[64,256]{1,0:T(8,128)S(1)}, f32[64,256]{1,0:T(8,128)S(1)}, u32[]{:S(2)}, u32[]{:S(2)}) %collective-permute-start.13) | collective-permute-done | bytes 65568 | tf_op jit(solution)/shard_map/ppermute | solution.py:68
  42.3 1.2 %collective-permute-start.17 = (f32[64,256]{1,0:T(8,128)S(1)}, f32[64,256]{1,0:T(8,128)S(1)}, u32[]{:S(2)}, u32[]{:S(2)}) collective-permute-start(f32[64,256]{1,0:T(8,128)S(1)} %leave.1.refs_10_), channel_id=1, source_target_pairs={{0,2},{1,3},{2,0},{3,1},{4,6},{5,7},{6,4},{7,5},{8,10},{9,11},{10,... | collective-permute-start | bytes 196616 | tf_op jit(solution)/shard_map/ppermute | solution.py:68
  43.5 3.1 %collective-permute-done.17.refs_12_ = f32[64,256]{1,0:T(8,128)S(1)} collective-permute-done((f32[64,256]{1,0:T(8,128)S(1)}, f32[64,256]{1,0:T(8,128)S(1)}, u32[]{:S(2)}, u32[]{:S(2)}) %collective-permute-start.17) | collective-permute-done | bytes 65568 | tf_op jit(solution)/shard_map/ppermute | solution.py:68
  46.6 1.2 %collective-permute-done.18.refs_13_ = f32[64,256]{1,0:T(8,128)S(1)} collective-permute-done((f32[64,256]{1,0:T(8,128)S(1)}, f32[64,256]{1,0:T(8,128)S(1)}, u32[]{:S(2)}, u32[]{:S(2)}) %collective-permute-start.18) | collective-permute-done | bytes 65568 | tf_op jit(solution)/shard_map/ppermute | solution.py:68
  47.9 4.5 %local_backward.1 = (f32[8,256,256]{2,1,0:T(8,128)}, f32[64,256]{1,0:T(8,128)}) custom-call(s32[8]{0:T(128)} %refs_0_.5, f32[8,256,256]{2,1,0:T(8,128)S(1)} %get-tuple-element.67.refs_1_, bf16[4,256,256]{2,1,0:T(8,128)(2,1)S(1)} %get-tuple-element.57.refs_4_.refs_2_, bf16[4,256,256]{2,1,0:T(8,128)(2,1)S(1)} %get-tuple-element.58.refs_5_.refs_3_, ...), custom_call_target="tpu_custom_call" | custom-call | tf_op jit(solution)/shard_map/local_backward/pallas_call | solution.py:278
  (29 shorter events, 6.4 us)
Async XLA Ops:
  1.5 7.3 %collective-permute-start.1 = (f32[2,64,256]{2,1,0:T(8,128)S(1)}, f32[2,64,256]{2,1,0:T(8,128)S(1)}, u32[]{:S(2)}, u32[]{:S(2)}) collective-permute-start(f32[2,64,256]{2,1,0:T(8,128)S(1)} %stack.1.refs_5_.refs_0_), channel_id=1, source_target_pairs={{0,2},{1,3},{2,0},{3,1},{4,6},{5,7},{6,4},{7,5},{8,10},{9,11},{10,... | collective-permute-start | bytes 393224 | tf_op jit(solution)/shard_map/ppermute | solution.py:68
  4.5 5.5 %collective-permute-start = (f32[2,64,256]{2,1,0:T(8,128)S(1)}, f32[2,64,256]{2,1,0:T(8,128)S(1)}, u32[]{:S(2)}, u32[]{:S(2)}) collective-permute-start(f32[2,64,256]{2,1,0:T(8,128)S(1)} %stack.1.refs_5_.refs_0_), channel_id=1, source_target_pairs={{0,1},{1,0},{2,3},{3,2},{4,5},{5,4},{6,7},{7,6},{8,9},{9,8},{10,11... | collective-permute-start | bytes 393224 | tf_op jit(solution)/shard_map/ppermute | solution.py:68
  8.8 1.6 %collective-permute-start.2 = (f32[2,64,256]{2,1,0:T(8,128)S(1)}, f32[2,64,256]{2,1,0:T(8,128)S(1)}, u32[]{:S(2)}, u32[]{:S(2)}) collective-permute-start(f32[2,64,256]{2,1,0:T(8,128)S(1)} %collective-permute-done.1.refs_2_), channel_id=1, source_target_pairs={{0,1},{1,0},{2,3},{3,2},{4,5},{5,4},{6,7},{7,6},{8,9},{9,8},{10,11... | collective-permute-start | bytes 393224 | tf_op jit(solution)/shard_map/ppermute | solution.py:68
  10.7 5.8 %collective-permute-start.3 = (f32[1,128,256]{2,1,0:T(8,128)S(1)}, f32[1,128,256]{2,1,0:T(8,128)S(1)}, u32[]{:S(2)}, u32[]{:S(2)}) collective-permute-start(f32[1,128,256]{2,1,0:T(8,128)S(1)} %get-tuple-element.69), channel_id=1, source_target_pairs={{0,4},{4,0},{8,12},{12,8},{16,20},{20,16},{24,28},{28,24},{1,5},{5... | collective-permute-start | bytes 393224 | tf_op jit(solution)/shard_map/ppermute | solution.py:68
  16.5 1.3 %collective-permute-start.4 = (f32[128,256]{1,0:T(8,128)S(1)}, f32[128,256]{1,0:T(8,128)S(1)}, u32[]{:S(2)}, u32[]{:S(2)}) collective-permute-start(f32[128,256]{1,0:T(8,128)S(1)} %get-tuple-element.71), channel_id=1, source_target_pairs={{0,1},{1,0},{2,3},{3,2},{4,5},{5,4},{6,7},{7,6},{8,9},{9,8},{10,11... | collective-permute-start | bytes 393224 | tf_op jit(solution)/shard_map/ppermute | solution.py:68
  16.5 2.1 %collective-permute-start.7 = (f32[1,128,256]{2,1,0:T(8,128)S(1)}, f32[1,128,256]{2,1,0:T(8,128)S(1)}, u32[]{:S(2)}, u32[]{:S(2)}) collective-permute-start(f32[1,128,256]{2,1,0:T(8,128)S(1)} %collective-permute-done.3.refs_1_), channel_id=1, source_target_pairs={{0,1},{1,0},{2,3},{3,2},{4,5},{5,4},{6,7},{7,6},{8,9},{9,8},{10,11... | collective-permute-start | bytes 393224 | tf_op jit(solution)/shard_map/ppermute | solution.py:68
  17.9 4.3 %collective-permute-start.5 = (f32[64,256]{1,0:T(8,128)S(1)}, f32[64,256]{1,0:T(8,128)S(1)}, u32[]{:S(2)}, u32[]{:S(2)}) collective-permute-start(f32[64,256]{1,0:T(8,128)S(1)} %get-tuple-element.73.refs_3_), channel_id=1, source_target_pairs={{0,2},{1,3},{2,0},{3,1},{4,6},{5,7},{6,4},{7,5},{8,10},{9,11},{10,... | collective-permute-start | bytes 196616 | tf_op jit(solution)/shard_map/ppermute | solution.py:68
  19.7 8.0 %collective-permute-start.8 = (f32[3,128,128]{2,1,0:T(8,128)S(1)}, f32[3,128,128]{2,1,0:T(8,128)S(1)}, u32[]{:S(2)}, u32[]{:S(2)}) collective-permute-start(f32[3,128,128]{2,1,0:T(8,128)S(1)} %get-tuple-element.82), channel_id=1, source_target_pairs={{0,8},{4,12},{8,0},{12,4},{16,24},{20,28},{24,16},{28,20},{1,9},{5... | collective-permute-start | bytes 589832 | tf_op jit(solution)/shard_map/ppermute | solution.py:68
  22.7 5.0 %collective-permute-start.6 = (f32[128,256]{1,0:T(8,128)S(1)}, f32[128,256]{1,0:T(8,128)S(1)}, u32[]{:S(2)}, u32[]{:S(2)}) collective-permute-start(f32[128,256]{1,0:T(8,128)S(1)} %get-tuple-element.76.refs_1_), channel_id=1, source_target_pairs={{0,4},{4,0},{8,12},{12,8},{16,20},{20,16},{24,28},{28,24},{1,5},{5... | collective-permute-start | bytes 393224 | tf_op jit(solution)/shard_map/ppermute | solution.py:68
  24.2 10.3 %collective-permute-start.14 = (f32[2,128,128]{2,1,0:T(8,128)S(1)}, f32[2,128,128]{2,1,0:T(8,128)S(1)}, u32[]{:S(2)}, u32[]{:S(2)}) collective-permute-start(f32[2,128,128]{2,1,0:T(8,128)S(1)} %get-tuple-element.96), channel_id=1, source_target_pairs={{0,8},{4,12},{8,0},{12,4},{16,24},{20,28},{24,16},{28,20},{1,9},{5... | collective-permute-start | bytes 393224 | tf_op jit(solution)/shard_map/ppermute | solution.py:68
  28.1 4.4 %collective-permute-start.9 = (f32[64,256]{1,0:T(8,128)S(1)}, f32[64,256]{1,0:T(8,128)S(1)}, u32[]{:S(2)}, u32[]{:S(2)}) collective-permute-start(f32[64,256]{1,0:T(8,128)S(1)} %get-tuple-element.85), channel_id=1, source_target_pairs={{0,8},{4,12},{8,0},{12,4},{16,24},{20,28},{24,16},{28,20},{1,9},{5... | collective-permute-start | bytes 196616 | tf_op jit(solution)/shard_map/ppermute | solution.py:68
  30.5 6.9 %collective-permute-start.11 = (f32[2,128,128]{2,1,0:T(8,128)S(1)}, f32[2,128,128]{2,1,0:T(8,128)S(1)}, u32[]{:S(2)}, u32[]{:S(2)}) collective-permute-start(f32[2,128,128]{2,1,0:T(8,128)S(1)} %get-tuple-element.94), channel_id=1, source_target_pairs={{8,16},{12,20},{16,8},{20,12},{0,4},{4,0},{24,28},{28,24},{9,17},{... | collective-permute-start | bytes 393224 | tf_op jit(solution)/shard_map/ppermute | solution.py:612
  32.1 4.3 %collective-permute-start.12 = (f32[1,128,128]{2,1,0:T(8,128)S(1)}, f32[1,128,128]{2,1,0:T(8,128)S(1)}, u32[]{:S(2)}, u32[]{:S(2)}) collective-permute-start(f32[1,128,128]{2,1,0:T(8,128)S(1)} %get-tuple-element.95), channel_id=1, source_target_pairs={{8,16},{12,20},{16,8},{20,12},{0,4},{4,0},{24,28},{28,24},{9,17},{... | collective-permute-start | bytes 196616 | tf_op jit(solution)/shard_map/ppermute | solution.py:612
  33.0 4.3 %collective-permute-start.10 = (f32[64,256]{1,0:T(8,128)S(1)}, f32[64,256]{1,0:T(8,128)S(1)}, u32[]{:S(2)}, u32[]{:S(2)}) collective-permute-start(f32[64,256]{1,0:T(8,128)S(1)} %get-tuple-element.93), channel_id=1, source_target_pairs={{8,16},{12,20},{16,8},{20,12},{0,4},{4,0},{24,28},{28,24},{9,17},{... | collective-permute-start | bytes 196616 | tf_op jit(solution)/shard_map/ppermute | solution.py:642
  34.6 4.6 %collective-permute-start.15 = (f32[2,128,128]{2,1,0:T(8,128)S(1)}, f32[2,128,128]{2,1,0:T(8,128)S(1)}, u32[]{:S(2)}, u32[]{:S(2)}) collective-permute-start(f32[2,128,128]{2,1,0:T(8,128)S(1)} %collective-permute-done.14.refs_1_), channel_id=1, source_target_pairs={{0,1},{1,0},{2,3},{3,2},{4,5},{5,4},{6,7},{7,6},{8,9},{9,8},{10,11... | collective-permute-start | bytes 393224 | tf_op jit(solution)/shard_map/ppermute | solution.py:68
  37.6 4.3 %collective-permute-start.13 = (f32[64,256]{1,0:T(8,128)S(1)}, f32[64,256]{1,0:T(8,128)S(1)}, u32[]{:S(2)}, u32[]{:S(2)}) collective-permute-start(f32[64,256]{1,0:T(8,128)S(1)} %turn.1.refs_1_), channel_id=1, source_target_pairs={{0,8},{4,12},{8,0},{12,4},{16,24},{20,28},{24,16},{28,20},{1,9},{5... | collective-permute-start | bytes 196616 | tf_op jit(solution)/shard_map/ppermute | solution.py:68
  42.3 4.3 %collective-permute-start.17 = (f32[64,256]{1,0:T(8,128)S(1)}, f32[64,256]{1,0:T(8,128)S(1)}, u32[]{:S(2)}, u32[]{:S(2)}) collective-permute-start(f32[64,256]{1,0:T(8,128)S(1)} %leave.1.refs_10_), channel_id=1, source_target_pairs={{0,2},{1,3},{2,0},{3,1},{4,6},{5,7},{6,4},{7,5},{8,10},{9,11},{10,... | collective-permute-start | bytes 196616 | tf_op jit(solution)/shard_map/ppermute | solution.py:68
  43.5 3.1 %collective-permute-start.16 = (f32[64,256]{1,0:T(8,128)S(1)}, f32[64,256]{1,0:T(8,128)S(1)}, u32[]{:S(2)}, u32[]{:S(2)}) collective-permute-start(f32[64,256]{1,0:T(8,128)S(1)} %leave.1.refs_10_), channel_id=1, source_target_pairs={{0,1},{1,0},{2,3},{3,2},{4,5},{5,4},{6,7},{7,6},{8,9},{9,8},{10,11... | collective-permute-start | bytes 196616 | tf_op jit(solution)/shard_map/ppermute | solution.py:68
  46.6 1.3 %collective-permute-start.18 = (f32[64,256]{1,0:T(8,128)S(1)}, f32[64,256]{1,0:T(8,128)S(1)}, u32[]{:S(2)}, u32[]{:S(2)}) collective-permute-start(f32[64,256]{1,0:T(8,128)S(1)} %collective-permute-done.17.refs_12_), channel_id=1, source_target_pairs={{0,1},{1,0},{2,3},{3,2},{4,5},{5,4},{6,7},{7,6},{8,9},{9,8},{10,11... | collective-permute-start | bytes 196616 | tf_op jit(solution)/shard_map/ppermute | solution.py:68
